TPU v7x, 32 devices: a whole 2x2x4 slice. The times are simulated.
32 devices in a mesh: dp: 8 (over z, x), vocab: 4 (over y, core).
Axes of the slice: x: 2, y: 2, z: 4, core: 2. Of those that a mesh axis runs over, the one named last changes fastest.
Arguments:
- token_ids: int32 [32, 1024], P(('dp', 'vocab')), may hold values from 0 to 51199
- scored: int32 [32, 512], P(('dp', 'vocab')), may hold values from 0 to 1023, as said below
- lengths: int32 [32], P(('dp', 'vocab')), may hold values from 768 to 1024, as said below
- times: int32 [32], P(('dp', 'vocab')), may hold values from 0 to 19
- step_count: int32 [1], replicated, may hold values from 1 to 20
- layer_w: float32 [768, 9216], P(('dp', 'vocab'))
- layer_m: float32 [768, 9216], P(('dp', 'vocab')), may hold values from -1.1444092e-05 to 1.1444092e-05
- layer_v: float32 [768, 9216], P(('dp', 'vocab')), may hold values from 8.477105e-12 to 1.3693785e-10
- layer_ema: float32 [768, 9216], P(('dp', 'vocab'))
- ada_w: float32 [128, 4608], P(('dp', 'vocab')), may hold values from -1 to 1
- ada_m: float32 [128, 4608], P(('dp', 'vocab')), may hold values from -1.1444092e-05 to 1.1444092e-05
- ada_v: float32 [128, 4608], P(('dp', 'vocab')), may hold values from 8.477105e-12 to 1.3693785e-10
- ada_ema: float32 [128, 4608], P(('dp', 'vocab')), may hold values from -1 to 1
- gains_w: float32 [4, 768], P(None, ('dp', 'vocab'))
- gains_m: float32 [4, 768], P(None, ('dp', 'vocab')), may hold values from -4.5776367e-05 to 4.5776367e-05
- gains_v: float32 [4, 768], P(None, ('dp', 'vocab')), may hold values from 1.3563368e-10 to 2.1910056e-09
- gains_ema: float32 [4, 768], P(None, ('dp', 'vocab'))
- embed_w: float32 [51200, 768], P('vocab', 'dp'), may hold values from -6 to 6
- embed_m: float32 [51200, 768], P('vocab', 'dp'), may hold values from -4.7683716e-07 to 4.7683716e-07
- embed_v: float32 [51200, 768], P('vocab', 'dp'), may hold values from 1.3563368e-14 to 2.1910056e-13
- embed_ema: float32 [51200, 768], P('vocab', 'dp'), may hold values from -6 to 6
- head_w: float32 [768, 51200], P('dp', 'vocab'), may hold values from -0.5 to 0.5
- head_m: float32 [768, 51200], P('dp', 'vocab'), may hold values from -4.7683716e-07 to 4.7683716e-07
- head_v: float32 [768, 51200], P('dp', 'vocab'), may hold values from 1.3563368e-14 to 2.1910056e-13
- head_ema: float32 [768, 51200], P('dp', 'vocab'), may hold values from -0.5 to 0.5
Outputs:
- loss: float32 [], replicated
- grad_norm: float32 [], replicated
- layer_first: float32 [768, 9216], P(('dp', 'vocab'))
- layer_second: float32 [768, 9216], P(('dp', 'vocab'))
- layer_new: float32 [768, 9216], P(('dp', 'vocab'))
- layer_avg: float32 [768, 9216], P(('dp', 'vocab'))
- ada_first: float32 [128, 4608], P(('dp', 'vocab'))
- ada_second: float32 [128, 4608], P(('dp', 'vocab'))
- ada_new: float32 [128, 4608], P(('dp', 'vocab'))
- ada_avg: float32 [128, 4608], P(('dp', 'vocab'))
- gains_first: float32 [4, 768], P(None, ('dp', 'vocab'))
- gains_second: float32 [4, 768], P(None, ('dp', 'vocab'))
- gains_new: float32 [4, 768], P(None, ('dp', 'vocab'))
- gains_avg: float32 [4, 768], P(None, ('dp', 'vocab'))
- embed_first: float32 [51200, 768], P('vocab', 'dp')
- embed_second: float32 [51200, 768], P('vocab', 'dp')
- embed_new: float32 [51200, 768], P('vocab', 'dp')
- embed_avg: float32 [51200, 768], P('vocab', 'dp')
- head_first: float32 [768, 51200], P('dp', 'vocab')
- head_second: float32 [768, 51200], P('dp', 'vocab')
- head_new: float32 [768, 51200], P('dp', 'vocab')
- head_avg: float32 [768, 51200], P('dp', 'vocab')
Inputs may be any that keep to these rules, and one draw needn't show every extreme that they name: `lengths`: each sequence has at least 768 tokens; the first sequence has exactly 1024. `scored`: each row holds 512 distinct positions in ascending order, each below that sequence's length.
All inputs are finite; a program needn't handle non-finite values.
Results may differ from a plain program's by a relative error of at most 0.0044.
The roundings to bfloat16 on the way count: a program that leaves them out, or rounds other values in their place, can miss the bound.
Values may be sent and summed in bfloat16 or wider, within the bound.
A program may use at most 448 MiB of HBM per device.

v0:
```python
import math

import jax
import jax.numpy as jnp
from jax import lax
from jax.sharding import PartitionSpec as P

D = 768
H = 12
HD = 64
FF = 3072
C = 128
TSTEPS = 20


NORM_EPS = 1e-05
CLIP_NORM = 0.05
BETA_ONE = 0.9
BETA_TWO = 0.95
ADAM_EPS = 1e-08
EMA_DECAY = 0.9999
LEARN_RATES = (0.03, 0.1, 0.1, 0.5, 0.05)
WEIGHT_DECAYS = (0.01, 0.01, 0.0, 0.01, 0.01)


def joined(x, axis, combine):
    everything = jax.tree.map(lambda part: lax.all_gather(part, axis), x)
    initial = jax.tree.map(lambda part: part[0], everything)

    def step(k, so_far):
        return combine(so_far, jax.tree.map(lambda part: part[k], everything))

    return lax.fori_loop(1, lax.axis_size(axis), step, initial)


def layer_norm(values):
    center = values - jnp.mean(values, axis=-1, keepdims=True)
    spread = jnp.mean(center * center, axis=-1, keepdims=True)
    inv_std = lax.rsqrt(spread + NORM_EPS)
    return (center * inv_std, inv_std)


def norm_back(d_normed, normed, inv_std):
    return inv_std * (
        d_normed
        - jnp.mean(d_normed, axis=-1, keepdims=True)
        - normed * jnp.mean(d_normed * normed, axis=-1, keepdims=True)
    )


def time_features(time_index, width, steps):
    t_value = (time_index.astype(jnp.float32) + 1.0) / steps
    half_width = width // 2
    frequencies = jnp.exp(
        -math.log(10000.0) * jnp.arange(half_width, dtype=jnp.float32) / half_width
    )
    angles = 1000.0 * t_value[:, None] * frequencies[None, :]
    return jax.nn.silu(jnp.concatenate([jnp.cos(angles), jnp.sin(angles)], axis=1))


def rope_tables(length, head_size):
    half_size = head_size // 2
    inverse = jnp.exp(
        -math.log(10000.0) * jnp.arange(half_size, dtype=jnp.float32) * 2.0 / head_size
    )
    angles = jnp.arange(length, dtype=jnp.float32)[:, None] * inverse[None, :]
    return (jnp.cos(angles)[:, None, :], jnp.sin(angles)[:, None, :])


def rotate(values, cosine_table, sine_table):
    half_size = values.shape[-1] // 2
    front_half = values[..., :half_size]
    back_half = values[..., half_size:]
    return jnp.concatenate(
        [
            front_half * cosine_table - back_half * sine_table,
            back_half * cosine_table + front_half * sine_table,
        ],
        axis=-1,
    )


def unrotate(grads, cosine_table, sine_table):
    half_size = grads.shape[-1] // 2
    front_half = grads[..., :half_size]
    back_half = grads[..., half_size:]
    return jnp.concatenate(
        [
            front_half * cosine_table + back_half * sine_table,
            back_half * cosine_table - front_half * sine_table,
        ],
        axis=-1,
    )


def gelu_tanh(values):
    return jax.nn.gelu(values, approximate=True)


def expand_rows(values, length):
    seq_count, width = values.shape
    return jnp.broadcast_to(values[:, None, :], (seq_count, length, width)).reshape(
        seq_count * length, width
    )


def sequence_sums(values, length):
    return jnp.sum(values.reshape(-1, length, values.shape[1]), axis=1)


def to_blocks(values, block_size):
    seq_count, length = (values.shape[0], values.shape[1])
    return jnp.moveaxis(
        values.reshape((seq_count, length // block_size, block_size) + values.shape[2:]), 1, 0
    )


def block_scores(query_block, key_vecs, key_valid):
    scores = jnp.einsum(
        "sqhd,skhd->shqk", query_block, key_vecs, preferred_element_type=jnp.float32
    ) * HD ** (-0.5)
    return jnp.where(key_valid[:, None, None, :], scores, -1e30)


def attend(queries, key_vecs, value_vecs, key_valid):
    seq_count, length = (queries.shape[0], queries.shape[1])
    block_size = min(512, length)

    def one_block(query_block):
        scores = block_scores(query_block, key_vecs, key_valid)
        row_max = jnp.max(scores, axis=-1, keepdims=True)
        weights = jnp.exp(scores - row_max)
        row_total = jnp.sum(weights, axis=-1, keepdims=True)
        probabilities = (weights / row_total).astype(jnp.bfloat16)
        mixed_out = jnp.einsum(
            "shqk,skhd->sqhd", probabilities, value_vecs, preferred_element_type=jnp.float32
        )
        return (mixed_out, (row_max + jnp.log(row_total))[..., 0])

    mixed_out, log_totals = lax.map(one_block, to_blocks(queries, block_size))
    return (jnp.moveaxis(mixed_out, 0, 1).reshape(seq_count, length, H, HD), log_totals)


def attend_back(queries, key_vecs, value_vecs, key_valid, log_totals, d_mixed):
    seq_count, length = (queries.shape[0], queries.shape[1])
    block_size = min(512, length)

    def one_block(carry, block_items):
        d_keys, d_values = carry
        query_block, d_block, total_block = block_items
        scores = block_scores(query_block, key_vecs, key_valid)
        probabilities = jnp.exp(scores - total_block[..., None])
        d_probs = jnp.einsum(
            "sqhd,skhd->shqk", d_block, value_vecs, preferred_element_type=jnp.float32
        )
        inner = jnp.sum(probabilities * d_probs, axis=-1, keepdims=True)
        d_scores = (probabilities * (d_probs - inner) * HD ** (-0.5)).astype(jnp.bfloat16)
        d_query = jnp.einsum(
            "shqk,skhd->sqhd", d_scores, key_vecs, preferred_element_type=jnp.float32
        )
        d_keys = d_keys + jnp.einsum(
            "shqk,sqhd->skhd", d_scores, query_block, preferred_element_type=jnp.float32
        )
        d_values = d_values + jnp.einsum(
            "shqk,sqhd->skhd",
            probabilities.astype(jnp.bfloat16),
            d_block,
            preferred_element_type=jnp.float32,
        )
        return ((d_keys, d_values), d_query)

    zero_grads = jnp.zeros(queries.shape, jnp.float32)
    (d_keys, d_values), d_queries = lax.scan(
        one_block,
        (zero_grads, zero_grads),
        (to_blocks(queries, block_size), to_blocks(d_mixed, block_size), log_totals),
    )
    return (jnp.moveaxis(d_queries, 0, 1).reshape(seq_count, length, H, HD), d_keys, d_values)


def split_mods(mod_rows):
    return [mod_rows[:, part_index * D : (part_index + 1) * D] for part_index in range(6)]


def layer_forward(hidden0, mod_rows, weights, gains, cosine_table, sine_table, key_valid):
    seq_count, length = key_valid.shape
    shift_a, scale_a, gate_a, shift_m, scale_m, gate_m = split_mods(mod_rows)
    normed_a, inv_a = layer_norm(hidden0)
    att_in = (normed_a * gains[0] * (1.0 + scale_a) + shift_a).astype(jnp.bfloat16)
    qkv_raw = jnp.dot(att_in, weights[:, : 3 * D], preferred_element_type=jnp.float32).reshape(
        seq_count, length, 3, H, HD
    )
    queries = rotate(qkv_raw[:, :, 0], cosine_table, sine_table).astype(jnp.bfloat16)
    key_vecs = rotate(qkv_raw[:, :, 1], cosine_table, sine_table).astype(jnp.bfloat16)
    value_vecs = qkv_raw[:, :, 2].astype(jnp.bfloat16)
    mixed_out, log_totals = attend(queries, key_vecs, value_vecs, key_valid)
    att_out = mixed_out.astype(jnp.bfloat16).reshape(seq_count * length, D)
    branch = jnp.dot(att_out, weights[:, 3 * D : 4 * D], preferred_element_type=jnp.float32)
    hidden1 = hidden0 + gate_a * branch
    normed_m, inv_m = layer_norm(hidden1)
    mlp_in = (normed_m * gains[1] * (1.0 + scale_m) + shift_m).astype(jnp.bfloat16)
    pre_act = jnp.dot(mlp_in, weights[:, 4 * D : 4 * D + FF], preferred_element_type=jnp.float32)
    activation = gelu_tanh(pre_act).astype(jnp.bfloat16)
    mlp_out = jnp.einsum(
        "rf,df->rd", activation, weights[:, 4 * D + FF :], preferred_element_type=jnp.float32
    )
    hidden2 = hidden1 + gate_m * mlp_out
    saved = (
        normed_a,
        inv_a,
        att_in,
        queries,
        key_vecs,
        value_vecs,
        log_totals,
        att_out,
        branch,
        normed_m,
        inv_m,
        mlp_in,
        pre_act,
        activation,
        mlp_out,
    )
    return (hidden2, saved)


def layer_backward(d_hidden2, saved, mod_rows, weights, gains, cosine_table, sine_table, key_valid):
    (
        normed_a,
        inv_a,
        att_in,
        queries,
        key_vecs,
        value_vecs,
        log_totals,
        att_out,
        branch,
        normed_m,
        inv_m,
        mlp_in,
        pre_act,
        activation,
        mlp_out,
    ) = saved
    seq_count, length = key_valid.shape
    shift_a, scale_a, gate_a, shift_m, scale_m, gate_m = split_mods(mod_rows)
    d_gate_m = d_hidden2 * mlp_out
    d_out = (d_hidden2 * gate_m).astype(jnp.bfloat16)
    d_down = jnp.einsum("rd,rf->df", d_out, activation, preferred_element_type=jnp.float32)
    d_activ = jnp.einsum(
        "rd,df->rf", d_out, weights[:, 4 * D + FF :], preferred_element_type=jnp.float32
    )
    gelu_value, gelu_pull = jax.vjp(gelu_tanh, pre_act)
    d_pre = gelu_pull(d_activ)[0].astype(jnp.bfloat16)
    d_up = jnp.einsum("rd,rf->df", mlp_in, d_pre, preferred_element_type=jnp.float32)
    d_mlp_in = jnp.einsum(
        "rf,df->rd", d_pre, weights[:, 4 * D : 4 * D + FF], preferred_element_type=jnp.float32
    )
    d_scale_m = d_mlp_in * (normed_m * gains[1])
    d_normed_m = d_mlp_in * (1.0 + scale_m)
    d_gain_m = jnp.sum(d_normed_m * normed_m, axis=0)
    d_hidden1 = d_hidden2 + norm_back(d_normed_m * gains[1], normed_m, inv_m)
    d_gate_a = d_hidden1 * branch
    d_branch = (d_hidden1 * gate_a).astype(jnp.bfloat16)
    d_wout = jnp.einsum("rd,re->de", att_out, d_branch, preferred_element_type=jnp.float32)
    d_mixed = jnp.einsum(
        "re,de->rd", d_branch, weights[:, 3 * D : 4 * D], preferred_element_type=jnp.float32
    )
    d_mixed = d_mixed.astype(jnp.bfloat16).reshape(seq_count, length, H, HD)
    d_queries, d_keys, d_values = attend_back(
        queries, key_vecs, value_vecs, key_valid, log_totals, d_mixed
    )
    d_qkv = jnp.stack(
        [
            unrotate(d_queries, cosine_table, sine_table),
            unrotate(d_keys, cosine_table, sine_table),
            d_values,
        ],
        axis=2,
    )
    d_qkv = d_qkv.astype(jnp.bfloat16).reshape(seq_count * length, 3 * D)
    d_wqkv = jnp.einsum("rd,re->de", att_in, d_qkv, preferred_element_type=jnp.float32)
    d_att_in = jnp.einsum(
        "re,de->rd", d_qkv, weights[:, : 3 * D], preferred_element_type=jnp.float32
    )
    d_scale_a = d_att_in * (normed_a * gains[0])
    d_normed_a = d_att_in * (1.0 + scale_a)
    d_gain_a = jnp.sum(d_normed_a * normed_a, axis=0)
    d_hidden0 = d_hidden1 + norm_back(d_normed_a * gains[0], normed_a, inv_a)
    d_mod = sequence_sums(
        jnp.concatenate([d_att_in, d_scale_a, d_gate_a, d_mlp_in, d_scale_m, d_gate_m], axis=1),
        length,
    )
    d_weights = jnp.concatenate([d_wqkv, d_wout, d_up, d_down], axis=1)
    return (d_hidden0, d_weights, d_mod, jnp.stack([d_gain_a, d_gain_m]))


def adam_step(weight, first, second, ema_copy, gradient, step_value, learn_rate, decay_rate):
    first_new = BETA_ONE * first + (1.0 - BETA_ONE) * gradient
    second_new = BETA_TWO * second + (1.0 - BETA_TWO) * gradient * gradient
    first_hat = first_new / (1.0 - BETA_ONE**step_value)
    second_hat = second_new / (1.0 - BETA_TWO**step_value)
    weight_new = weight - learn_rate * (
        first_hat / (jnp.sqrt(second_hat) + ADAM_EPS) + decay_rate * weight
    )
    ema_rate = jnp.minimum(EMA_DECAY, (1.0 + step_value) / (10.0 + step_value))
    ema_new = ema_rate * ema_copy + (1.0 - ema_rate) * weight_new
    return (first_new, second_new, weight_new, ema_new)


def combine_stats(earlier, later):
    row_max = jnp.maximum(earlier[0], later[0])
    row_total = earlier[1] * jnp.exp(earlier[0] - row_max) + later[1] * jnp.exp(later[0] - row_max)
    return (row_max, row_total, earlier[2] + later[2])


def local(
    token_ids,
    scored,
    lengths,
    times,
    step_count,
    layer_w,
    layer_m,
    layer_v,
    layer_ema,
    ada_w,
    ada_m,
    ada_v,
    ada_ema,
    gains_w,
    gains_m,
    gains_v,
    gains_ema,
    embed_w,
    embed_m,
    embed_v,
    embed_ema,
    head_w,
    head_m,
    head_v,
    head_ema,
):
    seq_count, length = token_ids.shape
    score_count = scored.shape[1]
    group_size = lax.axis_size("vocab")
    vocab_rows = embed_w.shape[0]
    vocab_start = lax.axis_index("vocab") * vocab_rows
    total_rows = seq_count * score_count * lax.axis_size("dp") * group_size
    is_scored = jnp.any(
        scored[:, :, None] == jnp.arange(length, dtype=jnp.int32)[None, None, :], axis=1
    )
    input_ids = jnp.where(is_scored, -1, token_ids)
    targets = jnp.take_along_axis(token_ids, scored, axis=1)
    layer_all, ada_all, gains_all = (
        lax.all_gather(layer_w.astype(jnp.bfloat16), ("dp", "vocab"), axis=0, tiled=True),
        lax.all_gather(ada_w.astype(jnp.bfloat16), ("dp", "vocab"), axis=0, tiled=True),
        lax.all_gather(gains_w.astype(jnp.bfloat16), ("dp", "vocab"), axis=1, tiled=True),
    )
    gains_float = gains_all.astype(jnp.float32)
    embed_all, head_all = (
        lax.all_gather(embed_w.astype(jnp.bfloat16), "dp", axis=1, tiled=True),
        lax.all_gather(head_w.astype(jnp.bfloat16), "dp", axis=0, tiled=True),
    )
    group_inputs, group_targets, group_times = (
        lax.all_gather(input_ids, "vocab", axis=0, tiled=True),
        lax.all_gather(targets, "vocab", axis=0, tiled=True),
        lax.all_gather(times, "vocab", axis=0, tiled=True),
    )
    flat_inputs = jnp.where(
        group_inputs.reshape(-1) < 0, -1 - vocab_rows, group_inputs.reshape(-1) - vocab_start
    )
    inside_inputs = (flat_inputs >= 0) & (flat_inputs < vocab_rows)
    masked_rows = is_scored.reshape(-1)
    local_ids = flat_inputs
    inside = (local_ids >= 0) & (local_ids < vocab_rows)
    picked = jnp.take(embed_all, jnp.clip(local_ids, 0, vocab_rows - 1), axis=0).astype(jnp.float32)
    table_part = lax.psum_scatter(
        jnp.where(inside[:, None], picked, 0.0).astype(jnp.bfloat16),
        "vocab",
        scatter_dimension=0,
        tiled=True,
    ).astype(jnp.float32)
    hidden0 = jnp.where(masked_rows[:, None], gains_float[3][None, :], table_part)
    condition = time_features(times, C, TSTEPS).astype(jnp.bfloat16)
    modulation = jnp.dot(condition, ada_all, preferred_element_type=jnp.float32)
    mod_rows = expand_rows(modulation, length)
    cosine_table, sine_table = rope_tables(length, HD)
    key_valid = jnp.arange(length, dtype=jnp.int32)[None, :] < lengths[:, None]
    hidden2, saved = layer_forward(
        hidden0, mod_rows, layer_all, gains_float, cosine_table, sine_table, key_valid
    )
    flat_positions = (jnp.arange(seq_count, dtype=jnp.int32)[:, None] * length + scored).reshape(-1)
    picked = jnp.take(hidden2, flat_positions, axis=0)
    normed_f, inv_f = layer_norm(picked)
    final_rows = (normed_f * gains_float[2]).astype(jnp.bfloat16)
    group_rows = lax.all_gather(final_rows, "vocab", axis=0, tiled=True)
    group_count = group_rows.shape[0]
    tile_size = min(512, group_count)
    tile_count = group_count // tile_size
    tiled_rows = group_rows.reshape(tile_count, tile_size, D)
    local_targets = (group_targets.reshape(-1) - vocab_start).reshape(tile_count, tile_size)
    row_weights = jnp.repeat(
        TSTEPS / (group_times.astype(jnp.float32) + 1.0) / total_rows, score_count
    )

    def tile_stats(tile_items):
        rows_tile, local_ids = tile_items
        logits = jnp.dot(rows_tile, head_all, preferred_element_type=jnp.float32)
        row_max = jnp.max(logits, axis=1)
        row_total = jnp.sum(jnp.exp(logits - row_max[:, None]), axis=1)
        inside = (local_ids >= 0) & (local_ids < vocab_rows)
        chosen = jnp.take_along_axis(
            logits, jnp.clip(local_ids, 0, vocab_rows - 1)[:, None], axis=1
        )[:, 0]
        return (row_max, row_total, jnp.where(inside, chosen, 0.0))

    tile_max, tile_total, tile_target = lax.map(tile_stats, (tiled_rows, local_targets))
    tile_max, tile_total, tile_target = joined(
        (tile_max, tile_total, tile_target), "vocab", combine_stats
    )
    log_totals = tile_max + jnp.log(tile_total)
    own_terms = lax.dynamic_slice_in_dim(
        row_weights * (log_totals.reshape(-1) - tile_target.reshape(-1)),
        lax.axis_index("vocab") * seq_count * score_count,
        seq_count * score_count,
        0,
    )
    loss_part = jnp.sum(own_terms)
    total_loss = lax.psum(loss_part, ("dp", "vocab"))

    def tile_back(d_head, tile_items):
        rows_tile, local_ids, total_tile, weight_tile = tile_items
        logits = jnp.dot(rows_tile, head_all, preferred_element_type=jnp.float32)
        probabilities = jnp.exp(logits - total_tile[:, None])
        onehot = (jnp.arange(vocab_rows, dtype=jnp.int32)[None, :] == local_ids[:, None]).astype(
            jnp.float32
        )
        d_logits = (weight_tile[:, None] * (probabilities - onehot)).astype(jnp.bfloat16)
        d_head = d_head + jnp.einsum(
            "rd,rv->dv", rows_tile, d_logits, preferred_element_type=jnp.float32
        )
        d_rows = jnp.einsum("rv,dv->rd", d_logits, head_all, preferred_element_type=jnp.float32)
        return (d_head, d_rows)

    d_head, d_rows = lax.scan(
        tile_back,
        jnp.zeros((D, vocab_rows), jnp.float32),
        (tiled_rows, local_targets, log_totals, row_weights.reshape(tile_count, tile_size)),
    )
    d_final = lax.psum_scatter(
        d_rows.reshape(group_count, D), "vocab", scatter_dimension=0, tiled=True
    )
    d_gain_f = jnp.sum(d_final * normed_f, axis=0)
    d_picked = norm_back(d_final * gains_float[2], normed_f, inv_f)
    d_hidden2 = jnp.zeros(hidden2.shape, jnp.float32).at[flat_positions].set(d_picked)
    d_hidden0, d_layer, d_mod, d_gains_pair = layer_backward(
        d_hidden2, saved, mod_rows, layer_all, gains_float, cosine_table, sine_table, key_valid
    )
    d_ada = jnp.dot(condition.astype(jnp.float32).T, d_mod, precision=lax.Precision.HIGHEST)
    d_mask = jnp.sum(jnp.where(masked_rows[:, None], d_hidden0, 0.0), axis=0)
    d_gains = jnp.concatenate([d_gains_pair, d_gain_f[None, :], d_mask[None, :]], axis=0)
    d_gathered = lax.all_gather(d_hidden0.astype(jnp.bfloat16), "vocab", axis=0, tiled=True).astype(
        d_hidden0.dtype
    )
    segment_ids = jnp.where(inside_inputs, flat_inputs, vocab_rows)
    d_embed = jax.ops.segment_sum(d_gathered, segment_ids, vocab_rows + 1)[:vocab_rows]
    g_embed, g_head = (
        lax.psum_scatter(d_embed, "dp", scatter_dimension=1, tiled=True),
        lax.psum_scatter(d_head, "dp", scatter_dimension=0, tiled=True),
    )
    g_layer, g_ada, g_gains = (
        lax.psum_scatter(d_layer, ("dp", "vocab"), scatter_dimension=0, tiled=True),
        lax.psum_scatter(d_ada, ("dp", "vocab"), scatter_dimension=0, tiled=True),
        lax.psum_scatter(d_gains, ("dp", "vocab"), scatter_dimension=1, tiled=True),
    )
    squares = (
        jnp.sum(g_layer * g_layer)
        + jnp.sum(g_ada * g_ada)
        + jnp.sum(g_gains * g_gains)
        + jnp.sum(g_embed * g_embed)
        + jnp.sum(g_head * g_head)
    )
    total_squares = lax.psum(squares, ("dp", "vocab"))
    grad_norm = jnp.sqrt(total_squares)
    factor = jnp.minimum(1.0, CLIP_NORM / grad_norm)
    step_value = step_count[0].astype(jnp.float32)
    layer_out = adam_step(
        layer_w,
        layer_m,
        layer_v,
        layer_ema,
        g_layer * factor,
        step_value,
        LEARN_RATES[0],
        WEIGHT_DECAYS[0],
    )
    ada_out = adam_step(
        ada_w, ada_m, ada_v, ada_ema, g_ada * factor, step_value, LEARN_RATES[1], WEIGHT_DECAYS[1]
    )
    gains_out = adam_step(
        gains_w,
        gains_m,
        gains_v,
        gains_ema,
        g_gains * factor,
        step_value,
        LEARN_RATES[2],
        WEIGHT_DECAYS[2],
    )
    embed_out = adam_step(
        embed_w,
        embed_m,
        embed_v,
        embed_ema,
        g_embed * factor,
        step_value,
        LEARN_RATES[3],
        WEIGHT_DECAYS[3],
    )
    head_out = adam_step(
        head_w,
        head_m,
        head_v,
        head_ema,
        g_head * factor,
        step_value,
        LEARN_RATES[4],
        WEIGHT_DECAYS[4],
    )
    return (
        total_loss,
        grad_norm,
        layer_out[0],
        layer_out[1],
        layer_out[2],
        layer_out[3],
        ada_out[0],
        ada_out[1],
        ada_out[2],
        ada_out[3],
        gains_out[0],
        gains_out[1],
        gains_out[2],
        gains_out[3],
        embed_out[0],
        embed_out[1],
        embed_out[2],
        embed_out[3],
        head_out[0],
        head_out[1],
        head_out[2],
        head_out[3],
    )


def solution(mesh):
    placed = (
        P(("dp", "vocab"), None),
        P(("dp", "vocab"), None),
        P(("dp", "vocab")),
        P(("dp", "vocab")),
        P(),
        P(("dp", "vocab"), None),
        P(("dp", "vocab"), None),
        P(("dp", "vocab"), None),
        P(("dp", "vocab"), None),
        P(("dp", "vocab"), None),
        P(("dp", "vocab"), None),
        P(("dp", "vocab"), None),
        P(("dp", "vocab"), None),
        P(None, ("dp", "vocab")),
        P(None, ("dp", "vocab")),
        P(None, ("dp", "vocab")),
        P(None, ("dp", "vocab")),
        P("vocab", "dp"),
        P("vocab", "dp"),
        P("vocab", "dp"),
        P("vocab", "dp"),
        P("dp", "vocab"),
        P("dp", "vocab"),
        P("dp", "vocab"),
        P("dp", "vocab"),
    )
    return jax.shard_map(
        local,
        mesh=mesh,
        in_specs=placed,
        out_specs=(
            P(),
            P(),
            P(("dp", "vocab"), None),
            P(("dp", "vocab"), None),
            P(("dp", "vocab"), None),
            P(("dp", "vocab"), None),
            P(("dp", "vocab"), None),
            P(("dp", "vocab"), None),
            P(("dp", "vocab"), None),
            P(("dp", "vocab"), None),
            P(None, ("dp", "vocab")),
            P(None, ("dp", "vocab")),
            P(None, ("dp", "vocab")),
            P(None, ("dp", "vocab")),
            P("vocab", "dp"),
            P("vocab", "dp"),
            P("vocab", "dp"),
            P("vocab", "dp"),
            P("dp", "vocab"),
            P("dp", "vocab"),
            P("dp", "vocab"),
            P("dp", "vocab"),
        ),
        check_vma=False,
    )
```

profile of v0, /device:TPU:0, one launch (start us, length us, event | category | flops | bytes accessed | tf_op | source)
XLA Modules:
  0.0 3766.7 jit_solution(9263785609730252794)
XLA Ops:
  19.6 371.8 %all-gather.17.cloned.1.call-done = bf16[12800,768]{0,1:T(8,128)(2,1)} async-done(((bf16[12800,96]{0,1:T(8,128)(2,1)}), bf16[12800,768]{0,1:T(8,128)(2,1)}) %all-gather.17.cloned.1.call-update) | async-done | bytes 19660816 | tf_op jit(solution)/shard_map/all_gather | solution.py:363
  391.4 26.2 copy.141
  417.6 28.3 gather_fusion.1
  468.4 40.6 %all-gather.3 = bf16[32,24,4]{1,2,0:T(4,128)(2,1)S(1)} all-gather(bf16[1,24,4]{1,2,0:T(4,128)(2,1)S(1)} %convert_bitcast_fusion.2), channel_id=1, replica_groups=mesh['dp'=8,'vocab'=4] {'dp','vocab'}, dimensions={0}, use_global_device_ids=true | all-gather | bytes 6336 | tf_op jit(solution)/shard_map/all_gather | solution.py:359
  524.6 103.0 %all-gather.19.cloned.1.call-done = bf16[768,9216]{1,0:T(8,128)(2,1)} async-done(((bf16[24,9216]{1,0:T(8,128)(2,1)}), bf16[768,9216]{1,0:T(8,128)(2,1)}) %all-gather.19.cloned.1.call-update) | async-done | bytes 14155792 | tf_op jit(solution)/shard_map/all_gather | solution.py:357
  638.7 73.1 %while.76 = (s32[]{:T(128)}, bf16[2,1,512,12,64]{2,4,3,1,0:T(8,128)(2,1)}, f32[2,1,12,512]{3,2,1,0:T(8,128)S(1)}, bf16[2,1,512,12,64]{2,4,3,1,0:T(8,128)(2,1)}, ...) while((s32[]{:T(128)}, ...), condition=%wide.region_7.8_spmd.clone, body=%wide.region_4.7_spmd.clone.sunk | while | flops 1686105088 | bytes 93827240 | solution.py:140
  731.3 13.9 multiply_add_fusion.6
  769.6 235.5 %all-gather.23.cloned.1.call-done = bf16[768,12800]{1,0:T(8,128)(2,1)} async-done(((bf16[96,12800]{1,0:T(8,128)(2,1)}), bf16[768,12800]{1,0:T(8,128)(2,1)}) %all-gather.23.cloned.1.call-update) | async-done | bytes 19660816 | tf_op jit(solution)/shard_map/all_gather | solution.py:364
  1005.1 30.6 all-gather.21.cloned.1.call-done
  1035.7 165.6 %while.74 = (s32[]{:T(128)}, f32[4,512]{1,0:T(4,128)S(1)}, f32[4,512]{1,0:T(4,128)S(1)}, f32[4,512]{1,0:T(4,128)S(1)}, bf16[4,512,768]{2,1,0:T(8,128)(2,1)}, /*i...) while((s32[]{:T(128)}, f32[4,512]{1,0:T(4,128)S(1)}, ...), condition=%wide.region_15.16_spmd, body=%wide.region_12.15_spmd.sunk | while | flops 10086002688 | bytes 72929392 | solution.py:419
  1036.1 22.1 fusion.190
  1077.4 22.1 fusion.190
  1118.8 22.1 fusion.190
  1160.1 22.1 fusion.190
  1217.7 256.4 %while.77 = (s32[]{:T(128)}, f32[768,12800]{1,0:T(8,128)}, f32[4,512,768]{2,1,0:T(8,128)}, bf16[4,512,768]{2,1,0:T(8,128)(2,1)}, f32[4,512]{1,0:T(4,128)S(1)}, /...) while((s32[]{:T(128)}, f32[768,12800]{1,0:T(8,128)}, ...), condition=%wide.region_21.22_spmd.clone, body=%wide.region_20.21_spmd.clone.sunk | while | flops 30257971200 | bytes 160450704 | solution.py:447
  1217.8 19.0 multiply_convert_fusion.13
  1236.8 20.3 select_add_fusion.2
  1257.1 17.5 bitcast_dynamic-update-slice_fusion.10
  1274.6 18.9 multiply_convert_fusion.13
  1293.6 30.1 select_add_fusion.2
  1323.6 17.5 bitcast_dynamic-update-slice_fusion.10
  1341.1 19.0 multiply_convert_fusion.13
  1360.1 30.2 select_add_fusion.2
  1390.3 17.5 bitcast_dynamic-update-slice_fusion.10
  1407.8 19.0 multiply_convert_fusion.13
  1426.8 29.8 select_add_fusion.2
  1456.7 17.5 bitcast_dynamic-update-slice_fusion.10
  1474.4 58.6 %reduce-scatter.11.cloned.1.call-done = f32[512,768]{1,0:T(8,128)} async-done(((f32[2048,768]{1,0:T(8,128)}), f32[512,768]{1,0:T(8,128)}) %reduce-scatter.11.cloned.1.call-update) | async-done | bytes 1572880 | tf_op jit(solution)/shard_map/reduce_scatter | solution.py:452
  1543.0 17.5 fusion.90
  1585.5 336.2 %while.78 = (s32[]{:T(128)}, f32[1,1024,12,64]{1,3,2,0:T(8,128)}, f32[1,1024,12,64]{1,3,2,0:T(8,128)}, f32[2,1,512,12,64]{2,0,4,3,1:T(2,128)}, bf16[2,1,512,12,6...) while((s32[]{:T(128)}, f32[1,1024,12,64]{1,3,2,0:T(8,128)}, ...), condition=%wide.region_30.31_spmd.clone, body=%wide.region_28.30_spmd.clone.sunk | while | flops 4193270784 | bytes 254973088 | solution.py:173
  1609.4 46.2 %bitcast_add_fusion.5 = f32[1,1024,12,64]{1,3,2,0:T(8,128)} fusion(f32[1,1024,12,64]{1,3,2,0:T(8,128)} %get-tuple-element.1143, f32[12,512,1024]{2,1,0:T(8,128)} %fusion.212, f32[12,512]{1,0:T(8,128)S(1)} %dynamic-slice_bitcast_fusion.2, f32[12,512,1024]{2,1,0:T(8,128)} %fusion.213, pred[1024]{0:T(1024)(128)(4,1)S(1)} %compare_reduce_fusion.5, ...), kind=kOutput, calls=%fused_computation.69.clone.1 | convolution fusion | flops 876092416 | bytes 107808776 | tf_op jit(solution)/shard_map/while/body/eval_jaxpr/shqk,sqhd->skhd/dot_general | solution.py:161
  1668.7 51.3 %fusion.214 = f32[1,1,512,12,64]{2,4,3,1,0:T(8,128)} fusion(bf16[1,1024,12,64]{1,3,2,0:T(8,128)(2,1)S(1)} %get-tuple-element.1159, f32[12,512,1024]{2,1,0:T(8,128)} %fusion.212, f32[12,512]{1,0:T(8,128)S(1)} %dynamic-slice_bitcast_fusion.2, f32[12,512,1024]{2,1,0:T(8,128)} %fusion.213, pred[1024]{0:T(1024)(128)(4,1)S(1)} %compare_reduce_fusion.5), kind=kOutput, calls=%fused_computation.75.clone.1 | convolution fusion | flops 874519552 | bytes 53502976 | tf_op jit(solution)/shard_map/while/body/eval_jaxpr/shqk,skhd->sqhd/dot_general | solution.py:158
  1724.3 28.8 dynamic_update_slice.45
  1776.5 46.6 %bitcast_add_fusion.5 = f32[1,1024,12,64]{1,3,2,0:T(8,128)} fusion(f32[1,1024,12,64]{1,3,2,0:T(8,128)} %get-tuple-element.1143, f32[12,512,1024]{2,1,0:T(8,128)} %fusion.212, f32[12,512]{1,0:T(8,128)S(1)} %dynamic-slice_bitcast_fusion.2, f32[12,512,1024]{2,1,0:T(8,128)} %fusion.213, pred[1024]{0:T(1024)(128)(4,1)S(1)} %compare_reduce_fusion.5, ...), kind=kOutput, calls=%fused_computation.69.clone.1 | convolution fusion | flops 876092416 | bytes 107808776 | tf_op jit(solution)/shard_map/while/body/eval_jaxpr/shqk,sqhd->skhd/dot_general | solution.py:161
  1823.1 14.1 bitcast_add_fusion.6
  1837.2 51.3 %fusion.214 = f32[1,1,512,12,64]{2,4,3,1,0:T(8,128)} fusion(bf16[1,1024,12,64]{1,3,2,0:T(8,128)(2,1)S(1)} %get-tuple-element.1159, f32[12,512,1024]{2,1,0:T(8,128)} %fusion.212, f32[12,512]{1,0:T(8,128)S(1)} %dynamic-slice_bitcast_fusion.2, f32[12,512,1024]{2,1,0:T(8,128)} %fusion.213, pred[1024]{0:T(1024)(128)(4,1)S(1)} %compare_reduce_fusion.5), kind=kOutput, calls=%fused_computation.75.clone.1 | convolution fusion | flops 874519552 | bytes 53502976 | tf_op jit(solution)/shard_map/while/body/eval_jaxpr/shqk,skhd->sqhd/dot_general | solution.py:158
  1892.8 28.8 dynamic_update_slice.45
  2015.3 19.4 pad_maximum_fusion
  2045.4 43.6 %scatter_custom_fusion.1 = f32[12801,768]{1,0:T(8,128)} fusion(s32[4096]{0:T(1024)} %bitcast.306, f32[4096,768]{1,0:T(8,128)} %copy.156, f32[]{:T(128)} %constant.184.clone.1), kind=kCustom, calls=%fused_computation.99 | custom fusion | flops 3145728 | bytes 39325184 | tf_op jit(solution)/shard_map/scatter-add | solution.py:468
  2089.0 27.0 slice.179
  2116.0 39.6 %copy.162 = f32[12800,768]{0,1:T(8,128)} copy(f32[12800,768]{1,0:T(8,128)} %slice.179) | data formatting | bytes 78643200
  2157.9 40.1 %all-reduce.2 = f32[4,768]{1,0:T(4,128)S(1)} all-reduce(f32[4,768]{1,0:T(4,128)S(1)} %pad_maximum_fusion.3), channel_id=9, replica_groups=mesh['dp'=8,'vocab'=4] {'dp','vocab'}, use_global_device_ids=true, to_apply=%region_42.43.clone | all-reduce | flops 3072 | bytes 24576
  2200.3 213.1 %reduce-scatter.13.cloned.1.call-done = f32[24,9216]{1,0:T(8,128)} async-done(((f32[768,9216]{1,0:T(8,128)}), f32[24,9216]{1,0:T(8,128)}) %reduce-scatter.13.cloned.1.call-update) | async-done | bytes 884752 | tf_op jit(solution)/shard_map/reduce_scatter | solution.py:474
  2417.4 625.6 %reduce-scatter.15.cloned.1.call-done = f32[96,12800]{1,0:T(8,128)} async-done(((f32[768,12800]{1,0:T(8,128)}), f32[96,12800]{1,0:T(8,128)}) %reduce-scatter.15.cloned.1.call-update) | async-done | bytes 4915216 | tf_op jit(solution)/shard_map/reduce_scatter | solution.py:471
  3047.3 623.8 %reduce-scatter.17.cloned.1.call-done = f32[96,12800]{1,0:T(8,128)} async-done(((f32[768,12800]{1,0:T(8,128)}), f32[96,12800]{1,0:T(8,128)}) %reduce-scatter.17.cloned.1.call-update) | async-done | bytes 4915216
  3683.4 39.7 %all-reduce.3 = (f32[]{:T(128)}, f32[]{:T(128)}) all-reduce(f32[]{:T(128)} %dynamic-slice_reduce_fusion, f32[]{:T(128)S(6)} %add.439), channel_id=1, replica_groups=mesh['dp'=8,'vocab'=4] {'dp','vocab'}, use_global_device_ids=true, to_apply=%region_19.20 | all-reduce | flops 2 | bytes 16 | tf_op jit(solution)/shard_map/psum | solution.py:431
  3730.6 14.0 multiply_add_fusion.2
  3744.7 13.9 multiply_add_fusion
  (469 shorter events, 504.9 us)
Async XLA Ops:
  7.2 384.2 %all-gather.17.cloned.1.call-start = ((), (), s32[]{:S(2)}) async-start(), calls=%async_computation.5 | async-start | bytes 22118400 | tf_op jit(solution)/shard_map/all_gather | solution.py:363
  11.4 501.2 %all-gather.27.cloned.1.call-start = ((), (), s32[]{:S(2)}) async-start(), calls=%async_computation.14 | async-start | bytes 1216512 | tf_op jit(solution)/shard_map/all_gather | solution.py:358
  12.1 508.6 %reduce-scatter.9.cloned.1.call-start = ((), (), s32[]{:S(2)}) async-start(), calls=%async_computation.6 | async-start | bytes 7864320 | tf_op jit(solution)/shard_map/reduce_scatter | solution.py:379
  12.6 615.1 %copy-start.46 = (pred[1024]{0:T(1024)(128)(4,1)}, pred[1024]{0:T(1024)(128)(4,1)S(1)}, u32[]{:S(2)}) copy-start(pred[1024]{0:T(1024)(128)(4,1)S(1)} %fusion.111) | copy-start | bytes 3076
  462.0 165.7 %all-gather.19.cloned.1.call-start = ((), (), s32[]{:S(2)}) async-start(), calls=%async_computation.7 | async-start | bytes 14598144 | tf_op jit(solution)/shard_map/all_gather | solution.py:357
  464.0 541.1 %all-gather.23.cloned.1.call-start = ((), (), s32[]{:S(2)}) async-start(), calls=%async_computation.9 | async-start | bytes 22118400 | tf_op jit(solution)/shard_map/all_gather | solution.py:364
  468.3 567.3 %all-gather.21.cloned.1.call-start = ((), (), s32[]{:S(2)}) async-start(), calls=%async_computation.8 | async-start | bytes 3932160 | tf_op jit(solution)/shard_map/all_gather | solution.py:398
  511.3 116.3 %copy-start.43 = (f32[768]{0:T(1024)}, f32[768]{0:T(1024)S(1)}, u32[]{:S(2)}) copy-start(f32[768]{0:T(1024)S(1)} %get-tuple-element.610) | copy-start | bytes 9220
  511.3 116.3 %copy-start.75 = (f32[768]{0:T(1024)}, f32[768]{0:T(1024)S(1)}, u32[]{:S(2)}) copy-start(f32[768]{0:T(1024)S(1)} %get-tuple-element.609) | copy-start | bytes 9220
  512.5 122.8 %copy-start.34 = (f32[1024,32]{0,1:T(8,128)}, f32[1024,32]{0,1:T(8,128)S(1)}, u32[]{:S(2)}) copy-start(f32[1024,32]{0,1:T(8,128)S(1)} %get-tuple-element.751) | copy-start | bytes 393220
  512.5 122.8 %copy-start.36 = (f32[1024,32]{0,1:T(8,128)}, f32[1024,32]{0,1:T(8,128)S(1)}, u32[]{:S(2)}) copy-start(f32[1024,32]{0,1:T(8,128)S(1)} %get-tuple-element.752) | copy-start | bytes 393220
  515.0 119.1 %copy-start.77 = (f32[768]{0:T(1024)}, f32[768]{0:T(1024)S(1)}, u32[]{:S(2)}) copy-start(f32[768]{0:T(1024)S(1)} %get-tuple-element.747) | copy-start | bytes 9220
  515.0 119.1 %copy-start.90 = (f32[768]{0:T(1024)}, f32[768]{0:T(1024)S(1)}, u32[]{:S(2)}) copy-start(f32[768]{0:T(1024)S(1)} %get-tuple-element.746) | copy-start | bytes 9220
  520.7 107.0 %copy-start.11 = (bf16[1024,768]{0,1:T(8,128)(2,1)S(1)}, bf16[1024,768]{0,1:T(8,128)(2,1)}, u32[]{:S(2)}) copy-start(bf16[1024,768]{0,1:T(8,128)(2,1)} %reduce-scatter.9.cloned.1.call-done) | copy-start | bytes 4718596
  522.6 111.5 %copy-start.66 = (f32[1024]{0:T(1024)}, f32[1024]{0:T(1024)S(1)}, u32[]{:S(2)}) copy-start(f32[1024]{0:T(1024)S(1)} %broadcast_multiply_fusion.6) | copy-start | bytes 12292
  524.6 109.5 %copy-start.83 = (f32[1024]{0:T(1024)}, f32[1024]{0:T(1024)S(1)}, u32[]{:S(2)}) copy-start(f32[1024]{0:T(1024)S(1)} %add_rsqrt_fusion.1) | copy-start | bytes 12292
  731.2 14.0 copy-start.108
  750.2 11.8 copy-start.1
  752.1 12.3 copy-start.69
  755.7 777.2 %reduce-scatter.11.cloned.1.call-start = ((), (), s32[]{:S(2)}) async-start(), calls=%async_computation.10 | async-start | bytes 7864320 | tf_op jit(solution)/shard_map/reduce_scatter | solution.py:452
  1474.1 58.9 %copy-start.10 = (f32[512,768]{1,0:T(8,128)S(1)}, f32[512,768]{1,0:T(8,128)}, u32[]{:S(2)}) copy-start(f32[512,768]{1,0:T(8,128)} %gather_fusion.2) | copy-start | bytes 4718596
  1474.1 58.9 %copy-start.54 = (f32[768]{0:T(1024)S(1)}, f32[768]{0:T(1024)}, u32[]{:S(2)}) copy-start(f32[768]{0:T(1024)} %get-tuple-element.608) | copy-start | bytes 9220
  1474.1 58.9 %copy-start.56 = (f32[512]{0:T(512)S(1)}, f32[512]{0:T(512)}, u32[]{:S(2)}) copy-start(f32[512]{0:T(512)} %copy-done.55) | copy-start | bytes 6148
  1474.1 58.9 %copy-start.72 = (f32[512]{0:T(512)S(1)}, f32[512]{0:T(512)}, u32[]{:S(2)}) copy-start(f32[512]{0:T(512)} %copy-done.71) | copy-start | bytes 6148
  1474.1 58.9 %copy-start.74 = (pred[512]{0:T(512)(128)(4,1)S(1)}, pred[512]{0:T(512)(128)(4,1)}, u32[]{:S(2)}) copy-start(pred[512]{0:T(512)(128)(4,1)} %compare_and_fusion.1) | copy-start | bytes 1540
  1474.2 561.8 %all-gather.25.cloned.1.call-start = ((), (), s32[]{:S(2)}) async-start(), calls=%async_computation.12 | async-start | bytes 7864320 | tf_op jit(solution)/shard_map/all_gather | solution.py:464
  1542.9 27.8 copy-start.19
  1542.9 17.5 copy-start.7
  1542.9 17.5 copy-start.51
  1542.9 17.5 copy-start.58
  1543.0 17.5 copy-start.61
  1543.0 17.5 copy-start.80
  1955.5 243.3 %all-reduce.6.cloned.1.call-start = ((), (), s32[]{:S(2)}) async-start(), calls=%async_computation.16 | async-start | bytes 4718592
  2006.3 407.1 %reduce-scatter.13.cloned.1.call-start = ((), (), s32[]{:S(2)}) async-start(), calls=%async_computation.11 | async-start | bytes 29196288 | tf_op jit(solution)/shard_map/reduce_scatter | solution.py:474
  2034.7 1008.3 %reduce-scatter.15.cloned.1.call-start = ((), (), s32[]{:S(2)}) async-start(), calls=%async_computation.13 | async-start | bytes 44236800 | tf_op jit(solution)/shard_map/reduce_scatter | solution.py:471
  2035.5 1635.6 %reduce-scatter.17.cloned.1.call-start = ((), (), s32[]{:S(2)}) async-start(), calls=%async_computation.15 | async-start | bytes 44236800
  3677.5 46.3 %copy-start.89 = (f32[4,24]{1,0:T(4,128)S(1)}, f32[4,24]{1,0:T(4,128)}, u32[]{:S(2)}) copy-start(f32[4,24]{1,0:T(4,128)} %param.48) | copy-start | bytes 1156
  3677.5 46.3 %copy-start.99 = (f32[4,24]{1,0:T(4,128)S(1)}, f32[4,24]{1,0:T(4,128)}, u32[]{:S(2)}) copy-start(f32[4,24]{1,0:T(4,128)} %param.51) | copy-start | bytes 1156
  3677.5 46.3 %copy-start.100 = (f32[4,24]{1,0:T(4,128)S(1)}, f32[4,24]{1,0:T(4,128)}, u32[]{:S(2)}) copy-start(f32[4,24]{1,0:T(4,128)} %param.50) | copy-start | bytes 1156
  3677.5 46.3 %copy-start.101 = (f32[4,24]{1,0:T(4,128)S(1)}, f32[4,24]{1,0:T(4,128)}, u32[]{:S(2)}) copy-start(f32[4,24]{1,0:T(4,128)} %param.49) | copy-start | bytes 1156
  3677.5 47.0 %copy-start.28 = (f32[24,9216]{1,0:T(8,128)S(1)}, f32[24,9216]{1,0:T(8,128)}, u32[]{:S(2)}) copy-start(f32[24,9216]{1,0:T(8,128)} %reduce-scatter.13.cloned.1.call-done) | copy-start | bytes 2654212
  3677.5 47.0 %copy-start.30 = (f32[24,9216]{1,0:T(8,128)S(1)}, f32[24,9216]{1,0:T(8,128)}, u32[]{:S(2)}) copy-start(f32[24,9216]{1,0:T(8,128)} %param.40) | copy-start | bytes 2654212
  3677.5 47.0 %copy-start.38 = (f32[24,9216]{1,0:T(8,128)S(1)}, f32[24,9216]{1,0:T(8,128)}, u32[]{:S(2)}) copy-start(f32[24,9216]{1,0:T(8,128)} %param.43) | copy-start | bytes 2654212
  3677.6 50.9 %copy-start.42 = (f32[4,4608]{1,0:T(4,128)S(1)}, f32[4,4608]{1,0:T(4,128)}, u32[]{:S(2)}) copy-start(f32[4,4608]{1,0:T(4,128)} %param.44) | copy-start | bytes 221188
  3677.6 50.9 %copy-start.49 = (f32[4,4608]{1,0:T(4,128)S(1)}, f32[4,4608]{1,0:T(4,128)}, u32[]{:S(2)}) copy-start(f32[4,4608]{1,0:T(4,128)} %param.47) | copy-start | bytes 221188
  3677.6 53.0 %slice-start = ((s8[4915200]{0:T(1024)(128)(4,1)}), s8[720896]{0:T(1024)(128)(4,1)S(1)}, s32[]{:S(2)}) async-start(s8[4915200]{0:T(1024)(128)(4,1)} %bitcast.276), calls=%async_computation.17 | async-start | bytes 1441792
  3724.6 20.1 slice-start.2
  3730.6 14.0 slice-start.3
  (79 other events, 374.3 us)
Sparse Core Ops, SparseCore 0:
  11.5 379.8 all-gather.16
  394.9 54.0 all-gather.26
  462.1 58.5 reduce-scatter.8
  524.4 103.1 all-gather.18
  629.7 375.3 all-gather.22
  1007.1 28.4 all-gather.20
  1474.3 58.6 reduce-scatter.10
  1955.6 46.3 all-gather.24
  2008.2 135.0 all-reduce.5
  2150.7 262.6 reduce-scatter.12
  2417.8 625.1 reduce-scatter.14
  3046.8 624.2 reduce-scatter.16
where the time goes:
time: 3780 us; the launch traced here: 3770 us
  waiting for transfers between devices  2270 us (60%)
  matrix products  768 us (20%)
  local copies, waits for them, and re-layouts  302 us (8%)
  other arithmetic  250 us (7%)
  blocking collectives  152 us (4%)
    reduce_scatter x1, waiting for transfers between devices, local(): lax.psum_scatter(d_head, 'dp', scatter_dimension=0, tiled=True)  626 us
    unnamed x14, waiting for transfers between devices  625 us
    all_gather x1, waiting for transfers between devices, local(): lax.all_gather(embed_w.astype(jnp.bfloat16), 'dp', axis=1, tiled=True)  372 us
    all_gather x1, waiting for transfers between devices, local(): lax.all_gather(head_w.astype(jnp.bfloat16), 'dp', axis=0, tiled=True)  235 us
    reduce_scatter x1, waiting for transfers between devices, local(): lax.psum_scatter(d_layer, ('dp', 'vocab'), scatter_dimension=0, tiled=True)  213 us
    dot_general x4, matrix products, tile_back(): jnp.einsum('rd,rv->dv', rows_tile, d_logits, preferred_element_type=jnp.f...  110 us
    all_gather x1, waiting for transfers between devices, local(): lax.all_gather(layer_w.astype(jnp.bfloat16), ('dp', 'vocab'), axis=0, til...  103 us
    dot_general x2, matrix products, one_block(): jnp.einsum('shqk,skhd->sqhd', d_scores, key_vecs, preferred_element_type=...  103 us
  transfers between devices with their start and end apart: 12, of which 9 were waited for; matrix products, arithmetic and copies ran while one was open for 11% of the time, Pallas kernels for 0%

commit v1 on v0

v1 whole, which is shorter than its diff:
```python
import functools
import math

import jax
import jax.numpy as jnp
from jax import lax
from jax.experimental import pallas as pl
from jax.experimental.pallas import tpu as pltpu
from jax.sharding import Mesh, PartitionSpec as P

D = 768
H = 12
HD = 64
FF = 3072
V = 51200
C = 128
TSTEPS = 20
SEGMENT = 3200
LANES = 128

NORM_EPS = 1e-05
CLIP_NORM = 0.05
BETA_ONE = 0.9
BETA_TWO = 0.95
ADAM_EPS = 1e-08
EMA_DECAY = 0.9999
LEARN_RATES = (0.03, 0.1, 0.1, 0.5, 0.05)
WEIGHT_DECAYS = (0.01, 0.01, 0.0, 0.01, 0.01)

ALL = ("z", "x", "y", "c")
BF = jnp.bfloat16
F32 = jnp.float32
MESH = pl.DeviceIdType.MESH
VMEM_LIMIT = 60 * 1024 * 1024


def dot(a, b, contract):
    return lax.dot_general(a, b, ((contract[0], contract[1]), ((), ())), preferred_element_type=F32)


def matmul(a, b):
    return dot(a, b, ((1,), (0,)))


def matmul_nt(a, b):
    return dot(a, b, ((1,), (1,)))


def matmul_tn(a, b):
    return dot(a, b, ((0,), (0,)))


def share_kernel(sizes, count, *refs):
    nz, nx, ny, nc = sizes
    n = nz * nx * ny * nc
    ins, outs = refs[:count], refs[count : 2 * count]
    send, recv, near = refs[2 * count :]
    me = ((lax.axis_index("z") * nx + lax.axis_index("x")) * ny + lax.axis_index("y")) * nc
    me = me + lax.axis_index("c")

    def device(k):
        peer = lax.rem(me + k, n)
        return (
            peer // (nx * ny * nc),
            lax.rem(peer // (ny * nc), nx),
            lax.rem(peer // nc, ny),
            lax.rem(peer, nc),
        )

    def remote(i, k):
        return pltpu.make_async_remote_copy(
            src_ref=ins[i],
            dst_ref=outs[i].at[me],
            send_sem=send.at[i, k],
            recv_sem=recv.at[i, k],
            device_id=device(k),
            device_id_type=MESH,
        )

    barrier = pltpu.get_barrier_semaphore()

    @pl.loop(1, n)
    def _(k):
        pl.semaphore_signal(barrier, inc=1, device_id=device(k), device_id_type=MESH)

    pl.semaphore_wait(barrier, n - 1)

    @pl.loop(1, n)
    def _(k):
        for i in range(count):
            remote(i, k).start()

    for i in range(count):
        pltpu.make_async_copy(ins[i], outs[i].at[me], near.at[i]).start()
    for i in range(count):
        pltpu.make_async_copy(ins[i], outs[i].at[me], near.at[i]).wait()

    @pl.loop(1, n)
    def _(k):
        for i in range(count):
            remote(i, k).wait()


def share(sizes, collective_id, *arrays):
    n = math.prod(sizes)
    count = len(arrays)
    return pl.pallas_call(
        functools.partial(share_kernel, sizes, count),
        out_shape=[jax.ShapeDtypeStruct((n,) + a.shape, a.dtype) for a in arrays],
        in_specs=[pl.BlockSpec(memory_space=pltpu.VMEM)] * count,
        out_specs=[pl.BlockSpec(memory_space=pltpu.VMEM)] * count,
        scratch_shapes=[
            pltpu.SemaphoreType.DMA((count, n)),
            pltpu.SemaphoreType.DMA((count, n)),
            pltpu.SemaphoreType.DMA((count,)),
        ],
        compiler_params=pltpu.CompilerParams(
            collective_id=collective_id, has_side_effects=True
        ),
        name=f"share{collective_id}",
    )(*arrays)


def axis_place(axes):
    index, size = 0, 1
    for axis in axes:
        index = index * lax.axis_size(axis) + lax.axis_index(axis)
        size = size * lax.axis_size(axis)
    return index, size


def exchange(piece_for, axes):
    me, n = axis_place(axes)
    got = [(me, piece_for(me))]
    for step in range(1, n):
        piece = piece_for(lax.rem(me + step, n))
        moved = lax.ppermute(piece, axes, [(i, (i + step) % n) for i in range(n)])
        got.append((lax.rem(me + n - step, n), moved))
    return got


def in_order(got):
    out = jnp.zeros((len(got),) + got[0][1].shape, got[0][1].dtype)
    for sender, piece in got:
        out = lax.dynamic_update_index_in_dim(out, piece, sender, 0)
    return out


def pick(values, index):
    return lax.dynamic_index_in_dim(values, index, 0, keepdims=False)


def gather_kernel(low_ref, high_ref, ids_ref, table_ref, out_ref, rows_ref):
    source = pl.program_id(0)
    low, high = low_ref[source], high_ref[source]
    rows_ref[...] = jnp.zeros_like(rows_ref)

    def chunk(k, carry):
        base = pl.multiple_of(k * 8, 8)
        rows = []
        for i in range(8):
            place = base + i
            valid = jnp.logical_and(place >= low, place < high)
            row = jnp.where(valid, ids_ref[source, place], 0)
            value = table_ref[pl.ds(row, 1), :]
            rows.append(jnp.where(valid, value, 0.0))
        rows_ref[pl.ds(base, 8), :] = jnp.concatenate(rows, axis=0)
        return carry

    lax.fori_loop(low // 8, (high + 7) // 8, chunk, 0)
    out_ref[0] = rows_ref[...].astype(BF)


def gather_rows(table, ids, low, high):
    sources, count = ids.shape
    width = table.shape[1]
    return pl.pallas_call(
        gather_kernel,
        out_shape=jax.ShapeDtypeStruct((sources, count, width), BF),
        grid_spec=pltpu.PrefetchScalarGridSpec(
            num_scalar_prefetch=3,
            grid=(sources,),
            in_specs=[
                pl.BlockSpec(table.shape, lambda i, *_: (0, 0), pipeline_mode=pl.Buffered(1))
            ],
            out_specs=pl.BlockSpec((1, count, width), lambda i, *_: (i, 0, 0)),
            scratch_shapes=[pltpu.VMEM((count, width), F32)],
        ),
        compiler_params=pltpu.CompilerParams(vmem_limit_bytes=VMEM_LIMIT),
        name="gather_rows",
    )(low, high, ids, table)


def scatter_kernel(low_ref, high_ref, ids_ref, rows_ref, out_ref, wide_ref):
    source = pl.program_id(0)

    @pl.when(source == 0)
    def _():
        out_ref[...] = jnp.zeros_like(out_ref)

    low, high = low_ref[source], high_ref[source]
    wide_ref[...] = rows_ref[0].astype(F32)

    def chunk(k, carry):
        base = pl.multiple_of(k * 8, 8)
        block = wide_ref[pl.ds(base, 8), :]
        for i in range(8):
            place = base + i
            valid = jnp.logical_and(place >= low, place < high)
            row = jnp.where(valid, ids_ref[source, place], 0)
            addend = jnp.where(valid, block[i : i + 1, :], 0.0)
            out_ref[pl.ds(row, 1), :] = out_ref[pl.ds(row, 1), :] + addend
        return carry

    lax.fori_loop(low // 8, (high + 7) // 8, chunk, 0)


def scatter_rows(rows, ids, low, high, table_rows):
    sources, count, width = rows.shape
    return pl.pallas_call(
        scatter_kernel,
        out_shape=jax.ShapeDtypeStruct((table_rows, width), F32),
        grid_spec=pltpu.PrefetchScalarGridSpec(
            num_scalar_prefetch=3,
            grid=(sources,),
            in_specs=[pl.BlockSpec((1, count, width), lambda i, *_: (i, 0, 0))],
            out_specs=pl.BlockSpec((table_rows, width), lambda i, *_: (0, 0)),
            scratch_shapes=[pltpu.VMEM((count, width), F32)],
        ),
        compiler_params=pltpu.CompilerParams(vmem_limit_bytes=VMEM_LIMIT),
        name="scatter_rows",
    )(low, high, ids, rows)


def swap_halves(values):
    lane = lax.broadcasted_iota(jnp.int32, values.shape, 1)
    half = HD // 2
    up = pltpu.roll(values, LANES - half, 1)
    down = pltpu.roll(values, half, 1)
    return jnp.where(lax.rem(lane, HD) < half, up, down)


def turn(values, cosine, sine):
    return values * cosine + swap_halves(values) * sine


def turn_back(values, cosine, sine):
    return values * cosine - swap_halves(values) * sine


def attend_kernel(kv_ref, vv_ref, qm_ref, km_ref, vm_ref, cu_ref, su_ref, cm_ref, sm_ref,
                  mask_ref, q_out, ku_out, km_out, att_out, lse_out):
    rows = cm_ref.shape[0]
    wide = (rows, LANES)
    cm, sm = cm_ref[...], sm_ref[...]
    q = turn(jnp.broadcast_to(qm_ref[0:1, :], wide), cm, sm).astype(BF)
    k_m = turn(jnp.broadcast_to(km_ref[0:1, :], wide), cm, sm).astype(BF)
    k_u = turn(kv_ref[...], cu_ref[...], su_ref[...]).astype(BF)
    v_u = vv_ref[...].astype(BF)
    v_m = vm_ref[0:1, :].astype(BF).astype(F32)
    q_out[...] = q
    ku_out[...] = k_u
    km_out[...] = k_m
    mask = mask_ref[0:1, :]
    outs, totals = [], []
    for head in range(LANES // HD):
        part = slice(head * HD, (head + 1) * HD)
        s_u = matmul_nt(q[:, part], k_u[:, part]) * HD ** (-0.5) + mask
        s_m = matmul_nt(q[:, part], k_m[:, part]) * HD ** (-0.5)
        top = jnp.maximum(
            jnp.max(s_u, axis=1, keepdims=True), jnp.max(s_m, axis=1, keepdims=True)
        )
        e_u = jnp.exp(s_u - top)
        e_m = jnp.exp(s_m - top)
        total = jnp.sum(e_u, axis=1, keepdims=True) + jnp.sum(e_m, axis=1, keepdims=True)
        inverse = 1.0 / total
        p_u = (e_u * inverse).astype(BF)
        p_m = (e_m * inverse).astype(BF).astype(F32)
        mixed = matmul(p_u, v_u[:, part]) + jnp.sum(p_m, axis=1, keepdims=True) * v_m[:, part]
        outs.append(mixed)
        totals.append(top + jnp.log(total))
    att_out[...] = jnp.concatenate(outs, axis=1).astype(BF)
    lse_out[0] = jnp.concatenate(totals, axis=1)


def attend(kv_u, qkv_m, tables, mask):
    count, rows = kv_u.shape[0], tables[2].shape[0]
    blocks = D // LANES
    per = LANES // HD
    row = lambda offset: pl.BlockSpec((qkv_m.shape[0], LANES), lambda i: (0, offset * blocks + i))
    column = lambda n: pl.BlockSpec((n, LANES), lambda i: (0, i))
    whole = lambda a: pl.BlockSpec(a.shape, lambda i: (0, 0))
    return pl.pallas_call(
        attend_kernel,
        grid=(blocks,),
        out_shape=[
            jax.ShapeDtypeStruct((rows, D), BF),
            jax.ShapeDtypeStruct((count, D), BF),
            jax.ShapeDtypeStruct((rows, D), BF),
            jax.ShapeDtypeStruct((rows, D), BF),
            jax.ShapeDtypeStruct((blocks, rows, per), F32),
        ],
        in_specs=[
            pl.BlockSpec((count, LANES), lambda i: (0, i)),
            pl.BlockSpec((count, LANES), lambda i: (0, blocks + i)),
            row(0), row(1), row(2),
            *[whole(t) for t in tables],
            whole(mask),
        ],
        out_specs=[column(rows), column(count), column(rows), column(rows),
                   pl.BlockSpec((1, rows, per), lambda i: (i, 0, 0))],
        compiler_params=pltpu.CompilerParams(vmem_limit_bytes=VMEM_LIMIT),
        cost_estimate=pl.CostEstimate(
            flops=2 * 3 * rows * count * D, bytes_accessed=12 * rows * D,
            transcendentals=2 * rows * count * H,
        ),
        name="attend",
    )(kv_u, kv_u, qkv_m, qkv_m, qkv_m, *tables, mask)


def attend_back_kernel(q_ref, ku_ref, km_ref, vv_ref, vm_ref, cu_ref, su_ref, cm_ref, sm_ref,
                       mask_ref, lse_ref, datt_ref, dk_out, dv_out, dm_out):
    q, k_u, k_m, datt = q_ref[...], ku_ref[...], km_ref[...], datt_ref[...]
    v_u = vv_ref[...].astype(BF)
    v_m = vm_ref[0:1, :].astype(BF).astype(F32)
    datt_f = datt.astype(F32)
    mask = mask_ref[0:1, :]
    scale = HD ** (-0.5)
    dq, dk_u, dk_m, dv_u, dv_m = [], [], [], [], []
    for head in range(LANES // HD):
        part = slice(head * HD, (head + 1) * HD)
        lse = lse_ref[0, :, head : head + 1]
        p_u = jnp.exp(matmul_nt(q[:, part], k_u[:, part]) * scale + mask - lse)
        p_m = jnp.exp(matmul_nt(q[:, part], k_m[:, part]) * scale - lse)
        dp_u = matmul_nt(datt[:, part], v_u[:, part])
        dp_m = jnp.sum(datt_f[:, part] * v_m[:, part], axis=1, keepdims=True)
        inner = jnp.sum(p_u * dp_u, axis=1, keepdims=True) + dp_m * jnp.sum(
            p_m, axis=1, keepdims=True
        )
        ds_u = (p_u * (dp_u - inner) * scale).astype(BF)
        ds_m = (p_m * ((dp_m - inner) * scale)).astype(BF)
        dq.append(matmul(ds_u, k_u[:, part]) + matmul(ds_m, k_m[:, part]))
        dk_u.append(matmul_tn(ds_u, q[:, part]))
        dk_m.append(matmul_tn(ds_m, q[:, part]))
        dv_u.append(matmul_tn(p_u.astype(BF), datt[:, part]))
        mass = jnp.sum(p_m.astype(BF).astype(F32), axis=1, keepdims=True)
        dv_m.append(jnp.sum(mass * datt_f[:, part], axis=0, keepdims=True))
    cm, sm = cm_ref[...], sm_ref[...]
    join = lambda parts: jnp.concatenate(parts, axis=1)
    low = lambda a: a.astype(BF).astype(F32)
    dk_out[...] = turn_back(join(dk_u), cu_ref[...], su_ref[...]).astype(BF)
    dv_out[...] = join(dv_u).astype(BF)
    dq_sum = jnp.sum(low(turn_back(join(dq), cm, sm)), axis=0, keepdims=True)
    dk_sum = jnp.sum(low(turn_back(join(dk_m), cm, sm)), axis=0, keepdims=True)
    filler = jnp.zeros((5, LANES), F32)
    dm_out[...] = jnp.concatenate([dq_sum, dk_sum, join(dv_m), filler], axis=0)


def attend_back(q, k_u, k_m, kv_u, qkv_m, tables, mask, lse, datt):
    count, rows = kv_u.shape[0], q.shape[0]
    blocks = D // LANES
    per = LANES // HD
    column = lambda n: pl.BlockSpec((n, LANES), lambda i: (0, i))
    whole = lambda a: pl.BlockSpec(a.shape, lambda i: (0, 0))
    return pl.pallas_call(
        attend_back_kernel,
        grid=(blocks,),
        out_shape=[
            jax.ShapeDtypeStruct((count, D), BF),
            jax.ShapeDtypeStruct((count, D), BF),
            jax.ShapeDtypeStruct((8, D), F32),
        ],
        in_specs=[
            column(rows), column(count), column(rows),
            pl.BlockSpec((count, LANES), lambda i: (0, blocks + i)),
            pl.BlockSpec((qkv_m.shape[0], LANES), lambda i: (0, 2 * blocks + i)),
            *[whole(t) for t in tables],
            whole(mask),
            pl.BlockSpec((1, rows, per), lambda i: (i, 0, 0)),
            column(rows),
        ],
        out_specs=[column(count), column(count), column(8)],
        compiler_params=pltpu.CompilerParams(vmem_limit_bytes=VMEM_LIMIT),
        cost_estimate=pl.CostEstimate(
            flops=2 * 8 * rows * count * D, bytes_accessed=14 * rows * D,
            transcendentals=2 * rows * count * H,
        ),
        name="attend_back",
    )(q, k_u, k_m, kv_u, qkv_m, *tables, mask, lse, datt)


def tile_of(segments):
    return max(16, 512 // segments)


def chunk_of(width):
    return next(n for n in (640, 400, 128, width) if width % n == 0)


def logits_kernel(x_ref, w_ref, target_ref, e_ref, stats_ref, logits_ref):
    segments, _, width = w_ref.shape
    chunk = chunk_of(width)
    rows = x_ref.shape[0]
    x = x_ref[...]
    spots = [(y, at) for y in range(segments) for at in range(0, width, chunk)]
    best = None
    for place, (y, at) in enumerate(spots):
        logits = matmul(x, w_ref[y, :, at : at + chunk])
        logits_ref[:, place * chunk : (place + 1) * chunk] = logits
        best = logits if best is None else jnp.maximum(best, logits)
    top = jnp.max(best, axis=1, keepdims=True)
    lane = lax.broadcasted_iota(jnp.int32, (rows, chunk), 1)
    total = jnp.zeros((rows, chunk), F32)
    chosen = jnp.zeros((rows, chunk), F32)
    target = target_ref[...]
    for place, (y, at) in enumerate(spots):
        logits = logits_ref[:, place * chunk : (place + 1) * chunk]
        e = jnp.exp(logits - top)
        total = total + e
        chosen = chosen + jnp.where(lane == target - place * chunk, logits, 0.0)
        e_ref[y, :, at : at + chunk] = e.astype(BF)
    stats_ref[...] = jnp.concatenate(
        [top, jnp.sum(total, axis=1, keepdims=True), jnp.sum(chosen, axis=1, keepdims=True), top],
        axis=1,
    )


def head_logits(rows, weights, targets):
    count = rows.shape[0]
    segments, _, width = weights.shape
    tile = tile_of(segments)
    return pl.pallas_call(
        logits_kernel,
        grid=(count // tile,),
        out_shape=[
            jax.ShapeDtypeStruct((segments, count, width), BF),
            jax.ShapeDtypeStruct((count, 4), F32),
        ],
        in_specs=[
            pl.BlockSpec((tile, D), lambda i: (i, 0)),
            pl.BlockSpec(weights.shape, lambda i: (0, 0, 0), pipeline_mode=pl.Buffered(1)),
            pl.BlockSpec((tile, 1), lambda i: (i, 0)),
        ],
        out_specs=[
            pl.BlockSpec((segments, tile, width), lambda i: (0, i, 0)),
            pl.BlockSpec((tile, 4), lambda i: (i, 0)),
        ],
        scratch_shapes=[pltpu.VMEM((tile, segments * width), F32)],
        compiler_params=pltpu.CompilerParams(vmem_limit_bytes=VMEM_LIMIT),
        cost_estimate=pl.CostEstimate(
            flops=2 * count * D * segments * width,
            bytes_accessed=2 * count * segments * width,
            transcendentals=count * segments * width,
        ),
        name="head_logits",
    )(rows, weights, targets)


def rows_back_kernel(e_ref, w_ref, target_ref, factor_ref, d_ref, dx_ref):
    segments, _, width = w_ref.shape
    chunk = chunk_of(width)
    rows = e_ref.shape[1]
    lane = lax.broadcasted_iota(jnp.int32, (rows, chunk), 1)
    target = target_ref[...]
    factor = factor_ref[:, 0:1]
    special = factor_ref[:, 1:2]
    total = None
    for y in range(segments):
        for at in range(0, width, chunk):
            e = e_ref[y, :, at : at + chunk].astype(F32)
            hit = lane == target - (y * width + at)
            d_ref[y, :, at : at + chunk] = jnp.where(hit, special, e * factor).astype(BF)
        part = matmul_nt(d_ref[y], w_ref[y])
        total = part if total is None else total + part
    dx_ref[...] = total


def head_rows_back(e, weights, targets, factors):
    segments, count, width = e.shape
    tile = tile_of(segments)
    return pl.pallas_call(
        rows_back_kernel,
        grid=(count // tile,),
        out_shape=[
            jax.ShapeDtypeStruct(e.shape, BF),
            jax.ShapeDtypeStruct((count, D), F32),
        ],
        in_specs=[
            pl.BlockSpec((segments, tile, width), lambda i: (0, i, 0)),
            pl.BlockSpec(weights.shape, lambda i: (0, 0, 0), pipeline_mode=pl.Buffered(1)),
            pl.BlockSpec((tile, 1), lambda i: (i, 0)),
            pl.BlockSpec((tile, 2), lambda i: (i, 0)),
        ],
        out_specs=[
            pl.BlockSpec((segments, tile, width), lambda i: (0, i, 0)),
            pl.BlockSpec((tile, D), lambda i: (i, 0)),
        ],
        input_output_aliases={0: 0},
        compiler_params=pltpu.CompilerParams(vmem_limit_bytes=VMEM_LIMIT),
        cost_estimate=pl.CostEstimate(
            flops=2 * count * D * segments * width,
            bytes_accessed=4 * count * segments * width,
            transcendentals=0,
        ),
        name="head_rows_back",
    )(e, weights, targets, factors)


def layer_norm(values):
    center = values - jnp.mean(values, axis=-1, keepdims=True)
    spread = jnp.mean(center * center, axis=-1, keepdims=True)
    inv_std = lax.rsqrt(spread + NORM_EPS)
    return (center * inv_std, inv_std)


def norm_back(d_normed, normed, inv_std):
    return inv_std * (
        d_normed
        - jnp.mean(d_normed, axis=-1, keepdims=True)
        - normed * jnp.mean(d_normed * normed, axis=-1, keepdims=True)
    )


def time_features(time_index, width, steps):
    t_value = (time_index.astype(F32) + 1.0) / steps
    half_width = width // 2
    frequencies = jnp.exp(-math.log(10000.0) * jnp.arange(half_width, dtype=F32) / half_width)
    angles = 1000.0 * t_value[:, None] * frequencies[None, :]
    return jax.nn.silu(jnp.concatenate([jnp.cos(angles), jnp.sin(angles)], axis=1))


def rope_rows(positions):
    half = HD // 2
    inverse = jnp.exp(-math.log(10000.0) * jnp.arange(half, dtype=F32) * 2.0 / HD)
    angles = positions.astype(F32)[:, None] * inverse[None, :]
    cosine, sine = jnp.cos(angles), jnp.sin(angles)
    return (jnp.tile(cosine, (1, LANES // half)),
            jnp.tile(jnp.concatenate([-sine, sine], axis=1), (1, LANES // HD)))


def gelu_tanh(values):
    return jax.nn.gelu(values, approximate=True)


def adam_step(weight, first, second, ema_copy, gradient, step_value, learn_rate, decay_rate):
    first_new = BETA_ONE * first + (1.0 - BETA_ONE) * gradient
    second_new = BETA_TWO * second + (1.0 - BETA_TWO) * gradient * gradient
    first_hat = first_new / (1.0 - BETA_ONE**step_value)
    second_hat = second_new / (1.0 - BETA_TWO**step_value)
    weight_new = weight - learn_rate * (
        first_hat / (jnp.sqrt(second_hat) + ADAM_EPS) + decay_rate * weight
    )
    ema_rate = jnp.minimum(EMA_DECAY, (1.0 + step_value) / (10.0 + step_value))
    ema_new = ema_rate * ema_copy + (1.0 - ema_rate) * weight_new
    return (first_new, second_new, weight_new, ema_new)


def split3(row):
    parts, rest = [], row
    for _ in range(3):
        part = lax.reduce_precision(rest, 8, 7)
        parts.append(part.astype(BF))
        rest = rest - part
    return parts


def local(sizes, token_ids, scored, lengths, times, step_count, layer_w, layer_m, layer_v, layer_ema,
          ada_w, ada_m, ada_v, ada_ema, gains_w, gains_m, gains_v, gains_ema,
          embed_w, embed_m, embed_v, embed_ema, head_w, head_m, head_v, head_ema):
    nz, nx, ny, nc = sizes
    n = nz * nx * ny * nc
    length, score_count = token_ids.shape[1], scored.shape[1]
    free_count = length - score_count
    total_rows = n * score_count
    table_rows, table_width = embed_w.shape
    iz, ix, iy, ic = [lax.axis_index(a) for a in ALL]
    vocab_index = iy * nc + ic
    vocab_start = vocab_index * table_rows
    me = (iz * nx + ix) * (ny * nc) + vocab_index

    layer_all = lax.all_gather(layer_w.astype(BF), ALL, axis=0, tiled=True)

    tokens, masked = token_ids[0], scored[0]
    positions = jnp.arange(length, dtype=jnp.int32)
    hits = masked[:, None] == positions[None, :]
    is_masked = jnp.any(hits, axis=0)
    targets = jnp.sum(jnp.where(hits, tokens[None, :], 0), axis=1)
    keys = jnp.where(is_masked, n * V, (tokens // table_rows) * length + positions)
    rank = jnp.sum((keys[None, :] < keys[:, None]).astype(jnp.int32), axis=1)
    rank = jnp.where(is_masked, length, rank)
    slots = rank[None, :] == jnp.arange(free_count, dtype=jnp.int32)[:, None]
    free_tokens = jnp.sum(jnp.where(slots, tokens[None, :], 0), axis=1)
    free_positions = jnp.sum(jnp.where(slots, positions[None, :], 0), axis=1)

    ints = jnp.concatenate([free_tokens.reshape(-1, LANES), targets.reshape(-1, LANES),
                            jnp.broadcast_to(times[:, None], (1, LANES))], axis=0)
    ints = jnp.pad(ints, ((0, -ints.shape[0] % 8), (0, 0)))
    gain_part = jnp.pad(gains_w.astype(BF).astype(F32),
                        ((0, 8 - gains_w.shape[0]), (0, LANES - gains_w.shape[1])))
    ada_part = ada_w.astype(BF).reshape(-1, LANES)
    ints_all, gains_all, ada_all = share(sizes, 0, ints, gain_part, ada_part)
    gains = jnp.moveaxis(gains_all[:, : gains_w.shape[0], : gains_w.shape[1]], 0, 1).reshape(4, D)
    ada = ada_all.reshape(C, 6 * D)
    free_rows = free_count // LANES
    score_rows = score_count // LANES
    all_tokens = ints_all[:, :free_rows].reshape(nz * nx, ny * nc, free_count)
    all_targets = ints_all[:, free_rows : free_rows + score_rows].reshape(
        nz, nx, ny, nc, score_count)
    all_times = ints_all[:, free_rows + score_rows, 0]

    wanted = jnp.swapaxes(all_tokens, 0, 1).reshape(n, free_count)
    owners = wanted // table_rows
    low = jnp.sum((owners < vocab_index).astype(jnp.int32), axis=1)
    high = jnp.sum((owners <= vocab_index).astype(jnp.int32), axis=1)
    local_ids = wanted - vocab_start
    looked_up = gather_rows(embed_w, local_ids, low, high)
    looked_up = looked_up.reshape(ny * nc, nz * nx * free_count, table_width)
    got = exchange(lambda k: pick(looked_up, k), ("y", "c"))
    mine = got[0][1].astype(F32)
    for _, piece in got[1:]:
        mine = mine + piece.astype(F32)
    mine = mine.astype(BF).reshape(nz * nx, free_count, table_width)
    columns = in_order(exchange(lambda k: pick(mine, k), ("z", "x")))
    x0_u = jnp.swapaxes(columns, 0, 1).reshape(free_count, D).astype(F32)

    head_low = head_w.astype(BF)
    piece_for = lambda k: lax.dynamic_slice_in_dim(head_low, k * SEGMENT, SEGMENT, 1)
    head_part = in_order(exchange(piece_for, ("z",))).reshape(-1, SEGMENT)

    mask_row = gains[3:4]
    condition = time_features(times, C, TSTEPS).astype(BF)
    modulation = matmul(condition, ada)
    shift_a, scale_a, gate_a, shift_m, scale_m, gate_m = [
        modulation[:, i * D : (i + 1) * D] for i in range(6)]
    normed_u, inv_u = layer_norm(x0_u)
    a_u = (normed_u * gains[0:1] * (1.0 + scale_a) + shift_a).astype(BF)
    normed_0, inv_0 = layer_norm(mask_row)
    a_m = (normed_0 * gains[0:1] * (1.0 + scale_a) + shift_a).astype(BF)
    w_qkv, w_o = layer_all[:, : 3 * D], layer_all[:, 3 * D : 4 * D]
    w_up, w_down = layer_all[:, 4 * D : 4 * D + FF], layer_all[:, 4 * D + FF :]
    qkv_m = matmul(jnp.broadcast_to(a_m, (16, D)), w_qkv)
    kv_u = matmul(a_u, w_qkv[:, D:])
    tables = (*rope_rows(free_positions), *rope_rows(masked))
    mask = jnp.where(free_positions[None, :] < lengths[:, None], 0.0, -1e30)
    mask = jnp.broadcast_to(mask, (8, free_count)).astype(F32)
    q, k_u, k_m, att, lse_a = attend(kv_u, qkv_m, tables, mask)
    branch = matmul(att, w_o)
    x1 = mask_row + gate_a * branch
    normed_m, inv_m = layer_norm(x1)
    b = (normed_m * gains[1:2] * (1.0 + scale_m) + shift_m).astype(BF)
    pre = matmul(b, w_up)
    act = gelu_tanh(pre).astype(BF)
    mlp = matmul_nt(act, w_down)
    x2 = x1 + gate_m * mlp
    normed_f, inv_f = layer_norm(x2)
    final = (normed_f * gains[2:3]).astype(BF)

    final_turned = jnp.swapaxes(final.reshape(score_count, nz, nx, -1), 1, 2).reshape(score_count, D)
    head_all = lax.all_gather(head_part, ("y", "x"), axis=0, tiled=True).reshape(ny, D, SEGMENT)
    rows = lax.all_gather(final_turned, ("z", "c"), axis=0, tiled=True)
    group = rows.shape[0]
    row_targets = pick(jnp.moveaxis(jnp.moveaxis(all_targets, 3, 1), (2, 3), (0, 1)).reshape(
        nx * ny, group), ix * ny + iy)
    row_times = pick(jnp.moveaxis(jnp.moveaxis(all_times.reshape(nz, nx, ny, nc), 3, 1), (2, 3), (0, 1))
                     .reshape(nx * ny, nz * nc), ix * ny + iy)
    row_weights = jnp.repeat(TSTEPS / (row_times.astype(F32) + 1.0) / total_rows, score_count)
    owner, within = row_targets // table_rows, row_targets % table_rows
    owned = jnp.logical_and(owner % nc == ic, within // SEGMENT == iz)
    column_of = jnp.where(owned, (owner // nc) * SEGMENT + within % SEGMENT, -1)[:, None]
    e, stats = head_logits(rows, head_all, column_of)
    top = stats[:, 0]
    every = lax.all_gather(stats.T, ("z", "c"), axis=0)
    best = jnp.max(every[:, 0], axis=0)
    log_total = best + jnp.log(jnp.sum(every[:, 1] * jnp.exp(every[:, 0] - best), axis=0))
    chosen = jnp.sum(every[:, 2], axis=0)
    own_start = (iz * nc + ic) * score_count
    own_terms = lax.dynamic_slice_in_dim(row_weights * (log_total - chosen), own_start, score_count)
    loss_part = jnp.sum(own_terms)
    factors = jnp.stack([row_weights * jnp.exp(top - log_total),
                         row_weights * (jnp.exp(chosen - log_total) - 1.0)], axis=1)
    d_logits, d_rows = head_rows_back(e, head_all, column_of, factors)
    d_final = lax.psum_scatter(d_rows, ("z", "c"), scatter_dimension=0, tiled=True)
    d_final = jnp.swapaxes(d_final.reshape(score_count, nx, nz, -1), 1, 2).reshape(score_count, D)

    d_head = jnp.einsum("rd,yrv->ydv", rows, d_logits, preferred_element_type=F32)
    d_head = d_head.reshape(ny * nx, -1, SEGMENT)
    block_for = lambda k: pick(d_head, lax.rem(k, ny) * nx + k // ny)
    got = exchange(lambda k: block_for(k).astype(BF), ("x", "y"))
    g_part = block_for(got[0][0])
    for _, piece in got[1:]:
        g_part = g_part + piece.astype(F32)
    g_part = g_part.reshape(nz, -1, SEGMENT)
    g_head = in_order(exchange(lambda k: pick(g_part, k), ("z",)))
    g_head = jnp.swapaxes(g_head, 0, 1).reshape(head_w.shape)

    d_gain_f = jnp.sum(d_final * normed_f, axis=0)
    d_x2 = norm_back(d_final * gains[2:3], normed_f, inv_f)
    d_gate_m = jnp.sum(d_x2 * mlp, axis=0)
    d_out = (d_x2 * gate_m).astype(BF)
    d_down = matmul_tn(d_out, act)
    d_act = matmul(d_out, w_down)
    d_pre = jax.vjp(gelu_tanh, pre)[1](d_act)[0].astype(BF)
    d_up = matmul_tn(b, d_pre)
    d_b = matmul_nt(d_pre, w_up)
    d_shift_m = jnp.sum(d_b, axis=0)
    product = jnp.sum(d_b * normed_m, axis=0)
    d_scale_m = product * gains[1]
    d_gain_m = product * (1.0 + scale_m[0])
    d_x1 = d_x2 + norm_back(d_b * ((1.0 + scale_m) * gains[1:2]), normed_m, inv_m)
    d_gate_a = jnp.sum(d_x1 * branch, axis=0)
    d_branch = (d_x1 * gate_a).astype(BF)
    d_wout = matmul_tn(att, d_branch)
    d_att = matmul_nt(d_branch, w_o).astype(BF)
    d_k, d_v, d_qkv_m = attend_back(q, k_u, k_m, kv_u, qkv_m, tables, mask, lse_a, d_att)
    d_kv = jnp.concatenate([d_k, d_v], axis=1)
    d_wkv = matmul_tn(a_u, d_kv)
    d_row_m = d_qkv_m[:3].reshape(3 * D)
    d_a_u = matmul_nt(d_kv, w_qkv[:, D:])
    d_parts = matmul_nt(jnp.pad(jnp.stack(split3(d_row_m)), ((0, 13), (0, 0))), w_qkv)
    d_a_m = jnp.sum(d_parts[:3], axis=0, keepdims=True)
    d_shift_a = jnp.sum(d_a_u, axis=0) + d_a_m[0]
    product = jnp.sum(d_a_u * normed_u, axis=0) + (d_a_m * normed_0)[0]
    d_scale_a = product * gains[0]
    d_gain_a = product * (1.0 + scale_a[0])
    scaling = (1.0 + scale_a) * gains[0:1]
    d_x0_u = norm_back(d_a_u * scaling, normed_u, inv_u)
    d_mask = jnp.sum(d_x1, axis=0) + norm_back(d_a_m * scaling, normed_0, inv_0)[0]

    sent = jnp.swapaxes(d_x0_u.astype(BF).reshape(free_count, nz * nx, -1), 0, 1)
    arrived = in_order(exchange(lambda k: pick(sent, k), ("z", "x")))
    arrived = in_order(exchange(lambda k: arrived, ("y", "c")))
    g_embed = scatter_rows(arrived.reshape(n, free_count, table_width), local_ids, low, high,
                           table_rows)

    small = jnp.concatenate([d_shift_a, d_scale_a, d_gate_a, d_shift_m, d_scale_m, d_gate_m,
                             d_gain_a, d_gain_m, d_gain_f, d_mask,
                             a_m[0].astype(F32), d_row_m, jnp.broadcast_to(loss_part, (LANES,))])
    small = small.reshape(-1, LANES)
    count_small = small.shape[0]
    small_all = share(sizes, 1, jnp.pad(small, ((0, -count_small % 8), (0, 0))))[0]
    small_all = small_all[:, :count_small].reshape(n, -1)
    d_mod_all = small_all[:, : 6 * D]
    d_gains = jnp.sum(small_all[:, 6 * D : 10 * D], axis=0).reshape(4, D)
    g_gains = lax.dynamic_slice_in_dim(d_gains, me * gains_w.shape[1], gains_w.shape[1], 1)
    total_loss = jnp.sum(small_all[:, 14 * D])
    condition_all = time_features(all_times, C, TSTEPS).astype(BF).astype(F32)
    condition_rows = lax.dynamic_slice_in_dim(condition_all, me * ada_w.shape[0], ada_w.shape[0], 1)
    exact = lambda a, b: jnp.einsum("nr,nc->rc", a, b, precision=lax.Precision.HIGHEST)
    g_ada = exact(condition_rows, d_mod_all)
    a_rows = lax.dynamic_slice_in_dim(small_all[:, 10 * D : 11 * D], me * layer_w.shape[0],
                                      layer_w.shape[0], 1)
    g_outer = exact(a_rows, small_all[:, 11 * D : 14 * D])

    scatter = lambda a: lax.psum_scatter(a, ALL, scatter_dimension=0, tiled=True)
    g_down, g_up = scatter(d_down), scatter(d_up)
    g_wout, g_wkv = scatter(d_wout), scatter(d_wkv)
    g_layer = jnp.concatenate(
        [g_outer[:, :D], g_outer[:, D:] + g_wkv, g_wout, g_up, g_down], axis=1)

    squares = sum(jnp.sum(g * g) for g in (g_layer, g_ada, g_gains, g_embed, g_head))
    squares_all = share(sizes, 2, jnp.broadcast_to(squares, (8, LANES)))[0]
    grad_norm = jnp.sqrt(jnp.sum(squares_all[:, 0, 0]))
    factor = jnp.minimum(1.0, CLIP_NORM / grad_norm)
    step_value = step_count[0].astype(F32)
    updates = (
        (layer_w, layer_m, layer_v, layer_ema, g_layer),
        (ada_w, ada_m, ada_v, ada_ema, g_ada),
        (gains_w, gains_m, gains_v, gains_ema, g_gains),
        (embed_w, embed_m, embed_v, embed_ema, g_embed),
        (head_w, head_m, head_v, head_ema, g_head),
    )
    results = []
    for (w, m, v, ema, g), rate, decay in zip(updates, LEARN_RATES, WEIGHT_DECAYS):
        results.extend(adam_step(w, m, v, ema, g * factor, step_value, rate, decay))
    return (total_loss, grad_norm, *results)


def solution(mesh):
    dp, vocab = mesh.shape["dp"], mesh.shape["vocab"]
    nz, nc = V // vocab // SEGMENT, 2
    sizes = (nz, dp // nz, vocab // nc, nc)
    fine = Mesh(mesh.devices.reshape(sizes), ALL)
    rows_all, columns_all = P(ALL, None), P(None, ALL)
    table, head = P(("y", "c"), ("z", "x")), P(("z", "x"), ("y", "c"))
    weights = [rows_all] * 8 + [columns_all] * 4 + [table] * 4 + [head] * 4
    return jax.shard_map(
        functools.partial(local, sizes),
        mesh=fine,
        in_specs=(rows_all, rows_all, P(ALL), P(ALL), P(), *weights),
        out_specs=(P(), P(), *weights),
        check_vma=False,
    )
```

time: 3780 us -> 1550 us (0.41)
  waiting for transfers between devices: 2270 us -> 518 us
  matrix products: 768 us -> 129 us
  Pallas kernels: 0 us -> 388 us
  other arithmetic: 250 us -> 108 us
  blocking collectives: 152 us -> 14.9 us
  starting transfers between devices: 1.29 us -> 115 us
  local copies, waits for them, and re-layouts: 302 us -> 243 us
    all_gather x6 -> x3, waiting for transfers between devices: 741 us -> 51.2 us  [the longest x1 51.2 us: local(): rows = lax.all_gather(final_turned, ('z', 'c'), axis=0, tiled=True)]
    reduce_scatter x4 -> x5, waiting for transfers between devices: 903 us -> 230 us  [the longest x1 128 us: local(): lax.psum_scatter(d_rows, ('z', 'c'), scatter_dimension=0, tiled=True)]
    dot_general x43 -> x18, matrix products: 768 us -> 129 us  [the longest x15 76 us: dot(): lax.dot_general(a, b, ((contract[0], contract[1]), ((), ())), preferred_e...]
    unnamed x14 -> x8, waiting for transfers between devices: 625 us -> 0.13 us
    pallas_call x0 -> x9, Pallas kernels: none -> 388 us  [the longest x3 138 us: share(): pl.pallas_call(functools.partial(share_kernel, sizes, count), out_shape=[...]
    ppermute x0 -> x29, waiting for transfers between devices: none -> 237 us  [exchange(): moved = lax.ppermute(piece, axes, [(i, (i + step) % n) for i in range(n)])]
    ppermute x0 -> x29, starting transfers between devices: none -> 114 us  [exchange(): moved = lax.ppermute(piece, axes, [(i, (i + step) % n) for i in range(n)])]
    gather x8 -> x0, local copies, waits for them, and re-layouts: 74.5 us -> none  [the longest x2 36.9 us: local(): jnp.take(embed_all, jnp.clip(local_ids, 0, vocab_rows - 1), axis=0)]
  transfers between devices with their start and end apart: 12 -> 37, of which waited for: 9 -> 16; matrix products, arithmetic and copies ran while one was open for 11% -> 23% of each run, Pallas kernels for 0% -> 14%
where the time goes in v1:
time: 1550 us; the launch traced here: 1540 us
  waiting for transfers between devices  518 us (33%)
  Pallas kernels  388 us (25%)
  local copies, waits for them, and re-layouts  243 us (16%)
  matrix products  129 us (8%)
  starting transfers between devices  115 us (7%)
  other arithmetic  108 us (7%)
  between operations  26 us (2%)
    ppermute x29, waiting for transfers between devices, exchange(): moved = lax.ppermute(piece, axes, [(i, (i + step) % n) for i in range(n)])  237 us
    pallas_call x3, Pallas kernels, share(): pl.pallas_call(functools.partial(share_kernel, sizes, count), out_shape=[...  138 us
    reduce_scatter x1, waiting for transfers between devices, local(): lax.psum_scatter(d_rows, ('z', 'c'), scatter_dimension=0, tiled=True)  128 us
    ppermute x29, starting transfers between devices, exchange(): moved = lax.ppermute(piece, axes, [(i, (i + step) % n) for i in range(n)])  114 us
    reduce_scatter x4, waiting for transfers between devices, local(): lax.psum_scatter(a, ALL, scatter_dimension=0, tiled=True)  102 us
    dynamic_update_slice x28, local copies, waits for them, and re-layouts, in_order(): out = lax.dynamic_update_index_in_dim(out, piece, sender, 0)  95.6 us
    pallas_call x1, Pallas kernels, head_logits(): pl.pallas_call(logits_kernel, grid=(count // tile,), out_shape=[jax.Shape...  79.5 us
    dot_general x15, matrix products, dot(): lax.dot_general(a, b, ((contract[0], contract[1]), ((), ())), preferred_e...  76 us
  transfers between devices with their start and end apart: 37, of which 16 were waited for; matrix products, arithmetic and copies ran while one was open for 23% of the time, Pallas kernels for 14%

profile of v1, /device:TPU:0, one launch (start us, length us, event | category | flops | bytes accessed | tf_op | source)
XLA Modules:
  0.0 1542.6 jit_solution(2736440296631644208)
XLA Ops:
  22.6 16.0 %collective-permute-done.10 = bf16[96,3200]{1,0:T(8,128)(2,1)} collective-permute-done((bf16[96,3200]{1,0:T(8,128)(2,1)}, bf16[96,3200]{1,0:T(8,128)(2,1)}, u32[]{:S(2)}, u32[]{:S(2)}) %collective-permute-start.10) | collective-permute-done | bytes 614432 | tf_op jit(solution)/shard_map/ppermute | solution.py:137
  40.6 27.7 %collective-permute-done.11 = bf16[96,3200]{1,0:T(8,128)(2,1)} collective-permute-done((bf16[96,3200]{1,0:T(8,128)(2,1)}, bf16[96,3200]{1,0:T(8,128)(2,1)}, u32[]{:S(2)}, u32[]{:S(2)}) %collective-permute-start.11) | collective-permute-done | bytes 614432 | tf_op jit(solution)/shard_map/ppermute | solution.py:137
  77.0 84.0 %share0.1 = (s32[32,16,128]{2,1,0:T(8,128)}, f32[32,8,128]{2,1,0:T(8,128)}, bf16[32,144,128]{2,1,0:T(8,128)(2,1)}) custom-call(s32[16,128]{1,0:T(8,128)} %pad.18.refs_0_, f32[8,128]{1,0:T(8,128)} %pad_convert_fusion.refs_1_, bf16[144,128]{1,0:T(8,128)(2,1)} %reshape.810.refs_2_), custom_call_target="tpu_custom_call" | custom-call | tf_op jit(solution)/shard_map/share0/pallas_call | solution.py:107
  165.5 6.4 copy.338.table_ref
  172.0 29.4 %gather_rows.1 = bf16[32,512,96]{2,1,0:T(8,128)(2,1)} custom-call(s32[32]{0:T(128)} %reduce_sum.388.low_ref, s32[32]{0:T(128)} %reduce_sum.390.high_ref, s32[32,512]{1,0:T(8,128)} %bitcast.266, f32[12800,96]{1,0:T(8,128)} %copy.338.table_ref), custom_call_target="tpu_custom_call" | custom-call | tf_op jit(solution)/shard_map/gather_rows/pallas_call | solution.py:177
  224.1 14.8 collective-permute-done
  240.4 30.9 %collective-permute-done.2 = bf16[4096,96]{0,1:T(8,128)(2,1)} collective-permute-done((bf16[4096,96]{0,1:T(8,128)(2,1)}, bf16[4096,96]{0,1:T(8,128)(2,1)}, u32[]{:S(2)}, u32[]{:S(2)}) %collective-permute-start.2) | collective-permute-done | bytes 786464 | tf_op jit(solution)/shard_map/ppermute | solution.py:137
  277.3 17.8 %collective-permute-start.4 = (bf16[512,96]{0,1:T(8,128)(2,1)S(1)}, bf16[512,96]{0,1:T(8,128)(2,1)S(1)}, u32[]{:S(2)}, u32[]{:S(2)}) collective-permute-start(bf16[512,96]{0,1:T(8,128)(2,1)S(1)} %bitcast.276), channel_id=1, source_target_pairs={{0,8},{4,12},{8,16},{12,20},{16,24},{20,28},{24,0},{28,4},{1,9},{5... | collective-permute-start | bytes 294920 | tf_op jit(solution)/shard_map/ppermute | solution.py:137
  321.1 18.7 %attend.1 = (bf16[512,768]{1,0:T(8,128)(2,1)}, bf16[512,768]{1,0:T(8,128)(2,1)}, bf16[512,768]{1,0:T(8,128)(2,1)}, bf16[512,768]{1,0:T(8,128)(2,1)}, f32[6,512,2]{2,1,0:T(8,128)}) custom-call(f32[512,1536]{1,0:T(8,128)} %fusion.42.kv_ref.vv_ref, f32[512,1536]{1,0:T(8,128)} %fusion.42.kv_ref.vv_ref, f32[16,2304]{1,0:T(8,128)} %fusion.23.qm_ref.km_ref.vm_ref, ...), custom_call_target="tpu_custom_call" | custom-call | flops 1207959552 | bytes 4718592 | tf_op jit(solution)/shard_map/attend/pallas_call | solution.py:293
  347.5 9.6 fusion.112
  368.8 7.8 fusion.34.target_ref
  376.6 51.2 %all-gather.8.cloned.1.call-done.x_ref = bf16[4096,768]{1,0:T(8,128)(2,1)} async-done(((bf16[512,768]{1,0:T(8,128)(2,1)}), bf16[4096,768]{1,0:T(8,128)(2,1)}) %all-gather.8.cloned.1.call-update) | async-done | bytes 6291472 | tf_op jit(solution)/shard_map/all_gather | solution.py:660
  427.8 79.5 %head_logits.1 = (bf16[2,4096,3200]{2,1,0:T(8,128)(2,1)}, f32[4096,4]{1,0:T(8,128)}) custom-call(bf16[4096,768]{1,0:T(8,128)(2,1)} %all-gather.8.cloned.1.call-done.x_ref, bf16[2,768,3200]{2,1,0:T(8,128)(2,1)} %bitcast.295, s32[4096,1]{1,0:T(8,128)} %fusion.34.target_ref), custom_call_target="tpu_custom_call" | custom-call | flops 40265318400 | bytes 52428800 | tf_op jit(solution)/shard_map/head_logits/pallas_call | solution.py:432
  509.6 14.9 all-gather.1
  534.9 65.6 %head_rows_back.1 = (bf16[2,4096,3200]{2,1,0:T(8,128)(2,1)}, f32[4096,768]{1,0:T(8,128)}) custom-call(bf16[2,4096,3200]{2,1,0:T(8,128)(2,1)} %get-tuple-element.45.e_ref, bf16[2,768,3200]{2,1,0:T(8,128)(2,1)} %bitcast.296, s32[4096,1]{1,0:T(8,128)} %fusion.34.target_ref, f32[4096,2]{1,0:T(8,128)} %pad_maximum_fusion.factor_ref), custom_call_target="tpu_custom_call", output_to_operand_aliasing={{0}: (0, {})} | custom-call | flops 40265318400 | bytes 104857600 | tf_op jit(solution)/shard_map/head_rows_back/pallas_call | solution.py:481
  600.6 127.7 %reduce-scatter.6.cloned.1.call-done = f32[512,768]{1,0:T(8,128)} async-done(((f32[4096,768]{1,0:T(8,128)}), f32[512,768]{1,0:T(8,128)}) %reduce-scatter.6.cloned.1.call-update) | async-done | bytes 1572880 | tf_op jit(solution)/shard_map/reduce_scatter | solution.py:682
  736.2 9.2 fusion.7
  745.4 7.1 multiply_reduce_fusion.5
  758.1 23.9 %attend_back.1 = (bf16[512,768]{1,0:T(8,128)(2,1)}, bf16[512,768]{1,0:T(8,128)(2,1)}, f32[8,768]{1,0:T(8,128)}) custom-call(bf16[512,768]{1,0:T(8,128)(2,1)} %get-tuple-element.40.q_ref, bf16[512,768]{1,0:T(8,128)(2,1)} %get-tuple-element.41.ku_ref, bf16[512,768]{1,0:T(8,128)(2,1)} %get-tuple-element.42.km_ref, f32[512,1536]{1,0:T(8,128)} %fusion.42.kv_ref.vv_ref, ...), custom_call_target="tpu_custom_call" | custom-call | flops 3221225472 | bytes 5505024 | tf_op jit(solution)/shard_map/attend_back/pallas_call | solution.py:365
  793.9 7.3 fusion.104
  801.4 50.4 %fusion.8 = f32[2,3200,768]{1,2,0:T(8,128)} fusion(bf16[2,4096,3200]{2,1,0:T(8,128)(2,1)} %get-tuple-element.51, bf16[4096,768]{1,0:T(8,128)(2,1)} %all-gather.8.cloned.1.call-done.x_ref), kind=kOutput, calls=%fused_computation.16 | convolution fusion | flops 40265318400 | bytes 78381056 | tf_op jit(solution)/shard_map/rd,yrv->ydv/dot_general | solution.py:685
  851.8 8.8 fusion.27
  865.0 9.2 fusion.57
  874.2 96.6 %collective-permute-done.23 = bf16[384,3200]{1,0:T(8,128)(2,1)} collective-permute-done((bf16[384,3200]{1,0:T(8,128)(2,1)}, bf16[384,3200]{1,0:T(8,128)(2,1)}, u32[]{:S(2)}, u32[]{:S(2)}) %collective-permute-start.23) | collective-permute-done | bytes 2457632 | tf_op jit(solution)/shard_map/ppermute | solution.py:137
  987.3 6.4 copy.384
  993.7 6.5 copy.386
  1000.2 6.4 copy.389
  1015.5 19.9 %dynamic_update_slice.112 = f32[4,96,3200]{2,0,1:T(4,128)} dynamic-update-slice(f32[4,96,3200]{2,0,1:T(4,128)} %broadcast_in_dim.238, f32[1,96,3200]{2,0,1:T(1,128)S(1)} %copy.404, s32[]{:T(128)S(6)} %select_n.303, s32[]{:T(128)} %constant.463.clone.1, s32[]{:T(128)} %constant.463.clone.1) | dynamic-update-slice | bytes 2457604 | tf_op jit(solution)/shard_map/jit(dynamic_update_index_in_dim)/dynamic_update_slice | solution.py:145
  1037.6 20.0 %dynamic_update_slice.113 = f32[4,96,3200]{2,0,1:T(4,128)} dynamic-update-slice(f32[4,96,3200]{2,0,1:T(4,128)} %dynamic_update_slice.112, f32[1,96,3200]{2,0,1:T(1,128)S(1)} %broadcast_in_dim.239, s32[]{:T(128)S(6)} %select_n.305, s32[]{:T(128)} %constant.463.clone.1, s32[]{:T(128)} %constant.463.clone.1) | dynamic-update-slice | bytes 2457604 | tf_op jit(solution)/shard_map/jit(dynamic_update_index_in_dim)/dynamic_update_slice | solution.py:145
  1057.6 12.1 collective-permute-done.27
  1071.9 20.0 %dynamic_update_slice.114 = f32[4,96,3200]{2,0,1:T(4,128)} dynamic-update-slice(f32[4,96,3200]{2,0,1:T(4,128)} %dynamic_update_slice.113, f32[1,96,3200]{2,0,1:T(1,128)S(1)} %broadcast_in_dim.240, s32[]{:T(128)S(6)} %select_n.307, s32[]{:T(128)} %constant.463.clone.1, s32[]{:T(128)} %constant.463.clone.1) | dynamic-update-slice | bytes 2457604 | tf_op jit(solution)/shard_map/jit(dynamic_update_index_in_dim)/dynamic_update_slice | solution.py:145
  1094.0 20.0 %dynamic_update_slice.115 = f32[4,96,3200]{2,0,1:T(4,128)} dynamic-update-slice(f32[4,96,3200]{2,0,1:T(4,128)} %dynamic_update_slice.114, f32[1,96,3200]{2,0,1:T(1,128)S(1)} %broadcast_in_dim.241, s32[]{:T(128)S(6)} %select_n.309, s32[]{:T(128)} %constant.463.clone.1, s32[]{:T(128)} %constant.463.clone.1) | dynamic-update-slice | bytes 2457604 | tf_op jit(solution)/shard_map/jit(dynamic_update_index_in_dim)/dynamic_update_slice | solution.py:145
  1114.0 5.7 multiply_reduce_fusion.1
  1126.9 30.2 %collective-permute-start.14 = (bf16[512,96]{0,1:T(8,128)(2,1)}, bf16[512,96]{0,1:T(8,128)(2,1)}, u32[]{:S(2)}, u32[]{:S(2)}) collective-permute-start(bf16[512,96]{0,1:T(8,128)(2,1)} %get-tuple-element.289), channel_id=1, source_target_pairs={{0,8},{4,12},{8,16},{12,20},{16,24},{20,28},{24,0},{28,4},{1,9},{5... | collective-permute-start | bytes 294920 | tf_op jit(solution)/shard_map/ppermute | solution.py:137
  1171.8 44.3 %share1.1 = f32[32,88,128]{2,1,0:T(8,128)} custom-call(f32[88,128]{1,0:T(8,128)} %pad.22.refs_0_), custom_call_target="tpu_custom_call" | custom-call | tf_op jit(solution)/shard_map/share1/pallas_call | solution.py:107
  1219.8 8.4 collective-permute-start.18
  1229.1 12.6 collective-permute-start.19
  1258.9 15.9 %collective-permute-done.20 = bf16[8,512,96]{1,2,0:T(8,128)(2,1)} collective-permute-done((bf16[8,512,96]{1,2,0:T(8,128)(2,1)S(1)}, bf16[8,512,96]{1,2,0:T(8,128)(2,1)}, u32[]{:S(2)}, u32[]{:S(2)}) %collective-permute-start.20) | collective-permute-done | bytes 786464 | tf_op jit(solution)/shard_map/ppermute | solution.py:137
  1278.8 15.0 collective-permute-done.22
  1298.6 33.1 %scatter_rows.1 = f32[12800,96]{1,0:T(8,128)} custom-call(s32[32]{0:T(128)} %reduce_sum.388.low_ref, s32[32]{0:T(128)} %reduce_sum.390.high_ref, s32[32,512]{1,0:T(8,128)} %bitcast.267, bf16[32,512,96]{2,1,0:T(8,128)(2,1)} %bitcast.79.rows_ref), custom_call_target="tpu_custom_call" | custom-call | tf_op jit(solution)/shard_map/scatter_rows/pallas_call | solution.py:220
  1339.4 101.9 %reduce-scatter.14.cloned.1.call-done = f32[24,3072]{1,0:T(8,128)} async-done(((f32[768,3072]{1,0:T(8,128)}), f32[24,3072]{1,0:T(8,128)}) %reduce-scatter.14.cloned.1.call-update) | async-done | bytes 294928 | tf_op jit(solution)/shard_map/reduce_scatter | solution.py:754
  1447.0 9.9 share2.1
  1464.4 22.0 %multiply_add_fusion = (f32[12800,96]{1,0:T(8,128)}, f32[12800,96]{1,0:T(8,128)}, f32[12800,96]{1,0:T(8,128)}, f32[12800,96]{1,0:T(8,128)}) fusion(f32[12800,96]{1,0:T(8,128)} %copy.389, f32[]{:T(128)S(6)} %sub.346, f32[]{:T(128)} %bitcast.94, f32[12800,96]{1,0:T(8,128)} %copy.338.table_ref, f32[]{:T(128)} %bitcast.93, f32[]{:T(128)} %bitcast.92, ...), kind=kLoop, calls=%fused_computation.5 | loop fusion | flops 23347200 | bytes 44236820 | tf_op jit(solution)/shard_map/add | solution.py:554
  1486.4 6.3 copy.390
  1492.7 6.3 copy.391
  1499.0 6.3 copy.392
  1505.3 6.5 copy.393
  1516.7 16.8 %multiply_add_fusion.2 = (f32[96,12800]{1,0:T(8,128)}, f32[96,12800]{1,0:T(8,128)}, f32[96,12800]{1,0:T(8,128)}, f32[96,12800]{1,0:T(8,128)}) fusion(f32[96,12800]{1,0:T(8,128)} %param.49, f32[]{:T(128)S(6)} %sub.346, f32[]{:T(128)} %bitcast.94, f32[96,12800]{1,0:T(8,128)} %param.46, f32[]{:T(128)} %bitcast.93, f32[]{:T(128)} %bitcast.92, ...), kind=kLoop, calls=%fused_computation.23 | loop fusion | flops 22118400 | bytes 44236816 | tf_op jit(solution)/shard_map/add | solution.py:554
  (439 shorter events, 249.4 us)
Async XLA Ops:
  7.2 305.1 %all-gather.6.cloned.1.call-start = ((), (), s32[]{:S(2)}) async-start(), calls=%async_computation.5 | async-start | bytes 14598144 | tf_op jit(solution)/shard_map/all_gather | solution.py:581
  9.2 367.4 %all-gather.10.cloned.1.call-start = ((), (), s32[]{:S(2)}) async-start(), calls=%async_computation.7 | async-start | bytes 12288000 | tf_op jit(solution)/shard_map/all_gather | solution.py:659
  13.1 25.5 %collective-permute-start.10 = (bf16[96,3200]{1,0:T(8,128)(2,1)}, bf16[96,3200]{1,0:T(8,128)(2,1)}, u32[]{:S(2)}, u32[]{:S(2)}) collective-permute-start(bf16[96,3200]{1,0:T(8,128)(2,1)} %get-tuple-element.281), channel_id=1, source_target_pairs={{0,8},{8,16},{16,24},{24,0},{1,9},{9,17},{17,25},{25,1},{2,10},{10... | collective-permute-start | bytes 1843208 | tf_op jit(solution)/shard_map/ppermute | solution.py:137
  16.2 52.1 %collective-permute-start.11 = (bf16[96,3200]{1,0:T(8,128)(2,1)}, bf16[96,3200]{1,0:T(8,128)(2,1)}, u32[]{:S(2)}, u32[]{:S(2)}) collective-permute-start(bf16[96,3200]{1,0:T(8,128)(2,1)} %get-tuple-element.280), channel_id=1, source_target_pairs={{0,16},{8,24},{16,0},{24,8},{1,17},{9,25},{17,1},{25,9},{2,18},{10... | collective-permute-start | bytes 1843208 | tf_op jit(solution)/shard_map/ppermute | solution.py:137
  18.7 51.5 %collective-permute-start.12 = (bf16[96,3200]{1,0:T(8,128)(2,1)S(1)}, bf16[96,3200]{1,0:T(8,128)(2,1)}, u32[]{:S(2)}, u32[]{:S(2)}) collective-permute-start(bf16[96,3200]{1,0:T(8,128)(2,1)S(1)} %get-tuple-element.279), channel_id=1, source_target_pairs={{0,24},{8,0},{16,8},{24,16},{1,25},{9,1},{17,9},{25,17},{2,26},{10... | collective-permute-start | bytes 1843208 | tf_op jit(solution)/shard_map/ppermute | solution.py:137
  72.3 355.5 %all-gather.8.cloned.1.call-start = ((), (), s32[]{:S(2)}) async-start(), calls=%async_computation.6 | async-start | bytes 7077888 | tf_op jit(solution)/shard_map/all_gather | solution.py:660
  207.1 31.9 %collective-permute-start = (bf16[4096,96]{0,1:T(8,128)(2,1)}, bf16[4096,96]{0,1:T(8,128)(2,1)}, u32[]{:S(2)}, u32[]{:S(2)}) collective-permute-start(bf16[4096,96]{0,1:T(8,128)(2,1)} %bitcast.262), channel_id=1, source_target_pairs={{0,1},{1,2},{2,3},{3,0},{4,5},{5,6},{6,7},{7,4},{8,9},{9,10},{10,1... | collective-permute-start | bytes 2359304 | tf_op jit(solution)/shard_map/ppermute | solution.py:137
  208.3 32.1 %collective-permute-start.1 = (bf16[4096,96]{0,1:T(8,128)(2,1)}, bf16[4096,96]{0,1:T(8,128)(2,1)}, u32[]{:S(2)}, u32[]{:S(2)}) collective-permute-start(bf16[4096,96]{0,1:T(8,128)(2,1)} %bitcast.263), channel_id=1, source_target_pairs={{0,2},{1,3},{2,0},{3,1},{4,6},{5,7},{6,4},{7,5},{8,10},{9,11},{10,... | collective-permute-start | bytes 2359304 | tf_op jit(solution)/shard_map/ppermute | solution.py:137
  211.2 60.1 %collective-permute-start.2 = (bf16[4096,96]{0,1:T(8,128)(2,1)}, bf16[4096,96]{0,1:T(8,128)(2,1)}, u32[]{:S(2)}, u32[]{:S(2)}) collective-permute-start(bf16[4096,96]{0,1:T(8,128)(2,1)} %bitcast.264), channel_id=1, source_target_pairs={{0,3},{1,0},{2,1},{3,2},{4,7},{5,4},{6,5},{7,6},{8,11},{9,8},{10,9... | collective-permute-start | bytes 2359304 | tf_op jit(solution)/shard_map/ppermute | solution.py:137
  217.9 97.7 %copy-start.47 = (f32[768]{0:T(1024)}, f32[768]{0:T(1024)S(1)}, u32[]{:S(2)}) copy-start(f32[768]{0:T(1024)S(1)} %mul.873) | copy-start | bytes 9220
  222.8 571.1 %copy-start.26 = (f32[768]{0:T(1024)}, f32[768]{0:T(1024)S(1)}, u32[]{:S(2)}) copy-start(f32[768]{0:T(1024)S(1)} %add.713) | copy-start | bytes 9220
  222.9 571.0 %copy-start.50 = (f32[768]{0:T(1024)}, f32[768]{0:T(1024)S(1)}, u32[]{:S(2)}) copy-start(f32[768]{0:T(1024)S(1)} %mul.903) | copy-start | bytes 9220
  223.4 50.3 %copy-start.20 = (f32[1,4608]{1,0:T(1,128)}, f32[1,4608]{1,0:T(1,128)S(1)}, u32[]{:S(2)}) copy-start(f32[1,4608]{1,0:T(1,128)S(1)} %fusion.90) | copy-start | bytes 55300
  223.4 88.8 %copy-start.37 = (bf16[768]{0:T(1024)(128)(2,1)}, bf16[768]{0:T(1024)(128)(2,1)S(1)}, u32[]{:S(2)}) copy-start(bf16[768]{0:T(1024)(128)(2,1)S(1)} %convert_reduce_fusion.4) | copy-start | bytes 4612
  224.1 91.5 %copy-start.44 = (f32[768]{0:T(1024)}, f32[768]{0:T(1024)S(1)}, u32[]{:S(2)}) copy-start(f32[768]{0:T(1024)S(1)} %get-tuple-element.233) | copy-start | bytes 9220
  224.1 91.5 %copy-start.61 = (f32[768]{0:T(1024)}, f32[768]{0:T(1024)S(1)}, u32[]{:S(2)}) copy-start(f32[768]{0:T(1024)S(1)} %get-tuple-element.232) | copy-start | bytes 9220
  224.1 569.8 %copy-start.42 = (f32[768]{0:T(1024)}, f32[768]{0:T(1024)S(1)}, u32[]{:S(2)}) copy-start(f32[768]{0:T(1024)S(1)} %get-tuple-element.229) | copy-start | bytes 9220
  275.5 24.3 %collective-permute-start.3 = (bf16[512,96]{0,1:T(8,128)(2,1)S(1)}, bf16[512,96]{0,1:T(8,128)(2,1)S(1)}, u32[]{:S(2)}, u32[]{:S(2)}) collective-permute-start(bf16[512,96]{0,1:T(8,128)(2,1)S(1)} %bitcast.277), channel_id=1, source_target_pairs={{0,4},{4,8},{8,12},{12,16},{16,20},{20,24},{24,28},{28,0},{1,5},{5... | collective-permute-start | bytes 294920 | tf_op jit(solution)/shard_map/ppermute | solution.py:137
  277.3 24.4 %collective-permute-start.4 = (bf16[512,96]{0,1:T(8,128)(2,1)S(1)}, bf16[512,96]{0,1:T(8,128)(2,1)S(1)}, u32[]{:S(2)}, u32[]{:S(2)}) collective-permute-start(bf16[512,96]{0,1:T(8,128)(2,1)S(1)} %bitcast.276), channel_id=1, source_target_pairs={{0,8},{4,12},{8,16},{12,20},{16,24},{20,28},{24,0},{28,4},{1,9},{5... | collective-permute-start | bytes 294920 | tf_op jit(solution)/shard_map/ppermute | solution.py:137
  295.1 10.9 collective-permute-start.5
  295.5 12.4 collective-permute-start.6
  298.9 9.5 collective-permute-start.7
  299.9 8.6 collective-permute-start.8
  301.8 6.8 collective-permute-start.9
  359.2 369.1 %reduce-scatter.6.cloned.1.call-start = ((), (), s32[]{:S(2)}) async-start(), calls=%async_computation.8 | async-start | bytes 14155776 | tf_op jit(solution)/shard_map/reduce_scatter | solution.py:682
  600.5 736.0 %reduce-scatter.8.cloned.1.call-start = ((), (), s32[]{:S(2)}) async-start(), calls=%async_computation.9 | async-start | bytes 4866048 | tf_op jit(solution)/shard_map/reduce_scatter | solution.py:754
  789.5 548.0 %reduce-scatter.10.cloned.1.call-start = ((), (), s32[]{:S(2)}) async-start(), calls=%async_computation.10 | async-start | bytes 2433024 | tf_op jit(solution)/shard_map/reduce_scatter | solution.py:754
  793.8 544.5 %reduce-scatter.12.cloned.1.call-start = ((), (), s32[]{:S(2)}) async-start(), calls=%async_computation.11 | async-start | bytes 9732096 | tf_op jit(solution)/shard_map/reduce_scatter | solution.py:754
  801.3 640.0 %reduce-scatter.14.cloned.1.call-start = ((), (), s32[]{:S(2)}) async-start(), calls=%async_computation.12 | async-start | bytes 9732096 | tf_op jit(solution)/shard_map/reduce_scatter | solution.py:754
  860.6 110.2 %collective-permute-start.23 = (bf16[384,3200]{1,0:T(8,128)(2,1)}, bf16[384,3200]{1,0:T(8,128)(2,1)}, u32[]{:S(2)}, u32[]{:S(2)}) collective-permute-start(bf16[384,3200]{1,0:T(8,128)(2,1)} %get-tuple-element.268), channel_id=1, source_target_pairs={{0,2},{2,4},{4,6},{6,0},{1,3},{3,5},{5,7},{7,1},{8,10},{10,12},{12... | collective-permute-start | bytes 7372808 | tf_op jit(solution)/shard_map/ppermute | solution.py:137
  862.1 108.8 %collective-permute-start.24 = (bf16[384,3200]{1,0:T(8,128)(2,1)}, bf16[384,3200]{1,0:T(8,128)(2,1)}, u32[]{:S(2)}, u32[]{:S(2)}) collective-permute-start(bf16[384,3200]{1,0:T(8,128)(2,1)} %get-tuple-element.270), channel_id=1, source_target_pairs={{0,4},{2,6},{4,0},{6,2},{1,5},{3,7},{5,1},{7,3},{8,12},{10,14},{12... | collective-permute-start | bytes 7372808 | tf_op jit(solution)/shard_map/ppermute | solution.py:137
  863.5 109.2 %collective-permute-start.25 = (bf16[384,3200]{1,0:T(8,128)(2,1)}, bf16[384,3200]{1,0:T(8,128)(2,1)}, u32[]{:S(2)}, u32[]{:S(2)}) collective-permute-start(bf16[384,3200]{1,0:T(8,128)(2,1)} %get-tuple-element.269), channel_id=1, source_target_pairs={{0,6},{2,0},{4,2},{6,4},{1,7},{3,1},{5,3},{7,5},{8,14},{10,8},{12,... | collective-permute-start | bytes 7372808 | tf_op jit(solution)/shard_map/ppermute | solution.py:137
  980.7 54.8 %collective-permute-start.26 = (f32[96,3200]{1,0:T(8,128)}, f32[96,3200]{1,0:T(8,128)}, u32[]{:S(2)}, u32[]{:S(2)}) collective-permute-start(f32[96,3200]{1,0:T(8,128)} %get-tuple-element.273), channel_id=1, source_target_pairs={{0,8},{8,16},{16,24},{24,0},{1,9},{9,17},{17,25},{25,1},{2,10},{10... | collective-permute-start | bytes 3686408 | tf_op jit(solution)/shard_map/ppermute | solution.py:137
  982.6 87.1 %collective-permute-start.27 = (f32[96,3200]{1,0:T(8,128)}, f32[96,3200]{1,0:T(8,128)}, u32[]{:S(2)}, u32[]{:S(2)}) collective-permute-start(f32[96,3200]{1,0:T(8,128)} %get-tuple-element.272), channel_id=1, source_target_pairs={{0,16},{8,24},{16,0},{24,8},{1,17},{9,25},{17,1},{25,9},{2,18},{10... | collective-permute-start | bytes 3686408 | tf_op jit(solution)/shard_map/ppermute | solution.py:137
  983.9 108.0 %collective-permute-start.28 = (f32[96,3200]{1,0:T(8,128)}, f32[96,3200]{1,0:T(8,128)}, u32[]{:S(2)}, u32[]{:S(2)}) collective-permute-start(f32[96,3200]{1,0:T(8,128)} %get-tuple-element.271), channel_id=1, source_target_pairs={{0,24},{8,0},{16,8},{24,16},{1,25},{9,1},{17,9},{25,17},{2,26},{10... | collective-permute-start | bytes 3686408 | tf_op jit(solution)/shard_map/ppermute | solution.py:137
  1125.4 45.0 %copy-start.40 = (f32[768]{0:T(1024)S(1)}, f32[768]{0:T(1024)}, u32[]{:S(2)}) copy-start(f32[768]{0:T(1024)} %get-tuple-element.210) | copy-start | bytes 9220
  1125.4 45.0 %copy-start.53 = (f32[768]{0:T(1024)S(1)}, f32[768]{0:T(1024)}, u32[]{:S(2)}) copy-start(f32[768]{0:T(1024)} %get-tuple-element.215) | copy-start | bytes 9220
  1125.4 45.0 %copy-start.38 = (bf16[768]{0:T(1024)(128)(2,1)S(1)}, bf16[768]{0:T(1024)(128)(2,1)}, u32[]{:S(2)}) copy-start(bf16[768]{0:T(1024)(128)(2,1)} %copy-done.37) | copy-start | bytes 4612
  1125.4 94.3 %collective-permute-start.13 = (bf16[512,96]{0,1:T(8,128)(2,1)}, bf16[512,96]{0,1:T(8,128)(2,1)}, u32[]{:S(2)}, u32[]{:S(2)}) collective-permute-start(bf16[512,96]{0,1:T(8,128)(2,1)} %get-tuple-element.290), channel_id=1, source_target_pairs={{0,4},{4,8},{8,12},{12,16},{16,20},{20,24},{24,28},{28,0},{1,5},{5... | collective-permute-start | bytes 294920 | tf_op jit(solution)/shard_map/ppermute | solution.py:137
  1126.9 102.2 %collective-permute-start.14 = (bf16[512,96]{0,1:T(8,128)(2,1)}, bf16[512,96]{0,1:T(8,128)(2,1)}, u32[]{:S(2)}, u32[]{:S(2)}) collective-permute-start(bf16[512,96]{0,1:T(8,128)(2,1)} %get-tuple-element.289), channel_id=1, source_target_pairs={{0,8},{4,12},{8,16},{12,20},{16,24},{20,28},{24,0},{28,4},{1,9},{5... | collective-permute-start | bytes 294920 | tf_op jit(solution)/shard_map/ppermute | solution.py:137
  1157.1 85.5 %collective-permute-start.15 = (bf16[512,96]{0,1:T(8,128)(2,1)S(1)}, bf16[512,96]{0,1:T(8,128)(2,1)}, u32[]{:S(2)}, u32[]{:S(2)}) collective-permute-start(bf16[512,96]{0,1:T(8,128)(2,1)S(1)} %get-tuple-element.288), channel_id=1, source_target_pairs={{0,12},{4,16},{8,20},{12,24},{16,28},{20,0},{24,4},{28,8},{1,13},{... | collective-permute-start | bytes 294920 | tf_op jit(solution)/shard_map/ppermute | solution.py:137
  1160.5 82.9 %collective-permute-start.16 = (bf16[512,96]{0,1:T(8,128)(2,1)S(1)}, bf16[512,96]{0,1:T(8,128)(2,1)}, u32[]{:S(2)}, u32[]{:S(2)}) collective-permute-start(bf16[512,96]{0,1:T(8,128)(2,1)S(1)} %get-tuple-element.287), channel_id=1, source_target_pairs={{0,16},{4,20},{8,24},{12,28},{16,0},{20,4},{24,8},{28,12},{1,17},{... | collective-permute-start | bytes 294920 | tf_op jit(solution)/shard_map/ppermute | solution.py:137
  1160.9 83.4 %collective-permute-start.17 = (bf16[512,96]{0,1:T(8,128)(2,1)S(1)}, bf16[512,96]{0,1:T(8,128)(2,1)}, u32[]{:S(2)}, u32[]{:S(2)}) collective-permute-start(bf16[512,96]{0,1:T(8,128)(2,1)S(1)} %get-tuple-element.286), channel_id=1, source_target_pairs={{0,20},{4,24},{8,28},{12,0},{16,4},{20,8},{24,12},{28,16},{1,21},{... | collective-permute-start | bytes 294920 | tf_op jit(solution)/shard_map/ppermute | solution.py:137
  1219.8 25.5 %collective-permute-start.18 = (bf16[512,96]{0,1:T(8,128)(2,1)S(1)}, bf16[512,96]{0,1:T(8,128)(2,1)S(1)}, u32[]{:S(2)}, u32[]{:S(2)}) collective-permute-start(bf16[512,96]{0,1:T(8,128)(2,1)S(1)} %get-tuple-element.285), channel_id=1, source_target_pairs={{0,24},{4,28},{8,0},{12,4},{16,8},{20,12},{24,16},{28,20},{1,25},{... | collective-permute-start | bytes 294920 | tf_op jit(solution)/shard_map/ppermute | solution.py:137
  1229.1 16.2 %collective-permute-start.19 = (bf16[512,96]{0,1:T(8,128)(2,1)S(1)}, bf16[512,96]{0,1:T(8,128)(2,1)S(1)}, u32[]{:S(2)}, u32[]{:S(2)}) collective-permute-start(bf16[512,96]{0,1:T(8,128)(2,1)S(1)} %get-tuple-element.284), channel_id=1, source_target_pairs={{0,28},{4,0},{8,4},{12,8},{16,12},{20,16},{24,20},{28,24},{1,29},{... | collective-permute-start | bytes 294920 | tf_op jit(solution)/shard_map/ppermute | solution.py:137
  1245.3 29.4 %collective-permute-start.20 = (bf16[8,512,96]{1,2,0:T(8,128)(2,1)S(1)}, bf16[8,512,96]{1,2,0:T(8,128)(2,1)}, u32[]{:S(2)}, u32[]{:S(2)}) collective-permute-start(bf16[8,512,96]{1,2,0:T(8,128)(2,1)S(1)} %bitcast_dynamic-update-slice_fusion.4), channel_id=1, source_target_pairs={{0,1},{1,2},{2,3},{3,0},{4,5},{5,6},{6,7},{7,4},{8,9},{9,10},{10,1... | collective-permute-start | bytes 2359304 | tf_op jit(solution)/shard_map/ppermute | solution.py:137
  1245.4 30.9 %collective-permute-start.21 = (bf16[8,512,96]{1,2,0:T(8,128)(2,1)S(1)}, bf16[8,512,96]{1,2,0:T(8,128)(2,1)S(1)}, u32[]{:S(2)}, u32[]{:S(2)}) collective-permute-start(bf16[8,512,96]{1,2,0:T(8,128)(2,1)S(1)} %bitcast_dynamic-update-slice_fusion.4), channel_id=1, source_target_pairs={{0,2},{1,3},{2,0},{3,1},{4,6},{5,7},{6,4},{7,5},{8,10},{9,11},{10,... | collective-permute-start | bytes 2359304 | tf_op jit(solution)/shard_map/ppermute | solution.py:137
  1249.2 44.7 %collective-permute-start.22 = (bf16[8,512,96]{1,2,0:T(8,128)(2,1)S(1)}, bf16[8,512,96]{1,2,0:T(8,128)(2,1)}, u32[]{:S(2)}, u32[]{:S(2)}) collective-permute-start(bf16[8,512,96]{1,2,0:T(8,128)(2,1)S(1)} %bitcast_dynamic-update-slice_fusion.4), channel_id=1, source_target_pairs={{0,3},{1,0},{2,1},{3,2},{4,7},{5,4},{6,5},{7,6},{8,11},{9,8},{10,9... | collective-permute-start | bytes 2359304 | tf_op jit(solution)/shard_map/ppermute | solution.py:137
  (60 other events, 930.7 us)
Sparse Core Ops, SparseCore 0:
  11.5 171.0 all-gather.5
  185.0 124.2 all-gather.9
  359.3 68.4 all-gather.7
  600.6 127.6 reduce-scatter.5
  789.6 181.0 reduce-scatter.7
  977.3 140.5 reduce-scatter.9
  1123.8 176.3 reduce-scatter.11
  1307.1 134.1 reduce-scatter.13

commit v2 on v1

--- a/solution.py
+++ b/solution.py
@@ -144,6 +144,10 @@
     for sender, piece in got:
         out = lax.dynamic_update_index_in_dim(out, piece, sender, 0)
     return out
+
+
+def together(*values):
+    return lax.optimization_barrier(values)
 
 
 def pick(values, index):
@@ -578,8 +582,6 @@
     vocab_start = vocab_index * table_rows
     me = (iz * nx + ix) * (ny * nc) + vocab_index
 
-    layer_all = lax.all_gather(layer_w.astype(BF), ALL, axis=0, tiled=True)
-
     tokens, masked = token_ids[0], scored[0]
     positions = jnp.arange(length, dtype=jnp.int32)
     hits = masked[:, None] == positions[None, :]
@@ -599,6 +601,13 @@
                         ((0, 8 - gains_w.shape[0]), (0, LANES - gains_w.shape[1])))
     ada_part = ada_w.astype(BF).reshape(-1, LANES)
     ints_all, gains_all, ada_all = share(sizes, 0, ints, gain_part, ada_part)
+
+    layer_low, head_low, ints_all = together(layer_w.astype(BF), head_w.astype(BF), ints_all)
+    layer_all = lax.all_gather(layer_low, ALL, axis=0, tiled=True)
+
+    piece_for = lambda k: lax.dynamic_slice_in_dim(head_low, k * SEGMENT, SEGMENT, 1)
+    head_parts = exchange(piece_for, ("z",))
+
     gains = jnp.moveaxis(gains_all[:, : gains_w.shape[0], : gains_w.shape[1]], 0, 1).reshape(4, D)
     ada = ada_all.reshape(C, 6 * D)
     free_rows = free_count // LANES
@@ -623,9 +632,9 @@
     columns = in_order(exchange(lambda k: pick(mine, k), ("z", "x")))
     x0_u = jnp.swapaxes(columns, 0, 1).reshape(free_count, D).astype(F32)
 
-    head_low = head_w.astype(BF)
-    piece_for = lambda k: lax.dynamic_slice_in_dim(head_low, k * SEGMENT, SEGMENT, 1)
-    head_part = in_order(exchange(piece_for, ("z",))).reshape(-1, SEGMENT)
+    senders = [sender for sender, _ in head_parts]
+    x0_u, *pieces = together(x0_u, *[piece for _, piece in head_parts])
+    head_part = in_order(list(zip(senders, pieces))).reshape(-1, SEGMENT)
 
     mask_row = gains[3:4]
     condition = time_features(times, C, TSTEPS).astype(BF)
@@ -679,19 +688,16 @@
     factors = jnp.stack([row_weights * jnp.exp(top - log_total),
                          row_weights * (jnp.exp(chosen - log_total) - 1.0)], axis=1)
     d_logits, d_rows = head_rows_back(e, head_all, column_of, factors)
-    d_final = lax.psum_scatter(d_rows, ("z", "c"), scatter_dimension=0, tiled=True)
-    d_final = jnp.swapaxes(d_final.reshape(score_count, nx, nz, -1), 1, 2).reshape(score_count, D)
+    d_final = lax.psum_scatter(d_rows.astype(BF), ("z", "c"), scatter_dimension=0, tiled=True)
 
     d_head = jnp.einsum("rd,yrv->ydv", rows, d_logits, preferred_element_type=F32)
     d_head = d_head.reshape(ny * nx, -1, SEGMENT)
+    d_final, d_head = together(d_final, d_head)
+    d_final = d_final.astype(F32)
+    d_final = jnp.swapaxes(d_final.reshape(score_count, nx, nz, -1), 1, 2).reshape(score_count, D)
     block_for = lambda k: pick(d_head, lax.rem(k, ny) * nx + k // ny)
-    got = exchange(lambda k: block_for(k).astype(BF), ("x", "y"))
-    g_part = block_for(got[0][0])
-    for _, piece in got[1:]:
-        g_part = g_part + piece.astype(F32)
-    g_part = g_part.reshape(nz, -1, SEGMENT)
-    g_head = in_order(exchange(lambda k: pick(g_part, k), ("z",)))
-    g_head = jnp.swapaxes(g_head, 0, 1).reshape(head_w.shape)
+    head_sums = exchange(lambda k: block_for(k).astype(BF), ("x", "y"))
+    head_own = block_for(head_sums[0][0])
 
     d_gain_f = jnp.sum(d_final * normed_f, axis=0)
     d_x2 = norm_back(d_final * gains[2:3], normed_f, inv_f)
@@ -702,6 +708,9 @@
     d_pre = jax.vjp(gelu_tanh, pre)[1](d_act)[0].astype(BF)
     d_up = matmul_tn(b, d_pre)
     d_b = matmul_nt(d_pre, w_up)
+    d_b, d_mlp = together(d_b, jnp.concatenate([d_up.astype(BF), d_down.astype(BF)], axis=1))
+    scatter = lambda a: lax.psum_scatter(a, ALL, scatter_dimension=0, tiled=True).astype(F32)
+    g_mlp = scatter(d_mlp)
     d_shift_m = jnp.sum(d_b, axis=0)
     product = jnp.sum(d_b * normed_m, axis=0)
     d_scale_m = product * gains[1]
@@ -712,6 +721,7 @@
     d_wout = matmul_tn(att, d_branch)
     d_att = matmul_nt(d_branch, w_o).astype(BF)
     d_k, d_v, d_qkv_m = attend_back(q, k_u, k_m, kv_u, qkv_m, tables, mask, lse_a, d_att)
+    d_k, *head_pieces = together(d_k, *[piece for _, piece in head_sums[1:]])
     d_kv = jnp.concatenate([d_k, d_v], axis=1)
     d_wkv = matmul_tn(a_u, d_kv)
     d_row_m = d_qkv_m[:3].reshape(3 * D)
@@ -730,7 +740,14 @@
     arrived = in_order(exchange(lambda k: pick(sent, k), ("z", "x")))
     arrived = in_order(exchange(lambda k: arrived, ("y", "c")))
     g_embed = scatter_rows(arrived.reshape(n, free_count, table_width), local_ids, low, high,
-                           table_rows)
+                           table_rows).T
+
+    g_part = head_own
+    for piece in head_pieces:
+        g_part = g_part + piece.astype(F32)
+    g_part = g_part.reshape(nz, -1, SEGMENT)
+    g_head = together(in_order(exchange(lambda k: pick(g_part, k), ("z",))))[0]
+    g_head = jnp.swapaxes(g_head, 0, 1).reshape(head_w.shape)
 
     small = jnp.concatenate([d_shift_a, d_scale_a, d_gate_a, d_shift_m, d_scale_m, d_gate_m,
                              d_gain_a, d_gain_m, d_gain_f, d_mask,
@@ -751,11 +768,9 @@
                                       layer_w.shape[0], 1)
     g_outer = exact(a_rows, small_all[:, 11 * D : 14 * D])
 
-    scatter = lambda a: lax.psum_scatter(a, ALL, scatter_dimension=0, tiled=True)
-    g_down, g_up = scatter(d_down), scatter(d_up)
-    g_wout, g_wkv = scatter(d_wout), scatter(d_wkv)
+    g_rest = scatter(jnp.concatenate([d_wkv.astype(BF), d_wout.astype(BF)], axis=1))
     g_layer = jnp.concatenate(
-        [g_outer[:, :D], g_outer[:, D:] + g_wkv, g_wout, g_up, g_down], axis=1)
+        [g_outer[:, :D], g_outer[:, D:] + g_rest[:, : 2 * D], g_rest[:, 2 * D :], g_mlp], axis=1)
 
     squares = sum(jnp.sum(g * g) for g in (g_layer, g_ada, g_gains, g_embed, g_head))
     squares_all = share(sizes, 2, jnp.broadcast_to(squares, (8, LANES)))[0]
@@ -766,12 +781,13 @@
         (layer_w, layer_m, layer_v, layer_ema, g_layer),
         (ada_w, ada_m, ada_v, ada_ema, g_ada),
         (gains_w, gains_m, gains_v, gains_ema, g_gains),
-        (embed_w, embed_m, embed_v, embed_ema, g_embed),
+        (embed_w.T, embed_m.T, embed_v.T, embed_ema.T, g_embed),
         (head_w, head_m, head_v, head_ema, g_head),
     )
     results = []
     for (w, m, v, ema, g), rate, decay in zip(updates, LEARN_RATES, WEIGHT_DECAYS):
         results.extend(adam_step(w, m, v, ema, g * factor, step_value, rate, decay))
+    results[12:16] = [a.T for a in results[12:16]]
     return (total_loss, grad_norm, *results)
 
 

time: 1550 us -> 1290 us (0.83)
  waiting for transfers between devices: 518 us -> 296 us
  Pallas kernels: 388 us -> 330 us
  other arithmetic: 108 us -> 127 us
    reduce_scatter x5 -> x3, waiting for transfers between devices: 230 us -> 17.2 us  [the longest x1 17.2 us: local(): lax.psum_scatter(d_rows.astype(BF), ('z', 'c'), scatter_dimension=0, tile...]
    pallas_call x3, Pallas kernels: 138 us -> 86.6 us  [share(): pl.pallas_call(functools.partial(share_kernel, sizes, count), out_shape=[...]
    ppermute x29, waiting for transfers between devices: 237 us -> 189 us  [exchange(): moved = lax.ppermute(piece, axes, [(i, (i + step) % n) for i in range(n)])]
    all_gather x1, waiting for transfers between devices: 0.01 us -> 22.2 us  [local(): lax.all_gather(head_part, ('y', 'x'), axis=0, tiled=True)]
    all_gather x1, waiting for transfers between devices: 51.2 us -> 67 us  [local(): rows = lax.all_gather(final_turned, ('z', 'c'), axis=0, tiled=True)]
    unnamed x177 -> x188, local copies, waits for them, and re-layouts: 71.9 us -> 68.3 us
  transfers between devices with their start and end apart: 37 -> 35, of which waited for: 16 -> 14; matrix products, arithmetic and copies ran while one was open for 23% -> 26% of each run, Pallas kernels for 14% -> 10%
where the time goes in v2:
time: 1290 us; the launch traced here: 1270 us
  Pallas kernels  330 us (26%)
  waiting for transfers between devices  296 us (23%)
  local copies, waits for them, and re-layouts  240 us (19%)
  other arithmetic  127 us (10%)
  starting transfers between devices  125 us (10%)
  matrix products  116 us (9%)
  between operations  26.1 us (2%)
  blocking collectives  14.9 us (1%)
    ppermute x29, waiting for transfers between devices, exchange(): moved = lax.ppermute(piece, axes, [(i, (i + step) % n) for i in range(n)])  189 us
    ppermute x29, starting transfers between devices, exchange(): moved = lax.ppermute(piece, axes, [(i, (i + step) % n) for i in range(n)])  124 us
    dynamic_update_slice x28, local copies, waits for them, and re-layouts, in_order(): out = lax.dynamic_update_index_in_dim(out, piece, sender, 0)  94.1 us
    pallas_call x3, Pallas kernels, share(): pl.pallas_call(functools.partial(share_kernel, sizes, count), out_shape=[...  86.6 us
    pallas_call x1, Pallas kernels, head_logits(): pl.pallas_call(logits_kernel, grid=(count // tile,), out_shape=[jax.Shape...  79.5 us
    unnamed x188, local copies, waits for them, and re-layouts  68.3 us
    all_gather x1, waiting for transfers between devices, local(): rows = lax.all_gather(final_turned, ('z', 'c'), axis=0, tiled=True)  67 us
    pallas_call x1, Pallas kernels, head_rows_back(): pl.pallas_call(rows_back_kernel, grid=(count // tile,), out_shape=[jax.Sh...  65.8 us
  transfers between devices with their start and end apart: 35, of which 14 were waited for; matrix products, arithmetic and copies ran while one was open for 26% of the time, Pallas kernels for 10%

profile of v2, /device:TPU:0, one launch (start us, length us, event | category | flops | bytes accessed | tf_op | source)
XLA Modules:
  0.0 1274.3 jit_solution(10794335492221067977)
XLA Ops:
  19.7 36.6 %share0.1 = (s32[32,16,128]{2,1,0:T(8,128)}, f32[32,8,128]{2,1,0:T(8,128)}, bf16[32,144,128]{2,1,0:T(8,128)(2,1)}) custom-call(s32[16,128]{1,0:T(8,128)} %pad.18.refs_0_, f32[8,128]{1,0:T(8,128)} %pad_convert_fusion.refs_1_, bf16[144,128]{1,0:T(8,128)(2,1)} %reshape.806.refs_2_), custom_call_target="tpu_custom_call" | custom-call | tf_op jit(solution)/shard_map/share0/pallas_call | solution.py:107
  61.7 6.4 copy.344.table_ref
  68.1 25.4 %gather_rows.1 = bf16[32,512,96]{2,1,0:T(8,128)(2,1)} custom-call(s32[32]{0:T(128)} %reduce_sum.388.low_ref, s32[32]{0:T(128)} %reduce_sum.390.high_ref, s32[32,512]{1,0:T(8,128)} %bitcast.265, f32[12800,96]{1,0:T(8,128)} %copy.344.table_ref), custom_call_target="tpu_custom_call" | custom-call | tf_op jit(solution)/shard_map/gather_rows/pallas_call | solution.py:181
  100.0 6.7 collective-permute-start
  113.9 9.0 collective-permute-start.10
  133.2 28.0 %collective-permute-done.2 = bf16[4096,96]{0,1:T(8,128)(2,1)} collective-permute-done((bf16[4096,96]{0,1:T(8,128)(2,1)}, bf16[4096,96]{0,1:T(8,128)(2,1)}, u32[]{:S(2)}, u32[]{:S(2)}) %collective-permute-start.2) | collective-permute-done | bytes 786464 | tf_op jit(solution)/shard_map/ppermute | solution.py:137
  169.0 14.1 %collective-permute-start.4 = (bf16[512,96]{0,1:T(8,128)(2,1)S(1)}, bf16[512,96]{0,1:T(8,128)(2,1)S(1)}, u32[]{:S(2)}, u32[]{:S(2)}) collective-permute-start(bf16[512,96]{0,1:T(8,128)(2,1)S(1)} %bitcast.275), channel_id=1, source_target_pairs={{0,8},{4,12},{8,16},{12,20},{16,24},{20,28},{24,0},{28,4},{1,9},{5... | collective-permute-start | bytes 294920 | tf_op jit(solution)/shard_map/ppermute | solution.py:137
  183.4 25.0 %collective-permute-done.3 = bf16[512,96]{0,1:T(8,128)(2,1)S(1)} collective-permute-done((bf16[512,96]{0,1:T(8,128)(2,1)S(1)}, bf16[512,96]{0,1:T(8,128)(2,1)S(1)}, u32[]{:S(2)}, u32[]{:S(2)}) %collective-permute-start.3) | collective-permute-done | bytes 98336 | tf_op jit(solution)/shard_map/ppermute | solution.py:137
  208.4 10.7 collective-permute-start.5
  221.1 7.5 collective-permute-done.5
  268.2 18.5 %attend.1 = (bf16[512,768]{1,0:T(8,128)(2,1)}, bf16[512,768]{1,0:T(8,128)(2,1)}, bf16[512,768]{1,0:T(8,128)(2,1)}, bf16[512,768]{1,0:T(8,128)(2,1)}, f32[6,512,2]{2,1,0:T(8,128)}) custom-call(f32[512,1536]{1,0:T(8,128)} %fusion.42.kv_ref.vv_ref, f32[512,1536]{1,0:T(8,128)} %fusion.42.kv_ref.vv_ref, f32[16,2304]{1,0:T(8,128)} %fusion.23.qm_ref.km_ref.vm_ref, ...), custom_call_target="tpu_custom_call" | custom-call | flops 1207959552 | bytes 4718592 | tf_op jit(solution)/shard_map/attend/pallas_call | solution.py:297
  295.5 9.6 fusion.107
  316.3 7.2 fusion.34.target_ref
  323.5 22.2 %all-gather.10.cloned.1.call-done = bf16[1536,3200]{1,0:T(8,128)(2,1)} async-done(((bf16[384,3200]{1,0:T(8,128)(2,1)}), bf16[1536,3200]{1,0:T(8,128)(2,1)}) %all-gather.10.cloned.1.call-update) | async-done | bytes 9830416 | tf_op jit(solution)/shard_map/all_gather | solution.py:668
  345.7 67.0 %all-gather.8.cloned.1.call-done.x_ref = bf16[4096,768]{1,0:T(8,128)(2,1)} async-done(((bf16[512,768]{1,0:T(8,128)(2,1)}), bf16[4096,768]{1,0:T(8,128)(2,1)}) %all-gather.8.cloned.1.call-update) | async-done | bytes 6291472 | tf_op jit(solution)/shard_map/all_gather | solution.py:669
  412.7 79.5 %head_logits.1 = (bf16[2,4096,3200]{2,1,0:T(8,128)(2,1)}, f32[4096,4]{1,0:T(8,128)}) custom-call(bf16[4096,768]{1,0:T(8,128)(2,1)} %all-gather.8.cloned.1.call-done.x_ref, bf16[2,768,3200]{2,1,0:T(8,128)(2,1)} %bitcast.294, s32[4096,1]{1,0:T(8,128)} %fusion.34.target_ref), custom_call_target="tpu_custom_call" | custom-call | flops 40265318400 | bytes 52428800 | tf_op jit(solution)/shard_map/head_logits/pallas_call | solution.py:436
  494.4 14.9 %all-gather.1 = f32[8,4,4096]{2,1,0:T(4,128)S(1)} all-gather(f32[1,4,4096]{2,1,0:T(4,128)S(1)} %copy.367), channel_id=2, replica_groups=mesh['z'=4,'x'=2,'y'=2,'c'=2] {'z','c'}, dimensions={0}, use_global_device_ids=true | all-gather | bytes 589824 | tf_op jit(solution)/shard_map/all_gather | solution.py:681
  519.1 65.8 %head_rows_back.1 = (bf16[2,4096,3200]{2,1,0:T(8,128)(2,1)}, f32[4096,768]{1,0:T(8,128)}) custom-call(bf16[2,4096,3200]{2,1,0:T(8,128)(2,1)} %get-tuple-element.69.e_ref, bf16[2,768,3200]{2,1,0:T(8,128)(2,1)} %bitcast.295, s32[4096,1]{1,0:T(8,128)} %fusion.34.target_ref, f32[4096,2]{1,0:T(8,128)} %pad_maximum_fusion.2.factor_ref), custom_call_target="tpu_custom_call", output_to_operand_aliasing={{0}: (0, {})} | custom-call | flops 40265318400 | bytes 104857600 | tf_op jit(solution)/shard_map/head_rows_back/pallas_call | solution.py:485
  584.9 7.8 convert_element_type.238
  593.0 51.0 %fusion.8 = f32[2,3200,768]{1,2,0:T(8,128)} fusion(bf16[2,4096,3200]{2,1,0:T(8,128)(2,1)} %get-tuple-element.72, bf16[4096,768]{1,0:T(8,128)(2,1)} %all-gather.8.cloned.1.call-done.x_ref), kind=kOutput, calls=%fused_computation.17 | convolution fusion | flops 40265318400 | bytes 78381056 | tf_op jit(solution)/shard_map/rd,yrv->ydv/dot_general | solution.py:693
  644.0 17.2 %reduce-scatter.4.cloned.1.call-done = bf16[512,768]{1,0:T(8,128)(2,1)} async-done(((bf16[4096,768]{1,0:T(8,128)(2,1)}), bf16[512,768]{1,0:T(8,128)(2,1)}) %reduce-scatter.4.cloned.1.call-update) | async-done | bytes 786448 | tf_op jit(solution)/shard_map/reduce_scatter | solution.py:691
  668.3 6.7 convolution_convert_fusion
  675.0 7.7 fusion.7
  689.2 8.6 fusion.29
  702.1 6.7 pad_maximum_fusion
  708.8 5.9 fusion.17
  720.0 23.9 %attend_back.1 = (bf16[512,768]{1,0:T(8,128)(2,1)}, bf16[512,768]{1,0:T(8,128)(2,1)}, f32[8,768]{1,0:T(8,128)}) custom-call(bf16[512,768]{1,0:T(8,128)(2,1)} %get-tuple-element.60.q_ref, bf16[512,768]{1,0:T(8,128)(2,1)} %get-tuple-element.61.ku_ref, bf16[512,768]{1,0:T(8,128)(2,1)} %get-tuple-element.62.km_ref, f32[512,1536]{1,0:T(8,128)} %fusion.42.kv_ref.vv_ref, ...), custom_call_target="tpu_custom_call" | custom-call | flops 3221225472 | bytes 5505024 | tf_op jit(solution)/shard_map/attend_back/pallas_call | solution.py:369
  744.8 10.4 collective-permute-done.13
  755.8 48.8 %collective-permute-done.15 = bf16[384,3200]{1,0:T(8,128)(2,1)} collective-permute-done((bf16[384,3200]{1,0:T(8,128)(2,1)}, bf16[384,3200]{1,0:T(8,128)(2,1)}, u32[]{:S(2)}, u32[]{:S(2)}) %collective-permute-start.15) | collective-permute-done | bytes 2457632 | tf_op jit(solution)/shard_map/ppermute | solution.py:137
  811.0 6.7 copy.391
  817.6 6.5 copy.393
  824.1 6.5 copy.396
  864.4 54.8 %collective-permute-done.16 = bf16[512,96]{0,1:T(8,128)(2,1)S(1)} collective-permute-done((bf16[512,96]{0,1:T(8,128)(2,1)S(1)}, bf16[512,96]{0,1:T(8,128)(2,1)S(1)}, u32[]{:S(2)}, u32[]{:S(2)}) %collective-permute-start.16) | collective-permute-done | bytes 98336 | tf_op jit(solution)/shard_map/ppermute | solution.py:137
  919.1 39.0 %collective-permute-start.19 = (bf16[512,96]{0,1:T(8,128)(2,1)S(1)}, bf16[512,96]{0,1:T(8,128)(2,1)S(1)}, u32[]{:S(2)}, u32[]{:S(2)}) collective-permute-start(bf16[512,96]{0,1:T(8,128)(2,1)S(1)} %get-tuple-element.320), channel_id=1, source_target_pairs={{0,16},{4,20},{8,24},{12,28},{16,0},{20,4},{24,8},{28,12},{1,17},{... | collective-permute-start | bytes 294920 | tf_op jit(solution)/shard_map/ppermute | solution.py:137
  972.4 31.6 %share1.1 = f32[32,88,128]{2,1,0:T(8,128)} custom-call(f32[88,128]{1,0:T(8,128)} %pad.22.refs_0_), custom_call_target="tpu_custom_call" | custom-call | tf_op jit(solution)/shard_map/share1/pallas_call | solution.py:107
  1012.1 20.0 %dynamic_update_slice.112 = f32[4,96,3200]{2,0,1:T(4,128)} dynamic-update-slice(f32[4,96,3200]{2,0,1:T(4,128)} %broadcast_in_dim.238, f32[1,96,3200]{2,0,1:T(1,128)S(1)} %copy.412, s32[]{:T(128)S(6)} %select_n.306, s32[]{:T(128)} %constant.457.clone.1, s32[]{:T(128)} %constant.457.clone.1) | dynamic-update-slice | bytes 2457604 | tf_op jit(solution)/shard_map/jit(dynamic_update_index_in_dim)/dynamic_update_slice | solution.py:145
  1032.8 7.0 collective-permute-start.28
  1055.9 30.4 %scatter_rows.1 = f32[12800,96]{1,0:T(8,128)} custom-call(s32[32]{0:T(128)} %reduce_sum.388.low_ref, s32[32]{0:T(128)} %reduce_sum.390.high_ref, s32[32,512]{1,0:T(8,128)} %bitcast.266, bf16[32,512,96]{2,1,0:T(8,128)(2,1)} %bitcast.85.rows_ref), custom_call_target="tpu_custom_call" | custom-call | tf_op jit(solution)/shard_map/scatter_rows/pallas_call | solution.py:224
  1092.8 20.1 %dynamic_update_slice.113 = f32[4,96,3200]{2,0,1:T(4,128)} dynamic-update-slice(f32[4,96,3200]{2,0,1:T(4,128)} %dynamic_update_slice.112, f32[1,96,3200]{2,0,1:T(1,128)S(1)} %broadcast_in_dim.239, s32[]{:T(128)S(6)} %select_n.307, s32[]{:T(128)} %constant.457.clone.1, s32[]{:T(128)} %constant.457.clone.1) | dynamic-update-slice | bytes 2457604 | tf_op jit(solution)/shard_map/jit(dynamic_update_index_in_dim)/dynamic_update_slice | solution.py:145
  1115.0 20.0 %dynamic_update_slice.114 = f32[4,96,3200]{2,0,1:T(4,128)} dynamic-update-slice(f32[4,96,3200]{2,0,1:T(4,128)} %dynamic_update_slice.113, f32[1,96,3200]{2,0,1:T(1,128)S(1)} %broadcast_in_dim.240, s32[]{:T(128)S(6)} %select_n.308, s32[]{:T(128)} %constant.457.clone.1, s32[]{:T(128)} %constant.457.clone.1) | dynamic-update-slice | bytes 2457604 | tf_op jit(solution)/shard_map/jit(dynamic_update_index_in_dim)/dynamic_update_slice | solution.py:145
  1137.2 20.0 %dynamic_update_slice.115 = f32[4,96,3200]{2,0,1:T(4,128)} dynamic-update-slice(f32[4,96,3200]{2,0,1:T(4,128)} %dynamic_update_slice.114, f32[1,96,3200]{2,0,1:T(1,128)S(1)} %broadcast_in_dim.241, s32[]{:T(128)S(6)} %select_n.309, s32[]{:T(128)} %constant.457.clone.1, s32[]{:T(128)} %constant.457.clone.1) | dynamic-update-slice | bytes 2457604 | tf_op jit(solution)/shard_map/jit(dynamic_update_index_in_dim)/dynamic_update_slice | solution.py:145
  1170.1 18.4 %share2.1 = f32[32,8,128]{2,1,0:T(8,128)} custom-call(f32[8,128]{1,0:T(8,128)} %broadcast_in_dim.242.refs_0_), custom_call_target="tpu_custom_call" | custom-call | tf_op jit(solution)/shard_map/share2/pallas_call | solution.py:107
  1196.1 21.8 %multiply_add_fusion = (f32[12800,96]{1,0:T(8,128)}, f32[12800,96]{1,0:T(8,128)}, f32[12800,96]{1,0:T(8,128)}, f32[12800,96]{1,0:T(8,128)}) fusion(f32[12800,96]{1,0:T(8,128)} %copy.396, f32[]{:T(128)S(6)} %sub.337, f32[]{:T(128)} %bitcast.93, f32[12800,96]{1,0:T(8,128)} %copy.344.table_ref, f32[]{:T(128)} %bitcast.92, f32[]{:T(128)} %bitcast.91, ...), kind=kLoop, calls=%fused_computation.6 | loop fusion | flops 23347200 | bytes 44236820 | tf_op jit(solution)/shard_map/add | solution.py:558
  1218.0 6.3 copy.397
  1224.3 6.3 copy.398
  1230.5 6.3 copy.399
  1236.9 6.6 copy.400
  1248.4 16.8 %multiply_add_fusion.2 = (f32[96,12800]{1,0:T(8,128)}, f32[96,12800]{1,0:T(8,128)}, f32[96,12800]{1,0:T(8,128)}, f32[96,12800]{1,0:T(8,128)}) fusion(f32[96,12800]{1,0:T(8,128)} %param.49, f32[]{:T(128)S(6)} %sub.337, f32[]{:T(128)} %bitcast.93, f32[96,12800]{1,0:T(8,128)} %param.46, f32[]{:T(128)} %bitcast.92, f32[]{:T(128)} %bitcast.91, ...), kind=kLoop, calls=%fused_computation.26 | loop fusion | flops 22118400 | bytes 44236816 | tf_op jit(solution)/shard_map/add | solution.py:558
  (452 shorter events, 254.3 us)
Async XLA Ops:
  7.2 252.2 %all-gather.6.cloned.1.call-start = ((), (), s32[]{:S(2)}) async-start(), calls=%async_computation.3 | async-start | bytes 14598144 | tf_op jit(solution)/shard_map/all_gather | solution.py:606
  56.4 289.2 %all-gather.10.cloned.1.call-start = ((), (), s32[]{:S(2)}) async-start(), calls=%async_computation.5 | async-start | bytes 12288000 | tf_op jit(solution)/shard_map/all_gather | solution.py:668
  100.0 26.4 %collective-permute-start = (bf16[4096,96]{0,1:T(8,128)(2,1)}, bf16[4096,96]{0,1:T(8,128)(2,1)}, u32[]{:S(2)}, u32[]{:S(2)}) collective-permute-start(bf16[4096,96]{0,1:T(8,128)(2,1)} %bitcast.263), channel_id=1, source_target_pairs={{0,1},{1,2},{2,3},{3,0},{4,5},{5,6},{6,7},{7,4},{8,9},{9,10},{10,1... | collective-permute-start | bytes 2359304 | tf_op jit(solution)/shard_map/ppermute | solution.py:137
  108.9 24.3 %collective-permute-start.1 = (bf16[4096,96]{0,1:T(8,128)(2,1)}, bf16[4096,96]{0,1:T(8,128)(2,1)}, u32[]{:S(2)}, u32[]{:S(2)}) collective-permute-start(bf16[4096,96]{0,1:T(8,128)(2,1)} %bitcast.262), channel_id=1, source_target_pairs={{0,2},{1,3},{2,0},{3,1},{4,6},{5,7},{6,4},{7,5},{8,10},{9,11},{10,... | collective-permute-start | bytes 2359304 | tf_op jit(solution)/shard_map/ppermute | solution.py:137
  111.1 50.1 %collective-permute-start.2 = (bf16[4096,96]{0,1:T(8,128)(2,1)}, bf16[4096,96]{0,1:T(8,128)(2,1)}, u32[]{:S(2)}, u32[]{:S(2)}) collective-permute-start(bf16[4096,96]{0,1:T(8,128)(2,1)} %bitcast.264), channel_id=1, source_target_pairs={{0,3},{1,0},{2,1},{3,2},{4,7},{5,4},{6,5},{7,6},{8,11},{9,8},{10,9... | collective-permute-start | bytes 2359304 | tf_op jit(solution)/shard_map/ppermute | solution.py:137
  113.9 126.1 %collective-permute-start.10 = (bf16[96,3200]{1,0:T(8,128)(2,1)}, bf16[96,3200]{1,0:T(8,128)(2,1)S(1)}, u32[]{:S(2)}, u32[]{:S(2)}) collective-permute-start(bf16[96,3200]{1,0:T(8,128)(2,1)} %get-tuple-element.313), channel_id=1, source_target_pairs={{0,8},{8,16},{16,24},{24,0},{1,9},{9,17},{17,25},{25,1},{2,10},{10... | collective-permute-start | bytes 1843208 | tf_op jit(solution)/shard_map/ppermute | solution.py:137
  122.9 117.2 %collective-permute-start.11 = (bf16[96,3200]{1,0:T(8,128)(2,1)}, bf16[96,3200]{1,0:T(8,128)(2,1)}, u32[]{:S(2)}, u32[]{:S(2)}) collective-permute-start(bf16[96,3200]{1,0:T(8,128)(2,1)} %get-tuple-element.312), channel_id=1, source_target_pairs={{0,16},{8,24},{16,0},{24,8},{1,17},{9,25},{17,1},{25,9},{2,18},{10... | collective-permute-start | bytes 1843208 | tf_op jit(solution)/shard_map/ppermute | solution.py:137
  126.4 113.7 %collective-permute-start.12 = (bf16[96,3200]{1,0:T(8,128)(2,1)}, bf16[96,3200]{1,0:T(8,128)(2,1)S(1)}, u32[]{:S(2)}, u32[]{:S(2)}) collective-permute-start(bf16[96,3200]{1,0:T(8,128)(2,1)} %get-tuple-element.311), channel_id=1, source_target_pairs={{0,24},{8,0},{16,8},{24,16},{1,25},{9,1},{17,9},{25,17},{2,26},{10... | collective-permute-start | bytes 1843208 | tf_op jit(solution)/shard_map/ppermute | solution.py:137
  165.4 43.0 %collective-permute-start.3 = (bf16[512,96]{0,1:T(8,128)(2,1)S(1)}, bf16[512,96]{0,1:T(8,128)(2,1)S(1)}, u32[]{:S(2)}, u32[]{:S(2)}) collective-permute-start(bf16[512,96]{0,1:T(8,128)(2,1)S(1)} %bitcast.276), channel_id=1, source_target_pairs={{0,4},{4,8},{8,12},{12,16},{16,20},{20,24},{24,28},{28,0},{1,5},{5... | collective-permute-start | bytes 294920 | tf_op jit(solution)/shard_map/ppermute | solution.py:137
  169.0 50.1 %collective-permute-start.4 = (bf16[512,96]{0,1:T(8,128)(2,1)S(1)}, bf16[512,96]{0,1:T(8,128)(2,1)S(1)}, u32[]{:S(2)}, u32[]{:S(2)}) collective-permute-start(bf16[512,96]{0,1:T(8,128)(2,1)S(1)} %bitcast.275), channel_id=1, source_target_pairs={{0,8},{4,12},{8,16},{12,20},{16,24},{20,28},{24,0},{28,4},{1,9},{5... | collective-permute-start | bytes 294920 | tf_op jit(solution)/shard_map/ppermute | solution.py:137
  208.4 20.2 %collective-permute-start.5 = (bf16[512,96]{0,1:T(8,128)(2,1)S(1)}, bf16[512,96]{0,1:T(8,128)(2,1)S(1)}, u32[]{:S(2)}, u32[]{:S(2)}) collective-permute-start(bf16[512,96]{0,1:T(8,128)(2,1)S(1)} %bitcast.274), channel_id=1, source_target_pairs={{0,12},{4,16},{8,20},{12,24},{16,28},{20,0},{24,4},{28,8},{1,13},{... | collective-permute-start | bytes 294920 | tf_op jit(solution)/shard_map/ppermute | solution.py:137
  219.1 9.6 collective-permute-start.6
  228.6 6.5 collective-permute-start.7
  228.7 6.5 collective-permute-start.8
  235.2 4.6 collective-permute-start.9
  246.3 166.4 %all-gather.8.cloned.1.call-start = ((), (), s32[]{:S(2)}) async-start(), calls=%async_computation.4 | async-start | bytes 7077888 | tf_op jit(solution)/shard_map/all_gather | solution.py:669
  257.1 38.3 %copy-start.25 = (f32[768]{0:T(1024)}, f32[768]{0:T(1024)S(1)}, u32[]{:S(2)}) copy-start(f32[768]{0:T(1024)S(1)} %add.723) | copy-start | bytes 9220
  257.3 48.1 %copy-start.33 = (f32[768]{0:T(1024)}, f32[768]{0:T(1024)S(1)}, u32[]{:S(2)}) copy-start(f32[768]{0:T(1024)S(1)} %mul.918) | copy-start | bytes 9220
  258.4 37.0 %copy-start.27 = (f32[768]{0:T(1024)}, f32[768]{0:T(1024)S(1)}, u32[]{:S(2)}) copy-start(f32[768]{0:T(1024)S(1)} %get-tuple-element.263) | copy-start | bytes 9220
  258.4 37.1 %copy-start.72 = (f32[768]{0:T(1024)}, f32[768]{0:T(1024)S(1)}, u32[]{:S(2)}) copy-start(f32[768]{0:T(1024)S(1)} %get-tuple-element.262) | copy-start | bytes 9220
  308.0 353.1 %reduce-scatter.4.cloned.1.call-start = ((), (), s32[]{:S(2)}) async-start(), calls=%async_computation.6 | async-start | bytes 7077888 | tf_op jit(solution)/shard_map/reduce_scatter | solution.py:691
  592.8 569.9 %reduce-scatter.6.cloned.1.call-start = ((), (), s32[]{:S(2)}) async-start(), calls=%async_computation.7 | async-start | bytes 3649536 | tf_op jit(solution)/shard_map/reduce_scatter | solution.py:712
  697.7 57.5 %collective-permute-start.13 = (bf16[384,3200]{1,0:T(8,128)(2,1)}, bf16[384,3200]{1,0:T(8,128)(2,1)}, u32[]{:S(2)}, u32[]{:S(2)}) collective-permute-start(bf16[384,3200]{1,0:T(8,128)(2,1)} %get-tuple-element.302), channel_id=1, source_target_pairs={{0,2},{2,4},{4,6},{6,0},{1,3},{3,5},{5,7},{7,1},{8,10},{10,12},{12... | collective-permute-start | bytes 7372808 | tf_op jit(solution)/shard_map/ppermute | solution.py:137
  699.2 56.6 %collective-permute-start.14 = (bf16[384,3200]{1,0:T(8,128)(2,1)}, bf16[384,3200]{1,0:T(8,128)(2,1)}, u32[]{:S(2)}, u32[]{:S(2)}) collective-permute-start(bf16[384,3200]{1,0:T(8,128)(2,1)} %get-tuple-element.301), channel_id=1, source_target_pairs={{0,4},{2,6},{4,0},{6,2},{1,5},{3,7},{5,1},{7,3},{8,12},{10,14},{12... | collective-permute-start | bytes 7372808 | tf_op jit(solution)/shard_map/ppermute | solution.py:137
  700.7 103.9 %collective-permute-start.15 = (bf16[384,3200]{1,0:T(8,128)(2,1)}, bf16[384,3200]{1,0:T(8,128)(2,1)}, u32[]{:S(2)}, u32[]{:S(2)}) collective-permute-start(bf16[384,3200]{1,0:T(8,128)(2,1)} %get-tuple-element.300), channel_id=1, source_target_pairs={{0,6},{2,0},{4,2},{6,4},{1,7},{3,1},{5,3},{7,5},{8,14},{10,8},{12,... | collective-permute-start | bytes 7372808 | tf_op jit(solution)/shard_map/ppermute | solution.py:137
  743.9 60.6 %copy-start.16 = (bf16[512,768]{1,0:T(8,128)(2,1)S(1)}, bf16[512,768]{1,0:T(8,128)(2,1)}, u32[]{:S(2)}) copy-start(bf16[512,768]{1,0:T(8,128)(2,1)} %get-tuple-element.77) | copy-start | bytes 2359300
  743.9 60.7 %copy-start.15 = (bf16[512,768]{1,0:T(8,128)(2,1)S(1)}, bf16[512,768]{1,0:T(8,128)(2,1)}, u32[]{:S(2)}) copy-start(bf16[512,768]{1,0:T(8,128)(2,1)} %get-tuple-element.78) | copy-start | bytes 2359300
  744.8 61.1 %copy-start.3 = (f32[512,768]{1,0:T(8,128)S(1)}, f32[512,768]{1,0:T(8,128)}, u32[]{:S(2)}) copy-start(f32[512,768]{1,0:T(8,128)} %copy-done.2) | copy-start | bytes 4718596
  744.8 61.1 %copy-start.49 = (f32[512]{0:T(512)S(1)}, f32[512]{0:T(512)}, u32[]{:S(2)}) copy-start(f32[512]{0:T(512)} %copy-done.48) | copy-start | bytes 6148
  744.8 61.1 %copy-start.58 = (f32[768]{0:T(1024)S(1)}, f32[768]{0:T(1024)}, u32[]{:S(2)}) copy-start(f32[768]{0:T(1024)} %copy-done.57) | copy-start | bytes 9220
  744.8 61.1 %copy-start.60 = (f32[768]{0:T(1024)S(1)}, f32[768]{0:T(1024)}, u32[]{:S(2)}) copy-start(f32[768]{0:T(1024)} %copy-done.59) | copy-start | bytes 9220
  744.8 61.1 %copy-start.64 = (f32[512]{0:T(512)S(1)}, f32[512]{0:T(512)}, u32[]{:S(2)}) copy-start(f32[512]{0:T(512)} %copy-done.63) | copy-start | bytes 6148
  744.8 61.1 %copy-start.69 = (f32[768]{0:T(1024)S(1)}, f32[768]{0:T(1024)}, u32[]{:S(2)}) copy-start(f32[768]{0:T(1024)} %copy-done.68) | copy-start | bytes 9220
  809.5 354.9 %reduce-scatter.8.cloned.1.call-start = ((), (), s32[]{:S(2)}) async-start(), calls=%async_computation.8 | async-start | bytes 9732096 | tf_op jit(solution)/shard_map/reduce_scatter | solution.py:712
  848.3 242.3 %collective-permute-start.26 = (f32[96,3200]{1,0:T(8,128)}, f32[96,3200]{1,0:T(8,128)}, u32[]{:S(2)}, u32[]{:S(2)}) collective-permute-start(f32[96,3200]{1,0:T(8,128)} %get-tuple-element.305), channel_id=1, source_target_pairs={{0,8},{8,16},{16,24},{24,0},{1,9},{9,17},{17,25},{25,1},{2,10},{10... | collective-permute-start | bytes 3686408 | tf_op jit(solution)/shard_map/ppermute | solution.py:137
  850.2 262.6 %collective-permute-start.27 = (f32[96,3200]{1,0:T(8,128)}, f32[96,3200]{1,0:T(8,128)}, u32[]{:S(2)}, u32[]{:S(2)}) collective-permute-start(f32[96,3200]{1,0:T(8,128)} %get-tuple-element.304), channel_id=1, source_target_pairs={{0,16},{8,24},{16,0},{24,8},{1,17},{9,25},{17,1},{25,9},{2,18},{10... | collective-permute-start | bytes 3686408 | tf_op jit(solution)/shard_map/ppermute | solution.py:137
  857.7 113.3 %copy-start.53 = (bf16[768]{0:T(1024)(128)(2,1)S(1)}, bf16[768]{0:T(1024)(128)(2,1)}, u32[]{:S(2)}) copy-start(bf16[768]{0:T(1024)(128)(2,1)} %copy-done.52) | copy-start | bytes 4612
  857.8 61.3 %collective-permute-start.16 = (bf16[512,96]{0,1:T(8,128)(2,1)S(1)}, bf16[512,96]{0,1:T(8,128)(2,1)S(1)}, u32[]{:S(2)}, u32[]{:S(2)}) collective-permute-start(bf16[512,96]{0,1:T(8,128)(2,1)S(1)} %get-tuple-element.323), channel_id=1, source_target_pairs={{0,4},{4,8},{8,12},{12,16},{16,20},{20,24},{24,28},{28,0},{1,5},{5... | collective-permute-start | bytes 294920 | tf_op jit(solution)/shard_map/ppermute | solution.py:137
  859.6 99.2 %collective-permute-start.17 = (bf16[512,96]{0,1:T(8,128)(2,1)S(1)}, bf16[512,96]{0,1:T(8,128)(2,1)S(1)}, u32[]{:S(2)}, u32[]{:S(2)}) collective-permute-start(bf16[512,96]{0,1:T(8,128)(2,1)S(1)} %get-tuple-element.322), channel_id=1, source_target_pairs={{0,8},{4,12},{8,16},{12,20},{16,24},{20,28},{24,0},{28,4},{1,9},{5... | collective-permute-start | bytes 294920 | tf_op jit(solution)/shard_map/ppermute | solution.py:137
  860.6 100.5 %collective-permute-start.18 = (bf16[512,96]{0,1:T(8,128)(2,1)S(1)}, bf16[512,96]{0,1:T(8,128)(2,1)S(1)}, u32[]{:S(2)}, u32[]{:S(2)}) collective-permute-start(bf16[512,96]{0,1:T(8,128)(2,1)S(1)} %get-tuple-element.321), channel_id=1, source_target_pairs={{0,12},{4,16},{8,20},{12,24},{16,28},{20,0},{24,4},{28,8},{1,13},{... | collective-permute-start | bytes 294920 | tf_op jit(solution)/shard_map/ppermute | solution.py:137
  919.1 46.7 %collective-permute-start.19 = (bf16[512,96]{0,1:T(8,128)(2,1)S(1)}, bf16[512,96]{0,1:T(8,128)(2,1)S(1)}, u32[]{:S(2)}, u32[]{:S(2)}) collective-permute-start(bf16[512,96]{0,1:T(8,128)(2,1)S(1)} %get-tuple-element.320), channel_id=1, source_target_pairs={{0,16},{4,20},{8,24},{12,28},{16,0},{20,4},{24,8},{28,12},{1,17},{... | collective-permute-start | bytes 294920 | tf_op jit(solution)/shard_map/ppermute | solution.py:137
  958.8 8.8 collective-permute-start.20
  961.1 7.2 collective-permute-start.21
  965.8 4.6 collective-permute-start.22
  971.1 61.7 %collective-permute-start.23 = (bf16[8,512,96]{1,2,0:T(8,128)(2,1)}, bf16[8,512,96]{1,2,0:T(8,128)(2,1)}, u32[]{:S(2)}, u32[]{:S(2)}) collective-permute-start(bf16[8,512,96]{1,2,0:T(8,128)(2,1)} %bitcast_dynamic-update-slice_fusion.4), channel_id=1, source_target_pairs={{0,1},{1,2},{2,3},{3,0},{4,5},{5,6},{6,7},{7,4},{8,9},{9,10},{10,1... | collective-permute-start | bytes 2359304 | tf_op jit(solution)/shard_map/ppermute | solution.py:137
  1005.6 43.9 %collective-permute-start.24 = (bf16[8,512,96]{1,2,0:T(8,128)(2,1)}, bf16[8,512,96]{1,2,0:T(8,128)(2,1)}, u32[]{:S(2)}, u32[]{:S(2)}) collective-permute-start(bf16[8,512,96]{1,2,0:T(8,128)(2,1)} %bitcast_dynamic-update-slice_fusion.4), channel_id=1, source_target_pairs={{0,2},{1,3},{2,0},{3,1},{4,6},{5,7},{6,4},{7,5},{8,10},{9,11},{10,... | collective-permute-start | bytes 2359304 | tf_op jit(solution)/shard_map/ppermute | solution.py:137
  1008.7 42.5 %collective-permute-start.25 = (bf16[8,512,96]{1,2,0:T(8,128)(2,1)}, bf16[8,512,96]{1,2,0:T(8,128)(2,1)}, u32[]{:S(2)}, u32[]{:S(2)}) collective-permute-start(bf16[8,512,96]{1,2,0:T(8,128)(2,1)} %bitcast_dynamic-update-slice_fusion.4), channel_id=1, source_target_pairs={{0,3},{1,0},{2,1},{3,2},{4,7},{5,4},{6,5},{7,6},{8,11},{9,8},{10,9... | collective-permute-start | bytes 2359304 | tf_op jit(solution)/shard_map/ppermute | solution.py:137
  1032.8 102.3 %collective-permute-start.28 = (f32[96,3200]{1,0:T(8,128)}, f32[96,3200]{1,0:T(8,128)}, u32[]{:S(2)}, u32[]{:S(2)}) collective-permute-start(f32[96,3200]{1,0:T(8,128)} %get-tuple-element.303), channel_id=1, source_target_pairs={{0,24},{8,0},{16,8},{24,16},{1,25},{9,1},{17,9},{25,17},{2,26},{10... | collective-permute-start | bytes 3686408 | tf_op jit(solution)/shard_map/ppermute | solution.py:137
  (65 other events, 485.1 us)
Sparse Core Ops, SparseCore 0:
  56.5 155.7 all-gather.5
  246.4 99.2 all-gather.9
  347.9 64.7 all-gather.7
  592.9 68.2 reduce-scatter.3
  809.6 156.9 reduce-scatter.5
  972.3 166.0 reduce-scatter.7

commit v3 on v2

--- a/solution.py
+++ b/solution.py
@@ -50,68 +50,64 @@
     return dot(a, b, ((0,), (0,)))
 
 
-def share_kernel(sizes, count, *refs):
-    nz, nx, ny, nc = sizes
-    n = nz * nx * ny * nc
+def neighbours(axes, sizes):
+    found = []
+    for place, (axis, size) in enumerate(zip(axes, sizes)):
+        for step in range(1, size):
+            found.append((place, step, {axis: lax.rem(lax.axis_index(axis) + step, size)}))
+    return found
+
+
+def meet(devices):
+    barrier = pltpu.get_barrier_semaphore()
+    for device in devices:
+        pl.semaphore_signal(barrier, inc=1, device_id=device, device_id_type=MESH)
+    pl.semaphore_wait(barrier, len(devices))
+
+
+def share_kernel(axes, sizes, count, *refs):
     ins, outs = refs[:count], refs[count : 2 * count]
     send, recv, near = refs[2 * count :]
-    me = ((lax.axis_index("z") * nx + lax.axis_index("x")) * ny + lax.axis_index("y")) * nc
-    me = me + lax.axis_index("c")
-
-    def device(k):
-        peer = lax.rem(me + k, n)
-        return (
-            peer // (nx * ny * nc),
-            lax.rem(peer // (ny * nc), nx),
-            lax.rem(peer // nc, ny),
-            lax.rem(peer, nc),
-        )
-
-    def remote(i, k):
-        return pltpu.make_async_remote_copy(
-            src_ref=ins[i],
-            dst_ref=outs[i].at[me],
-            send_sem=send.at[i, k],
-            recv_sem=recv.at[i, k],
-            device_id=device(k),
-            device_id_type=MESH,
-        )
-
-    barrier = pltpu.get_barrier_semaphore()
-
-    @pl.loop(1, n)
-    def _(k):
-        pl.semaphore_signal(barrier, inc=1, device_id=device(k), device_id_type=MESH)
-
-    pl.semaphore_wait(barrier, n - 1)
-
-    @pl.loop(1, n)
-    def _(k):
-        for i in range(count):
-            remote(i, k).start()
-
+    index = tuple(lax.axis_index(a) for a in axes)
+    peers = neighbours(axes, sizes)
+    meet([device for _, _, device in peers])
     for i in range(count):
-        pltpu.make_async_copy(ins[i], outs[i].at[me], near.at[i]).start()
+        pltpu.make_async_copy(ins[i], outs[i].at[index], near.at[i]).start()
     for i in range(count):
-        pltpu.make_async_copy(ins[i], outs[i].at[me], near.at[i]).wait()
-
-    @pl.loop(1, n)
-    def _(k):
-        for i in range(count):
-            remote(i, k).wait()
-
-
-def share(sizes, collective_id, *arrays):
-    n = math.prod(sizes)
-    count = len(arrays)
+        pltpu.make_async_copy(ins[i], outs[i].at[index], near.at[i]).wait()
+    for place in range(len(axes)):
+        view = (slice(None),) * place + index[place:]
+        copies = []
+        for number, (at, _, device) in enumerate(peers):
+            if at == place:
+                for i in range(count):
+                    copies.append(
+                        pltpu.make_async_remote_copy(
+                            src_ref=outs[i].at[view],
+                            dst_ref=outs[i].at[view],
+                            send_sem=send.at[i, number],
+                            recv_sem=recv.at[i, number],
+                            device_id=device,
+                            device_id_type=MESH,
+                        )
+                    )
+        for copy in copies:
+            copy.start()
+        for copy in copies:
+            copy.wait()
+
+
+def share(axes, collective_id, *arrays):
+    sizes = tuple(lax.axis_size(a) for a in axes)
+    count, peers = len(arrays), sum(sizes) - len(sizes)
     return pl.pallas_call(
-        functools.partial(share_kernel, sizes, count),
-        out_shape=[jax.ShapeDtypeStruct((n,) + a.shape, a.dtype) for a in arrays],
+        functools.partial(share_kernel, axes, sizes, count),
+        out_shape=[jax.ShapeDtypeStruct(sizes + a.shape, a.dtype) for a in arrays],
         in_specs=[pl.BlockSpec(memory_space=pltpu.VMEM)] * count,
         out_specs=[pl.BlockSpec(memory_space=pltpu.VMEM)] * count,
         scratch_shapes=[
-            pltpu.SemaphoreType.DMA((count, n)),
-            pltpu.SemaphoreType.DMA((count, n)),
+            pltpu.SemaphoreType.DMA((count, peers)),
+            pltpu.SemaphoreType.DMA((count, peers)),
             pltpu.SemaphoreType.DMA((count,)),
         ],
         compiler_params=pltpu.CompilerParams(
@@ -119,6 +115,150 @@
         ),
         name=f"share{collective_id}",
     )(*arrays)
+
+
+def remote(src, dst, send, recv, device):
+    return pltpu.make_async_remote_copy(
+        src_ref=src, dst_ref=dst, send_sem=send, recv_sem=recv, device_id=device,
+        device_id_type=MESH,
+    )
+
+
+def run_all(copies):
+    for copy in copies:
+        copy.start()
+    for copy in copies:
+        copy.wait()
+
+
+def block_peer(sizes, step):
+    nz, nx = sizes[:2]
+    me = lax.axis_index("z") * nx + lax.axis_index("x")
+    peer = lax.rem(me + step, nz * nx)
+    return me, peer, {"z": peer // nx, "x": lax.rem(peer, nx)}
+
+
+def fetch_kernel(sizes, in_ref, out_ref, from_c, from_y, half, total, sems_c, sems_y, sems_b):
+    nz, nx, ny, nc = sizes
+    blocks = nz * nx
+    iy, ic = lax.axis_index("y"), lax.axis_index("c")
+    along_y = [d for _, _, d in neighbours(("y",), (ny,))]
+    along_c = [d for _, _, d in neighbours(("c",), (nc,))]
+    along_b = [block_peer(sizes, step)[2] for step in range(1, blocks)]
+    meet(along_c + along_y + along_b)
+    run_all([
+        remote(in_ref.at[:, d["c"]], from_c.at[i], sems_c.at[0, i], sems_c.at[1, i], d)
+        for i, d in enumerate(along_c)
+    ])
+
+    @pl.loop(0, ny)
+    def _(y):
+        @pl.loop(0, blocks)
+        def _(k):
+            value = in_ref[y, ic, k]
+            for i in range(nc - 1):
+                value = value + from_c[i, y, k]
+            half[y, k] = value
+
+    run_all([
+        remote(half.at[d["y"]], from_y.at[i], sems_y.at[0, i], sems_y.at[1, i], d)
+        for i, d in enumerate(along_y)
+    ])
+
+    @pl.loop(0, blocks)
+    def _(k):
+        value = half[iy, k]
+        for i in range(ny - 1):
+            value = value + from_y[i, k]
+        total[k] = value
+
+    me = block_peer(sizes, 0)[0]
+    copies = []
+    for step in range(1, blocks):
+        _, peer, device = block_peer(sizes, step)
+        copies.append(
+            remote(total.at[peer], out_ref.at[me], sems_b.at[0, step], sems_b.at[1, step], device)
+        )
+    for copy in copies:
+        copy.start()
+    out_ref[me] = total[me]
+    for copy in copies:
+        copy.wait()
+
+
+def fetch_blocks(sizes, looked_up, collective_id):
+    nz, nx, ny, nc = sizes
+    block = looked_up.shape[3:]
+    blocks = nz * nx
+    return pl.pallas_call(
+        functools.partial(fetch_kernel, sizes),
+        out_shape=jax.ShapeDtypeStruct((blocks,) + block, BF),
+        in_specs=[pl.BlockSpec(memory_space=pltpu.VMEM)],
+        out_specs=pl.BlockSpec(memory_space=pltpu.VMEM),
+        scratch_shapes=[
+            pltpu.VMEM((nc - 1, ny, blocks) + block, BF),
+            pltpu.VMEM((ny - 1, blocks) + block, BF),
+            pltpu.VMEM((ny, blocks) + block, BF),
+            pltpu.VMEM((blocks,) + block, BF),
+            pltpu.SemaphoreType.DMA((2, nc - 1)),
+            pltpu.SemaphoreType.DMA((2, ny - 1)),
+            pltpu.SemaphoreType.DMA((2, blocks)),
+        ],
+        compiler_params=pltpu.CompilerParams(
+            collective_id=collective_id, has_side_effects=True, vmem_limit_bytes=VMEM_LIMIT
+        ),
+        name="fetch_blocks",
+    )(looked_up)
+
+
+def spread_kernel(sizes, in_ref, out_ref, sems_c, sems_y, sems_b):
+    nz, nx, ny, nc = sizes
+    blocks = nz * nx
+    iy, ic = lax.axis_index("y"), lax.axis_index("c")
+    along_y = [d for _, _, d in neighbours(("y",), (ny,))]
+    along_c = [d for _, _, d in neighbours(("c",), (nc,))]
+    along_b = [block_peer(sizes, step)[2] for step in range(1, blocks)]
+    meet(along_c + along_y + along_b)
+    me = block_peer(sizes, 0)[0]
+    copies = []
+    for step in range(1, blocks):
+        _, peer, device = block_peer(sizes, step)
+        copies.append(
+            remote(in_ref.at[peer], out_ref.at[iy, ic, me], sems_b.at[0, step],
+                   sems_b.at[1, step], device)
+        )
+    for copy in copies:
+        copy.start()
+    out_ref[iy, ic, me] = in_ref[me]
+    for copy in copies:
+        copy.wait()
+    run_all([
+        remote(out_ref.at[iy, ic], out_ref.at[iy, ic], sems_y.at[0, i], sems_y.at[1, i], d)
+        for i, d in enumerate(along_y)
+    ])
+    run_all([
+        remote(out_ref.at[:, ic], out_ref.at[:, ic], sems_c.at[0, i], sems_c.at[1, i], d)
+        for i, d in enumerate(along_c)
+    ])
+
+
+def spread_blocks(sizes, parts, collective_id):
+    nz, nx, ny, nc = sizes
+    return pl.pallas_call(
+        functools.partial(spread_kernel, sizes),
+        out_shape=jax.ShapeDtypeStruct((ny, nc) + parts.shape, parts.dtype),
+        in_specs=[pl.BlockSpec(memory_space=pltpu.VMEM)],
+        out_specs=pl.BlockSpec(memory_space=pltpu.VMEM),
+        scratch_shapes=[
+            pltpu.SemaphoreType.DMA((2, nc - 1)),
+            pltpu.SemaphoreType.DMA((2, ny - 1)),
+            pltpu.SemaphoreType.DMA((2, nz * nx)),
+        ],
+        compiler_params=pltpu.CompilerParams(
+            collective_id=collective_id, has_side_effects=True, vmem_limit_bytes=VMEM_LIMIT
+        ),
+        name="spread_blocks",
+    )(parts)
 
 
 def axis_place(axes):
@@ -154,8 +294,16 @@
     return lax.dynamic_index_in_dim(values, index, 0, keepdims=False)
 
 
-def gather_kernel(low_ref, high_ref, ids_ref, table_ref, out_ref, rows_ref):
+def gather_kernel(low_ref, high_ref, ids_ref, table_ref, out_ref, turned_ref, rows_ref):
     source = pl.program_id(0)
+
+    @pl.when(source == 0)
+    def _():
+        @pl.loop(0, table_ref.shape[1] // LANES)
+        def _(k):
+            at = pl.multiple_of(k * LANES, LANES)
+            turned_ref[pl.ds(at, LANES), :] = table_ref[:, pl.ds(at, LANES)].T
+
     low, high = low_ref[source], high_ref[source]
     rows_ref[...] = jnp.zeros_like(rows_ref)
 
@@ -166,44 +314,47 @@
             place = base + i
             valid = jnp.logical_and(place >= low, place < high)
             row = jnp.where(valid, ids_ref[source, place], 0)
-            value = table_ref[pl.ds(row, 1), :]
+            value = turned_ref[pl.ds(row, 1), :]
             rows.append(jnp.where(valid, value, 0.0))
         rows_ref[pl.ds(base, 8), :] = jnp.concatenate(rows, axis=0)
         return carry
 
     lax.fori_loop(low // 8, (high + 7) // 8, chunk, 0)
-    out_ref[0] = rows_ref[...].astype(BF)
+    out_ref[0] = rows_ref[...].T.astype(BF)
 
 
 def gather_rows(table, ids, low, high):
     sources, count = ids.shape
-    width = table.shape[1]
+    width = table.shape[0]
     return pl.pallas_call(
         gather_kernel,
-        out_shape=jax.ShapeDtypeStruct((sources, count, width), BF),
+        out_shape=jax.ShapeDtypeStruct((sources, width, count), BF),
         grid_spec=pltpu.PrefetchScalarGridSpec(
             num_scalar_prefetch=3,
             grid=(sources,),
             in_specs=[
                 pl.BlockSpec(table.shape, lambda i, *_: (0, 0), pipeline_mode=pl.Buffered(1))
             ],
-            out_specs=pl.BlockSpec((1, count, width), lambda i, *_: (i, 0, 0)),
-            scratch_shapes=[pltpu.VMEM((count, width), F32)],
+            out_specs=pl.BlockSpec((1, width, count), lambda i, *_: (i, 0, 0)),
+            scratch_shapes=[
+                pltpu.VMEM((table.shape[1], width), F32),
+                pltpu.VMEM((count, width), F32),
+            ],
         ),
         compiler_params=pltpu.CompilerParams(vmem_limit_bytes=VMEM_LIMIT),
         name="gather_rows",
     )(low, high, ids, table)
 
 
-def scatter_kernel(low_ref, high_ref, ids_ref, rows_ref, out_ref, wide_ref):
+def scatter_kernel(low_ref, high_ref, ids_ref, rows_ref, out_ref, total_ref, wide_ref):
     source = pl.program_id(0)
 
     @pl.when(source == 0)
     def _():
-        out_ref[...] = jnp.zeros_like(out_ref)
+        total_ref[...] = jnp.zeros_like(total_ref)
 
     low, high = low_ref[source], high_ref[source]
-    wide_ref[...] = rows_ref[0].astype(F32)
+    wide_ref[...] = rows_ref[0].astype(F32).T
 
     def chunk(k, carry):
         base = pl.multiple_of(k * 8, 8)
@@ -213,23 +364,33 @@
             valid = jnp.logical_and(place >= low, place < high)
             row = jnp.where(valid, ids_ref[source, place], 0)
             addend = jnp.where(valid, block[i : i + 1, :], 0.0)
-            out_ref[pl.ds(row, 1), :] = out_ref[pl.ds(row, 1), :] + addend
+            total_ref[pl.ds(row, 1), :] = total_ref[pl.ds(row, 1), :] + addend
         return carry
 
     lax.fori_loop(low // 8, (high + 7) // 8, chunk, 0)
 
+    @pl.when(source == pl.num_programs(0) - 1)
+    def _():
+        @pl.loop(0, out_ref.shape[1] // LANES)
+        def _(k):
+            at = pl.multiple_of(k * LANES, LANES)
+            out_ref[:, pl.ds(at, LANES)] = total_ref[pl.ds(at, LANES), :].T
+
 
 def scatter_rows(rows, ids, low, high, table_rows):
-    sources, count, width = rows.shape
+    sources, width, count = rows.shape
     return pl.pallas_call(
         scatter_kernel,
-        out_shape=jax.ShapeDtypeStruct((table_rows, width), F32),
+        out_shape=jax.ShapeDtypeStruct((width, table_rows), F32),
         grid_spec=pltpu.PrefetchScalarGridSpec(
             num_scalar_prefetch=3,
             grid=(sources,),
-            in_specs=[pl.BlockSpec((1, count, width), lambda i, *_: (i, 0, 0))],
-            out_specs=pl.BlockSpec((table_rows, width), lambda i, *_: (0, 0)),
-            scratch_shapes=[pltpu.VMEM((count, width), F32)],
+            in_specs=[pl.BlockSpec((1, width, count), lambda i, *_: (i, 0, 0))],
+            out_specs=pl.BlockSpec((width, table_rows), lambda i, *_: (0, 0)),
+            scratch_shapes=[
+                pltpu.VMEM((table_rows, width), F32),
+                pltpu.VMEM((count, width), F32),
+            ],
         ),
         compiler_params=pltpu.CompilerParams(vmem_limit_bytes=VMEM_LIMIT),
         name="scatter_rows",
@@ -599,17 +760,19 @@
     ints = jnp.pad(ints, ((0, -ints.shape[0] % 8), (0, 0)))
     gain_part = jnp.pad(gains_w.astype(BF).astype(F32),
                         ((0, 8 - gains_w.shape[0]), (0, LANES - gains_w.shape[1])))
-    ada_part = ada_w.astype(BF).reshape(-1, LANES)
-    ints_all, gains_all, ada_all = share(sizes, 0, ints, gain_part, ada_part)
-
-    layer_low, head_low, ints_all = together(layer_w.astype(BF), head_w.astype(BF), ints_all)
-    layer_all = lax.all_gather(layer_low, ALL, axis=0, tiled=True)
+    ints_all, gains_all = share(ALL, 0, ints, gain_part)
+    ints_all = ints_all.reshape((n,) + ints.shape)
+    gains_all = gains_all.reshape((n,) + gain_part.shape)
+
+    block_low = jnp.concatenate(
+        [layer_w.astype(BF), ada_w.astype(BF).reshape(layer_w.shape[0], -1)], axis=1)
+    block_low, head_low, ints_all = together(block_low, head_w.astype(BF), ints_all)
+    layer_all = lax.all_gather(block_low, ALL, axis=0, tiled=True)
 
     piece_for = lambda k: lax.dynamic_slice_in_dim(head_low, k * SEGMENT, SEGMENT, 1)
     head_parts = exchange(piece_for, ("z",))
 
     gains = jnp.moveaxis(gains_all[:, : gains_w.shape[0], : gains_w.shape[1]], 0, 1).reshape(4, D)
-    ada = ada_all.reshape(C, 6 * D)
     free_rows = free_count // LANES
     score_rows = score_count // LANES
     all_tokens = ints_all[:, :free_rows].reshape(nz * nx, ny * nc, free_count)
@@ -622,23 +785,16 @@
     low = jnp.sum((owners < vocab_index).astype(jnp.int32), axis=1)
     high = jnp.sum((owners <= vocab_index).astype(jnp.int32), axis=1)
     local_ids = wanted - vocab_start
-    looked_up = gather_rows(embed_w, local_ids, low, high)
-    looked_up = looked_up.reshape(ny * nc, nz * nx * free_count, table_width)
-    got = exchange(lambda k: pick(looked_up, k), ("y", "c"))
-    mine = got[0][1].astype(F32)
-    for _, piece in got[1:]:
-        mine = mine + piece.astype(F32)
-    mine = mine.astype(BF).reshape(nz * nx, free_count, table_width)
-    columns = in_order(exchange(lambda k: pick(mine, k), ("z", "x")))
-    x0_u = jnp.swapaxes(columns, 0, 1).reshape(free_count, D).astype(F32)
-
+    looked_up = gather_rows(embed_w.T, local_ids, low, high)
+    looked_up = looked_up.reshape((ny, nc, nz * nx) + looked_up.shape[1:])
+    x0_u = fetch_blocks(sizes, looked_up, 3).reshape(D, free_count).T.astype(F32)
     senders = [sender for sender, _ in head_parts]
     x0_u, *pieces = together(x0_u, *[piece for _, piece in head_parts])
     head_part = in_order(list(zip(senders, pieces))).reshape(-1, SEGMENT)
 
     mask_row = gains[3:4]
     condition = time_features(times, C, TSTEPS).astype(BF)
-    modulation = matmul(condition, ada)
+    modulation = matmul(condition, layer_all[:, layer_w.shape[1] :].reshape(C, 6 * D))
     shift_a, scale_a, gate_a, shift_m, scale_m, gate_m = [
         modulation[:, i * D : (i + 1) * D] for i in range(6)]
     normed_u, inv_u = layer_norm(x0_u)
@@ -646,7 +802,7 @@
     normed_0, inv_0 = layer_norm(mask_row)
     a_m = (normed_0 * gains[0:1] * (1.0 + scale_a) + shift_a).astype(BF)
     w_qkv, w_o = layer_all[:, : 3 * D], layer_all[:, 3 * D : 4 * D]
-    w_up, w_down = layer_all[:, 4 * D : 4 * D + FF], layer_all[:, 4 * D + FF :]
+    w_up, w_down = layer_all[:, 4 * D : 4 * D + FF], layer_all[:, 4 * D + FF : 4 * D + 2 * FF]
     qkv_m = matmul(jnp.broadcast_to(a_m, (16, D)), w_qkv)
     kv_u = matmul(a_u, w_qkv[:, D:])
     tables = (*rope_rows(free_positions), *rope_rows(masked))
@@ -678,7 +834,7 @@
     column_of = jnp.where(owned, (owner // nc) * SEGMENT + within % SEGMENT, -1)[:, None]
     e, stats = head_logits(rows, head_all, column_of)
     top = stats[:, 0]
-    every = lax.all_gather(stats.T, ("z", "c"), axis=0)
+    every = share(("z", "c"), 4, stats.T.reshape(4, -1, LANES))[0].reshape(nz * nc, 4, group)
     best = jnp.max(every[:, 0], axis=0)
     log_total = best + jnp.log(jnp.sum(every[:, 1] * jnp.exp(every[:, 0] - best), axis=0))
     chosen = jnp.sum(every[:, 2], axis=0)
@@ -708,9 +864,6 @@
     d_pre = jax.vjp(gelu_tanh, pre)[1](d_act)[0].astype(BF)
     d_up = matmul_tn(b, d_pre)
     d_b = matmul_nt(d_pre, w_up)
-    d_b, d_mlp = together(d_b, jnp.concatenate([d_up.astype(BF), d_down.astype(BF)], axis=1))
-    scatter = lambda a: lax.psum_scatter(a, ALL, scatter_dimension=0, tiled=True).astype(F32)
-    g_mlp = scatter(d_mlp)
     d_shift_m = jnp.sum(d_b, axis=0)
     product = jnp.sum(d_b * normed_m, axis=0)
     d_scale_m = product * gains[1]
@@ -721,7 +874,8 @@
     d_wout = matmul_tn(att, d_branch)
     d_att = matmul_nt(d_branch, w_o).astype(BF)
     d_k, d_v, d_qkv_m = attend_back(q, k_u, k_m, kv_u, qkv_m, tables, mask, lse_a, d_att)
-    d_k, *head_pieces = together(d_k, *[piece for _, piece in head_sums[1:]])
+    arrivals = [piece for _, piece in head_sums[1:]]
+    d_k, *arrivals[:-1] = together(d_k, *arrivals[:-1])
     d_kv = jnp.concatenate([d_k, d_v], axis=1)
     d_wkv = matmul_tn(a_u, d_kv)
     d_row_m = d_qkv_m[:3].reshape(3 * D)
@@ -736,25 +890,34 @@
     d_x0_u = norm_back(d_a_u * scaling, normed_u, inv_u)
     d_mask = jnp.sum(d_x1, axis=0) + norm_back(d_a_m * scaling, normed_0, inv_0)[0]
 
-    sent = jnp.swapaxes(d_x0_u.astype(BF).reshape(free_count, nz * nx, -1), 0, 1)
-    arrived = in_order(exchange(lambda k: pick(sent, k), ("z", "x")))
-    arrived = in_order(exchange(lambda k: arrived, ("y", "c")))
-    g_embed = scatter_rows(arrived.reshape(n, free_count, table_width), local_ids, low, high,
-                           table_rows).T
-
+    d_block = jnp.concatenate(
+        [d_wkv.astype(BF), d_wout.astype(BF), d_up.astype(BF), d_down.astype(BF)], axis=1)
+    width = d_block.shape[1]
+    d_block = jnp.transpose(d_block.reshape(nz, nx, ny, nc, -1, width), (3, 1, 2, 0, 4, 5))
+    d_block = d_block.reshape(nc, -1, width)
+    got = exchange(lambda k: pick(d_block, k), ("c",))
+    chip_sum = sum(piece.astype(F32) for _, piece in got).astype(BF)
+    plane_sum = lax.psum_scatter(chip_sum, ("x", "y"), scatter_dimension=0, tiled=True)
+
+    sent, chip_sum, *head_pieces = together(
+        d_x0_u.astype(BF).T.reshape(nz * nx, table_width, free_count), chip_sum, *arrivals)
     g_part = head_own
     for piece in head_pieces:
         g_part = g_part + piece.astype(F32)
     g_part = g_part.reshape(nz, -1, SEGMENT)
-    g_head = together(in_order(exchange(lambda k: pick(g_part, k), ("z",))))[0]
-    g_head = jnp.swapaxes(g_head, 0, 1).reshape(head_w.shape)
+    sent, g_part = together(sent, g_part)
+    head_got = exchange(lambda k: pick(g_part, k), ("z",))
+
+    arrived = spread_blocks(sizes, sent, 5).reshape(n, table_width, free_count)
+    g_embed = scatter_rows(arrived, local_ids, low, high, table_rows)
 
     small = jnp.concatenate([d_shift_a, d_scale_a, d_gate_a, d_shift_m, d_scale_m, d_gate_m,
                              d_gain_a, d_gain_m, d_gain_f, d_mask,
                              a_m[0].astype(F32), d_row_m, jnp.broadcast_to(loss_part, (LANES,))])
     small = small.reshape(-1, LANES)
     count_small = small.shape[0]
-    small_all = share(sizes, 1, jnp.pad(small, ((0, -count_small % 8), (0, 0))))[0]
+    small = jnp.pad(small, ((0, -count_small % 8), (0, 0)))
+    small_all = share(ALL, 1, small)[0].reshape((n,) + small.shape)
     small_all = small_all[:, :count_small].reshape(n, -1)
     d_mod_all = small_all[:, : 6 * D]
     d_gains = jnp.sum(small_all[:, 6 * D : 10 * D], axis=0).reshape(4, D)
@@ -768,13 +931,22 @@
                                       layer_w.shape[0], 1)
     g_outer = exact(a_rows, small_all[:, 11 * D : 14 * D])
 
-    g_rest = scatter(jnp.concatenate([d_wkv.astype(BF), d_wout.astype(BF)], axis=1))
+    plane_sum = plane_sum.reshape(nz, -1, width)
+    g_rest = sum(p.astype(F32) for _, p in exchange(lambda k: pick(plane_sum, k), ("z",)))
     g_layer = jnp.concatenate(
-        [g_outer[:, :D], g_outer[:, D:] + g_rest[:, : 2 * D], g_rest[:, 2 * D :], g_mlp], axis=1)
+        [g_outer[:, :D], g_outer[:, D:] + g_rest[:, : 2 * D], g_rest[:, 2 * D :]], axis=1)
+
+    segments = []
+    for k in range(nz):
+        segment = head_got[0][1]
+        for sender, piece in head_got[1:]:
+            segment = jnp.where(sender == k, piece, segment)
+        segments.append(segment)
+    g_head = jnp.concatenate(segments, axis=1)
 
     squares = sum(jnp.sum(g * g) for g in (g_layer, g_ada, g_gains, g_embed, g_head))
-    squares_all = share(sizes, 2, jnp.broadcast_to(squares, (8, LANES)))[0]
-    grad_norm = jnp.sqrt(jnp.sum(squares_all[:, 0, 0]))
+    squares_all = share(ALL, 2, jnp.broadcast_to(squares, (8, LANES)))[0]
+    grad_norm = jnp.sqrt(jnp.sum(squares_all[..., 0, 0]))
     factor = jnp.minimum(1.0, CLIP_NORM / grad_norm)
     step_value = step_count[0].astype(F32)
     updates = (

time: 1290 us -> 1220 us (0.946)
  Pallas kernels: 330 us -> 510 us
  local copies, waits for them, and re-layouts: 240 us -> 77.2 us
  starting transfers between devices: 125 us -> 20.3 us
  waiting for transfers between devices: 296 us -> 347 us
  other arithmetic: 127 us -> 110 us
  blocking collectives: 14.9 us -> 0 us
    pallas_call x5 -> x8, Pallas kernels: 142 us -> 322 us  [the longest x4 146 us: share(): pl.pallas_call(functools.partial(share_kernel, axes, sizes, count), out_s...]
    ppermute x29 -> x13, starting transfers between devices: 124 us -> 19.8 us  [exchange(): moved = lax.ppermute(piece, axes, [(i, (i + step) % n) for i in range(n)])]
    dynamic_update_slice x28 -> x4, local copies, waits for them, and re-layouts: 94.1 us -> 6.71 us  [in_order(): out = lax.dynamic_update_index_in_dim(out, piece, sender, 0)]
    unnamed x188 -> x179, local copies, waits for them, and re-layouts: 68.3 us -> 10 us
    all_gather x1, waiting for transfers between devices: 0.02 us -> 28.3 us  [local(): layer_all = lax.all_gather(block_low, ALL, axis=0, tiled=True)]
    add x5 -> x4, other arithmetic: 44.4 us -> 22.9 us  [adam_step(): ema_new = ema_rate * ema_copy + (1.0 - ema_rate) * weight_new]
    all_gather x1 -> x0, blocking collectives: 14.9 us -> none  [local(): every = lax.all_gather(stats.T, ('z', 'c'), axis=0)]
    transpose x0 -> x2, other arithmetic: none -> 14.3 us  [the longest x1 13.9 us: local(): results[12:16] = [a.T for a in results[12:16]]]
  transfers between devices with their start and end apart: 35 -> 18, of which waited for: 14 -> 11; matrix products, arithmetic and copies ran while one was open for 26% -> 15% of each run, Pallas kernels for 10% -> 27%
where the time goes in v3:
time: 1220 us; the launch traced here: 1210 us
  Pallas kernels  510 us (42%)
  waiting for transfers between devices  347 us (28%)
  matrix products  119 us (10%)
  other arithmetic  110 us (9%)
  local copies, waits for them, and re-layouts  77.2 us (6%)
  between operations  25.9 us (2%)
  starting transfers between devices  20.3 us (2%)
    ppermute x13, waiting for transfers between devices, exchange(): moved = lax.ppermute(piece, axes, [(i, (i + step) % n) for i in range(n)])  199 us
    pallas_call x4, Pallas kernels, share(): pl.pallas_call(functools.partial(share_kernel, axes, sizes, count), out_s...  146 us
    pallas_call x1, Pallas kernels, head_logits(): pl.pallas_call(logits_kernel, grid=(count // tile,), out_shape=[jax.Shape...  79.5 us
    all_gather x1, waiting for transfers between devices, local(): rows = lax.all_gather(final_turned, ('z', 'c'), axis=0, tiled=True)  67 us
    dot_general x15, matrix products, dot(): lax.dot_general(a, b, ((contract[0], contract[1]), ((), ())), preferred_e...  66 us
    pallas_call x1, Pallas kernels, head_rows_back(): pl.pallas_call(rows_back_kernel, grid=(count // tile,), out_shape=[jax.Sh...  65.6 us
    pallas_call x1, Pallas kernels, fetch_blocks(): pl.pallas_call(functools.partial(fetch_kernel, sizes), out_shape=jax.Shap...  57.6 us
    dot_general x1, matrix products, local(): jnp.einsum('rd,yrv->ydv', rows, d_logits, preferred_element_type=F32)  50.5 us
  transfers between devices with their start and end apart: 18, of which 11 were waited for; matrix products, arithmetic and copies ran while one was open for 15% of the time, Pallas kernels for 27%

profile of v3, /device:TPU:0, one launch (start us, length us, event | category | flops | bytes accessed | tf_op | source)
XLA Modules:
  0.0 1209.3 jit_solution(6659059082683931786)
XLA Ops:
  19.5 18.0 %share0.1 = (s32[4,2,2,2,16,128]{5,4,3,2,1,0:T(8,128)}, f32[4,2,2,2,8,128]{5,4,3,2,1,0:T(8,128)}) custom-call(s32[16,128]{1,0:T(8,128)} %pad.18.refs_0_, f32[8,128]{1,0:T(8,128)} %pad_convert_fusion.refs_1_), custom_call_target="tpu_custom_call" | custom-call | tf_op jit(solution)/shard_map/share0/pallas_call | solution.py:103
  39.9 3.3 collective-permute-start.2
  46.9 35.9 %gather_rows.1 = bf16[32,96,512]{2,1,0:T(8,128)(2,1)} custom-call(s32[32]{0:T(128)} %reduce_sum.388.low_ref, s32[32]{0:T(128)} %reduce_sum.390.high_ref, s32[32,512]{1,0:T(8,128)} %bitcast.261, f32[96,12800]{1,0:T(8,128)} %bitcast.233), custom_call_target="tpu_custom_call" | custom-call | tf_op jit(solution)/shard_map/gather_rows/pallas_call | solution.py:329
  82.8 57.6 %fetch_blocks.1 = bf16[8,96,512]{2,1,0:T(8,128)(2,1)} custom-call(bf16[2,2,8,96,512]{4,3,2,1,0:T(8,128)(2,1)} %bitcast.237), custom_call_target="tpu_custom_call" | custom-call | tf_op jit(solution)/shard_map/fetch_blocks/pallas_call | solution.py:193
  159.5 28.3 %all-gather.4.cloned.1.call-done = bf16[768,9984]{1,0:T(8,128)(2,1)} async-done(((bf16[24,9984]{1,0:T(8,128)(2,1)}), bf16[768,9984]{1,0:T(8,128)(2,1)}) %all-gather.4.cloned.1.call-update) | async-done | bytes 15335440 | tf_op jit(solution)/shard_map/all_gather | solution.py:770
  193.5 3.3 fusion.25.qm_ref.km_ref.vm_ref
  196.8 5.3 fusion.44.kv_ref.vv_ref
  202.7 18.8 %attend.1 = (bf16[512,768]{1,0:T(8,128)(2,1)}, bf16[512,768]{1,0:T(8,128)(2,1)}, bf16[512,768]{1,0:T(8,128)(2,1)}, bf16[512,768]{1,0:T(8,128)(2,1)}, f32[6,512,2]{2,1,0:T(8,128)}) custom-call(f32[512,1536]{1,0:T(8,128)} %fusion.44.kv_ref.vv_ref, f32[512,1536]{1,0:T(8,128)} %fusion.44.kv_ref.vv_ref, f32[16,2304]{1,0:T(8,128)} %fusion.25.qm_ref.km_ref.vm_ref, ...), custom_call_target="tpu_custom_call" | custom-call | flops 1207959552 | bytes 4718592 | tf_op jit(solution)/shard_map/attend/pallas_call | solution.py:458
  224.3 5.4 fusion.21
  229.8 9.6 fusion.119
  249.5 7.2 fusion.36.target_ref
  256.6 34.2 %all-gather.8.cloned.1.call-done = bf16[1536,3200]{1,0:T(8,128)(2,1)} async-done(((bf16[384,3200]{1,0:T(8,128)(2,1)}), bf16[1536,3200]{1,0:T(8,128)(2,1)}) %all-gather.8.cloned.1.call-update) | async-done | bytes 9830416 | tf_op jit(solution)/shard_map/all_gather | solution.py:824
  290.8 67.0 %all-gather.6.cloned.1.call-done.x_ref = bf16[4096,768]{1,0:T(8,128)(2,1)} async-done(((bf16[512,768]{1,0:T(8,128)(2,1)}), bf16[4096,768]{1,0:T(8,128)(2,1)}) %all-gather.6.cloned.1.call-update) | async-done | bytes 6291472 | tf_op jit(solution)/shard_map/all_gather | solution.py:825
  357.8 79.5 %head_logits.1 = (bf16[2,4096,3200]{2,1,0:T(8,128)(2,1)}, f32[4096,4]{1,0:T(8,128)}) custom-call(bf16[4096,768]{1,0:T(8,128)(2,1)} %all-gather.6.cloned.1.call-done.x_ref, bf16[2,768,3200]{2,1,0:T(8,128)(2,1)} %bitcast.285, s32[4096,1]{1,0:T(8,128)} %fusion.36.target_ref), custom_call_target="tpu_custom_call" | custom-call | flops 40265318400 | bytes 52428800 | tf_op jit(solution)/shard_map/head_logits/pallas_call | solution.py:597
  440.2 11.6 share4.1
  457.6 3.3 bitcast_multiply_fusion.1
  462.9 65.6 %head_rows_back.1 = (bf16[2,4096,3200]{2,1,0:T(8,128)(2,1)}, f32[4096,768]{1,0:T(8,128)}) custom-call(bf16[2,4096,3200]{2,1,0:T(8,128)(2,1)} %get-tuple-element.70.e_ref, bf16[2,768,3200]{2,1,0:T(8,128)(2,1)} %bitcast.286, s32[4096,1]{1,0:T(8,128)} %fusion.36.target_ref, f32[4096,2]{1,0:T(8,128)} %pad_maximum_fusion.2.factor_ref), custom_call_target="tpu_custom_call", output_to_operand_aliasing={{0}: (0, {})} | custom-call | flops 40265318400 | bytes 104857600 | tf_op jit(solution)/shard_map/head_rows_back/pallas_call | solution.py:646
  528.5 7.9 convert_element_type.235
  536.6 50.5 %fusion.8 = f32[2,3200,768]{1,2,0:T(8,128)} fusion(bf16[2,4096,3200]{2,1,0:T(8,128)(2,1)} %get-tuple-element.73, bf16[4096,768]{1,0:T(8,128)(2,1)} %all-gather.6.cloned.1.call-done.x_ref), kind=kOutput, calls=%fused_computation.15 | convolution fusion | flops 40265318400 | bytes 78381056 | tf_op jit(solution)/shard_map/rd,yrv->ydv/dot_general | solution.py:849
  587.1 19.0 %reduce-scatter.3.cloned.1.call-done = bf16[512,768]{1,0:T(8,128)(2,1)} async-done(((bf16[4096,768]{1,0:T(8,128)(2,1)}), bf16[512,768]{1,0:T(8,128)(2,1)}) %reduce-scatter.3.cloned.1.call-update) | async-done | bytes 786448 | tf_op jit(solution)/shard_map/reduce_scatter | solution.py:847
  613.2 9.3 fusion.7
  622.5 6.5 multiply_reduce_fusion.5
  629.0 8.6 fusion.31
  649.1 23.9 %attend_back.1 = (bf16[512,768]{1,0:T(8,128)(2,1)}, bf16[512,768]{1,0:T(8,128)(2,1)}, f32[8,768]{1,0:T(8,128)}) custom-call(bf16[512,768]{1,0:T(8,128)(2,1)} %get-tuple-element.61.q_ref, bf16[512,768]{1,0:T(8,128)(2,1)} %get-tuple-element.62.ku_ref, bf16[512,768]{1,0:T(8,128)(2,1)} %get-tuple-element.63.km_ref, f32[512,1536]{1,0:T(8,128)} %fusion.44.kv_ref.vv_ref, ...), custom_call_target="tpu_custom_call" | custom-call | flops 3221225472 | bytes 5505024 | tf_op jit(solution)/shard_map/attend_back/pallas_call | solution.py:530
  673.0 5.2 convolution_convert_fusion.1
  678.3 5.9 convolution_convert_fusion
  684.2 6.7 collective-permute-done.4
  690.9 53.6 %collective-permute-done.3 = bf16[384,3200]{1,0:T(8,128)(2,1)} collective-permute-done((bf16[384,3200]{1,0:T(8,128)(2,1)}, bf16[384,3200]{1,0:T(8,128)(2,1)}, u32[]{:S(2)}, u32[]{:S(2)}) %collective-permute-start.3) | collective-permute-done | bytes 2457632 | tf_op jit(solution)/shard_map/ppermute | solution.py:277
  747.2 3.3 copy.256
  750.5 3.4 dynamic-slice_bitcast_fusion
  753.9 3.2 copy-done
  757.1 10.8 collective-permute-done.5
  767.9 8.8 fusion
  785.7 3.4 multiply_reduce_fusion.2
  792.3 103.0 %share1.1 = f32[4,2,2,2,88,128]{5,4,3,2,1,0:T(8,128)} custom-call(f32[88,128]{1,0:T(8,128)} %pad.22.refs_0_), custom_call_target="tpu_custom_call" | custom-call | tf_op jit(solution)/shard_map/share1/pallas_call | solution.py:103
  900.4 7.8 fusion.14
  908.2 42.5 %spread_blocks.1 = bf16[2,2,8,96,512]{4,3,2,1,0:T(8,128)(2,1)} custom-call(bf16[8,96,512]{2,1,0:T(8,128)(2,1)} %bitcast.251), custom_call_target="tpu_custom_call" | custom-call | tf_op jit(solution)/shard_map/spread_blocks/pallas_call | solution.py:247
  950.7 39.7 %scatter_rows.1 = f32[96,12800]{1,0:T(8,128)} custom-call(s32[32]{0:T(128)} %reduce_sum.388.low_ref, s32[32]{0:T(128)} %reduce_sum.390.high_ref, s32[32,512]{1,0:T(8,128)} %bitcast.262, bf16[32,96,512]{2,1,0:T(8,128)(2,1)} %bitcast.236), custom_call_target="tpu_custom_call" | custom-call | tf_op jit(solution)/shard_map/scatter_rows/pallas_call | solution.py:382
  990.4 4.1 dynamic-slice_bitcast_fusion.1
  994.5 4.8 collective-permute-start.12
  1009.4 11.0 collective-permute-done.12
  1021.2 64.6 %collective-permute-done.11 = f32[96,3200]{1,0:T(8,128)S(1)} collective-permute-done((f32[96,3200]{1,0:T(8,128)}, f32[96,3200]{1,0:T(8,128)S(1)}, u32[]{:S(2)}, u32[]{:S(2)}) %collective-permute-start.11) | collective-permute-done | bytes 1228832 | tf_op jit(solution)/shard_map/ppermute | solution.py:277
  1090.3 8.2 collective-permute-done.8
  1098.5 44.0 %collective-permute-done.7 = bf16[24,8448]{1,0:T(8,128)(2,1)S(1)} collective-permute-done((bf16[24,8448]{1,0:T(8,128)(2,1)S(1)}, bf16[24,8448]{1,0:T(8,128)(2,1)S(1)}, u32[]{:S(2)}, u32[]{:S(2)}) %collective-permute-start.7) | collective-permute-done | bytes 405536 | tf_op jit(solution)/shard_map/ppermute | solution.py:277
  1148.4 13.8 %share2.1 = f32[4,2,2,2,8,128]{5,4,3,2,1,0:T(8,128)} custom-call(f32[8,128]{1,0:T(8,128)} %broadcast_in_dim.144.refs_0_), custom_call_target="tpu_custom_call" | custom-call | tf_op jit(solution)/shard_map/share2/pallas_call | solution.py:103
  1165.2 4.4 multiply_add_fusion.5
  1169.6 16.9 %multiply_add_fusion = (f32[96,12800]{1,0:T(8,128)}, f32[96,12800]{1,0:T(8,128)}, f32[96,12800]{1,0:T(8,128)}, f32[96,12800]{1,0:T(8,128)}) fusion(f32[96,12800]{1,0:T(8,128)} %param.49, f32[]{:T(128)} %bitcast.78, f32[]{:T(128)S(6)} %sub.309, f32[96,12800]{1,0:T(8,128)} %param.46, f32[]{:T(128)} %bitcast.77, f32[]{:T(128)} %bitcast.76, f32[]{:T(128)S(6)} %min.13, ...), kind=kLoop, calls=%fused_computation.29 | loop fusion | flops 27033600 | bytes 44236820 | tf_op jit(solution)/shard_map/add | solution.py:719
  1186.7 13.9 %fusion.12 = (f32[12800,96]{0,1:T(8,128)}, f32[96,12800]{1,0:T(8,128)}, f32[12800,96]{0,1:T(8,128)}, f32[12800,96]{0,1:T(8,128)}) fusion(f32[12800,96]{0,1:T(8,128)} %param.45, f32[]{:T(128)S(6)} %sub.309, f32[]{:T(128)} %bitcast.78, f32[]{:T(128)} %bitcast.77, f32[12800,96]{0,1:T(8,128)} %param.44, f32[]{:T(128)} %bitcast.76, f32[96,12800]{1,0:T(8,128)S(1)} %bitcast.224, ...), kind=kLoop, calls=%fused_computation.24 | loop fusion | flops 23347200 | bytes 44236820 | tf_op jit(solution)/shard_map/transpose | solution.py:962
  (375 shorter events, 121.1 us)
Async XLA Ops:
  7.2 180.6 %all-gather.4.cloned.1.call-start = ((), (), s32[]{:S(2)}) async-start(), calls=%async_computation.2 | async-start | bytes 15814656 | tf_op jit(solution)/shard_map/all_gather | solution.py:770
  38.3 252.6 %all-gather.8.cloned.1.call-start = ((), (), s32[]{:S(2)}) async-start(), calls=%async_computation.4 | async-start | bytes 12288000 | tf_op jit(solution)/shard_map/all_gather | solution.py:824
  39.9 102.3 %collective-permute-start.2 = (bf16[96,3200]{1,0:T(8,128)(2,1)}, bf16[96,3200]{1,0:T(8,128)(2,1)}, u32[]{:S(2)}, u32[]{:S(2)}) collective-permute-start(bf16[96,3200]{1,0:T(8,128)(2,1)} %get-tuple-element.155), channel_id=1, source_target_pairs={{0,24},{8,0},{16,8},{24,16},{1,25},{9,1},{17,9},{25,17},{2,26},{10... | collective-permute-start | bytes 1843208 | tf_op jit(solution)/shard_map/ppermute | solution.py:277
  43.1 99.1 %collective-permute-start.1 = (bf16[96,3200]{1,0:T(8,128)(2,1)}, bf16[96,3200]{1,0:T(8,128)(2,1)}, u32[]{:S(2)}, u32[]{:S(2)}) collective-permute-start(bf16[96,3200]{1,0:T(8,128)(2,1)} %get-tuple-element.156), channel_id=1, source_target_pairs={{0,16},{8,24},{16,0},{24,8},{1,17},{9,25},{17,1},{25,9},{2,18},{10... | collective-permute-start | bytes 1843208 | tf_op jit(solution)/shard_map/ppermute | solution.py:277
  43.2 99.1 %collective-permute-start = (bf16[96,3200]{1,0:T(8,128)(2,1)}, bf16[96,3200]{1,0:T(8,128)(2,1)}, u32[]{:S(2)}, u32[]{:S(2)}) collective-permute-start(bf16[96,3200]{1,0:T(8,128)(2,1)} %get-tuple-element.157), channel_id=1, source_target_pairs={{0,8},{8,16},{16,24},{24,0},{1,9},{9,17},{17,25},{25,1},{2,10},{10... | collective-permute-start | bytes 1843208 | tf_op jit(solution)/shard_map/ppermute | solution.py:277
  142.1 54.6 %copy-start.2 = (f32[768,512]{0,1:T(8,128)}, f32[768,512]{0,1:T(8,128)S(1)}, u32[]{:S(2)}) copy-start(f32[768,512]{0,1:T(8,128)S(1)} %copy.220) | copy-start | bytes 4718596
  150.6 207.3 %all-gather.6.cloned.1.call-start = ((), (), s32[]{:S(2)}) async-start(), calls=%async_computation.3 | async-start | bytes 7077888 | tf_op jit(solution)/shard_map/all_gather | solution.py:825
  151.7 41.1 %copy-start.40 = (f32[1,768]{1,0:T(1,128)}, f32[1,768]{1,0:T(1,128)S(1)}, u32[]{:S(2)}) copy-start(f32[1,768]{1,0:T(1,128)S(1)} %slice.136) | copy-start | bytes 9220
  151.8 45.0 %copy-start.60 = (f32[768]{0:T(1024)}, f32[768]{0:T(1024)S(1)}, u32[]{:S(2)}) copy-start(f32[768]{0:T(1024)S(1)} %mul.840) | copy-start | bytes 9220
  152.0 72.3 %copy-start.58 = (f32[768]{0:T(1024)}, f32[768]{0:T(1024)S(1)}, u32[]{:S(2)}) copy-start(f32[768]{0:T(1024)S(1)} %mul.870) | copy-start | bytes 9220
  154.7 38.1 %copy-start.42 = (f32[1,768]{1,0:T(1,128)}, f32[1,768]{1,0:T(1,128)S(1)}, u32[]{:S(2)}) copy-start(f32[1,768]{1,0:T(1,128)S(1)} %mul.854) | copy-start | bytes 9220
  154.8 74.9 %copy-start.34 = (f32[768]{0:T(1024)}, f32[768]{0:T(1024)S(1)}, u32[]{:S(2)}) copy-start(f32[768]{0:T(1024)S(1)} %add.553) | copy-start | bytes 9220
  154.9 84.8 %copy-start.31 = (f32[768]{0:T(1024)}, f32[768]{0:T(1024)S(1)}, u32[]{:S(2)}) copy-start(f32[768]{0:T(1024)S(1)} %mul.884) | copy-start | bytes 9220
  159.2 37.6 %copy-start.47 = (f32[512]{0:T(512)}, f32[512]{0:T(512)S(1)}, u32[]{:S(2)}) copy-start(f32[512]{0:T(512)S(1)} %broadcast_multiply_fusion.8) | copy-start | bytes 6148
  159.5 37.3 %copy-start.63 = (f32[512]{0:T(512)}, f32[512]{0:T(512)S(1)}, u32[]{:S(2)}) copy-start(f32[512]{0:T(512)S(1)} %add_rsqrt_fusion.2) | copy-start | bytes 6148
  193.4 30.8 %copy-start.54 = (f32[768]{0:T(1024)}, f32[768]{0:T(1024)S(1)}, u32[]{:S(2)}) copy-start(f32[768]{0:T(1024)S(1)} %get-tuple-element.106) | copy-start | bytes 9220
  193.4 30.8 %copy-start.74 = (f32[768]{0:T(1024)}, f32[768]{0:T(1024)S(1)}, u32[]{:S(2)}) copy-start(f32[768]{0:T(1024)S(1)} %get-tuple-element.111) | copy-start | bytes 9220
  193.4 36.3 %copy-start.36 = (f32[768]{0:T(1024)}, f32[768]{0:T(1024)S(1)}, u32[]{:S(2)}) copy-start(f32[768]{0:T(1024)S(1)} %get-tuple-element.108) | copy-start | bytes 9220
  193.5 36.3 %copy-start.72 = (f32[768]{0:T(1024)}, f32[768]{0:T(1024)S(1)}, u32[]{:S(2)}) copy-start(f32[768]{0:T(1024)S(1)} %get-tuple-element.107) | copy-start | bytes 9220
  242.4 363.8 %reduce-scatter.3.cloned.1.call-start = ((), (), s32[]{:S(2)}) async-start(), calls=%async_computation.5 | async-start | bytes 7077888 | tf_op jit(solution)/shard_map/reduce_scatter | solution.py:847
  536.4 467.9 %reduce-scatter.5.cloned.1.call-start = ((), (), s32[]{:S(2)}) async-start(), calls=%async_computation.6 | async-start | bytes 8110080 | tf_op jit(solution)/shard_map/reduce_scatter | solution.py:900
  613.0 27.5 %copy-start.13 = (f32[512,768]{1,0:T(8,128)}, f32[512,768]{1,0:T(8,128)S(1)}, u32[]{:S(2)}) copy-start(f32[512,768]{1,0:T(8,128)S(1)} %get-tuple-element.137) | copy-start | bytes 4718596
  637.6 53.3 %collective-permute-start.4 = (bf16[384,3200]{1,0:T(8,128)(2,1)}, bf16[384,3200]{1,0:T(8,128)(2,1)}, u32[]{:S(2)}, u32[]{:S(2)}) collective-permute-start(bf16[384,3200]{1,0:T(8,128)(2,1)} %get-tuple-element.144), channel_id=1, source_target_pairs={{0,4},{2,6},{4,0},{6,2},{1,5},{3,7},{5,1},{7,3},{8,12},{10,14},{12... | collective-permute-start | bytes 7372808 | tf_op jit(solution)/shard_map/ppermute | solution.py:277
  639.1 105.4 %collective-permute-start.3 = (bf16[384,3200]{1,0:T(8,128)(2,1)}, bf16[384,3200]{1,0:T(8,128)(2,1)}, u32[]{:S(2)}, u32[]{:S(2)}) collective-permute-start(bf16[384,3200]{1,0:T(8,128)(2,1)} %get-tuple-element.145), channel_id=1, source_target_pairs={{0,2},{2,4},{4,6},{6,0},{1,3},{3,5},{5,7},{7,1},{8,10},{10,12},{12... | collective-permute-start | bytes 7372808 | tf_op jit(solution)/shard_map/ppermute | solution.py:277
  649.1 23.9 %copy-start.55 = (f32[768]{0:T(1024)S(1)}, f32[768]{0:T(1024)}, u32[]{:S(2)}) copy-start(f32[768]{0:T(1024)} %copy-done.54) | copy-start | bytes 9220
  649.1 23.9 %copy-start.59 = (f32[768]{0:T(1024)S(1)}, f32[768]{0:T(1024)}, u32[]{:S(2)}) copy-start(f32[768]{0:T(1024)} %copy-done.58) | copy-start | bytes 9220
  649.1 23.9 %copy-start.75 = (f32[768]{0:T(1024)S(1)}, f32[768]{0:T(1024)}, u32[]{:S(2)}) copy-start(f32[768]{0:T(1024)} %copy-done.74) | copy-start | bytes 9220
  678.2 66.2 %copy-start.21 = (bf16[512,768]{1,0:T(8,128)(2,1)S(1)}, bf16[512,768]{1,0:T(8,128)(2,1)}, u32[]{:S(2)}) copy-start(bf16[512,768]{1,0:T(8,128)(2,1)} %get-tuple-element.77) | copy-start | bytes 2359300
  678.3 66.3 %copy-start.20 = (bf16[512,768]{1,0:T(8,128)(2,1)S(1)}, bf16[512,768]{1,0:T(8,128)(2,1)}, u32[]{:S(2)}) copy-start(bf16[512,768]{1,0:T(8,128)(2,1)} %get-tuple-element.78) | copy-start | bytes 2359300
  684.2 60.5 %copy-start.3 = (f32[768,512]{0,1:T(8,128)S(1)}, f32[768,512]{0,1:T(8,128)}, u32[]{:S(2)}) copy-start(f32[768,512]{0,1:T(8,128)} %copy-done.2) | copy-start | bytes 4718596
  684.2 60.5 %copy-start.48 = (f32[512]{0:T(512)S(1)}, f32[512]{0:T(512)}, u32[]{:S(2)}) copy-start(f32[512]{0:T(512)} %copy-done.47) | copy-start | bytes 6148
  684.2 60.5 %copy-start.57 = (f32[768]{0:T(1024)S(1)}, f32[768]{0:T(1024)}, u32[]{:S(2)}) copy-start(f32[768]{0:T(1024)} %copy-done.56) | copy-start | bytes 9220
  684.2 60.5 %copy-start.61 = (f32[768]{0:T(1024)S(1)}, f32[768]{0:T(1024)}, u32[]{:S(2)}) copy-start(f32[768]{0:T(1024)} %copy-done.60) | copy-start | bytes 9220
  684.2 60.5 %copy-start.64 = (f32[512]{0:T(512)S(1)}, f32[512]{0:T(512)}, u32[]{:S(2)}) copy-start(f32[512]{0:T(512)} %copy-done.63) | copy-start | bytes 6148
  684.2 60.5 %copy-start.71 = (f32[768]{0:T(1024)S(1)}, f32[768]{0:T(1024)}, u32[]{:S(2)}) copy-start(f32[768]{0:T(1024)} %copy-done.70) | copy-start | bytes 9220
  757.1 10.8 collective-permute-start.5
  785.6 114.8 %collective-permute-start.9 = (bf16[384,3200]{1,0:T(8,128)(2,1)}, bf16[384,3200]{1,0:T(8,128)(2,1)}, u32[]{:S(2)}, u32[]{:S(2)}) collective-permute-start(bf16[384,3200]{1,0:T(8,128)(2,1)} %get-tuple-element.143), channel_id=1, source_target_pairs={{0,6},{2,0},{4,2},{6,4},{1,7},{3,1},{5,3},{7,5},{8,14},{10,8},{12,... | collective-permute-start | bytes 7372808 | tf_op jit(solution)/shard_map/ppermute | solution.py:277
  994.5 25.9 %collective-permute-start.12 = (f32[96,3200]{1,0:T(8,128)}, f32[96,3200]{1,0:T(8,128)S(1)}, u32[]{:S(2)}, u32[]{:S(2)}) collective-permute-start(f32[96,3200]{1,0:T(8,128)} %get-tuple-element.152), channel_id=1, source_target_pairs={{0,8},{8,16},{16,24},{24,0},{1,9},{9,17},{17,25},{25,1},{2,10},{10... | collective-permute-start | bytes 3686408 | tf_op jit(solution)/shard_map/ppermute | solution.py:277
  999.3 86.5 %collective-permute-start.11 = (f32[96,3200]{1,0:T(8,128)}, f32[96,3200]{1,0:T(8,128)S(1)}, u32[]{:S(2)}, u32[]{:S(2)}) collective-permute-start(f32[96,3200]{1,0:T(8,128)} %get-tuple-element.153), channel_id=1, source_target_pairs={{0,16},{8,24},{16,0},{24,8},{1,17},{9,25},{17,1},{25,9},{2,18},{10... | collective-permute-start | bytes 3686408 | tf_op jit(solution)/shard_map/ppermute | solution.py:277
  1001.2 84.6 %collective-permute-start.10 = (f32[96,3200]{1,0:T(8,128)}, f32[96,3200]{1,0:T(8,128)}, u32[]{:S(2)}, u32[]{:S(2)}) collective-permute-start(f32[96,3200]{1,0:T(8,128)} %get-tuple-element.154), channel_id=1, source_target_pairs={{0,24},{8,0},{16,8},{24,16},{1,25},{9,1},{17,9},{25,17},{2,26},{10... | collective-permute-start | bytes 3686408 | tf_op jit(solution)/shard_map/ppermute | solution.py:277
  1005.5 84.7 %collective-permute-start.6 = (bf16[24,8448]{1,0:T(8,128)(2,1)S(1)}, bf16[24,8448]{1,0:T(8,128)(2,1)S(1)}, u32[]{:S(2)}, u32[]{:S(2)}) collective-permute-start(bf16[24,8448]{1,0:T(8,128)(2,1)S(1)} %get-tuple-element.161), channel_id=1, source_target_pairs={{0,8},{8,16},{16,24},{24,0},{1,9},{9,17},{17,25},{25,1},{2,10},{10... | collective-permute-start | bytes 1216520 | tf_op jit(solution)/shard_map/ppermute | solution.py:277
  1006.5 92.0 %collective-permute-start.8 = (bf16[24,8448]{1,0:T(8,128)(2,1)S(1)}, bf16[24,8448]{1,0:T(8,128)(2,1)S(1)}, u32[]{:S(2)}, u32[]{:S(2)}) collective-permute-start(bf16[24,8448]{1,0:T(8,128)(2,1)S(1)} %get-tuple-element.162), channel_id=1, source_target_pairs={{0,24},{8,0},{16,8},{24,16},{1,25},{9,1},{17,9},{25,17},{2,26},{10... | collective-permute-start | bytes 1216520 | tf_op jit(solution)/shard_map/ppermute | solution.py:277
  1020.4 122.1 %collective-permute-start.7 = (bf16[24,8448]{1,0:T(8,128)(2,1)S(1)}, bf16[24,8448]{1,0:T(8,128)(2,1)S(1)}, u32[]{:S(2)}, u32[]{:S(2)}) collective-permute-start(bf16[24,8448]{1,0:T(8,128)(2,1)S(1)} %get-tuple-element.163), channel_id=1, source_target_pairs={{0,16},{8,24},{16,0},{24,8},{1,17},{9,25},{17,1},{25,9},{2,18},{10... | collective-permute-start | bytes 1216520 | tf_op jit(solution)/shard_map/ppermute | solution.py:277
  1090.3 74.2 %copy-start.68 = (f32[4,24]{1,0:T(4,128)S(1)}, f32[4,24]{1,0:T(4,128)}, u32[]{:S(2)}) copy-start(f32[4,24]{1,0:T(4,128)} %param.38) | copy-start | bytes 1156
  1090.3 74.2 %copy-start.76 = (f32[4,24]{1,0:T(4,128)S(1)}, f32[4,24]{1,0:T(4,128)}, u32[]{:S(2)}) copy-start(f32[4,24]{1,0:T(4,128)} %param.41) | copy-start | bytes 1156
  1090.3 74.2 %copy-start.77 = (f32[4,24]{1,0:T(4,128)S(1)}, f32[4,24]{1,0:T(4,128)}, u32[]{:S(2)}) copy-start(f32[4,24]{1,0:T(4,128)} %param.40) | copy-start | bytes 1156
  1090.3 74.2 %copy-start.78 = (f32[4,24]{1,0:T(4,128)S(1)}, f32[4,24]{1,0:T(4,128)}, u32[]{:S(2)}) copy-start(f32[4,24]{1,0:T(4,128)} %param.39) | copy-start | bytes 1156
  1165.2 21.4 %slice-start = ((s8[4915200]{0:T(1024)(128)(4,1)}), s8[4194304]{0:T(1024)(128)(4,1)S(1)}, s32[]{:S(2)}) async-start(s8[4915200]{0:T(1024)(128)(4,1)} %bitcast.223), calls=%async_computation.7 | async-start | bytes 8388608
  (53 other events, 319.2 us)
Sparse Core Ops, SparseCore 0:
  38.4 149.3 all-gather.3
  190.2 100.5 all-gather.7
  293.1 64.7 all-gather.5
  536.5 69.5 reduce-scatter.2
  776.8 125.0 reduce-scatter.4

commit v4 on v3

--- a/solution.py
+++ b/solution.py
@@ -17,6 +17,7 @@
 TSTEPS = 20
 SEGMENT = 3200
 LANES = 128
+ROWS = 64
 
 NORM_EPS = 1e-05
 CLIP_NORM = 0.05
@@ -207,6 +208,7 @@
         compiler_params=pltpu.CompilerParams(
             collective_id=collective_id, has_side_effects=True, vmem_limit_bytes=VMEM_LIMIT
         ),
+        cost_estimate=pl.CostEstimate(flops=0, bytes_accessed=1 << 27, transcendentals=0),
         name="fetch_blocks",
     )(looked_up)
 
@@ -257,6 +259,7 @@
         compiler_params=pltpu.CompilerParams(
             collective_id=collective_id, has_side_effects=True, vmem_limit_bytes=VMEM_LIMIT
         ),
+        cost_estimate=pl.CostEstimate(flops=0, bytes_accessed=1 << 27, transcendentals=0),
         name="spread_blocks",
     )(parts)
 
@@ -290,8 +293,19 @@
     return lax.optimization_barrier(values)
 
 
-def pick(values, index):
-    return lax.dynamic_index_in_dim(values, index, 0, keepdims=False)
+def pick(values, index, dim=0):
+    return lax.dynamic_index_in_dim(values, index, dim, keepdims=False)
+
+
+def spread_parts(values, dim, axis):
+    got = exchange(lambda k: pick(values, k, dim).astype(jnp.float16), (axis,))
+    return pick(values, got[0][0], dim), [piece for _, piece in got[1:]]
+
+
+def added(own, pieces):
+    for piece in pieces:
+        own = own + piece.astype(F32)
+    return own
 
 
 def gather_kernel(low_ref, high_ref, ids_ref, table_ref, out_ref, turned_ref, rows_ref):
@@ -342,6 +356,7 @@
             ],
         ),
         compiler_params=pltpu.CompilerParams(vmem_limit_bytes=VMEM_LIMIT),
+        cost_estimate=pl.CostEstimate(flops=0, bytes_accessed=1 << 27, transcendentals=0),
         name="gather_rows",
     )(low, high, ids, table)
 
@@ -393,6 +408,7 @@
             ],
         ),
         compiler_params=pltpu.CompilerParams(vmem_limit_bytes=VMEM_LIMIT),
+        cost_estimate=pl.CostEstimate(flops=0, bytes_accessed=1 << 27, transcendentals=0),
         name="scatter_rows",
     )(low, high, ids, rows)
 
@@ -555,14 +571,15 @@
 
 
 def tile_of(segments):
-    return max(16, 512 // segments)
+    return max(16, 1024 // segments)
 
 
 def chunk_of(width):
     return next(n for n in (640, 400, 128, width) if width % n == 0)
 
 
-def logits_kernel(x_ref, w_ref, target_ref, e_ref, stats_ref, logits_ref):
+def logits_kernel(places_ref, x_ref, w_ref, target_ref, *refs):
+    e_ref, stats_ref, logits_ref = refs[-3:]
     segments, _, width = w_ref.shape
     chunk = chunk_of(width)
     rows = x_ref.shape[0]
@@ -590,27 +607,37 @@
     )
 
 
-def head_logits(rows, weights, targets):
-    count = rows.shape[0]
+def head_logits(rows, weights, targets, places, block, so_far):
+    count, group = rows.shape[0], targets.shape[0]
     segments, _, width = weights.shape
     tile = tile_of(segments)
+    per = group // places.shape[0] // tile
+    first = block * (count // tile)
+
+    def place(i, places):
+        return places[(first + i) // per] * per + lax.rem(first + i, per)
+
     return pl.pallas_call(
         logits_kernel,
-        grid=(count // tile,),
         out_shape=[
-            jax.ShapeDtypeStruct((segments, count, width), BF),
-            jax.ShapeDtypeStruct((count, 4), F32),
+            jax.ShapeDtypeStruct((segments, group, width), BF),
+            jax.ShapeDtypeStruct((group, 4), F32),
         ],
-        in_specs=[
-            pl.BlockSpec((tile, D), lambda i: (i, 0)),
-            pl.BlockSpec(weights.shape, lambda i: (0, 0, 0), pipeline_mode=pl.Buffered(1)),
-            pl.BlockSpec((tile, 1), lambda i: (i, 0)),
-        ],
-        out_specs=[
-            pl.BlockSpec((segments, tile, width), lambda i: (0, i, 0)),
-            pl.BlockSpec((tile, 4), lambda i: (i, 0)),
-        ],
-        scratch_shapes=[pltpu.VMEM((tile, segments * width), F32)],
+        grid_spec=pltpu.PrefetchScalarGridSpec(
+            num_scalar_prefetch=1,
+            grid=(count // tile,),
+            in_specs=[
+                pl.BlockSpec((tile, D), lambda i, p: (i, 0)),
+                pl.BlockSpec(weights.shape, lambda i, p: (0, 0, 0), pipeline_mode=pl.Buffered(1)),
+                pl.BlockSpec((tile, 1), lambda i, p: (place(i, p), 0)),
+            ] + [pl.BlockSpec(memory_space=pl.ANY)] * len(so_far),
+            out_specs=[
+                pl.BlockSpec((segments, tile, width), lambda i, p: (0, first + i, 0)),
+                pl.BlockSpec((tile, 4), lambda i, p: (place(i, p), 0)),
+            ],
+            scratch_shapes=[pltpu.VMEM((tile, segments * width), F32)],
+        ),
+        input_output_aliases={4 + i: i for i in range(len(so_far))},
         compiler_params=pltpu.CompilerParams(vmem_limit_bytes=VMEM_LIMIT),
         cost_estimate=pl.CostEstimate(
             flops=2 * count * D * segments * width,
@@ -618,49 +645,58 @@
             transcendentals=count * segments * width,
         ),
         name="head_logits",
-    )(rows, weights, targets)
-
-
-def rows_back_kernel(e_ref, w_ref, target_ref, factor_ref, d_ref, dx_ref):
+    )(places, rows, weights, targets, *so_far)
+
+
+def rows_back_kernel(places_ref, e_ref, w_ref, target_ref, factor_ref, d_ref, dx_ref):
     segments, _, width = w_ref.shape
-    chunk = chunk_of(width)
     rows = e_ref.shape[1]
-    lane = lax.broadcasted_iota(jnp.int32, (rows, chunk), 1)
-    target = target_ref[...]
-    factor = factor_ref[:, 0:1]
-    special = factor_ref[:, 1:2]
+    lane = lax.broadcasted_iota(jnp.int32, (ROWS, LANES), 1)
+    wide = lambda a: jnp.broadcast_to(a, (ROWS, LANES))
     total = None
     for y in range(segments):
-        for at in range(0, width, chunk):
-            e = e_ref[y, :, at : at + chunk].astype(F32)
-            hit = lane == target - (y * width + at)
-            d_ref[y, :, at : at + chunk] = jnp.where(hit, special, e * factor).astype(BF)
+        for r in range(0, rows, ROWS):
+            place = target_ref[r : r + ROWS, :] - (lane + y * width)
+            factor = wide(factor_ref[r : r + ROWS, 0:1])
+            special = wide(factor_ref[r : r + ROWS, 1:2])
+            for at in range(0, width, LANES):
+                e = e_ref[y, r : r + ROWS, at : at + LANES].astype(F32)
+                d_ref[y, r : r + ROWS, at : at + LANES] = jnp.where(
+                    place == at, special, e * factor).astype(BF)
         part = matmul_nt(d_ref[y], w_ref[y])
         total = part if total is None else total + part
-    dx_ref[...] = total
-
-
-def head_rows_back(e, weights, targets, factors):
+    dx_ref[...] = total.astype(BF)
+
+
+def head_rows_back(e, weights, targets, factors, places):
     segments, count, width = e.shape
     tile = tile_of(segments)
+    per = count // places.shape[0] // tile
+
+    def placed(i, places):
+        return (places[i // per] * per + lax.rem(i, per), 0)
+
     return pl.pallas_call(
         rows_back_kernel,
-        grid=(count // tile,),
         out_shape=[
             jax.ShapeDtypeStruct(e.shape, BF),
-            jax.ShapeDtypeStruct((count, D), F32),
+            jax.ShapeDtypeStruct((count, D), BF),
         ],
-        in_specs=[
-            pl.BlockSpec((segments, tile, width), lambda i: (0, i, 0)),
-            pl.BlockSpec(weights.shape, lambda i: (0, 0, 0), pipeline_mode=pl.Buffered(1)),
-            pl.BlockSpec((tile, 1), lambda i: (i, 0)),
-            pl.BlockSpec((tile, 2), lambda i: (i, 0)),
-        ],
-        out_specs=[
-            pl.BlockSpec((segments, tile, width), lambda i: (0, i, 0)),
-            pl.BlockSpec((tile, D), lambda i: (i, 0)),
-        ],
-        input_output_aliases={0: 0},
+        grid_spec=pltpu.PrefetchScalarGridSpec(
+            num_scalar_prefetch=1,
+            grid=(count // tile,),
+            in_specs=[
+                pl.BlockSpec((segments, tile, width), lambda i, p: (0, i, 0)),
+                pl.BlockSpec(weights.shape, lambda i, p: (0, 0, 0), pipeline_mode=pl.Buffered(1)),
+                pl.BlockSpec((tile, 1), placed),
+                pl.BlockSpec((tile, 2), placed),
+            ],
+            out_specs=[
+                pl.BlockSpec((segments, tile, width), lambda i, p: (0, i, 0)),
+                pl.BlockSpec((tile, D), placed),
+            ],
+        ),
+        input_output_aliases={1: 0},
         compiler_params=pltpu.CompilerParams(vmem_limit_bytes=VMEM_LIMIT),
         cost_estimate=pl.CostEstimate(
             flops=2 * count * D * segments * width,
@@ -668,7 +704,7 @@
             transcendentals=0,
         ),
         name="head_rows_back",
-    )(e, weights, targets, factors)
+    )(places, e, weights, targets, factors)
 
 
 def layer_norm(values):
@@ -822,8 +858,13 @@
 
     final_turned = jnp.swapaxes(final.reshape(score_count, nz, nx, -1), 1, 2).reshape(score_count, D)
     head_all = lax.all_gather(head_part, ("y", "x"), axis=0, tiled=True).reshape(ny, D, SEGMENT)
-    rows = lax.all_gather(final_turned, ("z", "c"), axis=0, tiled=True)
-    group = rows.shape[0]
+    group = nz * nc * score_count
+    blocks, places = [], []
+    for sender, piece in exchange(lambda k: final_turned, ("z",)):
+        for place, part in exchange(lambda k: piece, ("c",)):
+            blocks.append(part)
+            places.append(sender * nc + place)
+    places = jnp.stack(places).astype(jnp.int32)
     row_targets = pick(jnp.moveaxis(jnp.moveaxis(all_targets, 3, 1), (2, 3), (0, 1)).reshape(
         nx * ny, group), ix * ny + iy)
     row_times = pick(jnp.moveaxis(jnp.moveaxis(all_times.reshape(nz, nx, ny, nc), 3, 1), (2, 3), (0, 1))
@@ -832,7 +873,12 @@
     owner, within = row_targets // table_rows, row_targets % table_rows
     owned = jnp.logical_and(owner % nc == ic, within // SEGMENT == iz)
     column_of = jnp.where(owned, (owner // nc) * SEGMENT + within % SEGMENT, -1)[:, None]
-    e, stats = head_logits(rows, head_all, column_of)
+    so_far = ()
+    for block in range(nz):
+        part = jnp.concatenate(blocks[block * nc : (block + 1) * nc], axis=0)
+        so_far = head_logits(part, head_all, column_of, places, block, so_far)
+    e, stats = so_far
+    rows = jnp.concatenate(blocks, axis=0)
     top = stats[:, 0]
     every = share(("z", "c"), 4, stats.T.reshape(4, -1, LANES))[0].reshape(nz * nc, 4, group)
     best = jnp.max(every[:, 0], axis=0)
@@ -843,17 +889,19 @@
     loss_part = jnp.sum(own_terms)
     factors = jnp.stack([row_weights * jnp.exp(top - log_total),
                          row_weights * (jnp.exp(chosen - log_total) - 1.0)], axis=1)
-    d_logits, d_rows = head_rows_back(e, head_all, column_of, factors)
-    d_final = lax.psum_scatter(d_rows.astype(BF), ("z", "c"), scatter_dimension=0, tiled=True)
-
-    d_head = jnp.einsum("rd,yrv->ydv", rows, d_logits, preferred_element_type=F32)
-    d_head = d_head.reshape(ny * nx, -1, SEGMENT)
-    d_final, d_head = together(d_final, d_head)
+    d_logits, d_rows = head_rows_back(e, head_all, column_of, factors, places)
+    d_final = lax.psum_scatter(d_rows, ("z", "c"), scatter_dimension=0, tiled=True)
+
+    bound = D**0.5 * jnp.max(jnp.abs(gains[2])) * 1.02
+    bound = bound * score_count * jnp.sum(TSTEPS / (all_times.astype(F32) + 1.0) / total_rows)
+    enlarge = 60000.0 / jnp.maximum(bound, 1e-30)
+    d_head = jnp.einsum("rd,yrv->ydv", rows, d_logits, preferred_element_type=F32) * enlarge
+    d_final, d_head = together(d_final, d_head.reshape(ny, nx, nz, -1, SEGMENT))
+    cut = nz // 2
+    own_x, from_x = spread_parts(d_head[:, :, :cut], 1, "x")
+    own_y, from_y = spread_parts(d_head[:, :, cut:], 0, "y")
     d_final = d_final.astype(F32)
     d_final = jnp.swapaxes(d_final.reshape(score_count, nx, nz, -1), 1, 2).reshape(score_count, D)
-    block_for = lambda k: pick(d_head, lax.rem(k, ny) * nx + k // ny)
-    head_sums = exchange(lambda k: block_for(k).astype(BF), ("x", "y"))
-    head_own = block_for(head_sums[0][0])
 
     d_gain_f = jnp.sum(d_final * normed_f, axis=0)
     d_x2 = norm_back(d_final * gains[2:3], normed_f, inv_f)
@@ -872,10 +920,13 @@
     d_gate_a = jnp.sum(d_x1 * branch, axis=0)
     d_branch = (d_x1 * gate_a).astype(BF)
     d_wout = matmul_tn(att, d_branch)
-    d_att = matmul_nt(d_branch, w_o).astype(BF)
+    d_att, *from_xy = together(matmul_nt(d_branch, w_o).astype(BF), *from_x, *from_y)
+    own_xy, from_xy = (
+        spread_parts(added(own_x, from_xy[: nx - 1]), 0, "y"),
+        spread_parts(added(own_y, from_xy[nx - 1 :]), 0, "x"),
+    )
     d_k, d_v, d_qkv_m = attend_back(q, k_u, k_m, kv_u, qkv_m, tables, mask, lse_a, d_att)
-    arrivals = [piece for _, piece in head_sums[1:]]
-    d_k, *arrivals[:-1] = together(d_k, *arrivals[:-1])
+    d_k, *arrivals = together(d_k, *own_xy[1], *from_xy[1])
     d_kv = jnp.concatenate([d_k, d_v], axis=1)
     d_wkv = matmul_tn(a_u, d_kv)
     d_row_m = d_qkv_m[:3].reshape(3 * D)
@@ -899,16 +950,17 @@
     chip_sum = sum(piece.astype(F32) for _, piece in got).astype(BF)
     plane_sum = lax.psum_scatter(chip_sum, ("x", "y"), scatter_dimension=0, tiled=True)
 
-    sent, chip_sum, *head_pieces = together(
-        d_x0_u.astype(BF).T.reshape(nz * nx, table_width, free_count), chip_sum, *arrivals)
-    g_part = head_own
-    for piece in head_pieces:
-        g_part = g_part + piece.astype(F32)
-    g_part = g_part.reshape(nz, -1, SEGMENT)
-    sent, g_part = together(sent, g_part)
-    head_got = exchange(lambda k: pick(g_part, k), ("z",))
+    sent, chip_sum = together(
+        d_x0_u.astype(BF).T.reshape(nz * nx, table_width, free_count), chip_sum)
+    head_sum = jnp.concatenate(
+        [added(own_xy[0], arrivals[: ny - 1]), added(from_xy[0], arrivals[ny - 1 :])], axis=0)
+    sent, head_sum = together(sent, head_sum)
+    head_own, head_parts = spread_parts(head_sum, 0, "z")
 
     arrived = spread_blocks(sizes, sent, 5).reshape(n, table_width, free_count)
+    arrived, plane_sum, *head_parts = together(arrived, plane_sum, *head_parts)
+    plane_sum = plane_sum.reshape(nz, -1, width)
+    block_got = exchange(lambda k: pick(plane_sum, k), ("z",))
     g_embed = scatter_rows(arrived, local_ids, low, high, table_rows)
 
     small = jnp.concatenate([d_shift_a, d_scale_a, d_gate_a, d_shift_m, d_scale_m, d_gate_m,
@@ -917,6 +969,7 @@
     small = small.reshape(-1, LANES)
     count_small = small.shape[0]
     small = jnp.pad(small, ((0, -count_small % 8), (0, 0)))
+    small, g_embed, *block_parts = together(small, g_embed, *[p for _, p in block_got])
     small_all = share(ALL, 1, small)[0].reshape((n,) + small.shape)
     small_all = small_all[:, :count_small].reshape(n, -1)
     d_mod_all = small_all[:, : 6 * D]
@@ -931,18 +984,17 @@
                                       layer_w.shape[0], 1)
     g_outer = exact(a_rows, small_all[:, 11 * D : 14 * D])
 
-    plane_sum = plane_sum.reshape(nz, -1, width)
-    g_rest = sum(p.astype(F32) for _, p in exchange(lambda k: pick(plane_sum, k), ("z",)))
+    g_rest = sum(p.astype(F32) for p in block_parts)
     g_layer = jnp.concatenate(
         [g_outer[:, :D], g_outer[:, D:] + g_rest[:, : 2 * D], g_rest[:, 2 * D :]], axis=1)
 
     segments = []
     for k in range(nz):
-        segment = head_got[0][1]
-        for sender, piece in head_got[1:]:
-            segment = jnp.where(sender == k, piece, segment)
+        segment = head_own
+        for step, piece in enumerate(head_parts, 1):
+            segment = jnp.where(lax.rem(iz + nz - step, nz) == k, piece.astype(F32), segment)
         segments.append(segment)
-    g_head = jnp.concatenate(segments, axis=1)
+    g_head = jnp.concatenate(segments, axis=1) / enlarge
 
     squares = sum(jnp.sum(g * g) for g in (g_layer, g_ada, g_gains, g_embed, g_head))
     squares_all = share(ALL, 2, jnp.broadcast_to(squares, (8, LANES)))[0]

time: 1220 us -> 1030 us (0.84)
  waiting for transfers between devices: 347 us -> 114 us
  local copies, waits for them, and re-layouts: 77.2 us -> 103 us
    ppermute x13 -> x21, waiting for transfers between devices: 199 us -> 88.4 us  [exchange(): moved = lax.ppermute(piece, axes, [(i, (i + step) % n) for i in range(n)])]
    all_gather x1 -> x0, waiting for transfers between devices: 67 us -> none  [local(): rows = lax.all_gather(final_turned, ('z', 'c'), axis=0, tiled=True)]
    pallas_call x4, Pallas kernels: 146 us -> 92 us  [share(): pl.pallas_call(functools.partial(share_kernel, axes, sizes, count), out_s...]
    pallas_call x1, Pallas kernels: 42.5 us -> 85 us  [spread_blocks(): pl.pallas_call(functools.partial(spread_kernel, sizes), out_shape=jax.Sha...]
    all_gather x1, waiting for transfers between devices: 34.2 us -> 0.01 us  [local(): lax.all_gather(head_part, ('y', 'x'), axis=0, tiled=True)]
    unnamed x179 -> x270, local copies, waits for them, and re-layouts: 10 us -> 32.7 us
    reduce_scatter x1, waiting for transfers between devices: 19 us -> 2.84 us  [local(): lax.psum_scatter(d_rows, ('z', 'c'), scatter_dimension=0, tiled=True)]
    pallas_call x2 -> x5, Pallas kernels: 145 us -> 158 us  [the longest x4 101 us: head_logits(): pl.pallas_call(logits_kernel, out_shape=[jax.ShapeDtypeStruct((segments,...]
  transfers between devices with their start and end apart: 18 -> 25, of which waited for: 11 -> 9; matrix products, arithmetic and copies ran while one was open for 15% -> 21% of each run, Pallas kernels for 27% -> 29%
where the time goes in v4:
time: 1030 us; the launch traced here: 1020 us
  Pallas kernels  511 us (50%)
  other arithmetic  121 us (12%)
  matrix products  117 us (11%)
  waiting for transfers between devices  114 us (11%)
  local copies, waits for them, and re-layouts  103 us (10%)
  starting transfers between devices  30.1 us (3%)
  between operations  27.3 us (3%)
    pallas_call x4, Pallas kernels, head_logits(): pl.pallas_call(logits_kernel, out_shape=[jax.ShapeDtypeStruct((segments,...  101 us
    pallas_call x4, Pallas kernels, share(): pl.pallas_call(functools.partial(share_kernel, axes, sizes, count), out_s...  92 us
    ppermute x21, waiting for transfers between devices, exchange(): moved = lax.ppermute(piece, axes, [(i, (i + step) % n) for i in range(n)])  88.4 us
    pallas_call x1, Pallas kernels, spread_blocks(): pl.pallas_call(functools.partial(spread_kernel, sizes), out_shape=jax.Sha...  85 us
    dot_general x15, matrix products, dot(): lax.dot_general(a, b, ((contract[0], contract[1]), ((), ())), preferred_e...  64.8 us
    pallas_call x1, Pallas kernels, head_rows_back(): pl.pallas_call(rows_back_kernel, out_shape=[jax.ShapeDtypeStruct(e.shape,...  56.3 us
    pallas_call x1, Pallas kernels, fetch_blocks(): pl.pallas_call(functools.partial(fetch_kernel, sizes), out_shape=jax.Shap...  54 us
    dot_general x1, matrix products, local(): jnp.einsum('rd,yrv->ydv', rows, d_logits, preferred_element_type=F32)  50.2 us
  transfers between devices with their start and end apart: 25, of which 9 were waited for; matrix products, arithmetic and copies ran while one was open for 21% of the time, Pallas kernels for 29%

profile of v4, /device:TPU:0, one launch (start us, length us, event | category | flops | bytes accessed | tf_op | source)
XLA Modules:
  0.0 1024.6 jit_solution(11662720976070641532)
XLA Ops:
  17.5 17.9 %share0.1 = (s32[4,2,2,2,16,128]{5,4,3,2,1,0:T(8,128)}, f32[4,2,2,2,8,128]{5,4,3,2,1,0:T(8,128)}) custom-call(s32[16,128]{1,0:T(8,128)} %pad.18.refs_0_, f32[8,128]{1,0:T(8,128)} %pad_convert_fusion.refs_1_), custom_call_target="tpu_custom_call" | custom-call | tf_op jit(solution)/shard_map/share0/pallas_call | solution.py:104
  45.7 38.6 %gather_rows.1 = bf16[32,96,512]{2,1,0:T(8,128)(2,1)} custom-call(s32[32]{0:T(128)} %reduce_sum.397.low_ref, s32[32]{0:T(128)} %reduce_sum.399.high_ref, s32[32,512]{1,0:T(8,128)} %bitcast.262, f32[96,12800]{1,0:T(8,128)} %bitcast.234), custom_call_target="tpu_custom_call" | custom-call | bytes 134217728 | tf_op jit(solution)/shard_map/gather_rows/pallas_call | solution.py:343
  84.3 54.0 %fetch_blocks.1 = bf16[8,96,512]{2,1,0:T(8,128)(2,1)} custom-call(bf16[2,2,8,96,512]{4,3,2,1,0:T(8,128)(2,1)} %bitcast.238), custom_call_target="tpu_custom_call" | custom-call | bytes 134217728 | tf_op jit(solution)/shard_map/fetch_blocks/pallas_call | solution.py:194
  166.5 22.8 %all-gather.3.cloned.1.call-done = bf16[768,9984]{1,0:T(8,128)(2,1)} async-done(((bf16[24,9984]{1,0:T(8,128)(2,1)}), bf16[768,9984]{1,0:T(8,128)(2,1)}) %all-gather.3.cloned.1.call-update) | async-done | bytes 15335440 | tf_op jit(solution)/shard_map/all_gather | solution.py:806
  194.9 3.7 fusion.22.qm_ref.km_ref.vm_ref
  198.6 5.2 fusion.40.kv_ref.vv_ref
  204.4 18.5 %attend.1 = (bf16[512,768]{1,0:T(8,128)(2,1)}, bf16[512,768]{1,0:T(8,128)(2,1)}, bf16[512,768]{1,0:T(8,128)(2,1)}, bf16[512,768]{1,0:T(8,128)(2,1)}, f32[6,512,2]{2,1,0:T(8,128)}) custom-call(f32[512,1536]{1,0:T(8,128)} %fusion.40.kv_ref.vv_ref, f32[512,1536]{1,0:T(8,128)} %fusion.40.kv_ref.vv_ref, f32[16,2304]{1,0:T(8,128)} %fusion.22.qm_ref.km_ref.vm_ref, ...), custom_call_target="tpu_custom_call" | custom-call | flops 1207959552 | bytes 4718592 | tf_op jit(solution)/shard_map/attend/pallas_call | solution.py:474
  225.7 5.1 fusion.18
  230.9 10.2 fusion.110
  252.0 7.0 fusion.32.target_ref
  259.0 11.6 %collective-permute-done.7 = bf16[512,768]{1,0:T(8,128)(2,1)} collective-permute-done((bf16[512,768]{1,0:T(8,128)(2,1)S(1)}, bf16[512,768]{1,0:T(8,128)(2,1)}, u32[]{:S(2)}, u32[]{:S(2)}) %collective-permute-start.7) | collective-permute-done | bytes 786464 | tf_op jit(solution)/shard_map/ppermute | solution.py:280
  270.6 32.7 %collective-permute-done.5 = bf16[512,768]{1,0:T(8,128)(2,1)} collective-permute-done((bf16[512,768]{1,0:T(8,128)(2,1)S(1)}, bf16[512,768]{1,0:T(8,128)(2,1)}, u32[]{:S(2)}, u32[]{:S(2)}) %collective-permute-start.5) | collective-permute-done | bytes 786464 | tf_op jit(solution)/shard_map/ppermute | solution.py:280
  306.0 25.2 %head_logits.4 = (bf16[2,4096,3200]{2,1,0:T(8,128)(2,1)}, f32[4096,4]{1,0:T(8,128)}) custom-call(s32[8]{0:T(128)} %stack.46.places_ref, bf16[1024,768]{1,0:T(8,128)(2,1)} %pad_maximum_fusion.6.x_ref, bf16[2,768,3200]{2,1,0:T(8,128)(2,1)} %bitcast.214, s32[4096,1]{1,0:T(8,128)} %fusion.32.target_ref), custom_call_target="tpu_custom_call" | custom-call | flops 10066329600 | bytes 13107200 | tf_op jit(solution)/shard_map/head_logits/pallas_call | solution.py:620
  333.8 25.6 %head_logits.5 = (bf16[2,4096,3200]{2,1,0:T(8,128)(2,1)}, f32[4096,4]{1,0:T(8,128)}) custom-call(s32[8]{0:T(128)} %stack.46.places_ref, bf16[1024,768]{1,0:T(8,128)(2,1)} %pad_maximum_fusion.5.x_ref, bf16[2,768,3200]{2,1,0:T(8,128)(2,1)} %bitcast.215, s32[4096,1]{1,0:T(8,128)} %fusion.32.target_ref, ...), custom_call_target="tpu_custom_call", output_to_operand_aliasing={{0}: (4, {}), {1}: (5, {})} | custom-call | flops 10066329600 | bytes 13107200 | tf_op jit(solution)/shard_map/head_logits/pallas_call | solution.py:620
  362.1 25.3 %head_logits.6 = (bf16[2,4096,3200]{2,1,0:T(8,128)(2,1)}, f32[4096,4]{1,0:T(8,128)}) custom-call(s32[8]{0:T(128)} %stack.46.places_ref, bf16[1024,768]{1,0:T(8,128)(2,1)} %pad_maximum_fusion.4.x_ref, bf16[2,768,3200]{2,1,0:T(8,128)(2,1)} %bitcast.216, s32[4096,1]{1,0:T(8,128)} %fusion.32.target_ref, ...), custom_call_target="tpu_custom_call", output_to_operand_aliasing={{0}: (4, {}), {1}: (5, {})} | custom-call | flops 10066329600 | bytes 13107200 | tf_op jit(solution)/shard_map/head_logits/pallas_call | solution.py:620
  390.1 25.4 %head_logits.7 = (bf16[2,4096,3200]{2,1,0:T(8,128)(2,1)}, f32[4096,4]{1,0:T(8,128)}) custom-call(s32[8]{0:T(128)} %stack.46.places_ref, bf16[1024,768]{1,0:T(8,128)(2,1)} %pad_maximum_fusion.3.x_ref, bf16[2,768,3200]{2,1,0:T(8,128)(2,1)} %bitcast.217, s32[4096,1]{1,0:T(8,128)} %fusion.32.target_ref, ...), custom_call_target="tpu_custom_call", output_to_operand_aliasing={{0}: (4, {}), {1}: (5, {})} | custom-call | flops 10066329600 | bytes 13107200 | tf_op jit(solution)/shard_map/head_logits/pallas_call | solution.py:620
  418.3 26.4 %share4.1 = f32[4,2,4,32,128]{4,3,2,1,0:T(8,128)} custom-call(f32[4,32,128]{2,1,0:T(8,128)} %copy.295.refs_0_), custom_call_target="tpu_custom_call" | custom-call | tf_op jit(solution)/shard_map/share4/pallas_call | solution.py:104
  450.5 3.3 bitcast_multiply_fusion.1
  455.8 56.3 %head_rows_back.1 = (bf16[2,4096,3200]{2,1,0:T(8,128)(2,1)}, bf16[4096,768]{1,0:T(8,128)(2,1)}) custom-call(s32[8]{0:T(128)} %stack.46.places_ref, bf16[2,4096,3200]{2,1,0:T(8,128)(2,1)} %get-tuple-element.93.e_ref, bf16[2,768,3200]{2,1,0:T(8,128)(2,1)} %bitcast.218, s32[4096,1]{1,0:T(8,128)} %fusion.32.target_ref, ...), custom_call_target="tpu_custom_call", output_to_operand_aliasing={{0}: (1, {})} | custom-call | flops 40265318400 | bytes 104857600 | tf_op jit(solution)/shard_map/head_rows_back/pallas_call | solution.py:679
  528.3 50.2 %convolution_multiply_fusion = f32[2,3200,768]{1,2,0:T(8,128)} fusion(bf16[2,4096,3200]{2,1,0:T(8,128)(2,1)} %get-tuple-element.96, f32[]{:T(128)S(6)} %div.269, bf16[4096,768]{1,0:T(8,128)(2,1)} %constant_dynamic-update-slice_fusion), kind=kOutput, calls=%fused_computation | convolution fusion | flops 40270233600 | bytes 78381056 | tf_op jit(solution)/shard_map/rd,yrv->ydv/dot_general | solution.py:898
  581.3 7.7 fusion.111
  594.3 3.2 copy-done.3
  600.6 3.1 copy.284
  606.8 8.9 fusion.7
  615.8 6.5 multiply_reduce_fusion.5
  627.8 3.1 convolution_convert_fusion.4.datt_ref
  630.9 4.9 convolution_convert_fusion.1
  635.8 8.4 collective-permute-done.10
  644.2 6.6 collective-permute-done.11
  650.8 3.8 bitcast_add_fusion.2
  662.4 4.6 convolution_convert_fusion
  667.0 23.9 %attend_back.1 = (bf16[512,768]{1,0:T(8,128)(2,1)}, bf16[512,768]{1,0:T(8,128)(2,1)}, f32[8,768]{1,0:T(8,128)}) custom-call(bf16[512,768]{1,0:T(8,128)(2,1)} %get-tuple-element.78.q_ref, bf16[512,768]{1,0:T(8,128)(2,1)} %get-tuple-element.79.ku_ref, bf16[512,768]{1,0:T(8,128)(2,1)} %get-tuple-element.80.km_ref, f32[512,1536]{1,0:T(8,128)} %fusion.40.kv_ref.vv_ref, ...), custom_call_target="tpu_custom_call" | custom-call | flops 3221225472 | bytes 5505024 | tf_op jit(solution)/shard_map/attend_back/pallas_call | solution.py:546
  698.5 3.4 copy.293
  702.0 3.4 dynamic-slice_bitcast_fusion
  705.4 3.2 copy-done.1
  708.6 10.8 %collective-permute-done.14 = bf16[384,8448]{1,0:T(8,128)(2,1)} collective-permute-done((bf16[384,8448]{1,0:T(8,128)(2,1)}, bf16[384,8448]{1,0:T(8,128)(2,1)}, u32[]{:S(2)}, u32[]{:S(2)}) %collective-permute-start.14) | collective-permute-done | bytes 6488096 | tf_op jit(solution)/shard_map/ppermute | solution.py:280
  719.4 8.9 fusion
  731.4 3.1 fusion.45
  737.2 3.4 multiply_reduce_fusion.2
  757.0 85.0 %spread_blocks.1 = bf16[2,2,8,96,512]{4,3,2,1,0:T(8,128)(2,1)} custom-call(bf16[8,96,512]{2,1,0:T(8,128)(2,1)} %bitcast.253), custom_call_target="tpu_custom_call" | custom-call | bytes 134217728 | tf_op jit(solution)/shard_map/spread_blocks/pallas_call | solution.py:249
  842.1 41.5 %scatter_rows.1 = f32[96,12800]{1,0:T(8,128)} custom-call(s32[32]{0:T(128)} %reduce_sum.397.low_ref, s32[32]{0:T(128)} %reduce_sum.399.high_ref, s32[32,512]{1,0:T(8,128)} %bitcast.263, bf16[32,96,512]{2,1,0:T(8,128)(2,1)} %bitcast.237), custom_call_target="tpu_custom_call" | custom-call | bytes 134217728 | tf_op jit(solution)/shard_map/scatter_rows/pallas_call | solution.py:397
  884.5 4.8 collective-permute-start.18
  900.1 15.5 %collective-permute-done.19 = bf16[24,8448]{1,0:T(8,128)(2,1)S(1)} collective-permute-done((bf16[24,8448]{1,0:T(8,128)(2,1)S(1)}, bf16[24,8448]{1,0:T(8,128)(2,1)S(1)}, u32[]{:S(2)}, u32[]{:S(2)}) %collective-permute-start.19) | collective-permute-done | bytes 405536 | tf_op jit(solution)/shard_map/ppermute | solution.py:280
  917.2 35.1 %share1.1 = f32[4,2,2,2,88,128]{5,4,3,2,1,0:T(8,128)} custom-call(f32[88,128]{1,0:T(8,128)} %pad.22.refs_0_), custom_call_target="tpu_custom_call" | custom-call | tf_op jit(solution)/shard_map/share1/pallas_call | solution.py:104
  957.1 4.3 multiply_reduce_fusion.1
  968.1 12.5 %share2.1 = f32[4,2,2,2,8,128]{5,4,3,2,1,0:T(8,128)} custom-call(f32[8,128]{1,0:T(8,128)} %broadcast_in_dim.144.refs_0_), custom_call_target="tpu_custom_call" | custom-call | tf_op jit(solution)/shard_map/share2/pallas_call | solution.py:104
  982.9 15.9 %multiply_add_fusion = (f32[96,12800]{1,0:T(8,128)}, f32[96,12800]{1,0:T(8,128)}, f32[96,12800]{1,0:T(8,128)}, f32[96,12800]{1,0:T(8,128)}) fusion(f32[96,12800]{1,0:T(8,128)} %param.49, f32[]{:T(128)} %bitcast.90, f32[]{:T(128)S(6)} %sub.311, f32[96,12800]{1,0:T(8,128)} %param.46, f32[]{:T(128)} %bitcast.89, f32[]{:T(128)} %bitcast.88, f32[]{:T(128)S(6)} %min.13, ...), kind=kLoop, calls=%fused_computation.29 | loop fusion | flops 28262400 | bytes 44236824 | tf_op jit(solution)/shard_map/add | solution.py:755
  998.9 13.8 %fusion.11 = (f32[12800,96]{0,1:T(8,128)}, f32[96,12800]{1,0:T(8,128)}, f32[12800,96]{0,1:T(8,128)}, f32[12800,96]{0,1:T(8,128)}) fusion(f32[12800,96]{0,1:T(8,128)} %param.45, f32[]{:T(128)S(6)} %sub.311, f32[]{:T(128)} %bitcast.90, f32[]{:T(128)} %bitcast.89, f32[12800,96]{0,1:T(8,128)} %param.44, f32[]{:T(128)} %bitcast.88, f32[96,12800]{1,0:T(8,128)S(1)} %bitcast.224, ...), kind=kLoop, calls=%fused_computation.25 | loop fusion | flops 23347200 | bytes 44236820 | tf_op jit(solution)/shard_map/transpose | solution.py:1014
  (499 shorter events, 183.0 us)
Async XLA Ops:
  7.2 182.1 %all-gather.3.cloned.1.call-start = ((), (), s32[]{:S(2)}) async-start(), calls=%async_computation.2 | async-start | bytes 15814656 | tf_op jit(solution)/shard_map/all_gather | solution.py:806
  36.3 269.7 %all-gather.5.cloned.1.call-start = ((), (), s32[]{:S(2)}) async-start(), calls=%async_computation.3 | async-start | bytes 12288000 | tf_op jit(solution)/shard_map/all_gather | solution.py:860
  37.9 102.3 %collective-permute-start = (bf16[96,3200]{1,0:T(8,128)(2,1)}, bf16[96,3200]{1,0:T(8,128)(2,1)}, u32[]{:S(2)}, u32[]{:S(2)}) collective-permute-start(bf16[96,3200]{1,0:T(8,128)(2,1)} %get-tuple-element.192), channel_id=1, source_target_pairs={{0,8},{8,16},{16,24},{24,0},{1,9},{9,17},{17,25},{25,1},{2,10},{10... | collective-permute-start | bytes 1843208 | tf_op jit(solution)/shard_map/ppermute | solution.py:280
  39.1 101.1 %collective-permute-start.1 = (bf16[96,3200]{1,0:T(8,128)(2,1)}, bf16[96,3200]{1,0:T(8,128)(2,1)}, u32[]{:S(2)}, u32[]{:S(2)}) collective-permute-start(bf16[96,3200]{1,0:T(8,128)(2,1)} %get-tuple-element.191), channel_id=1, source_target_pairs={{0,16},{8,24},{16,0},{24,8},{1,17},{9,25},{17,1},{25,9},{2,18},{10... | collective-permute-start | bytes 1843208 | tf_op jit(solution)/shard_map/ppermute | solution.py:280
  41.8 98.5 %collective-permute-start.2 = (bf16[96,3200]{1,0:T(8,128)(2,1)}, bf16[96,3200]{1,0:T(8,128)(2,1)}, u32[]{:S(2)}, u32[]{:S(2)}) collective-permute-start(bf16[96,3200]{1,0:T(8,128)(2,1)} %get-tuple-element.190), channel_id=1, source_target_pairs={{0,24},{8,0},{16,8},{24,16},{1,25},{9,1},{17,9},{25,17},{2,26},{10... | collective-permute-start | bytes 1843208 | tf_op jit(solution)/shard_map/ppermute | solution.py:280
  140.2 58.5 %copy-start.4 = (f32[768,512]{0,1:T(8,128)}, f32[768,512]{0,1:T(8,128)S(1)}, u32[]{:S(2)}) copy-start(f32[768,512]{0,1:T(8,128)S(1)} %copy.250) | copy-start | bytes 4718596
  148.7 432.6 %reduce-scatter.3.cloned.1.call-start = ((), (), s32[]{:S(2)}) async-start(), calls=%async_computation.4 | async-start | bytes 7077888 | tf_op jit(solution)/shard_map/reduce_scatter | solution.py:893
  150.9 43.4 %copy-start.71 = (f32[1,768]{1,0:T(1,128)}, f32[1,768]{1,0:T(1,128)S(1)}, u32[]{:S(2)}) copy-start(f32[1,768]{1,0:T(1,128)S(1)} %slice.143) | copy-start | bytes 9220
  151.0 47.6 %copy-start.91 = (f32[768]{0:T(1024)}, f32[768]{0:T(1024)S(1)}, u32[]{:S(2)}) copy-start(f32[768]{0:T(1024)S(1)} %mul.857) | copy-start | bytes 9220
  151.2 74.5 %copy-start.89 = (f32[768]{0:T(1024)}, f32[768]{0:T(1024)S(1)}, u32[]{:S(2)}) copy-start(f32[768]{0:T(1024)S(1)} %mul.887) | copy-start | bytes 9220
  152.4 41.8 %copy-start.73 = (f32[1,768]{1,0:T(1,128)}, f32[1,768]{1,0:T(1,128)S(1)}, u32[]{:S(2)}) copy-start(f32[1,768]{1,0:T(1,128)S(1)} %mul.871) | copy-start | bytes 9220
  157.2 73.6 %copy-start.65 = (f32[768]{0:T(1024)}, f32[768]{0:T(1024)S(1)}, u32[]{:S(2)}) copy-start(f32[768]{0:T(1024)S(1)} %add.581) | copy-start | bytes 9220
  157.3 84.1 %copy-start.62 = (f32[768]{0:T(1024)}, f32[768]{0:T(1024)S(1)}, u32[]{:S(2)}) copy-start(f32[768]{0:T(1024)S(1)} %mul.905) | copy-start | bytes 9220
  166.2 32.4 %copy-start.78 = (f32[512]{0:T(512)}, f32[512]{0:T(512)S(1)}, u32[]{:S(2)}) copy-start(f32[512]{0:T(512)S(1)} %broadcast_multiply_fusion.8) | copy-start | bytes 6148
  166.5 32.1 %copy-start.94 = (f32[512]{0:T(512)}, f32[512]{0:T(512)S(1)}, u32[]{:S(2)}) copy-start(f32[512]{0:T(512)S(1)} %add_rsqrt_fusion.2) | copy-start | bytes 6148
  194.9 30.8 %copy-start.85 = (f32[768]{0:T(1024)}, f32[768]{0:T(1024)S(1)}, u32[]{:S(2)}) copy-start(f32[768]{0:T(1024)S(1)} %get-tuple-element.142) | copy-start | bytes 9220
  194.9 30.8 %copy-start.105 = (f32[768]{0:T(1024)}, f32[768]{0:T(1024)S(1)}, u32[]{:S(2)}) copy-start(f32[768]{0:T(1024)S(1)} %get-tuple-element.147) | copy-start | bytes 9220
  194.9 36.0 %copy-start.67 = (f32[768]{0:T(1024)}, f32[768]{0:T(1024)S(1)}, u32[]{:S(2)}) copy-start(f32[768]{0:T(1024)S(1)} %get-tuple-element.144) | copy-start | bytes 9220
  194.9 36.0 %copy-start.103 = (f32[768]{0:T(1024)}, f32[768]{0:T(1024)S(1)}, u32[]{:S(2)}) copy-start(f32[768]{0:T(1024)S(1)} %get-tuple-element.143) | copy-start | bytes 9220
  247.9 55.9 %collective-permute-start.9 = (bf16[512,768]{1,0:T(8,128)(2,1)S(1)}, bf16[512,768]{1,0:T(8,128)(2,1)S(1)}, u32[]{:S(2)}, u32[]{:S(2)}) collective-permute-start(bf16[512,768]{1,0:T(8,128)(2,1)S(1)} %copy.258), channel_id=1, source_target_pairs={{0,1},{1,0},{2,3},{3,2},{4,5},{5,4},{6,7},{7,6},{8,9},{9,8},{10,11... | collective-permute-start | bytes 2359304 | tf_op jit(solution)/shard_map/ppermute | solution.py:280
  248.2 22.4 %collective-permute-start.7 = (bf16[512,768]{1,0:T(8,128)(2,1)S(1)}, bf16[512,768]{1,0:T(8,128)(2,1)}, u32[]{:S(2)}, u32[]{:S(2)}) collective-permute-start(bf16[512,768]{1,0:T(8,128)(2,1)S(1)} %copy.258), channel_id=1, source_target_pairs={{0,8},{8,16},{16,24},{24,0},{1,9},{9,17},{17,25},{25,1},{2,10},{10... | collective-permute-start | bytes 2359304 | tf_op jit(solution)/shard_map/ppermute | solution.py:280
  248.2 55.1 %collective-permute-start.5 = (bf16[512,768]{1,0:T(8,128)(2,1)S(1)}, bf16[512,768]{1,0:T(8,128)(2,1)}, u32[]{:S(2)}, u32[]{:S(2)}) collective-permute-start(bf16[512,768]{1,0:T(8,128)(2,1)S(1)} %copy.258), channel_id=1, source_target_pairs={{0,16},{8,24},{16,0},{24,8},{1,17},{9,25},{17,1},{25,9},{2,18},{10... | collective-permute-start | bytes 2359304 | tf_op jit(solution)/shard_map/ppermute | solution.py:280
  249.4 53.9 %collective-permute-start.3 = (bf16[512,768]{1,0:T(8,128)(2,1)S(1)}, bf16[512,768]{1,0:T(8,128)(2,1)}, u32[]{:S(2)}, u32[]{:S(2)}) collective-permute-start(bf16[512,768]{1,0:T(8,128)(2,1)S(1)} %copy.258), channel_id=1, source_target_pairs={{0,24},{8,0},{16,8},{24,16},{1,25},{9,1},{17,9},{25,17},{2,26},{10... | collective-permute-start | bytes 2359304 | tf_op jit(solution)/shard_map/ppermute | solution.py:280
  270.6 60.5 %collective-permute-start.8 = (bf16[512,768]{1,0:T(8,128)(2,1)}, bf16[512,768]{1,0:T(8,128)(2,1)S(1)}, u32[]{:S(2)}, u32[]{:S(2)}) collective-permute-start(bf16[512,768]{1,0:T(8,128)(2,1)} %collective-permute-done.7), channel_id=1, source_target_pairs={{0,1},{1,0},{2,3},{3,2},{4,5},{5,4},{6,7},{7,6},{8,9},{9,8},{10,11... | collective-permute-start | bytes 2359304 | tf_op jit(solution)/shard_map/ppermute | solution.py:280
  303.3 56.1 %collective-permute-start.6 = (bf16[512,768]{1,0:T(8,128)(2,1)}, bf16[512,768]{1,0:T(8,128)(2,1)S(1)}, u32[]{:S(2)}, u32[]{:S(2)}) collective-permute-start(bf16[512,768]{1,0:T(8,128)(2,1)} %collective-permute-done.5), channel_id=1, source_target_pairs={{0,1},{1,0},{2,3},{3,2},{4,5},{5,4},{6,7},{7,6},{8,9},{9,8},{10,11... | collective-permute-start | bytes 2359304 | tf_op jit(solution)/shard_map/ppermute | solution.py:280
  303.3 84.1 %collective-permute-start.4 = (bf16[512,768]{1,0:T(8,128)(2,1)}, bf16[512,768]{1,0:T(8,128)(2,1)}, u32[]{:S(2)}, u32[]{:S(2)}) collective-permute-start(bf16[512,768]{1,0:T(8,128)(2,1)} %collective-permute-done.3), channel_id=1, source_target_pairs={{0,1},{1,0},{2,3},{3,2},{4,5},{5,4},{6,7},{7,6},{8,9},{9,8},{10,11... | collective-permute-start | bytes 2359304 | tf_op jit(solution)/shard_map/ppermute | solution.py:280
  331.2 28.2 %copy-start.27 = (bf16[512,768]{1,0:T(8,128)(2,1)}, bf16[512,768]{1,0:T(8,128)(2,1)S(1)}, u32[]{:S(2)}) copy-start(bf16[512,768]{1,0:T(8,128)(2,1)S(1)} %collective-permute-done.8) | copy-start | bytes 2359300
  359.4 28.0 %copy-start.29 = (bf16[512,768]{1,0:T(8,128)(2,1)}, bf16[512,768]{1,0:T(8,128)(2,1)S(1)}, u32[]{:S(2)}) copy-start(bf16[512,768]{1,0:T(8,128)(2,1)S(1)} %collective-permute-done.6) | copy-start | bytes 2359300
  512.1 329.9 %reduce-scatter.5.cloned.1.call-start = ((), (), s32[]{:S(2)}) async-start(), calls=%async_computation.5 | async-start | bytes 8110080 | tf_op jit(solution)/shard_map/reduce_scatter | solution.py:951
  590.9 53.3 %collective-permute-start.10 = (f16[2,2,96,3200]{3,2,1,0:T(8,128)(2,1)}, f16[2,2,96,3200]{3,2,1,0:T(8,128)(2,1)}, u32[]{:S(2)}, u32[]{:S(2)}) collective-permute-start(f16[2,2,96,3200]{3,2,1,0:T(8,128)(2,1)} %fusion.26), channel_id=1, source_target_pairs={{0,4},{4,0},{1,5},{5,1},{2,6},{6,2},{3,7},{7,3},{8,12},{12,8},{9,1... | collective-permute-start | bytes 7372808 | tf_op jit(solution)/shard_map/ppermute | solution.py:280
  597.5 53.3 %collective-permute-start.11 = (f16[2,2,96,3200]{3,2,1,0:T(8,128)(2,1)}, f16[2,2,96,3200]{3,2,1,0:T(8,128)(2,1)}, u32[]{:S(2)}, u32[]{:S(2)}) collective-permute-start(f16[2,2,96,3200]{3,2,1,0:T(8,128)(2,1)} %fusion.27), channel_id=1, source_target_pairs={{0,2},{2,0},{1,3},{3,1},{4,6},{6,4},{5,7},{7,5},{8,10},{10,8},{9,1... | collective-permute-start | bytes 7372808 | tf_op jit(solution)/shard_map/ppermute | solution.py:280
  606.7 15.6 %copy-start.17 = (f32[512,768]{1,0:T(8,128)}, f32[512,768]{1,0:T(8,128)S(1)}, u32[]{:S(2)}) copy-start(f32[512,768]{1,0:T(8,128)S(1)} %get-tuple-element.173) | copy-start | bytes 4718596
  630.9 26.4 %slice-start.2 = ((s8[9830400]{0:T(1024)(128)(4,1)}), s8[4194304]{0:T(1024)(128)(4,1)S(1)}, s32[]{:S(2)}) async-start(s8[9830400]{0:T(1024)(128)(4,1)} %bitcast.225), calls=%async_computation.8 | async-start | bytes 8388608
  630.9 26.4 %slice-start.3 = ((s8[9830400]{0:T(1024)(128)(4,1)}), s8[4194304]{0:T(1024)(128)(4,1)S(1)}, s32[]{:S(2)}) async-start(s8[9830400]{0:T(1024)(128)(4,1)} %bitcast.225), calls=%async_computation.9 | async-start | bytes 8388608
  635.8 21.5 %slice-start.4 = ((s8[9830400]{0:T(1024)(128)(4,1)}), s8[1441792]{0:T(1024)(128)(4,1)S(1)}, s32[]{:S(2)}) async-start(s8[9830400]{0:T(1024)(128)(4,1)} %bitcast.225), calls=%async_computation.10 | async-start | bytes 2883584
  655.9 35.1 %collective-permute-start.13 = (f16[2,96,3200]{2,1,0:T(8,128)(2,1)}, f16[2,96,3200]{2,1,0:T(8,128)(2,1)S(1)}, u32[]{:S(2)}, u32[]{:S(2)}) collective-permute-start(f16[2,96,3200]{2,1,0:T(8,128)(2,1)} %fusion.44), channel_id=1, source_target_pairs={{0,4},{4,0},{1,5},{5,1},{2,6},{6,2},{3,7},{7,3},{8,12},{12,8},{9,1... | collective-permute-start | bytes 3686408 | tf_op jit(solution)/shard_map/ppermute | solution.py:280
  660.9 30.1 %collective-permute-start.12 = (f16[2,96,3200]{2,1,0:T(8,128)(2,1)}, f16[2,96,3200]{2,1,0:T(8,128)(2,1)}, u32[]{:S(2)}, u32[]{:S(2)}) collective-permute-start(f16[2,96,3200]{2,1,0:T(8,128)(2,1)} %fusion.43), channel_id=1, source_target_pairs={{0,2},{2,0},{1,3},{3,1},{4,6},{6,4},{5,7},{7,5},{8,10},{10,8},{9,1... | collective-permute-start | bytes 3686408 | tf_op jit(solution)/shard_map/ppermute | solution.py:280
  708.6 10.8 %collective-permute-start.14 = (bf16[384,8448]{1,0:T(8,128)(2,1)}, bf16[384,8448]{1,0:T(8,128)(2,1)}, u32[]{:S(2)}, u32[]{:S(2)}) collective-permute-start(bf16[384,8448]{1,0:T(8,128)(2,1)} %dynamic-slice_bitcast_fusion), channel_id=1, source_target_pairs={{0,1},{1,0},{2,3},{3,2},{4,5},{5,4},{6,7},{7,6},{8,9},{9,8},{10,11... | collective-permute-start | bytes 19464200 | tf_op jit(solution)/shard_map/ppermute | solution.py:280
  749.9 92.1 %collective-permute-start.15 = (f16[96,3200]{1,0:T(8,128)(2,1)S(1)}, f16[96,3200]{1,0:T(8,128)(2,1)}, u32[]{:S(2)}, u32[]{:S(2)}) collective-permute-start(f16[96,3200]{1,0:T(8,128)(2,1)S(1)} %get-tuple-element.189), channel_id=1, source_target_pairs={{0,8},{8,16},{16,24},{24,0},{1,9},{9,17},{17,25},{25,1},{2,10},{10... | collective-permute-start | bytes 1843208 | tf_op jit(solution)/shard_map/ppermute | solution.py:280
  751.6 90.4 %collective-permute-start.16 = (f16[96,3200]{1,0:T(8,128)(2,1)S(1)}, f16[96,3200]{1,0:T(8,128)(2,1)}, u32[]{:S(2)}, u32[]{:S(2)}) collective-permute-start(f16[96,3200]{1,0:T(8,128)(2,1)S(1)} %get-tuple-element.188), channel_id=1, source_target_pairs={{0,16},{8,24},{16,0},{24,8},{1,17},{9,25},{17,1},{25,9},{2,18},{10... | collective-permute-start | bytes 1843208 | tf_op jit(solution)/shard_map/ppermute | solution.py:280
  753.3 88.8 %collective-permute-start.17 = (f16[96,3200]{1,0:T(8,128)(2,1)S(1)}, f16[96,3200]{1,0:T(8,128)(2,1)}, u32[]{:S(2)}, u32[]{:S(2)}) collective-permute-start(f16[96,3200]{1,0:T(8,128)(2,1)S(1)} %get-tuple-element.187), channel_id=1, source_target_pairs={{0,24},{8,0},{16,8},{24,16},{1,25},{9,1},{17,9},{25,17},{2,26},{10... | collective-permute-start | bytes 1843208 | tf_op jit(solution)/shard_map/ppermute | solution.py:280
  842.1 41.5 %copy-start.32 = (bf16[96,8448]{1,0:T(8,128)(2,1)S(1)}, bf16[96,8448]{1,0:T(8,128)(2,1)}, u32[]{:S(2)}) copy-start(bf16[96,8448]{1,0:T(8,128)(2,1)} %reduce-scatter.5.cloned.1.call-done) | copy-start | bytes 4866052
  884.5 15.7 %collective-permute-start.18 = (bf16[24,8448]{1,0:T(8,128)(2,1)S(1)}, bf16[24,8448]{1,0:T(8,128)(2,1)S(1)}, u32[]{:S(2)}, u32[]{:S(2)}) collective-permute-start(bf16[24,8448]{1,0:T(8,128)(2,1)S(1)} %get-tuple-element.198), channel_id=1, source_target_pairs={{0,8},{8,16},{16,24},{24,0},{1,9},{9,17},{17,25},{25,1},{2,10},{10... | collective-permute-start | bytes 1216520 | tf_op jit(solution)/shard_map/ppermute | solution.py:280
  889.2 26.4 %collective-permute-start.19 = (bf16[24,8448]{1,0:T(8,128)(2,1)S(1)}, bf16[24,8448]{1,0:T(8,128)(2,1)S(1)}, u32[]{:S(2)}, u32[]{:S(2)}) collective-permute-start(bf16[24,8448]{1,0:T(8,128)(2,1)S(1)} %get-tuple-element.197), channel_id=1, source_target_pairs={{0,16},{8,24},{16,0},{24,8},{1,17},{9,25},{17,1},{25,9},{2,18},{10... | collective-permute-start | bytes 1216520 | tf_op jit(solution)/shard_map/ppermute | solution.py:280
  890.3 25.4 %collective-permute-start.20 = (bf16[24,8448]{1,0:T(8,128)(2,1)S(1)}, bf16[24,8448]{1,0:T(8,128)(2,1)S(1)}, u32[]{:S(2)}, u32[]{:S(2)}) collective-permute-start(bf16[24,8448]{1,0:T(8,128)(2,1)S(1)} %get-tuple-element.196), channel_id=1, source_target_pairs={{0,24},{8,0},{16,8},{24,16},{1,25},{9,1},{17,9},{25,17},{2,26},{10... | collective-permute-start | bytes 1216520 | tf_op jit(solution)/shard_map/ppermute | solution.py:280
  917.2 37.4 %copy-start.33 = (bf16[24,8448]{1,0:T(8,128)(2,1)S(1)}, bf16[24,8448]{1,0:T(8,128)(2,1)}, u32[]{:S(2)}) copy-start(bf16[24,8448]{1,0:T(8,128)(2,1)} %get-tuple-element.114) | copy-start | bytes 1216516
  963.5 35.3 %slice-start = ((s8[4915200]{0:T(1024)(128)(4,1)}), s8[720896]{0:T(1024)(128)(4,1)S(1)}, s32[]{:S(2)}) async-start(s8[4915200]{0:T(1024)(128)(4,1)} %bitcast.223), calls=%async_computation.6 | async-start | bytes 1441792
  982.9 15.9 %slice-start.1 = ((s8[4915200]{0:T(1024)(128)(4,1)}), s8[4194304]{0:T(1024)(128)(4,1)S(1)}, s32[]{:S(2)}) async-start(s8[4915200]{0:T(1024)(128)(4,1)} %bitcast.223), calls=%async_computation.7 | async-start | bytes 8388608
  (102 other events, 566.3 us)
Sparse Core Ops, SparseCore 0:
  36.4 152.8 all-gather.2
  191.7 97.7 all-gather.4
  512.3 69.0 reduce-scatter.2
  728.5 80.1 reduce-scatter.4

commit v5 on v4

--- a/solution.py
+++ b/solution.py
@@ -213,55 +213,91 @@
     )(looked_up)
 
 
-def spread_kernel(sizes, in_ref, out_ref, sems_c, sems_y, sems_b):
+def spread_kernel(sizes, in_ref, small_ref, out_ref, all_ref, sems_c, sems_y, sems_b, sems_s, near):
     nz, nx, ny, nc = sizes
     blocks = nz * nx
-    iy, ic = lax.axis_index("y"), lax.axis_index("c")
+    index = tuple(lax.axis_index(a) for a in ALL)
+    iy, ic = index[2:]
     along_y = [d for _, _, d in neighbours(("y",), (ny,))]
     along_c = [d for _, _, d in neighbours(("c",), (nc,))]
     along_b = [block_peer(sizes, step)[2] for step in range(1, blocks)]
     meet(along_c + along_y + along_b)
     me = block_peer(sizes, 0)[0]
-    copies = []
+    peers = neighbours(ALL, sizes)
+
+    def small(place):
+        view = (slice(None),) * place + index[place:]
+        return [
+            remote(all_ref.at[view], all_ref.at[view], sems_s.at[0, i], sems_s.at[1, i], device)
+            for i, (at, _, device) in enumerate(peers)
+            if at == place
+        ]
+
+    def start(copies):
+        for copy in copies:
+            copy.start()
+        return copies
+
+    def wait(copies):
+        for copy in copies:
+            copy.wait()
+
+    own = pltpu.make_async_copy(small_ref, all_ref.at[index], near.at[0])
+    own.start()
+    own.wait()
+    along_z = start(small(0))
+    columns = []
     for step in range(1, blocks):
         _, peer, device = block_peer(sizes, step)
-        copies.append(
+        columns.append(
             remote(in_ref.at[peer], out_ref.at[iy, ic, me], sems_b.at[0, step],
                    sems_b.at[1, step], device)
         )
-    for copy in copies:
-        copy.start()
+    start(columns)
     out_ref[iy, ic, me] = in_ref[me]
-    for copy in copies:
-        copy.wait()
-    run_all([
+    wait(along_z)
+    along_x = start(small(1))
+    wait(along_x)
+    small_y = start(small(2))
+    wait(columns)
+    rows_y = start([
         remote(out_ref.at[iy, ic], out_ref.at[iy, ic], sems_y.at[0, i], sems_y.at[1, i], d)
         for i, d in enumerate(along_y)
     ])
-    run_all([
+    wait(small_y)
+    small_c = start(small(3))
+    wait(rows_y)
+    rows_c = start([
         remote(out_ref.at[:, ic], out_ref.at[:, ic], sems_c.at[0, i], sems_c.at[1, i], d)
         for i, d in enumerate(along_c)
     ])
-
-
-def spread_blocks(sizes, parts, collective_id):
+    wait(small_c)
+    wait(rows_c)
+
+
+def spread_blocks(sizes, parts, small, collective_id):
     nz, nx, ny, nc = sizes
     return pl.pallas_call(
         functools.partial(spread_kernel, sizes),
-        out_shape=jax.ShapeDtypeStruct((ny, nc) + parts.shape, parts.dtype),
-        in_specs=[pl.BlockSpec(memory_space=pltpu.VMEM)],
-        out_specs=pl.BlockSpec(memory_space=pltpu.VMEM),
+        out_shape=[
+            jax.ShapeDtypeStruct((ny, nc) + parts.shape, parts.dtype),
+            jax.ShapeDtypeStruct(sizes + small.shape, small.dtype),
+        ],
+        in_specs=[pl.BlockSpec(memory_space=pltpu.VMEM)] * 2,
+        out_specs=[pl.BlockSpec(memory_space=pltpu.VMEM)] * 2,
         scratch_shapes=[
             pltpu.SemaphoreType.DMA((2, nc - 1)),
             pltpu.SemaphoreType.DMA((2, ny - 1)),
             pltpu.SemaphoreType.DMA((2, nz * nx)),
+            pltpu.SemaphoreType.DMA((2, sum(sizes) - 4)),
+            pltpu.SemaphoreType.DMA((1,)),
         ],
         compiler_params=pltpu.CompilerParams(
             collective_id=collective_id, has_side_effects=True, vmem_limit_bytes=VMEM_LIMIT
         ),
         cost_estimate=pl.CostEstimate(flops=0, bytes_accessed=1 << 27, transcendentals=0),
         name="spread_blocks",
-    )(parts)
+    )(parts, small)
 
 
 def axis_place(axes):
@@ -361,12 +397,13 @@
     )(low, high, ids, table)
 
 
-def scatter_kernel(low_ref, high_ref, ids_ref, rows_ref, out_ref, total_ref, wide_ref):
+def scatter_kernel(low_ref, high_ref, ids_ref, rows_ref, out_ref, wide_ref, *totals):
     source = pl.program_id(0)
 
     @pl.when(source == 0)
     def _():
-        total_ref[...] = jnp.zeros_like(total_ref)
+        for total_ref in totals:
+            total_ref[...] = jnp.zeros_like(total_ref)
 
     low, high = low_ref[source], high_ref[source]
     wide_ref[...] = rows_ref[0].astype(F32).T
@@ -375,6 +412,7 @@
         base = pl.multiple_of(k * 8, 8)
         block = wide_ref[pl.ds(base, 8), :]
         for i in range(8):
+            total_ref = totals[i % len(totals)]
             place = base + i
             valid = jnp.logical_and(place >= low, place < high)
             row = jnp.where(valid, ids_ref[source, place], 0)
@@ -389,7 +427,10 @@
         @pl.loop(0, out_ref.shape[1] // LANES)
         def _(k):
             at = pl.multiple_of(k * LANES, LANES)
-            out_ref[:, pl.ds(at, LANES)] = total_ref[pl.ds(at, LANES), :].T
+            value = totals[0][pl.ds(at, LANES), :]
+            for total_ref in totals[1:]:
+                value = value + total_ref[pl.ds(at, LANES), :]
+            out_ref[:, pl.ds(at, LANES)] = value.T
 
 
 def scatter_rows(rows, ids, low, high, table_rows):
@@ -402,10 +443,8 @@
             grid=(sources,),
             in_specs=[pl.BlockSpec((1, width, count), lambda i, *_: (i, 0, 0))],
             out_specs=pl.BlockSpec((width, table_rows), lambda i, *_: (0, 0)),
-            scratch_shapes=[
-                pltpu.VMEM((table_rows, width), F32),
-                pltpu.VMEM((count, width), F32),
-            ],
+            scratch_shapes=[pltpu.VMEM((count, width), F32)]
+            + [pltpu.VMEM((table_rows, width), F32)] * 4,
         ),
         compiler_params=pltpu.CompilerParams(vmem_limit_bytes=VMEM_LIMIT),
         cost_estimate=pl.CostEstimate(flops=0, bytes_accessed=1 << 27, transcendentals=0),
@@ -574,54 +613,53 @@
     return max(16, 1024 // segments)
 
 
-def chunk_of(width):
-    return next(n for n in (640, 400, 128, width) if width % n == 0)
-
-
-def logits_kernel(places_ref, x_ref, w_ref, target_ref, *refs):
-    e_ref, stats_ref, logits_ref = refs[-3:]
+def logits_kernel(places_ref, x_ref, w_ref, target_ref, e_ref, stats_ref, logits_ref):
     segments, _, width = w_ref.shape
-    chunk = chunk_of(width)
     rows = x_ref.shape[0]
     x = x_ref[...]
-    spots = [(y, at) for y in range(segments) for at in range(0, width, chunk)]
+    starts = list(range(0, width - width % 768 or width, 768))
     best = None
-    for place, (y, at) in enumerate(spots):
-        logits = matmul(x, w_ref[y, :, at : at + chunk])
-        logits_ref[:, place * chunk : (place + 1) * chunk] = logits
-        best = logits if best is None else jnp.maximum(best, logits)
-    top = jnp.max(best, axis=1, keepdims=True)
-    lane = lax.broadcasted_iota(jnp.int32, (rows, chunk), 1)
-    total = jnp.zeros((rows, chunk), F32)
-    chosen = jnp.zeros((rows, chunk), F32)
-    target = target_ref[...]
-    for place, (y, at) in enumerate(spots):
-        logits = logits_ref[:, place * chunk : (place + 1) * chunk]
-        e = jnp.exp(logits - top)
-        total = total + e
-        chosen = chosen + jnp.where(lane == target - place * chunk, logits, 0.0)
-        e_ref[y, :, at : at + chunk] = e.astype(BF)
-    stats_ref[...] = jnp.concatenate(
-        [top, jnp.sum(total, axis=1, keepdims=True), jnp.sum(chosen, axis=1, keepdims=True), top],
-        axis=1,
-    )
-
-
-def head_logits(rows, weights, targets, places, block, so_far):
-    count, group = rows.shape[0], targets.shape[0]
+    for y in range(segments):
+        for at, end in zip(starts, starts[1:] + [width]):
+            logits = matmul(x, w_ref[y, :, at:end])
+            logits_ref[:, y * width + at : y * width + end] = logits
+            for g in range(0, end - at, LANES):
+                part = logits[:, g : g + LANES]
+                best = part if best is None else jnp.maximum(best, part)
+    lane = lax.broadcasted_iota(jnp.int32, (ROWS, LANES), 1)
+    peaks = jnp.max(best, axis=1, keepdims=True)
+    for r in range(0, rows, ROWS):
+        peak = peaks[r : r + ROWS]
+        top = jnp.broadcast_to(peak, (ROWS, LANES))
+        place = target_ref[r : r + ROWS, :] - lane
+        total = jnp.zeros((ROWS, LANES), F32)
+        chosen = jnp.zeros((ROWS, LANES), F32)
+        for y in range(segments):
+            for at in range(0, width, LANES):
+                column = y * width + at
+                logits = logits_ref[r : r + ROWS, column : column + LANES]
+                e = jnp.exp(logits - top)
+                total = total + e
+                chosen = chosen + jnp.where(place == column, logits, 0.0)
+                e_ref[y, r : r + ROWS, at : at + LANES] = e.astype(BF)
+        sums = [jnp.sum(a, axis=1, keepdims=True) for a in (total, chosen)]
+        stats_ref[r : r + ROWS, :] = jnp.concatenate([peak, *sums, peak], axis=1)
+
+
+def head_logits(rows, weights, targets, places):
+    count = rows.shape[0]
     segments, _, width = weights.shape
     tile = tile_of(segments)
-    per = group // places.shape[0] // tile
-    first = block * (count // tile)
-
-    def place(i, places):
-        return places[(first + i) // per] * per + lax.rem(first + i, per)
+    per = count // places.shape[0] // tile
+
+    def placed(i, places):
+        return (places[i // per] * per + lax.rem(i, per), 0)
 
     return pl.pallas_call(
         logits_kernel,
         out_shape=[
-            jax.ShapeDtypeStruct((segments, group, width), BF),
-            jax.ShapeDtypeStruct((group, 4), F32),
+            jax.ShapeDtypeStruct((segments, count, width), BF),
+            jax.ShapeDtypeStruct((count, 4), F32),
         ],
         grid_spec=pltpu.PrefetchScalarGridSpec(
             num_scalar_prefetch=1,
@@ -629,15 +667,14 @@
             in_specs=[
                 pl.BlockSpec((tile, D), lambda i, p: (i, 0)),
                 pl.BlockSpec(weights.shape, lambda i, p: (0, 0, 0), pipeline_mode=pl.Buffered(1)),
-                pl.BlockSpec((tile, 1), lambda i, p: (place(i, p), 0)),
-            ] + [pl.BlockSpec(memory_space=pl.ANY)] * len(so_far),
+                pl.BlockSpec((tile, 1), placed),
+            ],
             out_specs=[
-                pl.BlockSpec((segments, tile, width), lambda i, p: (0, first + i, 0)),
-                pl.BlockSpec((tile, 4), lambda i, p: (place(i, p), 0)),
+                pl.BlockSpec((segments, tile, width), lambda i, p: (0, i, 0)),
+                pl.BlockSpec((tile, 4), placed),
             ],
             scratch_shapes=[pltpu.VMEM((tile, segments * width), F32)],
         ),
-        input_output_aliases={4 + i: i for i in range(len(so_far))},
         compiler_params=pltpu.CompilerParams(vmem_limit_bytes=VMEM_LIMIT),
         cost_estimate=pl.CostEstimate(
             flops=2 * count * D * segments * width,
@@ -645,7 +682,7 @@
             transcendentals=count * segments * width,
         ),
         name="head_logits",
-    )(places, rows, weights, targets, *so_far)
+    )(places, rows, weights, targets)
 
 
 def rows_back_kernel(places_ref, e_ref, w_ref, target_ref, factor_ref, d_ref, dx_ref):
@@ -873,12 +910,8 @@
     owner, within = row_targets // table_rows, row_targets % table_rows
     owned = jnp.logical_and(owner % nc == ic, within // SEGMENT == iz)
     column_of = jnp.where(owned, (owner // nc) * SEGMENT + within % SEGMENT, -1)[:, None]
-    so_far = ()
-    for block in range(nz):
-        part = jnp.concatenate(blocks[block * nc : (block + 1) * nc], axis=0)
-        so_far = head_logits(part, head_all, column_of, places, block, so_far)
-    e, stats = so_far
     rows = jnp.concatenate(blocks, axis=0)
+    e, stats = head_logits(rows, head_all, column_of, places)
     top = stats[:, 0]
     every = share(("z", "c"), 4, stats.T.reshape(4, -1, LANES))[0].reshape(nz * nc, 4, group)
     best = jnp.max(every[:, 0], axis=0)
@@ -921,10 +954,21 @@
     d_branch = (d_x1 * gate_a).astype(BF)
     d_wout = matmul_tn(att, d_branch)
     d_att, *from_xy = together(matmul_nt(d_branch, w_o).astype(BF), *from_x, *from_y)
+    def over_cores(gradient):
+        width = gradient.shape[1]
+        parts = jnp.transpose(gradient.reshape(nz, nx, ny, nc, -1, width), (3, 1, 2, 0, 4, 5))
+        parts = parts.reshape(nc, -1, width)
+        got = exchange(lambda k: pick(parts, k), ("c",))
+        return sum(piece.astype(F32) for _, piece in got).astype(BF)
+
+    over_plane = lambda a: lax.psum_scatter(a, ("x", "y"), scatter_dimension=0, tiled=True)
     own_xy, from_xy = (
         spread_parts(added(own_x, from_xy[: nx - 1]), 0, "y"),
         spread_parts(added(own_y, from_xy[nx - 1 :]), 0, "x"),
     )
+    mlp_sum = over_cores(jnp.concatenate([d_up.astype(BF), d_down.astype(BF)], axis=1))
+    d_att, mlp_sum = together(d_att, mlp_sum)
+    mlp_sum = over_plane(mlp_sum)
     d_k, d_v, d_qkv_m = attend_back(q, k_u, k_m, kv_u, qkv_m, tables, mask, lse_a, d_att)
     d_k, *arrivals = together(d_k, *own_xy[1], *from_xy[1])
     d_kv = jnp.concatenate([d_k, d_v], axis=1)
@@ -941,27 +985,7 @@
     d_x0_u = norm_back(d_a_u * scaling, normed_u, inv_u)
     d_mask = jnp.sum(d_x1, axis=0) + norm_back(d_a_m * scaling, normed_0, inv_0)[0]
 
-    d_block = jnp.concatenate(
-        [d_wkv.astype(BF), d_wout.astype(BF), d_up.astype(BF), d_down.astype(BF)], axis=1)
-    width = d_block.shape[1]
-    d_block = jnp.transpose(d_block.reshape(nz, nx, ny, nc, -1, width), (3, 1, 2, 0, 4, 5))
-    d_block = d_block.reshape(nc, -1, width)
-    got = exchange(lambda k: pick(d_block, k), ("c",))
-    chip_sum = sum(piece.astype(F32) for _, piece in got).astype(BF)
-    plane_sum = lax.psum_scatter(chip_sum, ("x", "y"), scatter_dimension=0, tiled=True)
-
-    sent, chip_sum = together(
-        d_x0_u.astype(BF).T.reshape(nz * nx, table_width, free_count), chip_sum)
-    head_sum = jnp.concatenate(
-        [added(own_xy[0], arrivals[: ny - 1]), added(from_xy[0], arrivals[ny - 1 :])], axis=0)
-    sent, head_sum = together(sent, head_sum)
-    head_own, head_parts = spread_parts(head_sum, 0, "z")
-
-    arrived = spread_blocks(sizes, sent, 5).reshape(n, table_width, free_count)
-    arrived, plane_sum, *head_parts = together(arrived, plane_sum, *head_parts)
-    plane_sum = plane_sum.reshape(nz, -1, width)
-    block_got = exchange(lambda k: pick(plane_sum, k), ("z",))
-    g_embed = scatter_rows(arrived, local_ids, low, high, table_rows)
+    rest_sum = over_cores(jnp.concatenate([d_wkv.astype(BF), d_wout.astype(BF)], axis=1))
 
     small = jnp.concatenate([d_shift_a, d_scale_a, d_gate_a, d_shift_m, d_scale_m, d_gate_m,
                              d_gain_a, d_gain_m, d_gain_f, d_mask,
@@ -969,8 +993,27 @@
     small = small.reshape(-1, LANES)
     count_small = small.shape[0]
     small = jnp.pad(small, ((0, -count_small % 8), (0, 0)))
-    small, g_embed, *block_parts = together(small, g_embed, *[p for _, p in block_got])
-    small_all = share(ALL, 1, small)[0].reshape((n,) + small.shape)
+
+    sent, rest_sum = together(
+        d_x0_u.astype(BF).T.reshape(nz * nx, table_width, free_count), rest_sum)
+    rest_sum, mlp_sum = together(rest_sum, mlp_sum)
+    rest_sum = over_plane(rest_sum)
+    head_sum = jnp.concatenate(
+        [added(own_xy[0], arrivals[: ny - 1]), added(from_xy[0], arrivals[ny - 1 :])], axis=0)
+    sent, head_sum = together(sent, head_sum)
+    head_own, head_parts = spread_parts(head_sum, 0, "z")
+
+    arrived, small_all = spread_blocks(sizes, sent, small, 5)
+    arrived, mlp_sum, rest_sum, *head_parts = together(arrived, mlp_sum, rest_sum, *head_parts)
+    plane_sum = jnp.concatenate([rest_sum, mlp_sum], axis=1)
+    plane_sum = plane_sum.reshape(nz, -1, plane_sum.shape[1])
+    block_parts = [p for _, p in exchange(lambda k: pick(plane_sum, k), ("z",))]
+    g_embed = scatter_rows(arrived.reshape(n, table_width, free_count), local_ids, low, high,
+                           table_rows)
+    together_now = together(g_embed, small_all, head_own, *head_parts, *block_parts)
+    g_embed, small_all, head_own = together_now[:3]
+    head_parts, block_parts = together_now[3 : 2 + nz], together_now[2 + nz :]
+    small_all = small_all.reshape((n,) + small.shape)
     small_all = small_all[:, :count_small].reshape(n, -1)
     d_mod_all = small_all[:, : 6 * D]
     d_gains = jnp.sum(small_all[:, 6 * D : 10 * D], axis=0).reshape(4, D)

time: 1030 us -> 1030 us (level)
  Pallas kernels: 511 us -> 457 us
  waiting for transfers between devices: 114 us -> 155 us
  other arithmetic: 121 us -> 134 us
    pallas_call x4 -> x3, Pallas kernels: 92 us -> 51 us  [share(): pl.pallas_call(functools.partial(share_kernel, axes, sizes, count), out_s...]
    pallas_call x4 -> x1, Pallas kernels: 101 us -> 70.3 us  [head_logits(): pl.pallas_call(logits_kernel, out_shape=[jax.ShapeDtypeStruct((segments,...]
    ppermute x21 -> x22, waiting for transfers between devices: 88.4 us -> 116 us  [exchange(): moved = lax.ppermute(piece, axes, [(i, (i + step) % n) for i in range(n)])]
    pallas_call x1, Pallas kernels: 85 us -> 102 us  [spread_blocks(): pl.pallas_call(functools.partial(spread_kernel, sizes), out_shape=[jax.Sh...]
    reduce_scatter x1, waiting for transfers between devices: 2.84 us -> 16.1 us  [local(): lax.psum_scatter(d_rows, ('z', 'c'), scatter_dimension=0, tiled=True)]
    ppermute x21 -> x22, starting transfers between devices: 29.8 us -> 23.2 us  [exchange(): moved = lax.ppermute(piece, axes, [(i, (i + step) % n) for i in range(n)])]
    unnamed x270 -> x224, local copies, waits for them, and re-layouts: 32.7 us -> 34 us
  transfers between devices with their start and end apart: 25 -> 27, of which waited for: 9 -> 7; matrix products, arithmetic and copies ran while one was open for 21% -> 22% of each run, Pallas kernels for 29% -> 27%
where the time goes in v5:
time: 1030 us
  Pallas kernels  457 us (44%)
  waiting for transfers between devices  155 us (15%)
  other arithmetic  134 us (13%)
  matrix products  117 us (11%)
  local copies, waits for them, and re-layouts  113 us (11%)
  between operations  27.4 us (3%)
  starting transfers between devices  23.6 us (2%)
    ppermute x22, waiting for transfers between devices, exchange(): moved = lax.ppermute(piece, axes, [(i, (i + step) % n) for i in range(n)])  116 us
    pallas_call x1, Pallas kernels, spread_blocks(): pl.pallas_call(functools.partial(spread_kernel, sizes), out_shape=[jax.Sh...  102 us
    pallas_call x1, Pallas kernels, head_logits(): pl.pallas_call(logits_kernel, out_shape=[jax.ShapeDtypeStruct((segments,...  70.3 us
    dot_general x15, matrix products, dot(): lax.dot_general(a, b, ((contract[0], contract[1]), ((), ())), preferred_e...  63.3 us
    pallas_call x1, Pallas kernels, fetch_blocks(): pl.pallas_call(functools.partial(fetch_kernel, sizes), out_shape=jax.Shap...  56.9 us
    pallas_call x1, Pallas kernels, head_rows_back(): pl.pallas_call(rows_back_kernel, out_shape=[jax.ShapeDtypeStruct(e.shape,...  55.9 us
    dot_general x1, matrix products, local(): jnp.einsum('rd,yrv->ydv', rows, d_logits, preferred_element_type=F32)  51.2 us
    pallas_call x3, Pallas kernels, share(): pl.pallas_call(functools.partial(share_kernel, axes, sizes, count), out_s...  51 us
  transfers between devices with their start and end apart: 27, of which 7 were waited for; matrix products, arithmetic and copies ran while one was open for 22% of the time, Pallas kernels for 27%

profile of v5, /device:TPU:0, one launch (start us, length us, event | category | flops | bytes accessed | tf_op | source)
XLA Modules:
  0.0 1027.5 jit_solution(16506115137878952840)
XLA Ops:
  19.5 18.0 %share0.1 = (s32[4,2,2,2,16,128]{5,4,3,2,1,0:T(8,128)}, f32[4,2,2,2,8,128]{5,4,3,2,1,0:T(8,128)}) custom-call(s32[16,128]{1,0:T(8,128)} %pad.18.refs_0_, f32[8,128]{1,0:T(8,128)} %pad_convert_fusion.refs_1_), custom_call_target="tpu_custom_call" | custom-call | tf_op jit(solution)/shard_map/share0/pallas_call | solution.py:104
  39.9 3.3 collective-permute-start.2
  46.8 37.4 %gather_rows.1 = bf16[32,96,512]{2,1,0:T(8,128)(2,1)} custom-call(s32[32]{0:T(128)} %reduce_sum.397.low_ref, s32[32]{0:T(128)} %reduce_sum.399.high_ref, s32[32,512]{1,0:T(8,128)} %bitcast.266, f32[96,12800]{1,0:T(8,128)} %bitcast.236), custom_call_target="tpu_custom_call" | custom-call | bytes 134217728 | tf_op jit(solution)/shard_map/gather_rows/pallas_call | solution.py:379
  84.2 56.9 %fetch_blocks.1 = bf16[8,96,512]{2,1,0:T(8,128)(2,1)} custom-call(bf16[2,2,8,96,512]{4,3,2,1,0:T(8,128)(2,1)} %bitcast.244), custom_call_target="tpu_custom_call" | custom-call | bytes 134217728 | tf_op jit(solution)/shard_map/fetch_blocks/pallas_call | solution.py:194
  165.3 22.7 %all-gather.3.cloned.1.call-done = bf16[768,9984]{1,0:T(8,128)(2,1)} async-done(((bf16[24,9984]{1,0:T(8,128)(2,1)}), bf16[768,9984]{1,0:T(8,128)(2,1)}) %all-gather.3.cloned.1.call-update) | async-done | bytes 15335440 | tf_op jit(solution)/shard_map/all_gather | solution.py:843
  193.7 3.3 fusion.23.qm_ref.km_ref.vm_ref
  197.0 5.3 fusion.41.kv_ref.vv_ref
  202.9 18.7 %attend.1 = (bf16[512,768]{1,0:T(8,128)(2,1)}, bf16[512,768]{1,0:T(8,128)(2,1)}, bf16[512,768]{1,0:T(8,128)(2,1)}, bf16[512,768]{1,0:T(8,128)(2,1)}, f32[6,512,2]{2,1,0:T(8,128)}) custom-call(f32[512,1536]{1,0:T(8,128)} %fusion.41.kv_ref.vv_ref, f32[512,1536]{1,0:T(8,128)} %fusion.41.kv_ref.vv_ref, f32[16,2304]{1,0:T(8,128)} %fusion.23.qm_ref.km_ref.vm_ref, ...), custom_call_target="tpu_custom_call" | custom-call | flops 1207959552 | bytes 4718592 | tf_op jit(solution)/shard_map/attend/pallas_call | solution.py:513
  224.4 5.3 fusion.18
  229.8 9.6 fusion.110
  246.2 3.6 collective-permute-start.8
  250.5 7.0 fusion.33.target_ref
  258.8 42.9 %collective-permute-done.4 = bf16[512,768]{1,0:T(8,128)(2,1)} collective-permute-done((bf16[512,768]{1,0:T(8,128)(2,1)S(1)}, bf16[512,768]{1,0:T(8,128)(2,1)}, u32[]{:S(2)}, u32[]{:S(2)}) %collective-permute-start.4) | collective-permute-done | bytes 786464 | tf_op jit(solution)/shard_map/ppermute | solution.py:316
  301.9 13.1 %collective-permute-done.6 = bf16[512,768]{1,0:T(8,128)(2,1)} collective-permute-done((bf16[512,768]{1,0:T(8,128)(2,1)S(1)}, bf16[512,768]{1,0:T(8,128)(2,1)}, u32[]{:S(2)}, u32[]{:S(2)}) %collective-permute-start.6) | collective-permute-done | bytes 786464 | tf_op jit(solution)/shard_map/ppermute | solution.py:316
  331.9 70.3 %head_logits.1 = (bf16[2,4096,3200]{2,1,0:T(8,128)(2,1)}, f32[4096,4]{1,0:T(8,128)}) custom-call(s32[8]{0:T(128)} %stack.46.places_ref, bf16[4096,768]{1,0:T(8,128)(2,1)} %constant_dynamic-update-slice_fusion.x_ref, bf16[2,768,3200]{2,1,0:T(8,128)(2,1)} %bitcast.290, s32[4096,1]{1,0:T(8,128)} %fusion.33.target_ref), custom_call_target="tpu_custom_call" | custom-call | flops 40265318400 | bytes 52428800 | tf_op jit(solution)/shard_map/head_logits/pallas_call | solution.py:658
  402.2 2.8 copy.283.refs_0_
  405.0 14.8 %share4.1 = f32[4,2,4,32,128]{4,3,2,1,0:T(8,128)} custom-call(f32[4,32,128]{2,1,0:T(8,128)} %copy.283.refs_0_), custom_call_target="tpu_custom_call" | custom-call | tf_op jit(solution)/shard_map/share4/pallas_call | solution.py:104
  425.7 3.3 bitcast_multiply_fusion.1
  430.9 55.9 %head_rows_back.1 = (bf16[2,4096,3200]{2,1,0:T(8,128)(2,1)}, bf16[4096,768]{1,0:T(8,128)(2,1)}) custom-call(s32[8]{0:T(128)} %stack.46.places_ref, bf16[2,4096,3200]{2,1,0:T(8,128)(2,1)} %get-tuple-element.93.e_ref, bf16[2,768,3200]{2,1,0:T(8,128)(2,1)} %bitcast.291, s32[4096,1]{1,0:T(8,128)} %fusion.33.target_ref, ...), custom_call_target="tpu_custom_call", output_to_operand_aliasing={{0}: (1, {})} | custom-call | flops 40265318400 | bytes 104857600 | tf_op jit(solution)/shard_map/head_rows_back/pallas_call | solution.py:716
  490.2 51.2 %convolution_multiply_fusion = f32[2,3200,768]{1,2,0:T(8,128)} fusion(bf16[2,4096,3200]{2,1,0:T(8,128)(2,1)} %get-tuple-element.96, f32[]{:T(128)S(6)} %div.269, bf16[4096,768]{1,0:T(8,128)(2,1)} %constant_dynamic-update-slice_fusion.x_ref), kind=kOutput, calls=%fused_computation | convolution fusion | flops 40270233600 | bytes 78381056 | tf_op jit(solution)/shard_map/rd,yrv->ydv/dot_general | solution.py:931
  541.4 16.1 %reduce-scatter.4.cloned.1.call-done = bf16[512,768]{1,0:T(8,128)(2,1)} async-done(((bf16[4096,768]{1,0:T(8,128)(2,1)}), bf16[512,768]{1,0:T(8,128)(2,1)}) %reduce-scatter.4.cloned.1.call-update) | async-done | bytes 786448 | tf_op jit(solution)/shard_map/reduce_scatter | solution.py:926
  565.0 6.4 convolution_convert_fusion
  571.5 7.7 fusion.7
  579.3 3.3 convolution_convert_fusion.1
  582.6 4.0 pad_maximum_fusion
  586.6 8.5 copy.273
  595.1 5.1 dynamic-slice_bitcast_fusion
  600.2 7.7 fusion.111
  617.5 7.1 multiply_reduce_fusion.4
  626.0 3.2 convolution_convert_fusion.4.datt_ref
  629.2 36.7 %collective-permute-done.10 = f16[2,2,96,3200]{3,2,1,0:T(8,128)(2,1)} collective-permute-done((f16[2,2,96,3200]{3,2,1,0:T(8,128)(2,1)}, f16[2,2,96,3200]{3,2,1,0:T(8,128)(2,1)}, u32[]{:S(2)}, u32[]{:S(2)}) %collective-permute-start.10) | collective-permute-done | bytes 2457632 | tf_op jit(solution)/shard_map/ppermute | solution.py:316
  665.9 6.2 collective-permute-done.11
  672.2 4.6 bitcast_add_fusion.3
  676.8 6.3 fusion
  683.2 2.9 fusion.44
  686.0 4.4 bitcast_add_fusion.2
  698.8 24.1 %attend_back.1 = (bf16[512,768]{1,0:T(8,128)(2,1)}, bf16[512,768]{1,0:T(8,128)(2,1)}, f32[8,768]{1,0:T(8,128)}) custom-call(bf16[512,768]{1,0:T(8,128)(2,1)} %get-tuple-element.84.q_ref, bf16[512,768]{1,0:T(8,128)(2,1)} %get-tuple-element.85.ku_ref, bf16[512,768]{1,0:T(8,128)(2,1)} %get-tuple-element.86.km_ref, f32[512,1536]{1,0:T(8,128)} %fusion.41.kv_ref.vv_ref, ...), custom_call_target="tpu_custom_call" | custom-call | flops 3221225472 | bytes 5505024 | tf_op jit(solution)/shard_map/attend_back/pallas_call | solution.py:585
  724.4 17.4 %collective-permute-done.14 = f16[2,96,3200]{2,1,0:T(8,128)(2,1)} collective-permute-done((f16[2,96,3200]{2,1,0:T(8,128)(2,1)}, f16[2,96,3200]{2,1,0:T(8,128)(2,1)}, u32[]{:S(2)}, u32[]{:S(2)}) %collective-permute-start.14) | collective-permute-done | bytes 1228832 | tf_op jit(solution)/shard_map/ppermute | solution.py:316
  747.8 4.1 multiply_reduce_fusion.6
  751.9 3.1 fusion.46
  775.6 3.1 fusion.20
  785.5 3.3 collective-permute-start.18
  791.2 101.6 %spread_blocks.1 = (bf16[2,2,8,96,512]{4,3,2,1,0:T(8,128)(2,1)}, f32[4,2,2,2,88,128]{5,4,3,2,1,0:T(8,128)}) custom-call(bf16[8,96,512]{2,1,0:T(8,128)(2,1)} %bitcast.255, f32[88,128]{1,0:T(8,128)} %pad.22.small_ref), custom_call_target="tpu_custom_call" | custom-call | bytes 134217728 | tf_op jit(solution)/shard_map/spread_blocks/pallas_call | solution.py:280
  900.4 41.4 %scatter_rows.1 = f32[96,12800]{1,0:T(8,128)} custom-call(s32[32]{0:T(128)} %reduce_sum.397.low_ref, s32[32]{0:T(128)} %reduce_sum.399.high_ref, s32[32,512]{1,0:T(8,128)} %bitcast.267, bf16[32,96,512]{2,1,0:T(8,128)(2,1)} %bitcast.254), custom_call_target="tpu_custom_call" | custom-call | bytes 134217728 | tf_op jit(solution)/shard_map/scatter_rows/pallas_call | solution.py:438
  962.0 18.2 %share2.1 = f32[4,2,2,2,8,128]{5,4,3,2,1,0:T(8,128)} custom-call(f32[8,128]{1,0:T(8,128)} %broadcast_in_dim.144.refs_0_), custom_call_target="tpu_custom_call" | custom-call | tf_op jit(solution)/shard_map/share2/pallas_call | solution.py:104
  983.9 4.4 multiply_add_fusion.5
  988.3 16.5 %multiply_add_fusion = (f32[96,12800]{1,0:T(8,128)}, f32[96,12800]{1,0:T(8,128)}, f32[96,12800]{1,0:T(8,128)}, f32[96,12800]{1,0:T(8,128)}) fusion(f32[96,12800]{1,0:T(8,128)} %param.49, f32[]{:T(128)} %bitcast.96, f32[]{:T(128)S(6)} %sub.311, f32[96,12800]{1,0:T(8,128)} %param.46, f32[]{:T(128)} %bitcast.95, f32[]{:T(128)} %bitcast.94, f32[]{:T(128)S(6)} %min.13, ...), kind=kLoop, calls=%fused_computation.28 | loop fusion | flops 28262400 | bytes 44236824 | tf_op jit(solution)/shard_map/add | solution.py:792
  1004.9 13.6 %fusion.11 = (f32[12800,96]{0,1:T(8,128)}, f32[96,12800]{1,0:T(8,128)}, f32[12800,96]{0,1:T(8,128)}, f32[12800,96]{0,1:T(8,128)}) fusion(f32[12800,96]{0,1:T(8,128)} %param.45, f32[]{:T(128)S(6)} %sub.311, f32[]{:T(128)} %bitcast.96, f32[]{:T(128)} %bitcast.95, f32[12800,96]{0,1:T(8,128)} %param.44, f32[]{:T(128)} %bitcast.94, f32[96,12800]{1,0:T(8,128)S(1)} %bitcast.221, ...), kind=kLoop, calls=%fused_computation.24 | loop fusion | flops 23347200 | bytes 44236820 | tf_op jit(solution)/shard_map/transpose | solution.py:1057
  (454 shorter events, 173.8 us)
Async XLA Ops:
  7.2 180.9 %all-gather.3.cloned.1.call-start = ((), (), s32[]{:S(2)}) async-start(), calls=%async_computation.3 | async-start | bytes 15814656 | tf_op jit(solution)/shard_map/all_gather | solution.py:843
  38.3 293.6 %all-gather.5.cloned.1.call-start = ((), (), s32[]{:S(2)}) async-start(), calls=%async_computation.4 | async-start | bytes 12288000 | tf_op jit(solution)/shard_map/all_gather | solution.py:897
  39.9 103.1 %collective-permute-start.2 = (bf16[96,3200]{1,0:T(8,128)(2,1)}, bf16[96,3200]{1,0:T(8,128)(2,1)}, u32[]{:S(2)}, u32[]{:S(2)}) collective-permute-start(bf16[96,3200]{1,0:T(8,128)(2,1)} %get-tuple-element.203), channel_id=1, source_target_pairs={{0,24},{8,0},{16,8},{24,16},{1,25},{9,1},{17,9},{25,17},{2,26},{10... | collective-permute-start | bytes 1843208 | tf_op jit(solution)/shard_map/ppermute | solution.py:316
  43.2 99.8 %collective-permute-start.1 = (bf16[96,3200]{1,0:T(8,128)(2,1)}, bf16[96,3200]{1,0:T(8,128)(2,1)}, u32[]{:S(2)}, u32[]{:S(2)}) collective-permute-start(bf16[96,3200]{1,0:T(8,128)(2,1)} %get-tuple-element.204), channel_id=1, source_target_pairs={{0,16},{8,24},{16,0},{24,8},{1,17},{9,25},{17,1},{25,9},{2,18},{10... | collective-permute-start | bytes 1843208 | tf_op jit(solution)/shard_map/ppermute | solution.py:316
  43.2 99.8 %collective-permute-start = (bf16[96,3200]{1,0:T(8,128)(2,1)}, bf16[96,3200]{1,0:T(8,128)(2,1)}, u32[]{:S(2)}, u32[]{:S(2)}) collective-permute-start(bf16[96,3200]{1,0:T(8,128)(2,1)} %get-tuple-element.205), channel_id=1, source_target_pairs={{0,8},{8,16},{16,24},{24,0},{1,9},{9,17},{17,25},{25,1},{2,10},{10... | collective-permute-start | bytes 1843208 | tf_op jit(solution)/shard_map/ppermute | solution.py:316
  142.9 54.0 %copy-start.3 = (f32[768,512]{0,1:T(8,128)}, f32[768,512]{0,1:T(8,128)S(1)}, u32[]{:S(2)}) copy-start(f32[768,512]{0,1:T(8,128)S(1)} %copy.239) | copy-start | bytes 4718596
  151.4 406.1 %reduce-scatter.4.cloned.1.call-start = ((), (), s32[]{:S(2)}) async-start(), calls=%async_computation.5 | async-start | bytes 7077888 | tf_op jit(solution)/shard_map/reduce_scatter | solution.py:926
  153.7 39.3 %copy-start.45 = (f32[1,768]{1,0:T(1,128)}, f32[1,768]{1,0:T(1,128)S(1)}, u32[]{:S(2)}) copy-start(f32[1,768]{1,0:T(1,128)S(1)} %slice.143) | copy-start | bytes 9220
  153.8 43.2 %copy-start.68 = (f32[768]{0:T(1024)}, f32[768]{0:T(1024)S(1)}, u32[]{:S(2)}) copy-start(f32[768]{0:T(1024)S(1)} %mul.857) | copy-start | bytes 9220
  154.0 70.4 %copy-start.66 = (f32[768]{0:T(1024)}, f32[768]{0:T(1024)S(1)}, u32[]{:S(2)}) copy-start(f32[768]{0:T(1024)S(1)} %mul.887) | copy-start | bytes 9220
  155.5 37.5 %copy-start.48 = (f32[1,768]{1,0:T(1,128)}, f32[1,768]{1,0:T(1,128)S(1)}, u32[]{:S(2)}) copy-start(f32[1,768]{1,0:T(1,128)S(1)} %mul.871) | copy-start | bytes 9220
  155.5 74.2 %copy-start.39 = (f32[768]{0:T(1024)}, f32[768]{0:T(1024)S(1)}, u32[]{:S(2)}) copy-start(f32[768]{0:T(1024)S(1)} %add.590) | copy-start | bytes 9220
  155.6 84.0 %copy-start.36 = (f32[768]{0:T(1024)}, f32[768]{0:T(1024)S(1)}, u32[]{:S(2)}) copy-start(f32[768]{0:T(1024)S(1)} %mul.905) | copy-start | bytes 9220
  165.0 31.9 %copy-start.55 = (f32[512]{0:T(512)}, f32[512]{0:T(512)S(1)}, u32[]{:S(2)}) copy-start(f32[512]{0:T(512)S(1)} %broadcast_multiply_fusion.8) | copy-start | bytes 6148
  165.3 31.6 %copy-start.72 = (f32[512]{0:T(512)}, f32[512]{0:T(512)S(1)}, u32[]{:S(2)}) copy-start(f32[512]{0:T(512)S(1)} %add_rsqrt_fusion.2) | copy-start | bytes 6148
  193.7 30.7 %copy-start.62 = (f32[768]{0:T(1024)}, f32[768]{0:T(1024)S(1)}, u32[]{:S(2)}) copy-start(f32[768]{0:T(1024)S(1)} %get-tuple-element.154) | copy-start | bytes 9220
  193.7 30.7 %copy-start.80 = (f32[768]{0:T(1024)}, f32[768]{0:T(1024)S(1)}, u32[]{:S(2)}) copy-start(f32[768]{0:T(1024)S(1)} %get-tuple-element.159) | copy-start | bytes 9220
  193.7 36.0 %copy-start.41 = (f32[768]{0:T(1024)}, f32[768]{0:T(1024)S(1)}, u32[]{:S(2)}) copy-start(f32[768]{0:T(1024)S(1)} %get-tuple-element.156) | copy-start | bytes 9220
  193.7 36.1 %copy-start.82 = (f32[768]{0:T(1024)}, f32[768]{0:T(1024)S(1)}, u32[]{:S(2)}) copy-start(f32[768]{0:T(1024)S(1)} %get-tuple-element.155) | copy-start | bytes 9220
  246.2 71.8 %collective-permute-start.8 = (bf16[512,768]{1,0:T(8,128)(2,1)S(1)}, bf16[512,768]{1,0:T(8,128)(2,1)}, u32[]{:S(2)}, u32[]{:S(2)}) collective-permute-start(bf16[512,768]{1,0:T(8,128)(2,1)S(1)} %copy.251), channel_id=1, source_target_pairs={{0,24},{8,0},{16,8},{24,16},{1,25},{9,1},{17,9},{25,17},{2,26},{10... | collective-permute-start | bytes 2359304 | tf_op jit(solution)/shard_map/ppermute | solution.py:316
  249.8 65.2 %collective-permute-start.6 = (bf16[512,768]{1,0:T(8,128)(2,1)S(1)}, bf16[512,768]{1,0:T(8,128)(2,1)}, u32[]{:S(2)}, u32[]{:S(2)}) collective-permute-start(bf16[512,768]{1,0:T(8,128)(2,1)S(1)} %copy.251), channel_id=1, source_target_pairs={{0,16},{8,24},{16,0},{24,8},{1,17},{9,25},{17,1},{25,9},{2,18},{10... | collective-permute-start | bytes 2359304 | tf_op jit(solution)/shard_map/ppermute | solution.py:316
  249.8 51.8 %collective-permute-start.4 = (bf16[512,768]{1,0:T(8,128)(2,1)S(1)}, bf16[512,768]{1,0:T(8,128)(2,1)}, u32[]{:S(2)}, u32[]{:S(2)}) collective-permute-start(bf16[512,768]{1,0:T(8,128)(2,1)S(1)} %copy.251), channel_id=1, source_target_pairs={{0,8},{8,16},{16,24},{24,0},{1,9},{9,17},{17,25},{25,1},{2,10},{10... | collective-permute-start | bytes 2359304 | tf_op jit(solution)/shard_map/ppermute | solution.py:316
  250.4 68.1 %collective-permute-start.3 = (bf16[512,768]{1,0:T(8,128)(2,1)S(1)}, bf16[512,768]{1,0:T(8,128)(2,1)}, u32[]{:S(2)}, u32[]{:S(2)}) collective-permute-start(bf16[512,768]{1,0:T(8,128)(2,1)S(1)} %copy.251), channel_id=1, source_target_pairs={{0,1},{1,0},{2,3},{3,2},{4,5},{5,4},{6,7},{7,6},{8,9},{9,8},{10,11... | collective-permute-start | bytes 2359304 | tf_op jit(solution)/shard_map/ppermute | solution.py:316
  258.8 57.0 %copy-start.20 = (s32[32,16,128]{0,2,1:T(8,128)}, s32[32,16,128]{0,2,1:T(8,128)S(1)}, u32[]{:S(2)}) copy-start(s32[32,16,128]{0,2,1:T(8,128)S(1)} %copy.260) | copy-start | bytes 786436
  301.7 21.0 %collective-permute-start.5 = (bf16[512,768]{1,0:T(8,128)(2,1)}, bf16[512,768]{1,0:T(8,128)(2,1)}, u32[]{:S(2)}, u32[]{:S(2)}) collective-permute-start(bf16[512,768]{1,0:T(8,128)(2,1)} %collective-permute-done.4), channel_id=1, source_target_pairs={{0,1},{1,0},{2,3},{3,2},{4,5},{5,4},{6,7},{7,6},{8,9},{9,8},{10,11... | collective-permute-start | bytes 2359304 | tf_op jit(solution)/shard_map/ppermute | solution.py:316
  315.1 11.8 %collective-permute-start.7 = (bf16[512,768]{1,0:T(8,128)(2,1)}, bf16[512,768]{1,0:T(8,128)(2,1)}, u32[]{:S(2)}, u32[]{:S(2)}) collective-permute-start(bf16[512,768]{1,0:T(8,128)(2,1)} %collective-permute-done.6), channel_id=1, source_target_pairs={{0,1},{1,0},{2,3},{3,2},{4,5},{5,4},{6,7},{7,6},{8,9},{9,8},{10,11... | collective-permute-start | bytes 2359304 | tf_op jit(solution)/shard_map/ppermute | solution.py:316
  318.0 13.0 %collective-permute-start.9 = (bf16[512,768]{1,0:T(8,128)(2,1)}, bf16[512,768]{1,0:T(8,128)(2,1)S(1)}, u32[]{:S(2)}, u32[]{:S(2)}) collective-permute-start(bf16[512,768]{1,0:T(8,128)(2,1)} %collective-permute-done.8), channel_id=1, source_target_pairs={{0,1},{1,0},{2,3},{3,2},{4,5},{5,4},{6,7},{7,6},{8,9},{9,8},{10,11... | collective-permute-start | bytes 2359304 | tf_op jit(solution)/shard_map/ppermute | solution.py:316
  486.9 291.8 %reduce-scatter.6.cloned.1.call-start = ((), (), s32[]{:S(2)}) async-start(), calls=%async_computation.6 | async-start | bytes 5898240 | tf_op jit(solution)/shard_map/reduce_scatter | solution.py:964
  600.2 76.6 %collective-permute-start.12 = (bf16[384,6144]{1,0:T(8,128)(2,1)}, bf16[384,6144]{1,0:T(8,128)(2,1)}, u32[]{:S(2)}, u32[]{:S(2)}) collective-permute-start(bf16[384,6144]{1,0:T(8,128)(2,1)} %dynamic-slice_bitcast_fusion), channel_id=1, source_target_pairs={{0,1},{1,0},{2,3},{3,2},{4,5},{5,4},{6,7},{7,6},{8,9},{9,8},{10,11... | collective-permute-start | bytes 14155784 | tf_op jit(solution)/shard_map/ppermute | solution.py:316
  609.8 56.1 %collective-permute-start.10 = (f16[2,2,96,3200]{3,2,1,0:T(8,128)(2,1)}, f16[2,2,96,3200]{3,2,1,0:T(8,128)(2,1)}, u32[]{:S(2)}, u32[]{:S(2)}) collective-permute-start(f16[2,2,96,3200]{3,2,1,0:T(8,128)(2,1)} %fusion.27), channel_id=1, source_target_pairs={{0,4},{4,0},{1,5},{5,1},{2,6},{6,2},{3,7},{7,3},{8,12},{12,8},{9,1... | collective-permute-start | bytes 7372808 | tf_op jit(solution)/shard_map/ppermute | solution.py:316
  616.1 56.1 %collective-permute-start.11 = (f16[2,2,96,3200]{3,2,1,0:T(8,128)(2,1)}, f16[2,2,96,3200]{3,2,1,0:T(8,128)(2,1)}, u32[]{:S(2)}, u32[]{:S(2)}) collective-permute-start(f16[2,2,96,3200]{3,2,1,0:T(8,128)(2,1)} %fusion.28), channel_id=1, source_target_pairs={{0,2},{2,0},{1,3},{3,1},{4,6},{6,4},{5,7},{7,5},{8,10},{10,8},{9,1... | collective-permute-start | bytes 7372808 | tf_op jit(solution)/shard_map/ppermute | solution.py:316
  617.5 54.6 %slice-start.2 = ((s8[9830400]{0:T(1024)(128)(4,1)}), s8[4194304]{0:T(1024)(128)(4,1)S(1)}, s32[]{:S(2)}) async-start(s8[9830400]{0:T(1024)(128)(4,1)} %bitcast.222), calls=%async_computation.10 | async-start | bytes 8388608
  617.5 54.6 %slice-start.3 = ((s8[9830400]{0:T(1024)(128)(4,1)}), s8[4194304]{0:T(1024)(128)(4,1)S(1)}, s32[]{:S(2)}) async-start(s8[9830400]{0:T(1024)(128)(4,1)} %bitcast.222), calls=%async_computation.11 | async-start | bytes 8388608
  624.6 47.6 %slice-start.4 = ((s8[9830400]{0:T(1024)(128)(4,1)}), s8[1441792]{0:T(1024)(128)(4,1)S(1)}, s32[]{:S(2)}) async-start(s8[9830400]{0:T(1024)(128)(4,1)} %bitcast.222), calls=%async_computation.12 | async-start | bytes 2883584
  624.6 52.2 %slice-start.5 = ((s8[9437184]{0:T(1024)(128)(4,1)}), s8[4194304]{0:T(1024)(128)(4,1)S(1)}, s32[]{:S(2)}) async-start(s8[9437184]{0:T(1024)(128)(4,1)} %bitcast.225), calls=%async_computation.13 | async-start | bytes 8388608
  626.0 50.7 %slice-start.6 = ((s8[9437184]{0:T(1024)(128)(4,1)}), s8[4194304]{0:T(1024)(128)(4,1)S(1)}, s32[]{:S(2)}) async-start(s8[9437184]{0:T(1024)(128)(4,1)} %bitcast.225), calls=%async_computation.14 | async-start | bytes 8388608
  629.2 47.5 %slice-start.7 = ((s8[9437184]{0:T(1024)(128)(4,1)}), s8[1048576]{0:T(1024)(128)(4,1)S(1)}, s32[]{:S(2)}) async-start(s8[9437184]{0:T(1024)(128)(4,1)} %bitcast.225), calls=%async_computation.15 | async-start | bytes 2097152
  683.1 209.8 %reduce-scatter.8.cloned.1.call-start = ((), (), s32[]{:S(2)}) async-start(), calls=%async_computation.7 | async-start | bytes 2211840 | tf_op jit(solution)/shard_map/reduce_scatter | solution.py:964
  693.8 48.0 %collective-permute-start.14 = (f16[2,96,3200]{2,1,0:T(8,128)(2,1)}, f16[2,96,3200]{2,1,0:T(8,128)(2,1)}, u32[]{:S(2)}, u32[]{:S(2)}) collective-permute-start(f16[2,96,3200]{2,1,0:T(8,128)(2,1)} %fusion.45), channel_id=1, source_target_pairs={{0,4},{4,0},{1,5},{5,1},{2,6},{6,2},{3,7},{7,3},{8,12},{12,8},{9,1... | collective-permute-start | bytes 3686408 | tf_op jit(solution)/shard_map/ppermute | solution.py:316
  695.1 46.8 %collective-permute-start.13 = (f16[2,96,3200]{2,1,0:T(8,128)(2,1)}, f16[2,96,3200]{2,1,0:T(8,128)(2,1)}, u32[]{:S(2)}, u32[]{:S(2)}) collective-permute-start(f16[2,96,3200]{2,1,0:T(8,128)(2,1)} %fusion.44), channel_id=1, source_target_pairs={{0,2},{2,0},{1,3},{3,1},{4,6},{6,4},{5,7},{7,5},{8,10},{10,8},{9,1... | collective-permute-start | bytes 3686408 | tf_op jit(solution)/shard_map/ppermute | solution.py:316
  747.8 27.8 %collective-permute-start.15 = (bf16[384,2304]{1,0:T(8,128)(2,1)}, bf16[384,2304]{1,0:T(8,128)(2,1)}, u32[]{:S(2)}, u32[]{:S(2)}) collective-permute-start(bf16[384,2304]{1,0:T(8,128)(2,1)} %dynamic-slice_bitcast_fusion.1), channel_id=1, source_target_pairs={{0,1},{1,0},{2,3},{3,2},{4,5},{5,4},{6,7},{7,6},{8,9},{9,8},{10,11... | collective-permute-start | bytes 5308424 | tf_op jit(solution)/shard_map/ppermute | solution.py:316
  783.7 109.2 %copy-start.19 = (bf16[96,6144]{1,0:T(8,128)(2,1)S(1)}, bf16[96,6144]{1,0:T(8,128)(2,1)}, u32[]{:S(2)}) copy-start(bf16[96,6144]{1,0:T(8,128)(2,1)} %reduce-scatter.6.cloned.1.call-done) | copy-start | bytes 3538948
  785.5 107.4 %collective-permute-start.18 = (f16[96,3200]{1,0:T(8,128)(2,1)}, f16[96,3200]{1,0:T(8,128)(2,1)S(1)}, u32[]{:S(2)}, u32[]{:S(2)}) collective-permute-start(f16[96,3200]{1,0:T(8,128)(2,1)} %get-tuple-element.196), channel_id=1, source_target_pairs={{0,24},{8,0},{16,8},{24,16},{1,25},{9,1},{17,9},{25,17},{2,26},{10... | collective-permute-start | bytes 1843208 | tf_op jit(solution)/shard_map/ppermute | solution.py:316
  788.8 104.1 %collective-permute-start.17 = (f16[96,3200]{1,0:T(8,128)(2,1)}, f16[96,3200]{1,0:T(8,128)(2,1)S(1)}, u32[]{:S(2)}, u32[]{:S(2)}) collective-permute-start(f16[96,3200]{1,0:T(8,128)(2,1)} %get-tuple-element.197), channel_id=1, source_target_pairs={{0,16},{8,24},{16,0},{24,8},{1,17},{9,25},{17,1},{25,9},{2,18},{10... | collective-permute-start | bytes 1843208 | tf_op jit(solution)/shard_map/ppermute | solution.py:316
  788.8 104.1 %collective-permute-start.16 = (f16[96,3200]{1,0:T(8,128)(2,1)}, f16[96,3200]{1,0:T(8,128)(2,1)S(1)}, u32[]{:S(2)}, u32[]{:S(2)}) collective-permute-start(f16[96,3200]{1,0:T(8,128)(2,1)} %get-tuple-element.198), channel_id=1, source_target_pairs={{0,8},{8,16},{16,24},{24,0},{1,9},{9,17},{17,25},{25,1},{2,10},{10... | collective-permute-start | bytes 1843208 | tf_op jit(solution)/shard_map/ppermute | solution.py:316
  895.4 46.4 %collective-permute-start.21 = (bf16[24,8448]{1,0:T(8,128)(2,1)}, bf16[24,8448]{1,0:T(8,128)(2,1)S(1)}, u32[]{:S(2)}, u32[]{:S(2)}) collective-permute-start(bf16[24,8448]{1,0:T(8,128)(2,1)} %get-tuple-element.209), channel_id=1, source_target_pairs={{0,24},{8,0},{16,8},{24,16},{1,25},{9,1},{17,9},{25,17},{2,26},{10... | collective-permute-start | bytes 1216520 | tf_op jit(solution)/shard_map/ppermute | solution.py:316
  895.5 46.3 %collective-permute-start.20 = (bf16[24,8448]{1,0:T(8,128)(2,1)S(1)}, bf16[24,8448]{1,0:T(8,128)(2,1)S(1)}, u32[]{:S(2)}, u32[]{:S(2)}) collective-permute-start(bf16[24,8448]{1,0:T(8,128)(2,1)S(1)} %get-tuple-element.210), channel_id=1, source_target_pairs={{0,16},{8,24},{16,0},{24,8},{1,17},{9,25},{17,1},{25,9},{2,18},{10... | collective-permute-start | bytes 1216520 | tf_op jit(solution)/shard_map/ppermute | solution.py:316
  897.4 44.4 %collective-permute-start.19 = (bf16[24,8448]{1,0:T(8,128)(2,1)S(1)}, bf16[24,8448]{1,0:T(8,128)(2,1)S(1)}, u32[]{:S(2)}, u32[]{:S(2)}) collective-permute-start(bf16[24,8448]{1,0:T(8,128)(2,1)S(1)} %get-tuple-element.211), channel_id=1, source_target_pairs={{0,8},{8,16},{16,24},{24,0},{1,9},{9,17},{17,25},{25,1},{2,10},{10... | collective-permute-start | bytes 1216520 | tf_op jit(solution)/shard_map/ppermute | solution.py:316
  (81 other events, 690.9 us)
Sparse Core Ops, SparseCore 0:
  38.4 149.6 all-gather.2
  190.5 100.3 all-gather.4
  487.0 70.3 reduce-scatter.3
  683.2 77.4 reduce-scatter.5
  778.8 34.1 reduce-scatter.7

commit v6 on v5

--- a/solution.py
+++ b/solution.py
@@ -357,19 +357,30 @@
     low, high = low_ref[source], high_ref[source]
     rows_ref[...] = jnp.zeros_like(rows_ref)
 
-    def chunk(k, carry):
+    first, last = low // 8, (high - 1) // 8
+
+    def edge(k):
         base = pl.multiple_of(k * 8, 8)
-        rows = []
         for i in range(8):
             place = base + i
             valid = jnp.logical_and(place >= low, place < high)
             row = jnp.where(valid, ids_ref[source, place], 0)
             value = turned_ref[pl.ds(row, 1), :]
-            rows.append(jnp.where(valid, value, 0.0))
-        rows_ref[pl.ds(base, 8), :] = jnp.concatenate(rows, axis=0)
+            rows_ref[pl.ds(place, 1), :] = jnp.where(valid, value, 0.0)
+
+    @pl.when(high > low)
+    def _():
+        edge(first)
+        edge(last)
+
+    def chunk(k, carry):
+        base = pl.multiple_of(k * 8, 8)
+        for i in range(8):
+            row = ids_ref[source, base + i]
+            rows_ref[pl.ds(base + i, 1), :] = turned_ref[pl.ds(row, 1), :]
         return carry
 
-    lax.fori_loop(low // 8, (high + 7) // 8, chunk, 0)
+    lax.fori_loop(first + 1, last, chunk, 0)
     out_ref[0] = rows_ref[...].T.astype(BF)
 
 
@@ -408,19 +419,36 @@
     low, high = low_ref[source], high_ref[source]
     wide_ref[...] = rows_ref[0].astype(F32).T
 
-    def chunk(k, carry):
+    first, last = low // 8, (high - 1) // 8
+
+    def edge(k):
         base = pl.multiple_of(k * 8, 8)
-        block = wide_ref[pl.ds(base, 8), :]
         for i in range(8):
             total_ref = totals[i % len(totals)]
             place = base + i
             valid = jnp.logical_and(place >= low, place < high)
             row = jnp.where(valid, ids_ref[source, place], 0)
-            addend = jnp.where(valid, block[i : i + 1, :], 0.0)
+            addend = jnp.where(valid, wide_ref[pl.ds(place, 1), :], 0.0)
+            total_ref[pl.ds(row, 1), :] = total_ref[pl.ds(row, 1), :] + addend
+
+    @pl.when(high > low)
+    def _():
+        edge(first)
+
+    @pl.when(jnp.logical_and(high > low, last > first))
+    def _():
+        edge(last)
+
+    def chunk(k, carry):
+        base = pl.multiple_of(k * 8, 8)
+        for i in range(8):
+            total_ref = totals[i % len(totals)]
+            row = ids_ref[source, base + i]
+            addend = wide_ref[pl.ds(base + i, 1), :]
             total_ref[pl.ds(row, 1), :] = total_ref[pl.ds(row, 1), :] + addend
         return carry
 
-    lax.fori_loop(low // 8, (high + 7) // 8, chunk, 0)
+    lax.fori_loop(first + 1, last, chunk, 0)
 
     @pl.when(source == pl.num_programs(0) - 1)
     def _():
@@ -444,7 +472,7 @@
             in_specs=[pl.BlockSpec((1, width, count), lambda i, *_: (i, 0, 0))],
             out_specs=pl.BlockSpec((width, table_rows), lambda i, *_: (0, 0)),
             scratch_shapes=[pltpu.VMEM((count, width), F32)]
-            + [pltpu.VMEM((table_rows, width), F32)] * 4,
+            + [pltpu.VMEM((table_rows, width), F32)] * 2,
         ),
         compiler_params=pltpu.CompilerParams(vmem_limit_bytes=VMEM_LIMIT),
         cost_estimate=pl.CostEstimate(flops=0, bytes_accessed=1 << 27, transcendentals=0),
@@ -613,9 +641,18 @@
     return max(16, 1024 // segments)
 
 
-def logits_kernel(places_ref, x_ref, w_ref, target_ref, e_ref, stats_ref, logits_ref):
+def logits_kernel(places_ref, w_ref, target_ref, *refs):
+    blocks, (e_ref, stats_ref, x_ref, logits_ref) = refs[:-4], refs[-4:]
     segments, _, width = w_ref.shape
     rows = x_ref.shape[0]
+    per = blocks[0].shape[0] // rows
+    step = pl.program_id(0)
+    for number, block in enumerate(blocks):
+
+        @pl.when(step // per == number)
+        def _(block=block):
+            x_ref[...] = block[pl.ds(pl.multiple_of(lax.rem(step, per) * rows, rows), rows), :]
+
     x = x_ref[...]
     starts = list(range(0, width - width % 768 or width, 768))
     best = None
@@ -646,11 +683,11 @@
         stats_ref[r : r + ROWS, :] = jnp.concatenate([peak, *sums, peak], axis=1)
 
 
-def head_logits(rows, weights, targets, places):
-    count = rows.shape[0]
+def head_logits(blocks, weights, targets, places):
+    count = targets.shape[0]
     segments, _, width = weights.shape
     tile = tile_of(segments)
-    per = count // places.shape[0] // tile
+    per = blocks[0].shape[0] // tile
 
     def placed(i, places):
         return (places[i // per] * per + lax.rem(i, per), 0)
@@ -660,18 +697,22 @@
         out_shape=[
             jax.ShapeDtypeStruct((segments, count, width), BF),
             jax.ShapeDtypeStruct((count, 4), F32),
+            jax.ShapeDtypeStruct((count, D), BF),
         ],
         grid_spec=pltpu.PrefetchScalarGridSpec(
             num_scalar_prefetch=1,
             grid=(count // tile,),
             in_specs=[
-                pl.BlockSpec((tile, D), lambda i, p: (i, 0)),
                 pl.BlockSpec(weights.shape, lambda i, p: (0, 0, 0), pipeline_mode=pl.Buffered(1)),
                 pl.BlockSpec((tile, 1), placed),
+            ] + [
+                pl.BlockSpec(b.shape, lambda i, p: (0, 0), pipeline_mode=pl.Buffered(1))
+                for b in blocks
             ],
             out_specs=[
                 pl.BlockSpec((segments, tile, width), lambda i, p: (0, i, 0)),
                 pl.BlockSpec((tile, 4), placed),
+                pl.BlockSpec((tile, D), lambda i, p: (i, 0)),
             ],
             scratch_shapes=[pltpu.VMEM((tile, segments * width), F32)],
         ),
@@ -682,7 +723,7 @@
             transcendentals=count * segments * width,
         ),
         name="head_logits",
-    )(places, rows, weights, targets)
+    )(places, weights, targets, *blocks)
 
 
 def rows_back_kernel(places_ref, e_ref, w_ref, target_ref, factor_ref, d_ref, dx_ref):
@@ -910,8 +951,7 @@
     owner, within = row_targets // table_rows, row_targets % table_rows
     owned = jnp.logical_and(owner % nc == ic, within // SEGMENT == iz)
     column_of = jnp.where(owned, (owner // nc) * SEGMENT + within % SEGMENT, -1)[:, None]
-    rows = jnp.concatenate(blocks, axis=0)
-    e, stats = head_logits(rows, head_all, column_of, places)
+    e, stats, rows = head_logits(blocks, head_all, column_of, places)
     top = stats[:, 0]
     every = share(("z", "c"), 4, stats.T.reshape(4, -1, LANES))[0].reshape(nz * nc, 4, group)
     best = jnp.max(every[:, 0], axis=0)
@@ -966,11 +1006,12 @@
         spread_parts(added(own_x, from_xy[: nx - 1]), 0, "y"),
         spread_parts(added(own_y, from_xy[nx - 1 :]), 0, "x"),
     )
-    mlp_sum = over_cores(jnp.concatenate([d_up.astype(BF), d_down.astype(BF)], axis=1))
-    d_att, mlp_sum = together(d_att, mlp_sum)
-    mlp_sum = over_plane(mlp_sum)
     d_k, d_v, d_qkv_m = attend_back(q, k_u, k_m, kv_u, qkv_m, tables, mask, lse_a, d_att)
     d_k, *arrivals = together(d_k, *own_xy[1], *from_xy[1])
+    head_sum = jnp.concatenate(
+        [added(own_xy[0], arrivals[: ny - 1]), added(from_xy[0], arrivals[ny - 1 :])], axis=0)
+    d_k, head_sum = together(d_k, head_sum)
+    head_own, head_parts = spread_parts(head_sum, 0, "z")
     d_kv = jnp.concatenate([d_k, d_v], axis=1)
     d_wkv = matmul_tn(a_u, d_kv)
     d_row_m = d_qkv_m[:3].reshape(3 * D)
@@ -985,7 +1026,8 @@
     d_x0_u = norm_back(d_a_u * scaling, normed_u, inv_u)
     d_mask = jnp.sum(d_x1, axis=0) + norm_back(d_a_m * scaling, normed_0, inv_0)[0]
 
-    rest_sum = over_cores(jnp.concatenate([d_wkv.astype(BF), d_wout.astype(BF)], axis=1))
+    chip_sum = over_cores(jnp.concatenate(
+        [d_wkv.astype(BF), d_wout.astype(BF), d_up.astype(BF), d_down.astype(BF)], axis=1))
 
     small = jnp.concatenate([d_shift_a, d_scale_a, d_gate_a, d_shift_m, d_scale_m, d_gate_m,
                              d_gain_a, d_gain_m, d_gain_f, d_mask,
@@ -994,18 +1036,13 @@
     count_small = small.shape[0]
     small = jnp.pad(small, ((0, -count_small % 8), (0, 0)))
 
-    sent, rest_sum = together(
-        d_x0_u.astype(BF).T.reshape(nz * nx, table_width, free_count), rest_sum)
-    rest_sum, mlp_sum = together(rest_sum, mlp_sum)
-    rest_sum = over_plane(rest_sum)
-    head_sum = jnp.concatenate(
-        [added(own_xy[0], arrivals[: ny - 1]), added(from_xy[0], arrivals[ny - 1 :])], axis=0)
-    sent, head_sum = together(sent, head_sum)
-    head_own, head_parts = spread_parts(head_sum, 0, "z")
+    sent = d_x0_u.astype(BF).T.reshape(nz * nx, table_width, free_count)
+    sent, chip_sum = together(sent, chip_sum)
+    plane_sum = over_plane(chip_sum)
+    sent, *head_parts = together(sent, *head_parts)
 
     arrived, small_all = spread_blocks(sizes, sent, small, 5)
-    arrived, mlp_sum, rest_sum, *head_parts = together(arrived, mlp_sum, rest_sum, *head_parts)
-    plane_sum = jnp.concatenate([rest_sum, mlp_sum], axis=1)
+    arrived, plane_sum = together(arrived, plane_sum)
     plane_sum = plane_sum.reshape(nz, -1, plane_sum.shape[1])
     block_parts = [p for _, p in exchange(lambda k: pick(plane_sum, k), ("z",))]
     g_embed = scatter_rows(arrived.reshape(n, table_width, free_count), local_ids, low, high,

time: 1030 us -> 963 us (0.935)
  Pallas kernels: 457 us -> 392 us
  waiting for transfers between devices: 155 us -> 192 us
  local copies, waits for them, and re-layouts: 113 us -> 86.3 us
  other arithmetic: 134 us -> 116 us
    pallas_call x1, Pallas kernels: 102 us -> 47.3 us  [spread_blocks(): pl.pallas_call(functools.partial(spread_kernel, sizes), out_shape=[jax.Sh...]
    ppermute x22 -> x21, waiting for transfers between devices: 116 us -> 140 us  [exchange(): moved = lax.ppermute(piece, axes, [(i, (i + step) % n) for i in range(n)])]
    all_gather x1, waiting for transfers between devices: 22.7 us -> 35.6 us  [local(): layer_all = lax.all_gather(block_low, ALL, axis=0, tiled=True)]
    unnamed x224 -> x225, local copies, waits for them, and re-layouts: 34 us -> 23 us
    ppermute x22 -> x21, starting transfers between devices: 23.2 us -> 24.8 us  [exchange(): moved = lax.ppermute(piece, axes, [(i, (i + step) % n) for i in range(n)])]
  transfers between devices with their start and end apart: 27 -> 25, of which waited for: 7 -> 9; matrix products, arithmetic and copies ran while one was open for 22% -> 18% of each run, Pallas kernels for 27% -> 23%
where the time goes in v6:
time: 963 us; the launch traced here: 955 us
  Pallas kernels  392 us (41%)
  waiting for transfers between devices  192 us (20%)
  matrix products  117 us (12%)
  other arithmetic  116 us (12%)
  local copies, waits for them, and re-layouts  86.3 us (9%)
  between operations  27.2 us (3%)
  starting transfers between devices  25.2 us (3%)
    ppermute x21, waiting for transfers between devices, exchange(): moved = lax.ppermute(piece, axes, [(i, (i + step) % n) for i in range(n)])  140 us
    pallas_call x1, Pallas kernels, head_logits(): pl.pallas_call(logits_kernel, out_shape=[jax.ShapeDtypeStruct((segments,...  72.9 us
    dot_general x15, matrix products, dot(): lax.dot_general(a, b, ((contract[0], contract[1]), ((), ())), preferred_e...  64.2 us
    pallas_call x1, Pallas kernels, fetch_blocks(): pl.pallas_call(functools.partial(fetch_kernel, sizes), out_shape=jax.Shap...  59.1 us
    pallas_call x1, Pallas kernels, head_rows_back(): pl.pallas_call(rows_back_kernel, out_shape=[jax.ShapeDtypeStruct(e.shape,...  56.2 us
    dot_general x1, matrix products, local(): jnp.einsum('rd,yrv->ydv', rows, d_logits, preferred_element_type=F32)  50.6 us
    pallas_call x1, Pallas kernels, spread_blocks(): pl.pallas_call(functools.partial(spread_kernel, sizes), out_shape=[jax.Sh...  47.3 us
    pallas_call x3, Pallas kernels, share(): pl.pallas_call(functools.partial(share_kernel, axes, sizes, count), out_s...  46.4 us
  transfers between devices with their start and end apart: 25, of which 9 were waited for; matrix products, arithmetic and copies ran while one was open for 18% of the time, Pallas kernels for 23%

profile of v6, /device:TPU:0, one launch (start us, length us, event | category | flops | bytes accessed | tf_op | source)
XLA Modules:
  0.0 955.5 jit_solution(8077363517135643995)
XLA Ops:
  19.5 18.0 %share0.1 = (s32[4,2,2,2,16,128]{5,4,3,2,1,0:T(8,128)}, f32[4,2,2,2,8,128]{5,4,3,2,1,0:T(8,128)}) custom-call(s32[16,128]{1,0:T(8,128)} %pad.18.refs_0_, f32[8,128]{1,0:T(8,128)} %pad_convert_fusion.refs_1_), custom_call_target="tpu_custom_call" | custom-call | tf_op jit(solution)/shard_map/share0/pallas_call | solution.py:104
  39.9 3.3 collective-permute-start.2
  46.8 31.6 %gather_rows.1 = bf16[32,96,512]{2,1,0:T(8,128)(2,1)} custom-call(s32[32]{0:T(128)} %reduce_sum.397.low_ref, s32[32]{0:T(128)} %reduce_sum.399.high_ref, s32[32,512]{1,0:T(8,128)} %bitcast.256, f32[96,12800]{1,0:T(8,128)} %bitcast.225), custom_call_target="tpu_custom_call" | custom-call | bytes 134217728 | tf_op jit(solution)/shard_map/gather_rows/pallas_call | solution.py:390
  78.4 59.1 %fetch_blocks.1 = bf16[8,96,512]{2,1,0:T(8,128)(2,1)} custom-call(bf16[2,2,8,96,512]{4,3,2,1,0:T(8,128)(2,1)} %bitcast.230), custom_call_target="tpu_custom_call" | custom-call | bytes 134217728 | tf_op jit(solution)/shard_map/fetch_blocks/pallas_call | solution.py:194
  158.6 35.6 %all-gather.3.cloned.1.call-done = bf16[768,9984]{1,0:T(8,128)(2,1)} async-done(((bf16[24,9984]{1,0:T(8,128)(2,1)}), bf16[768,9984]{1,0:T(8,128)(2,1)}) %all-gather.3.cloned.1.call-update) | async-done | bytes 15335440 | tf_op jit(solution)/shard_map/all_gather | solution.py:884
  199.9 3.7 fusion.22.qm_ref.km_ref.vm_ref
  203.6 5.2 fusion.40.kv_ref.vv_ref
  209.4 18.5 %attend.1 = (bf16[512,768]{1,0:T(8,128)(2,1)}, bf16[512,768]{1,0:T(8,128)(2,1)}, bf16[512,768]{1,0:T(8,128)(2,1)}, bf16[512,768]{1,0:T(8,128)(2,1)}, f32[6,512,2]{2,1,0:T(8,128)}) custom-call(f32[512,1536]{1,0:T(8,128)} %fusion.40.kv_ref.vv_ref, f32[512,1536]{1,0:T(8,128)} %fusion.40.kv_ref.vv_ref, f32[16,2304]{1,0:T(8,128)} %fusion.22.qm_ref.km_ref.vm_ref, ...), custom_call_target="tpu_custom_call" | custom-call | flops 1207959552 | bytes 4718592 | tf_op jit(solution)/shard_map/attend/pallas_call | solution.py:541
  230.7 5.4 fusion.18
  236.2 10.2 %fusion.110 = (f32[512]{0:T(512)S(1)}, f32[512,768]{1,0:T(8,128)S(1)}, f32[512,768]{1,0:T(8,128)}) fusion(f32[768]{0:T(1024)S(1)} %get-tuple-element.149, f32[512,768]{1,0:T(8,128)S(1)} %get-tuple-element.240, f32[768]{0:T(1024)S(1)} %get-tuple-element.150, f32[768]{0:T(1024)S(1)} %add.581, bf16[768,9984]{1,0:T(8,128)(2,1)} %all-gather.3.cloned.1.call-done, ...), kind=kOutput, calls=%fused_computation.336 | convolution fusion | flops 2432040448 | bytes 15739904 | tf_op jit(solution)/shard_map/dot_general | solution.py:39
  258.1 12.1 %collective-permute-done.8.refs_6_ = bf16[512,768]{1,0:T(8,128)(2,1)} collective-permute-done((bf16[512,768]{1,0:T(8,128)(2,1)}, bf16[512,768]{1,0:T(8,128)(2,1)}, u32[]{:S(2)}, u32[]{:S(2)}) %collective-permute-start.8) | collective-permute-done | bytes 786464 | tf_op jit(solution)/shard_map/ppermute | solution.py:316
  270.3 48.8 %collective-permute-done.6.refs_4_ = bf16[512,768]{1,0:T(8,128)(2,1)} collective-permute-done((bf16[512,768]{1,0:T(8,128)(2,1)}, bf16[512,768]{1,0:T(8,128)(2,1)}, u32[]{:S(2)}, u32[]{:S(2)}) %collective-permute-start.6) | collective-permute-done | bytes 786464 | tf_op jit(solution)/shard_map/ppermute | solution.py:316
  319.6 7.2 fusion.32.target_ref
  326.8 72.9 %head_logits.1 = (bf16[2,4096,3200]{2,1,0:T(8,128)(2,1)}, f32[4096,4]{1,0:T(8,128)}, bf16[4096,768]{1,0:T(8,128)(2,1)}) custom-call(s32[8]{0:T(128)} %stack.46.places_ref, bf16[2,768,3200]{2,1,0:T(8,128)(2,1)} %bitcast.280, s32[4096,1]{1,0:T(8,128)} %fusion.32.target_ref, bf16[512,768]{1,0:T(8,128)(2,1)} %copy.260.refs_0_, ...), custom_call_target="tpu_custom_call" | custom-call | flops 40265318400 | bytes 52428800 | tf_op jit(solution)/shard_map/head_logits/pallas_call | solution.py:695
  402.5 11.4 %share4.1 = f32[4,2,4,32,128]{4,3,2,1,0:T(8,128)} custom-call(f32[4,32,128]{2,1,0:T(8,128)} %copy.284.refs_0_), custom_call_target="tpu_custom_call" | custom-call | tf_op jit(solution)/shard_map/share4/pallas_call | solution.py:104
  419.7 3.3 bitcast_multiply_fusion.1
  425.0 56.2 %head_rows_back.1 = (bf16[2,4096,3200]{2,1,0:T(8,128)(2,1)}, bf16[4096,768]{1,0:T(8,128)(2,1)}) custom-call(s32[8]{0:T(128)} %stack.46.places_ref, bf16[2,4096,3200]{2,1,0:T(8,128)(2,1)} %get-tuple-element.90.e_ref, bf16[2,768,3200]{2,1,0:T(8,128)(2,1)} %bitcast.281, s32[4096,1]{1,0:T(8,128)} %fusion.32.target_ref, ...), custom_call_target="tpu_custom_call", output_to_operand_aliasing={{0}: (1, {})} | custom-call | flops 40265318400 | bytes 104857600 | tf_op jit(solution)/shard_map/head_rows_back/pallas_call | solution.py:757
  484.5 50.6 %convolution_multiply_fusion = f32[2,3200,768]{1,2,0:T(8,128)} fusion(bf16[2,4096,3200]{2,1,0:T(8,128)(2,1)} %get-tuple-element.93, f32[]{:T(128)S(6)} %div.269, bf16[4096,768]{1,0:T(8,128)(2,1)} %get-tuple-element.94), kind=kOutput, calls=%fused_computation | convolution fusion | flops 40270233600 | bytes 78381056 | tf_op jit(solution)/shard_map/rd,yrv->ydv/dot_general | solution.py:971
  535.1 16.1 %reduce-scatter.3.cloned.1.call-done = bf16[512,768]{1,0:T(8,128)(2,1)} async-done(((bf16[4096,768]{1,0:T(8,128)(2,1)}), bf16[512,768]{1,0:T(8,128)(2,1)}) %reduce-scatter.3.cloned.1.call-update) | async-done | bytes 786448 | tf_op jit(solution)/shard_map/reduce_scatter | solution.py:966
  556.8 7.7 fusion.111
  571.8 3.2 copy-done.3
  577.3 8.0 fusion.7
  585.3 6.5 multiply_reduce_fusion.4
  597.3 3.1 convolution_convert_fusion.4.datt_ref
  600.5 4.9 convolution_convert_fusion.1
  605.4 14.1 %collective-permute-done.10 = f16[2,2,96,3200]{3,2,1,0:T(8,128)(2,1)} collective-permute-done((f16[2,2,96,3200]{3,2,1,0:T(8,128)(2,1)}, f16[2,2,96,3200]{3,2,1,0:T(8,128)(2,1)}, u32[]{:S(2)}, u32[]{:S(2)}) %collective-permute-start.10) | collective-permute-done | bytes 2457632 | tf_op jit(solution)/shard_map/ppermute | solution.py:316
  619.5 8.8 collective-permute-done.11
  628.4 3.8 bitcast_add_fusion.3
  632.3 4.0 bitcast_add_fusion.2
  640.5 4.6 convolution_convert_fusion
  645.1 23.9 %attend_back.1 = (bf16[512,768]{1,0:T(8,128)(2,1)}, bf16[512,768]{1,0:T(8,128)(2,1)}, f32[8,768]{1,0:T(8,128)}) custom-call(bf16[512,768]{1,0:T(8,128)(2,1)} %get-tuple-element.81.q_ref, bf16[512,768]{1,0:T(8,128)(2,1)} %get-tuple-element.82.ku_ref, bf16[512,768]{1,0:T(8,128)(2,1)} %get-tuple-element.83.km_ref, f32[512,1536]{1,0:T(8,128)} %fusion.40.kv_ref.vv_ref, ...), custom_call_target="tpu_custom_call" | custom-call | flops 3221225472 | bytes 5505024 | tf_op jit(solution)/shard_map/attend_back/pallas_call | solution.py:613
  680.6 3.4 copy.281
  684.1 3.4 dynamic-slice_bitcast_fusion
  687.5 3.2 copy-done
  690.7 3.4 multiply_reduce_fusion.6
  695.8 5.7 collective-permute-done.14
  701.5 8.8 fusion
  712.5 3.1 fusion.45
  718.2 3.7 dynamic-slice_bitcast_fusion.1
  728.3 10.8 %collective-permute-done.17 = f16[96,3200]{1,0:T(8,128)(2,1)} collective-permute-done((f16[96,3200]{1,0:T(8,128)(2,1)S(1)}, f16[96,3200]{1,0:T(8,128)(2,1)}, u32[]{:S(2)}, u32[]{:S(2)}) %collective-permute-start.17) | collective-permute-done | bytes 614432 | tf_op jit(solution)/shard_map/ppermute | solution.py:316
  739.1 39.6 %collective-permute-done.16 = f16[96,3200]{1,0:T(8,128)(2,1)} collective-permute-done((f16[96,3200]{1,0:T(8,128)(2,1)S(1)}, f16[96,3200]{1,0:T(8,128)(2,1)}, u32[]{:S(2)}, u32[]{:S(2)}) %collective-permute-start.16) | collective-permute-done | bytes 614432 | tf_op jit(solution)/shard_map/ppermute | solution.py:316
  778.7 47.3 %spread_blocks.1 = (bf16[2,2,8,96,512]{4,3,2,1,0:T(8,128)(2,1)}, f32[4,2,2,2,88,128]{5,4,3,2,1,0:T(8,128)}) custom-call(bf16[8,96,512]{2,1,0:T(8,128)(2,1)} %bitcast.244, f32[88,128]{1,0:T(8,128)} %pad.22.small_ref), custom_call_target="tpu_custom_call" | custom-call | bytes 134217728 | tf_op jit(solution)/shard_map/spread_blocks/pallas_call | solution.py:280
  830.0 4.0 collective-permute-start.19
  834.9 36.4 %scatter_rows.1 = f32[96,12800]{1,0:T(8,128)} custom-call(s32[32]{0:T(128)} %reduce_sum.397.low_ref, s32[32]{0:T(128)} %reduce_sum.399.high_ref, s32[32,512]{1,0:T(8,128)} %bitcast.257, bf16[32,96,512]{2,1,0:T(8,128)(2,1)} %bitcast.243), custom_call_target="tpu_custom_call" | custom-call | bytes 134217728 | tf_op jit(solution)/shard_map/scatter_rows/pallas_call | solution.py:466
  891.5 17.0 %share2.1 = f32[4,2,2,2,8,128]{5,4,3,2,1,0:T(8,128)} custom-call(f32[8,128]{1,0:T(8,128)} %broadcast_in_dim.144.refs_0_), custom_call_target="tpu_custom_call" | custom-call | tf_op jit(solution)/shard_map/share2/pallas_call | solution.py:104
  912.2 4.4 multiply_add_fusion.5
  916.6 16.5 %multiply_add_fusion = (f32[96,12800]{1,0:T(8,128)}, f32[96,12800]{1,0:T(8,128)}, f32[96,12800]{1,0:T(8,128)}, f32[96,12800]{1,0:T(8,128)}) fusion(f32[96,12800]{1,0:T(8,128)} %param.49, f32[]{:T(128)} %bitcast.90, f32[]{:T(128)S(6)} %sub.311, f32[96,12800]{1,0:T(8,128)} %param.46, f32[]{:T(128)} %bitcast.89, f32[]{:T(128)} %bitcast.88, f32[]{:T(128)S(6)} %min.13, ...), kind=kLoop, calls=%fused_computation.29 | loop fusion | flops 28262400 | bytes 44236824 | tf_op jit(solution)/shard_map/add | solution.py:833
  933.2 13.6 %fusion.11 = (f32[12800,96]{0,1:T(8,128)}, f32[96,12800]{1,0:T(8,128)}, f32[12800,96]{0,1:T(8,128)}, f32[12800,96]{0,1:T(8,128)}) fusion(f32[12800,96]{0,1:T(8,128)} %param.45, f32[]{:T(128)S(6)} %sub.311, f32[]{:T(128)} %bitcast.90, f32[]{:T(128)} %bitcast.89, f32[12800,96]{0,1:T(8,128)} %param.44, f32[]{:T(128)} %bitcast.88, f32[96,12800]{1,0:T(8,128)S(1)} %bitcast.215, ...), kind=kLoop, calls=%fused_computation.25 | loop fusion | flops 23347200 | bytes 44236820 | tf_op jit(solution)/shard_map/transpose | solution.py:1094
  (447 shorter events, 142.3 us)
Async XLA Ops:
  7.2 187.1 %all-gather.3.cloned.1.call-start = ((), (), s32[]{:S(2)}) async-start(), calls=%async_computation.2 | async-start | bytes 15814656 | tf_op jit(solution)/shard_map/all_gather | solution.py:884
  38.3 288.5 %all-gather.5.cloned.1.call-start = ((), (), s32[]{:S(2)}) async-start(), calls=%async_computation.3 | async-start | bytes 12288000 | tf_op jit(solution)/shard_map/all_gather | solution.py:938
  39.9 99.5 %collective-permute-start.2 = (bf16[96,3200]{1,0:T(8,128)(2,1)}, bf16[96,3200]{1,0:T(8,128)(2,1)}, u32[]{:S(2)}, u32[]{:S(2)}) collective-permute-start(bf16[96,3200]{1,0:T(8,128)(2,1)} %get-tuple-element.197), channel_id=1, source_target_pairs={{0,24},{8,0},{16,8},{24,16},{1,25},{9,1},{17,9},{25,17},{2,26},{10... | collective-permute-start | bytes 1843208 | tf_op jit(solution)/shard_map/ppermute | solution.py:316
  43.2 96.2 %collective-permute-start.1 = (bf16[96,3200]{1,0:T(8,128)(2,1)}, bf16[96,3200]{1,0:T(8,128)(2,1)}, u32[]{:S(2)}, u32[]{:S(2)}) collective-permute-start(bf16[96,3200]{1,0:T(8,128)(2,1)} %get-tuple-element.198), channel_id=1, source_target_pairs={{0,16},{8,24},{16,0},{24,8},{1,17},{9,25},{17,1},{25,9},{2,18},{10... | collective-permute-start | bytes 1843208 | tf_op jit(solution)/shard_map/ppermute | solution.py:316
  43.2 96.2 %collective-permute-start = (bf16[96,3200]{1,0:T(8,128)(2,1)}, bf16[96,3200]{1,0:T(8,128)(2,1)}, u32[]{:S(2)}, u32[]{:S(2)}) collective-permute-start(bf16[96,3200]{1,0:T(8,128)(2,1)} %get-tuple-element.199), channel_id=1, source_target_pairs={{0,8},{8,16},{16,24},{24,0},{1,9},{9,17},{17,25},{25,1},{2,10},{10... | collective-permute-start | bytes 1843208 | tf_op jit(solution)/shard_map/ppermute | solution.py:316
  139.3 64.2 %copy-start.4 = (f32[768,512]{0,1:T(8,128)}, f32[768,512]{0,1:T(8,128)S(1)}, u32[]{:S(2)}) copy-start(f32[768,512]{0,1:T(8,128)S(1)} %copy.240) | copy-start | bytes 4718596
  147.9 403.3 %reduce-scatter.3.cloned.1.call-start = ((), (), s32[]{:S(2)}) async-start(), calls=%async_computation.4 | async-start | bytes 7077888 | tf_op jit(solution)/shard_map/reduce_scatter | solution.py:966
  150.4 48.8 %copy-start.47 = (f32[1,768]{1,0:T(1,128)}, f32[1,768]{1,0:T(1,128)S(1)}, u32[]{:S(2)}) copy-start(f32[1,768]{1,0:T(1,128)S(1)} %slice.143) | copy-start | bytes 9220
  150.5 53.0 %copy-start.68 = (f32[768]{0:T(1024)}, f32[768]{0:T(1024)S(1)}, u32[]{:S(2)}) copy-start(f32[768]{0:T(1024)S(1)} %mul.857) | copy-start | bytes 9220
  150.7 79.9 %copy-start.66 = (f32[768]{0:T(1024)}, f32[768]{0:T(1024)S(1)}, u32[]{:S(2)}) copy-start(f32[768]{0:T(1024)S(1)} %mul.887) | copy-start | bytes 9220
  152.5 46.7 %copy-start.49 = (f32[1,768]{1,0:T(1,128)}, f32[1,768]{1,0:T(1,128)S(1)}, u32[]{:S(2)}) copy-start(f32[1,768]{1,0:T(1,128)S(1)} %mul.871) | copy-start | bytes 9220
  152.6 83.5 %copy-start.41 = (f32[768]{0:T(1024)}, f32[768]{0:T(1024)S(1)}, u32[]{:S(2)}) copy-start(f32[768]{0:T(1024)S(1)} %add.581) | copy-start | bytes 9220
  152.7 94.0 %copy-start.38 = (f32[768]{0:T(1024)}, f32[768]{0:T(1024)S(1)}, u32[]{:S(2)}) copy-start(f32[768]{0:T(1024)S(1)} %mul.907) | copy-start | bytes 9220
  158.3 45.2 %copy-start.55 = (f32[512]{0:T(512)}, f32[512]{0:T(512)S(1)}, u32[]{:S(2)}) copy-start(f32[512]{0:T(512)S(1)} %broadcast_multiply_fusion.8) | copy-start | bytes 6148
  158.6 44.9 %copy-start.71 = (f32[512]{0:T(512)}, f32[512]{0:T(512)S(1)}, u32[]{:S(2)}) copy-start(f32[512]{0:T(512)S(1)} %add_rsqrt_fusion.2) | copy-start | bytes 6148
  199.9 30.8 %copy-start.62 = (f32[768]{0:T(1024)}, f32[768]{0:T(1024)S(1)}, u32[]{:S(2)}) copy-start(f32[768]{0:T(1024)S(1)} %get-tuple-element.148) | copy-start | bytes 9220
  199.9 30.8 %copy-start.82 = (f32[768]{0:T(1024)}, f32[768]{0:T(1024)S(1)}, u32[]{:S(2)}) copy-start(f32[768]{0:T(1024)S(1)} %get-tuple-element.153) | copy-start | bytes 9220
  199.9 36.3 %copy-start.43 = (f32[768]{0:T(1024)}, f32[768]{0:T(1024)S(1)}, u32[]{:S(2)}) copy-start(f32[768]{0:T(1024)S(1)} %get-tuple-element.150) | copy-start | bytes 9220
  199.9 36.3 %copy-start.80 = (f32[768]{0:T(1024)}, f32[768]{0:T(1024)S(1)}, u32[]{:S(2)}) copy-start(f32[768]{0:T(1024)S(1)} %get-tuple-element.149) | copy-start | bytes 9220
  249.3 21.0 %collective-permute-start.8 = (bf16[512,768]{1,0:T(8,128)(2,1)}, bf16[512,768]{1,0:T(8,128)(2,1)}, u32[]{:S(2)}, u32[]{:S(2)}) collective-permute-start(bf16[512,768]{1,0:T(8,128)(2,1)} %copy.260.refs_0_), channel_id=1, source_target_pairs={{0,24},{8,0},{16,8},{24,16},{1,25},{9,1},{17,9},{25,17},{2,26},{10... | collective-permute-start | bytes 2359304 | tf_op jit(solution)/shard_map/ppermute | solution.py:316
  250.0 69.1 %collective-permute-start.6 = (bf16[512,768]{1,0:T(8,128)(2,1)}, bf16[512,768]{1,0:T(8,128)(2,1)}, u32[]{:S(2)}, u32[]{:S(2)}) collective-permute-start(bf16[512,768]{1,0:T(8,128)(2,1)} %copy.260.refs_0_), channel_id=1, source_target_pairs={{0,16},{8,24},{16,0},{24,8},{1,17},{9,25},{17,1},{25,9},{2,18},{10... | collective-permute-start | bytes 2359304 | tf_op jit(solution)/shard_map/ppermute | solution.py:316
  250.6 68.5 %collective-permute-start.4 = (bf16[512,768]{1,0:T(8,128)(2,1)}, bf16[512,768]{1,0:T(8,128)(2,1)}, u32[]{:S(2)}, u32[]{:S(2)}) collective-permute-start(bf16[512,768]{1,0:T(8,128)(2,1)} %copy.260.refs_0_), channel_id=1, source_target_pairs={{0,8},{8,16},{16,24},{24,0},{1,9},{9,17},{17,25},{25,1},{2,10},{10... | collective-permute-start | bytes 2359304 | tf_op jit(solution)/shard_map/ppermute | solution.py:316
  258.1 68.6 %collective-permute-start.3 = (bf16[512,768]{1,0:T(8,128)(2,1)}, bf16[512,768]{1,0:T(8,128)(2,1)}, u32[]{:S(2)}, u32[]{:S(2)}) collective-permute-start(bf16[512,768]{1,0:T(8,128)(2,1)} %copy.260.refs_0_), channel_id=1, source_target_pairs={{0,1},{1,0},{2,3},{3,2},{4,5},{5,4},{6,7},{7,6},{8,9},{9,8},{10,11... | collective-permute-start | bytes 2359304 | tf_op jit(solution)/shard_map/ppermute | solution.py:316
  270.3 56.5 %collective-permute-start.9 = (bf16[512,768]{1,0:T(8,128)(2,1)}, bf16[512,768]{1,0:T(8,128)(2,1)}, u32[]{:S(2)}, u32[]{:S(2)}) collective-permute-start(bf16[512,768]{1,0:T(8,128)(2,1)} %collective-permute-done.8.refs_6_), channel_id=1, source_target_pairs={{0,1},{1,0},{2,3},{3,2},{4,5},{5,4},{6,7},{7,6},{8,9},{9,8},{10,11... | collective-permute-start | bytes 2359304 | tf_op jit(solution)/shard_map/ppermute | solution.py:316
  319.1 7.7 collective-permute-start.7
  319.1 7.7 collective-permute-start.5
  481.2 344.8 %reduce-scatter.5.cloned.1.call-start = ((), (), s32[]{:S(2)}) async-start(), calls=%async_computation.5 | async-start | bytes 8110080 | tf_op jit(solution)/shard_map/reduce_scatter | solution.py:1004
  566.2 53.3 %collective-permute-start.10 = (f16[2,2,96,3200]{3,2,1,0:T(8,128)(2,1)}, f16[2,2,96,3200]{3,2,1,0:T(8,128)(2,1)}, u32[]{:S(2)}, u32[]{:S(2)}) collective-permute-start(f16[2,2,96,3200]{3,2,1,0:T(8,128)(2,1)} %fusion.26), channel_id=1, source_target_pairs={{0,4},{4,0},{1,5},{5,1},{2,6},{6,2},{3,7},{7,3},{8,12},{12,8},{9,1... | collective-permute-start | bytes 7372808 | tf_op jit(solution)/shard_map/ppermute | solution.py:316
  575.1 53.3 %collective-permute-start.11 = (f16[2,2,96,3200]{3,2,1,0:T(8,128)(2,1)}, f16[2,2,96,3200]{3,2,1,0:T(8,128)(2,1)}, u32[]{:S(2)}, u32[]{:S(2)}) collective-permute-start(f16[2,2,96,3200]{3,2,1,0:T(8,128)(2,1)} %fusion.27), channel_id=1, source_target_pairs={{0,2},{2,0},{1,3},{3,1},{4,6},{6,4},{5,7},{7,5},{8,10},{10,8},{9,1... | collective-permute-start | bytes 7372808 | tf_op jit(solution)/shard_map/ppermute | solution.py:316
  600.5 31.8 %slice-start.2 = ((s8[9830400]{0:T(1024)(128)(4,1)}), s8[4194304]{0:T(1024)(128)(4,1)S(1)}, s32[]{:S(2)}) async-start(s8[9830400]{0:T(1024)(128)(4,1)} %bitcast.216), calls=%async_computation.8 | async-start | bytes 8388608
  600.5 31.8 %slice-start.3 = ((s8[9830400]{0:T(1024)(128)(4,1)}), s8[4194304]{0:T(1024)(128)(4,1)S(1)}, s32[]{:S(2)}) async-start(s8[9830400]{0:T(1024)(128)(4,1)} %bitcast.216), calls=%async_computation.9 | async-start | bytes 8388608
  605.4 26.9 %slice-start.4 = ((s8[9830400]{0:T(1024)(128)(4,1)}), s8[1441792]{0:T(1024)(128)(4,1)S(1)}, s32[]{:S(2)}) async-start(s8[9830400]{0:T(1024)(128)(4,1)} %bitcast.216), calls=%async_computation.10 | async-start | bytes 2883584
  637.5 31.5 %collective-permute-start.13 = (f16[2,96,3200]{2,1,0:T(8,128)(2,1)}, f16[2,96,3200]{2,1,0:T(8,128)(2,1)S(1)}, u32[]{:S(2)}, u32[]{:S(2)}) collective-permute-start(f16[2,96,3200]{2,1,0:T(8,128)(2,1)} %fusion.44), channel_id=1, source_target_pairs={{0,4},{4,0},{1,5},{5,1},{2,6},{6,2},{3,7},{7,3},{8,12},{12,8},{9,1... | collective-permute-start | bytes 3686408 | tf_op jit(solution)/shard_map/ppermute | solution.py:316
  639.0 30.0 %collective-permute-start.12 = (f16[2,96,3200]{2,1,0:T(8,128)(2,1)S(1)}, f16[2,96,3200]{2,1,0:T(8,128)(2,1)S(1)}, u32[]{:S(2)}, u32[]{:S(2)}) collective-permute-start(f16[2,96,3200]{2,1,0:T(8,128)(2,1)S(1)} %fusion.43), channel_id=1, source_target_pairs={{0,2},{2,0},{1,3},{3,1},{4,6},{6,4},{5,7},{7,5},{8,10},{10,8},{9,1... | collective-permute-start | bytes 3686408 | tf_op jit(solution)/shard_map/ppermute | solution.py:316
  690.7 10.8 %collective-permute-start.14 = (bf16[384,8448]{1,0:T(8,128)(2,1)}, bf16[384,8448]{1,0:T(8,128)(2,1)}, u32[]{:S(2)}, u32[]{:S(2)}) collective-permute-start(bf16[384,8448]{1,0:T(8,128)(2,1)} %dynamic-slice_bitcast_fusion), channel_id=1, source_target_pairs={{0,1},{1,0},{2,3},{3,2},{4,5},{5,4},{6,7},{7,6},{8,9},{9,8},{10,11... | collective-permute-start | bytes 19464200 | tf_op jit(solution)/shard_map/ppermute | solution.py:316
  721.9 17.2 %collective-permute-start.17 = (f16[96,3200]{1,0:T(8,128)(2,1)S(1)}, f16[96,3200]{1,0:T(8,128)(2,1)}, u32[]{:S(2)}, u32[]{:S(2)}) collective-permute-start(f16[96,3200]{1,0:T(8,128)(2,1)S(1)} %get-tuple-element.190), channel_id=1, source_target_pairs={{0,24},{8,0},{16,8},{24,16},{1,25},{9,1},{17,9},{25,17},{2,26},{10... | collective-permute-start | bytes 1843208 | tf_op jit(solution)/shard_map/ppermute | solution.py:316
  724.8 53.9 %collective-permute-start.16 = (f16[96,3200]{1,0:T(8,128)(2,1)S(1)}, f16[96,3200]{1,0:T(8,128)(2,1)}, u32[]{:S(2)}, u32[]{:S(2)}) collective-permute-start(f16[96,3200]{1,0:T(8,128)(2,1)S(1)} %get-tuple-element.191), channel_id=1, source_target_pairs={{0,16},{8,24},{16,0},{24,8},{1,17},{9,25},{17,1},{25,9},{2,18},{10... | collective-permute-start | bytes 1843208 | tf_op jit(solution)/shard_map/ppermute | solution.py:316
  725.2 53.5 %collective-permute-start.15 = (f16[96,3200]{1,0:T(8,128)(2,1)S(1)}, f16[96,3200]{1,0:T(8,128)(2,1)}, u32[]{:S(2)}, u32[]{:S(2)}) collective-permute-start(f16[96,3200]{1,0:T(8,128)(2,1)S(1)} %get-tuple-element.192), channel_id=1, source_target_pairs={{0,8},{8,16},{16,24},{24,0},{1,9},{9,17},{17,25},{25,1},{2,10},{10... | collective-permute-start | bytes 1843208 | tf_op jit(solution)/shard_map/ppermute | solution.py:316
  728.3 106.4 %copy-start.87 = (f32[32]{0:T(128)S(1)}, f32[32]{0:T(128)}, u32[]{:S(2)}) copy-start(f32[32]{0:T(128)} %get-tuple-element.207) | copy-start | bytes 388
  827.5 43.8 %collective-permute-start.20 = (bf16[24,8448]{1,0:T(8,128)(2,1)S(1)}, bf16[24,8448]{1,0:T(8,128)(2,1)S(1)}, u32[]{:S(2)}, u32[]{:S(2)}) collective-permute-start(bf16[24,8448]{1,0:T(8,128)(2,1)S(1)} %get-tuple-element.203), channel_id=1, source_target_pairs={{0,24},{8,0},{16,8},{24,16},{1,25},{9,1},{17,9},{25,17},{2,26},{10... | collective-permute-start | bytes 1216520 | tf_op jit(solution)/shard_map/ppermute | solution.py:316
  830.0 41.4 %collective-permute-start.19 = (bf16[24,8448]{1,0:T(8,128)(2,1)S(1)}, bf16[24,8448]{1,0:T(8,128)(2,1)S(1)}, u32[]{:S(2)}, u32[]{:S(2)}) collective-permute-start(bf16[24,8448]{1,0:T(8,128)(2,1)S(1)} %get-tuple-element.204), channel_id=1, source_target_pairs={{0,16},{8,24},{16,0},{24,8},{1,17},{9,25},{17,1},{25,9},{2,18},{10... | collective-permute-start | bytes 1216520 | tf_op jit(solution)/shard_map/ppermute | solution.py:316
  833.9 37.4 %collective-permute-start.18 = (bf16[24,8448]{1,0:T(8,128)(2,1)S(1)}, bf16[24,8448]{1,0:T(8,128)(2,1)S(1)}, u32[]{:S(2)}, u32[]{:S(2)}) collective-permute-start(bf16[24,8448]{1,0:T(8,128)(2,1)S(1)} %get-tuple-element.205), channel_id=1, source_target_pairs={{0,8},{8,16},{16,24},{24,0},{1,9},{9,17},{17,25},{25,1},{2,10},{10... | collective-permute-start | bytes 1216520 | tf_op jit(solution)/shard_map/ppermute | solution.py:316
  888.3 22.4 %copy-start.76 = (f32[4,24]{1,0:T(4,128)S(1)}, f32[4,24]{1,0:T(4,128)}, u32[]{:S(2)}) copy-start(f32[4,24]{1,0:T(4,128)} %param.38) | copy-start | bytes 1156
  888.3 22.4 %copy-start.84 = (f32[4,24]{1,0:T(4,128)S(1)}, f32[4,24]{1,0:T(4,128)}, u32[]{:S(2)}) copy-start(f32[4,24]{1,0:T(4,128)} %param.41) | copy-start | bytes 1156
  888.3 22.4 %copy-start.85 = (f32[4,24]{1,0:T(4,128)S(1)}, f32[4,24]{1,0:T(4,128)}, u32[]{:S(2)}) copy-start(f32[4,24]{1,0:T(4,128)} %param.40) | copy-start | bytes 1156
  888.3 22.5 %copy-start.86 = (f32[4,24]{1,0:T(4,128)S(1)}, f32[4,24]{1,0:T(4,128)}, u32[]{:S(2)}) copy-start(f32[4,24]{1,0:T(4,128)} %param.39) | copy-start | bytes 1156
  888.3 23.8 %copy-start.22 = (f32[24,1536]{1,0:T(8,128)S(1)}, f32[24,1536]{1,0:T(8,128)}, u32[]{:S(2)}) copy-start(f32[24,1536]{1,0:T(8,128)} %copy-done.21) | copy-start | bytes 442372
  912.1 21.0 %slice-start.5 = ((s8[4915200]{0:T(1024)(128)(4,1)}), s8[4194304]{0:T(1024)(128)(4,1)S(1)}, s32[]{:S(2)}) async-start(s8[4915200]{0:T(1024)(128)(4,1)} %bitcast.226), calls=%async_computation.11 | async-start | bytes 8388608
  (83 other events, 488.2 us)
Sparse Core Ops, SparseCore 0:
  38.4 155.7 all-gather.2
  196.7 97.7 all-gather.4
  481.3 69.9 reduce-scatter.2
  710.5 70.6 reduce-scatter.4

commit v7 on v6

--- a/solution.py
+++ b/solution.py
@@ -333,9 +333,21 @@
     return lax.dynamic_index_in_dim(values, index, dim, keepdims=False)
 
 
+def cut_parts(values, dim, axis):
+    me, n = lax.axis_index(axis), lax.axis_size(axis)
+    return pick(values, me, dim), [
+        pick(values, lax.rem(me + step, n), dim).astype(jnp.float16) for step in range(1, n)]
+
+
+def send_parts(parts, axis):
+    n = lax.axis_size(axis)
+    return [lax.ppermute(part, axis, [(i, (i + step) % n) for i in range(n)])
+            for step, part in enumerate(parts, 1)]
+
+
 def spread_parts(values, dim, axis):
-    got = exchange(lambda k: pick(values, k, dim).astype(jnp.float16), (axis,))
-    return pick(values, got[0][0], dim), [piece for _, piece in got[1:]]
+    own, parts = cut_parts(values, dim, axis)
+    return own, send_parts(parts, axis)
 
 
 def added(own, pieces):
@@ -349,10 +361,11 @@
 
     @pl.when(source == 0)
     def _():
-        @pl.loop(0, table_ref.shape[1] // LANES)
+        @pl.loop(0, table_ref.shape[1] // LANES // 5)
         def _(k):
-            at = pl.multiple_of(k * LANES, LANES)
-            turned_ref[pl.ds(at, LANES), :] = table_ref[:, pl.ds(at, LANES)].T
+            for i in range(5):
+                at = pl.multiple_of((k * 5 + i) * LANES, LANES)
+                turned_ref[pl.ds(at, LANES), :] = table_ref[:, pl.ds(at, LANES)].T
 
     low, high = low_ref[source], high_ref[source]
     rows_ref[...] = jnp.zeros_like(rows_ref)
@@ -452,13 +465,14 @@
 
     @pl.when(source == pl.num_programs(0) - 1)
     def _():
-        @pl.loop(0, out_ref.shape[1] // LANES)
+        @pl.loop(0, out_ref.shape[1] // LANES // 5)
         def _(k):
-            at = pl.multiple_of(k * LANES, LANES)
-            value = totals[0][pl.ds(at, LANES), :]
-            for total_ref in totals[1:]:
-                value = value + total_ref[pl.ds(at, LANES), :]
-            out_ref[:, pl.ds(at, LANES)] = value.T
+            for i in range(5):
+                at = pl.multiple_of((k * 5 + i) * LANES, LANES)
+                value = totals[0][pl.ds(at, LANES), :]
+                for total_ref in totals[1:]:
+                    value = value + total_ref[pl.ds(at, LANES), :]
+                out_ref[:, pl.ds(at, LANES)] = value.T
 
 
 def scatter_rows(rows, ids, low, high, table_rows):
@@ -902,6 +916,16 @@
     looked_up = gather_rows(embed_w.T, local_ids, low, high)
     looked_up = looked_up.reshape((ny, nc, nz * nx) + looked_up.shape[1:])
     x0_u = fetch_blocks(sizes, looked_up, 3).reshape(D, free_count).T.astype(F32)
+    group = nz * nc * score_count
+    row_targets = pick(jnp.moveaxis(jnp.moveaxis(all_targets, 3, 1), (2, 3), (0, 1)).reshape(
+        nx * ny, group), ix * ny + iy)
+    row_times = pick(jnp.moveaxis(jnp.moveaxis(all_times.reshape(nz, nx, ny, nc), 3, 1), (2, 3), (0, 1))
+                     .reshape(nx * ny, nz * nc), ix * ny + iy)
+    row_weights = jnp.repeat(TSTEPS / (row_times.astype(F32) + 1.0) / total_rows, score_count)
+    owner, within = row_targets // table_rows, row_targets % table_rows
+    owned = jnp.logical_and(owner % nc == ic, within // SEGMENT == iz)
+    column_of = jnp.where(owned, (owner // nc) * SEGMENT + within % SEGMENT, -1)[:, None]
+    x0_u, column_of, row_weights = together(x0_u, column_of, row_weights)
     senders = [sender for sender, _ in head_parts]
     x0_u, *pieces = together(x0_u, *[piece for _, piece in head_parts])
     head_part = in_order(list(zip(senders, pieces))).reshape(-1, SEGMENT)
@@ -936,21 +960,12 @@
 
     final_turned = jnp.swapaxes(final.reshape(score_count, nz, nx, -1), 1, 2).reshape(score_count, D)
     head_all = lax.all_gather(head_part, ("y", "x"), axis=0, tiled=True).reshape(ny, D, SEGMENT)
-    group = nz * nc * score_count
     blocks, places = [], []
     for sender, piece in exchange(lambda k: final_turned, ("z",)):
         for place, part in exchange(lambda k: piece, ("c",)):
             blocks.append(part)
             places.append(sender * nc + place)
     places = jnp.stack(places).astype(jnp.int32)
-    row_targets = pick(jnp.moveaxis(jnp.moveaxis(all_targets, 3, 1), (2, 3), (0, 1)).reshape(
-        nx * ny, group), ix * ny + iy)
-    row_times = pick(jnp.moveaxis(jnp.moveaxis(all_times.reshape(nz, nx, ny, nc), 3, 1), (2, 3), (0, 1))
-                     .reshape(nx * ny, nz * nc), ix * ny + iy)
-    row_weights = jnp.repeat(TSTEPS / (row_times.astype(F32) + 1.0) / total_rows, score_count)
-    owner, within = row_targets // table_rows, row_targets % table_rows
-    owned = jnp.logical_and(owner % nc == ic, within // SEGMENT == iz)
-    column_of = jnp.where(owned, (owner // nc) * SEGMENT + within % SEGMENT, -1)[:, None]
     e, stats, rows = head_logits(blocks, head_all, column_of, places)
     top = stats[:, 0]
     every = share(("z", "c"), 4, stats.T.reshape(4, -1, LANES))[0].reshape(nz * nc, 4, group)
@@ -969,10 +984,12 @@
     bound = bound * score_count * jnp.sum(TSTEPS / (all_times.astype(F32) + 1.0) / total_rows)
     enlarge = 60000.0 / jnp.maximum(bound, 1e-30)
     d_head = jnp.einsum("rd,yrv->ydv", rows, d_logits, preferred_element_type=F32) * enlarge
-    d_final, d_head = together(d_final, d_head.reshape(ny, nx, nz, -1, SEGMENT))
+    d_head = d_head.reshape(ny, nx, nz, -1, SEGMENT)
     cut = nz // 2
-    own_x, from_x = spread_parts(d_head[:, :, :cut], 1, "x")
-    own_y, from_y = spread_parts(d_head[:, :, cut:], 0, "y")
+    own_x, to_x = cut_parts(d_head[:, :, :cut], 1, "x")
+    own_y, to_y = cut_parts(d_head[:, :, cut:], 0, "y")
+    d_final, *to_xy = together(d_final, *to_x, *to_y)
+    from_x, from_y = send_parts(to_xy[: nx - 1], "x"), send_parts(to_xy[nx - 1 :], "y")
     d_final = d_final.astype(F32)
     d_final = jnp.swapaxes(d_final.reshape(score_count, nx, nz, -1), 1, 2).reshape(score_count, D)
 

time: 963 us -> 943 us (0.979)
    ppermute x0 -> x7, waiting for transfers between devices: none -> 76.5 us  [send_parts(): lax.ppermute(part, axis, [(i, (i + step) % n) for i in range(n)])]
    ppermute x21 -> x14, waiting for transfers between devices: 140 us -> 77 us  [exchange(): moved = lax.ppermute(piece, axes, [(i, (i + step) % n) for i in range(n)])]
    reduce_scatter x1, waiting for transfers between devices: 16.1 us -> 0.01 us  [local(): lax.psum_scatter(d_rows, ('z', 'c'), scatter_dimension=0, tiled=True)]
    pallas_call x1, Pallas kernels: 56.2 us -> 67.7 us  [head_rows_back(): pl.pallas_call(rows_back_kernel, out_shape=[jax.ShapeDtypeStruct(e.shape,...]
    ppermute x21 -> x14, starting transfers between devices: 24.8 us -> 16.2 us  [exchange(): moved = lax.ppermute(piece, axes, [(i, (i + step) % n) for i in range(n)])]
  transfers between devices with their start and end apart: 25 -> 25, of which waited for: 9 -> 11; matrix products, arithmetic and copies ran while one was open for 18% -> 20% of each run, Pallas kernels for 23% -> 22%
where the time goes in v7:
time: 943 us; the launch traced here: 934 us
  Pallas kernels  388 us (41%)
  waiting for transfers between devices  183 us (19%)
  matrix products  118 us (13%)
  other arithmetic  112 us (12%)
  local copies, waits for them, and re-layouts  81.9 us (9%)
  between operations  27.1 us (3%)
  starting transfers between devices  24 us (3%)
    ppermute x14, waiting for transfers between devices, exchange(): moved = lax.ppermute(piece, axes, [(i, (i + step) % n) for i in range(n)])  77 us
    ppermute x7, waiting for transfers between devices, send_parts(): lax.ppermute(part, axis, [(i, (i + step) % n) for i in range(n)])  76.5 us
    pallas_call x1, Pallas kernels, head_logits(): pl.pallas_call(logits_kernel, out_shape=[jax.ShapeDtypeStruct((segments,...  73.2 us
    pallas_call x1, Pallas kernels, head_rows_back(): pl.pallas_call(rows_back_kernel, out_shape=[jax.ShapeDtypeStruct(e.shape,...  67.7 us
    dot_general x15, matrix products, dot(): lax.dot_general(a, b, ((contract[0], contract[1]), ((), ())), preferred_e...  65.1 us
    pallas_call x1, Pallas kernels, fetch_blocks(): pl.pallas_call(functools.partial(fetch_kernel, sizes), out_shape=jax.Shap...  59.1 us
    dot_general x1, matrix products, local(): jnp.einsum('rd,yrv->ydv', rows, d_logits, preferred_element_type=F32)  50.6 us
    pallas_call x1, Pallas kernels, spread_blocks(): pl.pallas_call(functools.partial(spread_kernel, sizes), out_shape=[jax.Sh...  47.8 us
  transfers between devices with their start and end apart: 25, of which 11 were waited for; matrix products, arithmetic and copies ran while one was open for 20% of the time, Pallas kernels for 22%

profile of v7, /device:TPU:0, one launch (start us, length us, event | category | flops | bytes accessed | tf_op | source)
XLA Modules:
  0.0 933.9 jit_solution(453623908513617382)
XLA Ops:
  16.8 2.6 convert_element_type.257
  19.5 18.0 %share0.1 = (s32[4,2,2,2,16,128]{5,4,3,2,1,0:T(8,128)}, f32[4,2,2,2,8,128]{5,4,3,2,1,0:T(8,128)}) custom-call(s32[16,128]{1,0:T(8,128)} %pad.18.refs_0_, f32[8,128]{1,0:T(8,128)} %pad_convert_fusion.refs_1_), custom_call_target="tpu_custom_call" | custom-call | tf_op jit(solution)/shard_map/share0/pallas_call | solution.py:104
  39.8 3.3 collective-permute-start.2
  53.2 25.4 %gather_rows.1 = bf16[32,96,512]{2,1,0:T(8,128)(2,1)} custom-call(s32[32]{0:T(128)} %reduce_sum.395.low_ref, s32[32]{0:T(128)} %reduce_sum.397.high_ref, s32[32,512]{1,0:T(8,128)} %bitcast.249, f32[96,12800]{1,0:T(8,128)} %bitcast.218), custom_call_target="tpu_custom_call" | custom-call | bytes 134217728 | tf_op jit(solution)/shard_map/gather_rows/pallas_call | solution.py:403
  78.6 59.1 %fetch_blocks.1 = bf16[8,96,512]{2,1,0:T(8,128)(2,1)} custom-call(bf16[2,2,8,96,512]{4,3,2,1,0:T(8,128)(2,1)} %bitcast.223), custom_call_target="tpu_custom_call" | custom-call | bytes 134217728 | tf_op jit(solution)/shard_map/fetch_blocks/pallas_call | solution.py:194
  139.6 7.9 fusion.32.target_ref
  164.6 29.6 %all-gather.3.cloned.1.call-done = bf16[768,9984]{1,0:T(8,128)(2,1)} async-done(((bf16[24,9984]{1,0:T(8,128)(2,1)}), bf16[768,9984]{1,0:T(8,128)(2,1)}) %all-gather.3.cloned.1.call-update) | async-done | bytes 15335440 | tf_op jit(solution)/shard_map/all_gather | solution.py:898
  199.8 3.7 fusion.22.qm_ref.km_ref.vm_ref
  203.5 5.2 fusion.40.kv_ref.vv_ref
  209.3 18.5 %attend.1 = (bf16[512,768]{1,0:T(8,128)(2,1)}, bf16[512,768]{1,0:T(8,128)(2,1)}, bf16[512,768]{1,0:T(8,128)(2,1)}, bf16[512,768]{1,0:T(8,128)(2,1)}, f32[6,512,2]{2,1,0:T(8,128)}) custom-call(f32[512,1536]{1,0:T(8,128)} %fusion.40.kv_ref.vv_ref, f32[512,1536]{1,0:T(8,128)} %fusion.40.kv_ref.vv_ref, f32[16,2304]{1,0:T(8,128)} %fusion.22.qm_ref.km_ref.vm_ref, ...), custom_call_target="tpu_custom_call" | custom-call | flops 1207959552 | bytes 4718592 | tf_op jit(solution)/shard_map/attend/pallas_call | solution.py:555
  230.6 5.1 fusion.18
  235.8 10.1 %fusion.110 = (f32[512]{0:T(512)S(1)}, f32[512,768]{1,0:T(8,128)S(1)}, f32[512,768]{1,0:T(8,128)}) fusion(f32[768]{0:T(1024)S(1)} %get-tuple-element.157, f32[512,768]{1,0:T(8,128)S(1)} %get-tuple-element.246, f32[768]{0:T(1024)S(1)} %get-tuple-element.158, f32[768]{0:T(1024)S(1)} %add.567, bf16[768,9984]{1,0:T(8,128)(2,1)} %all-gather.3.cloned.1.call-done, ...), kind=kOutput, calls=%fused_computation.335 | convolution fusion | flops 2432040448 | bytes 15739904 | tf_op jit(solution)/shard_map/dot_general | solution.py:39
  250.8 17.8 %collective-permute-done.8.refs_6_ = bf16[512,768]{1,0:T(8,128)(2,1)S(1)} collective-permute-done((bf16[512,768]{1,0:T(8,128)(2,1)S(1)}, bf16[512,768]{1,0:T(8,128)(2,1)S(1)}, u32[]{:S(2)}, u32[]{:S(2)}) %collective-permute-start.8) | collective-permute-done | bytes 786464 | tf_op jit(solution)/shard_map/ppermute | solution.py:316
  268.7 48.9 %collective-permute-done.6.refs_4_ = bf16[512,768]{1,0:T(8,128)(2,1)S(1)} collective-permute-done((bf16[512,768]{1,0:T(8,128)(2,1)S(1)}, bf16[512,768]{1,0:T(8,128)(2,1)S(1)}, u32[]{:S(2)}, u32[]{:S(2)}) %collective-permute-start.6) | collective-permute-done | bytes 786464 | tf_op jit(solution)/shard_map/ppermute | solution.py:316
  321.3 73.2 %head_logits.1 = (bf16[2,4096,3200]{2,1,0:T(8,128)(2,1)}, f32[4096,4]{1,0:T(8,128)}, bf16[4096,768]{1,0:T(8,128)(2,1)}) custom-call(s32[8]{0:T(128)} %stack.50.places_ref, bf16[2,768,3200]{2,1,0:T(8,128)(2,1)} %bitcast.273, s32[4096,1]{1,0:T(8,128)} %fusion.32.target_ref, bf16[512,768]{1,0:T(8,128)(2,1)} %copy-done.25, ...), custom_call_target="tpu_custom_call" | custom-call | flops 40265318400 | bytes 52428800 | tf_op jit(solution)/shard_map/head_logits/pallas_call | solution.py:709
  398.1 11.5 %share4.1 = f32[4,2,4,32,128]{4,3,2,1,0:T(8,128)} custom-call(f32[4,32,128]{2,1,0:T(8,128)} %copy.225.refs_0_), custom_call_target="tpu_custom_call" | custom-call | tf_op jit(solution)/shard_map/share4/pallas_call | solution.py:104
  413.5 67.7 %head_rows_back.1 = (bf16[2,4096,3200]{2,1,0:T(8,128)(2,1)}, bf16[4096,768]{1,0:T(8,128)(2,1)}) custom-call(s32[8]{0:T(128)} %stack.50.places_ref, bf16[2,4096,3200]{2,1,0:T(8,128)(2,1)} %get-tuple-element.96.e_ref, bf16[2,768,3200]{2,1,0:T(8,128)(2,1)} %bitcast.274, s32[4096,1]{1,0:T(8,128)} %fusion.32.target_ref, ...), custom_call_target="tpu_custom_call", output_to_operand_aliasing={{0}: (1, {})} | custom-call | flops 40265318400 | bytes 104857600 | tf_op jit(solution)/shard_map/head_rows_back/pallas_call | solution.py:771
  484.4 50.6 %convolution_multiply_fusion = f32[2,3200,768]{1,2,0:T(8,128)} fusion(bf16[2,4096,3200]{2,1,0:T(8,128)(2,1)} %get-tuple-element.100, f32[]{:T(128)S(6)} %div.269, bf16[4096,768]{1,0:T(8,128)(2,1)} %get-tuple-element.101), kind=kOutput, calls=%fused_computation | convolution fusion | flops 40270233600 | bytes 78381056 | tf_op jit(solution)/shard_map/rd,yrv->ydv/dot_general | solution.py:986
  535.0 7.8 fusion.111
  542.8 3.7 copy-done.2
  546.5 2.5 fusion.27
  560.5 9.3 fusion.7
  569.9 6.5 multiply_reduce_fusion.4
  581.8 3.1 convolution_convert_fusion.4.datt_ref
  585.0 4.7 convolution_convert_fusion.1
  589.7 24.0 %collective-permute-done.10 = f16[2,2,96,3200]{3,2,1,0:T(8,128)(2,1)} collective-permute-done((f16[2,2,96,3200]{3,2,1,0:T(8,128)(2,1)}, f16[2,2,96,3200]{3,2,1,0:T(8,128)(2,1)}, u32[]{:S(2)}, u32[]{:S(2)}) %collective-permute-start.10) | collective-permute-done | bytes 2457632 | tf_op jit(solution)/shard_map/ppermute | solution.py:344
  614.9 3.8 bitcast_add_fusion.3
  618.9 4.0 bitcast_add_fusion.2
  626.1 4.8 convolution_convert_fusion
  630.9 23.9 %attend_back.1 = (bf16[512,768]{1,0:T(8,128)(2,1)}, bf16[512,768]{1,0:T(8,128)(2,1)}, f32[8,768]{1,0:T(8,128)}) custom-call(bf16[512,768]{1,0:T(8,128)(2,1)} %get-tuple-element.86.q_ref, bf16[512,768]{1,0:T(8,128)(2,1)} %get-tuple-element.87.ku_ref, bf16[512,768]{1,0:T(8,128)(2,1)} %get-tuple-element.88.km_ref, f32[512,1536]{1,0:T(8,128)} %fusion.40.kv_ref.vv_ref, ...), custom_call_target="tpu_custom_call" | custom-call | flops 3221225472 | bytes 5505024 | tf_op jit(solution)/shard_map/attend_back/pallas_call | solution.py:627
  658.3 2.6 pad_maximum_fusion.1
  666.4 3.0 copy.222
  669.5 3.4 dynamic-slice_bitcast_fusion
  672.9 3.1 copy-done
  676.0 3.4 multiply_reduce_fusion.6
  681.1 5.7 collective-permute-done.14
  686.8 8.9 fusion
  697.2 3.1 fusion.45
  703.0 3.7 dynamic-slice_bitcast_fusion.1
  711.5 11.8 %collective-permute-done.17 = f16[96,3200]{1,0:T(8,128)(2,1)} collective-permute-done((f16[96,3200]{1,0:T(8,128)(2,1)S(1)}, f16[96,3200]{1,0:T(8,128)(2,1)}, u32[]{:S(2)}, u32[]{:S(2)}) %collective-permute-start.17) | collective-permute-done | bytes 614432 | tf_op jit(solution)/shard_map/ppermute | solution.py:344
  723.4 39.5 %collective-permute-done.16 = f16[96,3200]{1,0:T(8,128)(2,1)} collective-permute-done((f16[96,3200]{1,0:T(8,128)(2,1)S(1)}, f16[96,3200]{1,0:T(8,128)(2,1)}, u32[]{:S(2)}, u32[]{:S(2)}) %collective-permute-start.16) | collective-permute-done | bytes 614432 | tf_op jit(solution)/shard_map/ppermute | solution.py:344
  762.8 47.8 %spread_blocks.1 = (bf16[2,2,8,96,512]{4,3,2,1,0:T(8,128)(2,1)}, f32[4,2,2,2,88,128]{5,4,3,2,1,0:T(8,128)}) custom-call(bf16[8,96,512]{2,1,0:T(8,128)(2,1)} %bitcast.237, f32[88,128]{1,0:T(8,128)} %pad.22.small_ref), custom_call_target="tpu_custom_call" | custom-call | bytes 134217728 | tf_op jit(solution)/shard_map/spread_blocks/pallas_call | solution.py:280
  812.3 6.5 collective-permute-start.19
  821.7 30.9 %scatter_rows.1 = f32[96,12800]{1,0:T(8,128)} custom-call(s32[32]{0:T(128)} %reduce_sum.395.low_ref, s32[32]{0:T(128)} %reduce_sum.397.high_ref, s32[32,512]{1,0:T(8,128)} %bitcast.250, bf16[32,96,512]{2,1,0:T(8,128)(2,1)} %bitcast.236), custom_call_target="tpu_custom_call" | custom-call | bytes 134217728 | tf_op jit(solution)/shard_map/scatter_rows/pallas_call | solution.py:480
  874.8 12.0 %share2.1 = f32[4,2,2,2,8,128]{5,4,3,2,1,0:T(8,128)} custom-call(f32[8,128]{1,0:T(8,128)} %broadcast_in_dim.144.refs_0_), custom_call_target="tpu_custom_call" | custom-call | tf_op jit(solution)/shard_map/share2/pallas_call | solution.py:104
  890.5 4.4 multiply_add_fusion.5
  894.9 16.5 %multiply_add_fusion = (f32[96,12800]{1,0:T(8,128)}, f32[96,12800]{1,0:T(8,128)}, f32[96,12800]{1,0:T(8,128)}, f32[96,12800]{1,0:T(8,128)}) fusion(f32[96,12800]{1,0:T(8,128)} %param.49, f32[]{:T(128)} %bitcast.91, f32[]{:T(128)S(6)} %sub.303, f32[96,12800]{1,0:T(8,128)} %param.46, f32[]{:T(128)} %bitcast.90, f32[]{:T(128)} %bitcast.89, f32[]{:T(128)S(6)} %min.13, ...), kind=kLoop, calls=%fused_computation.29 | loop fusion | flops 28262400 | bytes 44236824 | tf_op jit(solution)/shard_map/add | solution.py:847
  911.6 13.6 %fusion.11 = (f32[12800,96]{0,1:T(8,128)}, f32[96,12800]{1,0:T(8,128)}, f32[12800,96]{0,1:T(8,128)}, f32[12800,96]{0,1:T(8,128)}) fusion(f32[12800,96]{0,1:T(8,128)} %param.45, f32[]{:T(128)S(6)} %sub.303, f32[]{:T(128)} %bitcast.91, f32[]{:T(128)} %bitcast.90, f32[12800,96]{0,1:T(8,128)} %param.44, f32[]{:T(128)} %bitcast.89, f32[96,12800]{1,0:T(8,128)S(1)} %bitcast.208, ...), kind=kLoop, calls=%fused_computation.25 | loop fusion | flops 23347200 | bytes 44236820 | tf_op jit(solution)/shard_map/transpose | solution.py:1111
  (445 shorter events, 130.8 us)
Async XLA Ops:
  7.2 187.0 %all-gather.3.cloned.1.call-start = ((), (), s32[]{:S(2)}) async-start(), calls=%async_computation.2 | async-start | bytes 15814656 | tf_op jit(solution)/shard_map/all_gather | solution.py:898
  38.3 280.5 %all-gather.5.cloned.1.call-start = ((), (), s32[]{:S(2)}) async-start(), calls=%async_computation.3 | async-start | bytes 12288000 | tf_op jit(solution)/shard_map/all_gather | solution.py:962
  39.8 107.6 %collective-permute-start.2 = (bf16[96,3200]{1,0:T(8,128)(2,1)}, bf16[96,3200]{1,0:T(8,128)(2,1)}, u32[]{:S(2)}, u32[]{:S(2)}) collective-permute-start(bf16[96,3200]{1,0:T(8,128)(2,1)} %get-tuple-element.207), channel_id=1, source_target_pairs={{0,24},{8,0},{16,8},{24,16},{1,25},{9,1},{17,9},{25,17},{2,26},{10... | collective-permute-start | bytes 1843208 | tf_op jit(solution)/shard_map/ppermute | solution.py:316
  43.1 104.3 %collective-permute-start.1 = (bf16[96,3200]{1,0:T(8,128)(2,1)}, bf16[96,3200]{1,0:T(8,128)(2,1)}, u32[]{:S(2)}, u32[]{:S(2)}) collective-permute-start(bf16[96,3200]{1,0:T(8,128)(2,1)} %get-tuple-element.208), channel_id=1, source_target_pairs={{0,16},{8,24},{16,0},{24,8},{1,17},{9,25},{17,1},{25,9},{2,18},{10... | collective-permute-start | bytes 1843208 | tf_op jit(solution)/shard_map/ppermute | solution.py:316
  43.1 104.3 %collective-permute-start = (bf16[96,3200]{1,0:T(8,128)(2,1)}, bf16[96,3200]{1,0:T(8,128)(2,1)}, u32[]{:S(2)}, u32[]{:S(2)}) collective-permute-start(bf16[96,3200]{1,0:T(8,128)(2,1)} %get-tuple-element.209), channel_id=1, source_target_pairs={{0,8},{8,16},{16,24},{24,0},{1,9},{9,17},{17,25},{25,1},{2,10},{10... | collective-permute-start | bytes 1843208 | tf_op jit(solution)/shard_map/ppermute | solution.py:316
  49.1 362.3 %copy-start.33 = (f32[1,4,8,128]{3,1,2,0:T(4,128)}, f32[1,4,8,128]{3,1,2,0:T(4,128)S(1)}, u32[]{:S(2)}) copy-start(f32[1,4,8,128]{3,1,2,0:T(4,128)S(1)} %copy.231) | copy-start | bytes 49156
  139.5 64.0 %copy-start.4 = (f32[768,512]{0,1:T(8,128)}, f32[768,512]{0,1:T(8,128)S(1)}, u32[]{:S(2)}) copy-start(f32[768,512]{0,1:T(8,128)S(1)} %copy.185) | copy-start | bytes 4718596
  155.8 396.4 %reduce-scatter.3.cloned.1.call-start = ((), (), s32[]{:S(2)}) async-start(), calls=%async_computation.4 | async-start | bytes 7077888 | tf_op jit(solution)/shard_map/reduce_scatter | solution.py:981
  158.0 41.1 %copy-start.48 = (f32[1,768]{1,0:T(1,128)}, f32[1,768]{1,0:T(1,128)S(1)}, u32[]{:S(2)}) copy-start(f32[1,768]{1,0:T(1,128)S(1)} %slice.145) | copy-start | bytes 9220
  158.1 45.4 %copy-start.69 = (f32[768]{0:T(1024)}, f32[768]{0:T(1024)S(1)}, u32[]{:S(2)}) copy-start(f32[768]{0:T(1024)S(1)} %mul.851) | copy-start | bytes 9220
  158.3 72.3 %copy-start.67 = (f32[768]{0:T(1024)}, f32[768]{0:T(1024)S(1)}, u32[]{:S(2)}) copy-start(f32[768]{0:T(1024)S(1)} %mul.881) | copy-start | bytes 9220
  159.8 39.4 %copy-start.50 = (f32[1,768]{1,0:T(1,128)}, f32[1,768]{1,0:T(1,128)S(1)}, u32[]{:S(2)}) copy-start(f32[1,768]{1,0:T(1,128)S(1)} %mul.865) | copy-start | bytes 9220
  159.9 75.9 %copy-start.42 = (f32[768]{0:T(1024)}, f32[768]{0:T(1024)S(1)}, u32[]{:S(2)}) copy-start(f32[768]{0:T(1024)S(1)} %add.567) | copy-start | bytes 9220
  160.0 86.3 %copy-start.40 = (f32[768]{0:T(1024)}, f32[768]{0:T(1024)S(1)}, u32[]{:S(2)}) copy-start(f32[768]{0:T(1024)S(1)} %mul.899) | copy-start | bytes 9220
  164.3 39.3 %copy-start.56 = (f32[512]{0:T(512)}, f32[512]{0:T(512)S(1)}, u32[]{:S(2)}) copy-start(f32[512]{0:T(512)S(1)} %broadcast_multiply_fusion.8) | copy-start | bytes 6148
  164.6 38.9 %copy-start.72 = (f32[512]{0:T(512)}, f32[512]{0:T(512)S(1)}, u32[]{:S(2)}) copy-start(f32[512]{0:T(512)S(1)} %add_rsqrt_fusion.2) | copy-start | bytes 6148
  199.8 30.8 %copy-start.63 = (f32[768]{0:T(1024)}, f32[768]{0:T(1024)S(1)}, u32[]{:S(2)}) copy-start(f32[768]{0:T(1024)S(1)} %get-tuple-element.156) | copy-start | bytes 9220
  199.8 30.8 %copy-start.83 = (f32[768]{0:T(1024)}, f32[768]{0:T(1024)S(1)}, u32[]{:S(2)}) copy-start(f32[768]{0:T(1024)S(1)} %get-tuple-element.161) | copy-start | bytes 9220
  199.8 36.0 %copy-start.44 = (f32[768]{0:T(1024)}, f32[768]{0:T(1024)S(1)}, u32[]{:S(2)}) copy-start(f32[768]{0:T(1024)S(1)} %get-tuple-element.158) | copy-start | bytes 9220
  199.8 36.0 %copy-start.81 = (f32[768]{0:T(1024)}, f32[768]{0:T(1024)S(1)}, u32[]{:S(2)}) copy-start(f32[768]{0:T(1024)S(1)} %get-tuple-element.157) | copy-start | bytes 9220
  248.0 73.3 %copy-start.25 = (bf16[512,768]{1,0:T(8,128)(2,1)}, bf16[512,768]{1,0:T(8,128)(2,1)S(1)}, u32[]{:S(2)}) copy-start(bf16[512,768]{1,0:T(8,128)(2,1)S(1)} %copy.207.refs_0_) | copy-start | bytes 2359300
  248.0 20.7 %collective-permute-start.8 = (bf16[512,768]{1,0:T(8,128)(2,1)S(1)}, bf16[512,768]{1,0:T(8,128)(2,1)S(1)}, u32[]{:S(2)}, u32[]{:S(2)}) collective-permute-start(bf16[512,768]{1,0:T(8,128)(2,1)S(1)} %copy.207.refs_0_), channel_id=1, source_target_pairs={{0,24},{8,0},{16,8},{24,16},{1,25},{9,1},{17,9},{25,17},{2,26},{10... | collective-permute-start | bytes 2359304 | tf_op jit(solution)/shard_map/ppermute | solution.py:316
  248.7 68.8 %collective-permute-start.6 = (bf16[512,768]{1,0:T(8,128)(2,1)S(1)}, bf16[512,768]{1,0:T(8,128)(2,1)S(1)}, u32[]{:S(2)}, u32[]{:S(2)}) collective-permute-start(bf16[512,768]{1,0:T(8,128)(2,1)S(1)} %copy.207.refs_0_), channel_id=1, source_target_pairs={{0,16},{8,24},{16,0},{24,8},{1,17},{9,25},{17,1},{25,9},{2,18},{10... | collective-permute-start | bytes 2359304 | tf_op jit(solution)/shard_map/ppermute | solution.py:316
  249.3 68.2 %collective-permute-start.4 = (bf16[512,768]{1,0:T(8,128)(2,1)S(1)}, bf16[512,768]{1,0:T(8,128)(2,1)}, u32[]{:S(2)}, u32[]{:S(2)}) collective-permute-start(bf16[512,768]{1,0:T(8,128)(2,1)S(1)} %copy.207.refs_0_), channel_id=1, source_target_pairs={{0,8},{8,16},{16,24},{24,0},{1,9},{9,17},{17,25},{25,1},{2,10},{10... | collective-permute-start | bytes 2359304 | tf_op jit(solution)/shard_map/ppermute | solution.py:316
  250.8 67.9 %collective-permute-start.3 = (bf16[512,768]{1,0:T(8,128)(2,1)S(1)}, bf16[512,768]{1,0:T(8,128)(2,1)}, u32[]{:S(2)}, u32[]{:S(2)}) collective-permute-start(bf16[512,768]{1,0:T(8,128)(2,1)S(1)} %copy.207.refs_0_), channel_id=1, source_target_pairs={{0,1},{1,0},{2,3},{3,2},{4,5},{5,4},{6,7},{7,6},{8,9},{9,8},{10,11... | collective-permute-start | bytes 2359304 | tf_op jit(solution)/shard_map/ppermute | solution.py:316
  268.7 52.6 %copy-start.89 = (bf16[512,768]{1,0:T(8,128)(2,1)}, bf16[512,768]{1,0:T(8,128)(2,1)S(1)}, u32[]{:S(2)}) copy-start(bf16[512,768]{1,0:T(8,128)(2,1)S(1)} %collective-permute-done.8.refs_6_) | copy-start | bytes 2359300
  268.7 50.1 %collective-permute-start.9 = (bf16[512,768]{1,0:T(8,128)(2,1)S(1)}, bf16[512,768]{1,0:T(8,128)(2,1)}, u32[]{:S(2)}, u32[]{:S(2)}) collective-permute-start(bf16[512,768]{1,0:T(8,128)(2,1)S(1)} %collective-permute-done.8.refs_6_), channel_id=1, source_target_pairs={{0,1},{1,0},{2,3},{3,2},{4,5},{5,4},{6,7},{7,6},{8,9},{9,8},{10,11... | collective-permute-start | bytes 2359304 | tf_op jit(solution)/shard_map/ppermute | solution.py:316
  317.5 2.8 collective-permute-start.7
  317.6 3.7 collective-permute-start.5
  411.2 70.0 %copy-start.35 = (f32[4096]{0:T(1024)}, f32[4096]{0:T(1024)S(1)}, u32[]{:S(2)}) copy-start(f32[4096]{0:T(1024)S(1)} %get-tuple-element.149) | copy-start | bytes 49156
  411.4 69.8 %copy-start.36 = (f32[4096]{0:T(1024)}, f32[4096]{0:T(1024)S(1)}, u32[]{:S(2)}) copy-start(f32[4096]{0:T(1024)S(1)} %get-tuple-element.192) | copy-start | bytes 49156
  481.2 329.4 %reduce-scatter.5.cloned.1.call-start = ((), (), s32[]{:S(2)}) async-start(), calls=%async_computation.5 | async-start | bytes 8110080 | tf_op jit(solution)/shard_map/reduce_scatter | solution.py:1021
  557.7 56.0 %collective-permute-start.10 = (f16[2,2,96,3200]{3,2,1,0:T(8,128)(2,1)}, f16[2,2,96,3200]{3,2,1,0:T(8,128)(2,1)}, u32[]{:S(2)}, u32[]{:S(2)}) collective-permute-start(f16[2,2,96,3200]{3,2,1,0:T(8,128)(2,1)} %fusion.26), channel_id=1, source_target_pairs={{0,4},{4,0},{1,5},{5,1},{2,6},{6,2},{3,7},{7,3},{8,12},{12,8},{9,1... | collective-permute-start | bytes 7372808 | tf_op jit(solution)/shard_map/ppermute | solution.py:344
  559.3 55.6 %collective-permute-start.11 = (f16[2,2,96,3200]{3,2,1,0:T(8,128)(2,1)}, f16[2,2,96,3200]{3,2,1,0:T(8,128)(2,1)}, u32[]{:S(2)}, u32[]{:S(2)}) collective-permute-start(f16[2,2,96,3200]{3,2,1,0:T(8,128)(2,1)} %fusion.27), channel_id=1, source_target_pairs={{0,2},{2,0},{1,3},{3,1},{4,6},{6,4},{5,7},{7,5},{8,10},{10,8},{9,1... | collective-permute-start | bytes 7372808 | tf_op jit(solution)/shard_map/ppermute | solution.py:344
  585.0 33.9 %slice-start.2 = ((s8[9830400]{0:T(1024)(128)(4,1)}), s8[4194304]{0:T(1024)(128)(4,1)S(1)}, s32[]{:S(2)}) async-start(s8[9830400]{0:T(1024)(128)(4,1)} %bitcast.209), calls=%async_computation.8 | async-start | bytes 8388608
  585.0 33.9 %slice-start.3 = ((s8[9830400]{0:T(1024)(128)(4,1)}), s8[4194304]{0:T(1024)(128)(4,1)S(1)}, s32[]{:S(2)}) async-start(s8[9830400]{0:T(1024)(128)(4,1)} %bitcast.209), calls=%async_computation.9 | async-start | bytes 8388608
  589.7 29.1 %slice-start.4 = ((s8[9830400]{0:T(1024)(128)(4,1)}), s8[1441792]{0:T(1024)(128)(4,1)S(1)}, s32[]{:S(2)}) async-start(s8[9830400]{0:T(1024)(128)(4,1)} %bitcast.209), calls=%async_computation.10 | async-start | bytes 2883584
  624.1 30.7 %collective-permute-start.13 = (f16[2,96,3200]{2,1,0:T(8,128)(2,1)}, f16[2,96,3200]{2,1,0:T(8,128)(2,1)S(1)}, u32[]{:S(2)}, u32[]{:S(2)}) collective-permute-start(f16[2,96,3200]{2,1,0:T(8,128)(2,1)} %fusion.44), channel_id=1, source_target_pairs={{0,4},{4,0},{1,5},{5,1},{2,6},{6,2},{3,7},{7,3},{8,12},{12,8},{9,1... | collective-permute-start | bytes 3686408 | tf_op jit(solution)/shard_map/ppermute | solution.py:344
  624.6 30.1 %collective-permute-start.12 = (f16[2,96,3200]{2,1,0:T(8,128)(2,1)S(1)}, f16[2,96,3200]{2,1,0:T(8,128)(2,1)S(1)}, u32[]{:S(2)}, u32[]{:S(2)}) collective-permute-start(f16[2,96,3200]{2,1,0:T(8,128)(2,1)S(1)} %fusion.43), channel_id=1, source_target_pairs={{0,2},{2,0},{1,3},{3,1},{4,6},{6,4},{5,7},{7,5},{8,10},{10,8},{9,1... | collective-permute-start | bytes 3686408 | tf_op jit(solution)/shard_map/ppermute | solution.py:344
  676.0 10.8 %collective-permute-start.14 = (bf16[384,8448]{1,0:T(8,128)(2,1)}, bf16[384,8448]{1,0:T(8,128)(2,1)}, u32[]{:S(2)}, u32[]{:S(2)}) collective-permute-start(bf16[384,8448]{1,0:T(8,128)(2,1)} %dynamic-slice_bitcast_fusion), channel_id=1, source_target_pairs={{0,1},{1,0},{2,3},{3,2},{4,5},{5,4},{6,7},{7,6},{8,9},{9,8},{10,11... | collective-permute-start | bytes 19464200 | tf_op jit(solution)/shard_map/ppermute | solution.py:316
  706.7 16.7 %collective-permute-start.17 = (f16[96,3200]{1,0:T(8,128)(2,1)S(1)}, f16[96,3200]{1,0:T(8,128)(2,1)}, u32[]{:S(2)}, u32[]{:S(2)}) collective-permute-start(f16[96,3200]{1,0:T(8,128)(2,1)S(1)} %get-tuple-element.200), channel_id=1, source_target_pairs={{0,24},{8,0},{16,8},{24,16},{1,25},{9,1},{17,9},{25,17},{2,26},{10... | collective-permute-start | bytes 1843208 | tf_op jit(solution)/shard_map/ppermute | solution.py:344
  709.1 53.8 %collective-permute-start.16 = (f16[96,3200]{1,0:T(8,128)(2,1)S(1)}, f16[96,3200]{1,0:T(8,128)(2,1)}, u32[]{:S(2)}, u32[]{:S(2)}) collective-permute-start(f16[96,3200]{1,0:T(8,128)(2,1)S(1)} %get-tuple-element.201), channel_id=1, source_target_pairs={{0,16},{8,24},{16,0},{24,8},{1,17},{9,25},{17,1},{25,9},{2,18},{10... | collective-permute-start | bytes 1843208 | tf_op jit(solution)/shard_map/ppermute | solution.py:344
  709.4 53.5 %collective-permute-start.15 = (f16[96,3200]{1,0:T(8,128)(2,1)S(1)}, f16[96,3200]{1,0:T(8,128)(2,1)}, u32[]{:S(2)}, u32[]{:S(2)}) collective-permute-start(f16[96,3200]{1,0:T(8,128)(2,1)S(1)} %get-tuple-element.202), channel_id=1, source_target_pairs={{0,8},{8,16},{16,24},{24,0},{1,9},{9,17},{17,25},{25,1},{2,10},{10... | collective-permute-start | bytes 1843208 | tf_op jit(solution)/shard_map/ppermute | solution.py:344
  711.5 110.0 %copy-start.88 = (f32[32]{0:T(128)S(1)}, f32[32]{0:T(128)}, u32[]{:S(2)}) copy-start(f32[32]{0:T(128)} %get-tuple-element.215) | copy-start | bytes 388
  812.2 40.4 %collective-permute-start.20 = (bf16[24,8448]{1,0:T(8,128)(2,1)S(1)}, bf16[24,8448]{1,0:T(8,128)(2,1)S(1)}, u32[]{:S(2)}, u32[]{:S(2)}) collective-permute-start(bf16[24,8448]{1,0:T(8,128)(2,1)S(1)} %get-tuple-element.211), channel_id=1, source_target_pairs={{0,24},{8,0},{16,8},{24,16},{1,25},{9,1},{17,9},{25,17},{2,26},{10... | collective-permute-start | bytes 1216520 | tf_op jit(solution)/shard_map/ppermute | solution.py:316
  812.3 42.4 %collective-permute-start.19 = (bf16[24,8448]{1,0:T(8,128)(2,1)S(1)}, bf16[24,8448]{1,0:T(8,128)(2,1)S(1)}, u32[]{:S(2)}, u32[]{:S(2)}) collective-permute-start(bf16[24,8448]{1,0:T(8,128)(2,1)S(1)} %get-tuple-element.212), channel_id=1, source_target_pairs={{0,16},{8,24},{16,0},{24,8},{1,17},{9,25},{17,1},{25,9},{2,18},{10... | collective-permute-start | bytes 1216520 | tf_op jit(solution)/shard_map/ppermute | solution.py:316
  818.8 35.9 %collective-permute-start.18 = (bf16[24,8448]{1,0:T(8,128)(2,1)S(1)}, bf16[24,8448]{1,0:T(8,128)(2,1)S(1)}, u32[]{:S(2)}, u32[]{:S(2)}) collective-permute-start(bf16[24,8448]{1,0:T(8,128)(2,1)S(1)} %get-tuple-element.213), channel_id=1, source_target_pairs={{0,8},{8,16},{16,24},{24,0},{1,9},{9,17},{17,25},{25,1},{2,10},{10... | collective-permute-start | bytes 1216520 | tf_op jit(solution)/shard_map/ppermute | solution.py:316
  890.5 21.0 %slice-start.5 = ((s8[4915200]{0:T(1024)(128)(4,1)}), s8[4194304]{0:T(1024)(128)(4,1)S(1)}, s32[]{:S(2)}) async-start(s8[4915200]{0:T(1024)(128)(4,1)} %bitcast.219), calls=%async_computation.11 | async-start | bytes 8388608
  (84 other events, 537.7 us)
Sparse Core Ops, SparseCore 0:
  38.4 155.7 all-gather.2
  196.6 97.7 all-gather.4
  481.4 68.8 reduce-scatter.2
  695.8 70.7 reduce-scatter.4

commit v8 on v7

--- a/solution.py
+++ b/solution.py
@@ -894,7 +894,7 @@
 
     block_low = jnp.concatenate(
         [layer_w.astype(BF), ada_w.astype(BF).reshape(layer_w.shape[0], -1)], axis=1)
-    block_low, head_low, ints_all = together(block_low, head_w.astype(BF), ints_all)
+    head_low, ints_all = together(head_w.astype(BF), ints_all)
     layer_all = lax.all_gather(block_low, ALL, axis=0, tiled=True)
 
     piece_for = lambda k: lax.dynamic_slice_in_dim(head_low, k * SEGMENT, SEGMENT, 1)
@@ -1010,25 +1010,15 @@
     d_gate_a = jnp.sum(d_x1 * branch, axis=0)
     d_branch = (d_x1 * gate_a).astype(BF)
     d_wout = matmul_tn(att, d_branch)
-    d_att, *from_xy = together(matmul_nt(d_branch, w_o).astype(BF), *from_x, *from_y)
-    def over_cores(gradient):
-        width = gradient.shape[1]
-        parts = jnp.transpose(gradient.reshape(nz, nx, ny, nc, -1, width), (3, 1, 2, 0, 4, 5))
-        parts = parts.reshape(nc, -1, width)
-        got = exchange(lambda k: pick(parts, k), ("c",))
-        return sum(piece.astype(F32) for _, piece in got).astype(BF)
+    d_att = matmul_nt(d_branch, w_o).astype(BF)
+    d_k, d_v, d_qkv_m = attend_back(q, k_u, k_m, kv_u, qkv_m, tables, mask, lse_a, d_att)
+    d_k, *from_xy = together(d_k, *from_x, *from_y)
 
     over_plane = lambda a: lax.psum_scatter(a, ("x", "y"), scatter_dimension=0, tiled=True)
     own_xy, from_xy = (
         spread_parts(added(own_x, from_xy[: nx - 1]), 0, "y"),
         spread_parts(added(own_y, from_xy[nx - 1 :]), 0, "x"),
     )
-    d_k, d_v, d_qkv_m = attend_back(q, k_u, k_m, kv_u, qkv_m, tables, mask, lse_a, d_att)
-    d_k, *arrivals = together(d_k, *own_xy[1], *from_xy[1])
-    head_sum = jnp.concatenate(
-        [added(own_xy[0], arrivals[: ny - 1]), added(from_xy[0], arrivals[ny - 1 :])], axis=0)
-    d_k, head_sum = together(d_k, head_sum)
-    head_own, head_parts = spread_parts(head_sum, 0, "z")
     d_kv = jnp.concatenate([d_k, d_v], axis=1)
     d_wkv = matmul_tn(a_u, d_kv)
     d_row_m = d_qkv_m[:3].reshape(3 * D)
@@ -1043,8 +1033,16 @@
     d_x0_u = norm_back(d_a_u * scaling, normed_u, inv_u)
     d_mask = jnp.sum(d_x1, axis=0) + norm_back(d_a_m * scaling, normed_0, inv_0)[0]
 
-    chip_sum = over_cores(jnp.concatenate(
-        [d_wkv.astype(BF), d_wout.astype(BF), d_up.astype(BF), d_down.astype(BF)], axis=1))
+    d_block = jnp.concatenate(
+        [d_wkv.astype(BF), d_wout.astype(BF), d_up.astype(BF), d_down.astype(BF)], axis=1)
+    width = d_block.shape[1]
+    d_block = jnp.transpose(d_block.reshape(nz, nx, ny, nc, -1, width), (3, 1, 2, 0, 4, 5))
+    d_block, *arrivals = together(d_block.reshape(nc, -1, width), *own_xy[1], *from_xy[1])
+    head_sum = jnp.concatenate(
+        [added(own_xy[0], arrivals[: ny - 1]), added(from_xy[0], arrivals[ny - 1 :])], axis=0)
+    head_own, head_parts = spread_parts(head_sum, 0, "z")
+    got = exchange(lambda k: pick(d_block, k), ("c",))
+    chip_sum = sum(piece.astype(F32) for _, piece in got).astype(BF)
 
     small = jnp.concatenate([d_shift_a, d_scale_a, d_gate_a, d_shift_m, d_scale_m, d_gate_m,
                              d_gain_a, d_gain_m, d_gain_f, d_mask,
@@ -1054,7 +1052,6 @@
     small = jnp.pad(small, ((0, -count_small % 8), (0, 0)))
 
     sent = d_x0_u.astype(BF).T.reshape(nz * nx, table_width, free_count)
-    sent, chip_sum = together(sent, chip_sum)
     plane_sum = over_plane(chip_sum)
     sent, *head_parts = together(sent, *head_parts)
 

time: 943 us -> 948 us (level)
  waiting for transfers between devices: 183 us -> 138 us
  Pallas kernels: 388 us -> 417 us
  starting transfers between devices: 24 us -> 43.9 us
    all_gather x1, waiting for transfers between devices: 29.6 us -> 0.02 us  [local(): layer_all = lax.all_gather(block_low, ALL, axis=0, tiled=True)]
    ppermute x7, waiting for transfers between devices: 76.5 us -> 56.8 us  [send_parts(): lax.ppermute(part, axis, [(i, (i + step) % n) for i in range(n)])]
    ppermute x14, starting transfers between devices: 16.2 us -> 34.5 us  [exchange(): moved = lax.ppermute(piece, axes, [(i, (i + step) % n) for i in range(n)])]
    pallas_call x1, Pallas kernels: 59.1 us -> 72.8 us  [fetch_blocks(): pl.pallas_call(functools.partial(fetch_kernel, sizes), out_shape=jax.Shap...]
    pallas_call x1, Pallas kernels: 47.8 us -> 58.2 us  [spread_blocks(): pl.pallas_call(functools.partial(spread_kernel, sizes), out_shape=[jax.Sh...]
    unnamed x225 -> x229, local copies, waits for them, and re-layouts: 19.4 us -> 15.6 us
  transfers between devices with their start and end apart: 25 -> 25, of which waited for: 11 -> 10; matrix products, arithmetic and copies ran while one was open for 20% -> 22% of each run, Pallas kernels for 22% -> 27%
where the time goes in v8:
time: 948 us; the launch traced here: 938 us
  Pallas kernels  417 us (44%)
  waiting for transfers between devices  138 us (15%)
  matrix products  124 us (13%)
  other arithmetic  110 us (12%)
  local copies, waits for them, and re-layouts  78.3 us (8%)
  starting transfers between devices  43.9 us (5%)
  between operations  27.2 us (3%)
    ppermute x14, waiting for transfers between devices, exchange(): moved = lax.ppermute(piece, axes, [(i, (i + step) % n) for i in range(n)])  81.5 us
    pallas_call x1, Pallas kernels, head_logits(): pl.pallas_call(logits_kernel, out_shape=[jax.ShapeDtypeStruct((segments,...  73.2 us
    pallas_call x1, Pallas kernels, fetch_blocks(): pl.pallas_call(functools.partial(fetch_kernel, sizes), out_shape=jax.Shap...  72.8 us
    dot_general x15, matrix products, dot(): lax.dot_general(a, b, ((contract[0], contract[1]), ((), ())), preferred_e...  71.1 us
    pallas_call x1, Pallas kernels, head_rows_back(): pl.pallas_call(rows_back_kernel, out_shape=[jax.ShapeDtypeStruct(e.shape,...  67.7 us
    pallas_call x1, Pallas kernels, spread_blocks(): pl.pallas_call(functools.partial(spread_kernel, sizes), out_shape=[jax.Sh...  58.2 us
    ppermute x7, waiting for transfers between devices, send_parts(): lax.ppermute(part, axis, [(i, (i + step) % n) for i in range(n)])  56.8 us
    dot_general x1, matrix products, local(): jnp.einsum('rd,yrv->ydv', rows, d_logits, preferred_element_type=F32)  50.6 us
  transfers between devices with their start and end apart: 25, of which 10 were waited for; matrix products, arithmetic and copies ran while one was open for 22% of the time, Pallas kernels for 27%

profile of v8, /device:TPU:0, one launch (start us, length us, event | category | flops | bytes accessed | tf_op | source)
XLA Modules:
  0.0 938.1 jit_solution(8641715199761813707)
XLA Ops:
  13.8 2.6 convert_element_type.255
  17.0 19.0 %share0.1 = (s32[4,2,2,2,16,128]{5,4,3,2,1,0:T(8,128)}, f32[4,2,2,2,8,128]{5,4,3,2,1,0:T(8,128)}) custom-call(s32[16,128]{1,0:T(8,128)} %pad.18.refs_0_, f32[8,128]{1,0:T(8,128)} %pad_convert_fusion.refs_1_), custom_call_target="tpu_custom_call" | custom-call | tf_op jit(solution)/shard_map/share0/pallas_call | solution.py:104
  37.5 3.6 collective-permute-start.2
  51.0 26.4 %gather_rows.1 = bf16[32,96,512]{2,1,0:T(8,128)(2,1)} custom-call(s32[32]{0:T(128)} %reduce_sum.395.low_ref, s32[32]{0:T(128)} %reduce_sum.397.high_ref, s32[32,512]{1,0:T(8,128)} %bitcast.249, f32[96,12800]{1,0:T(8,128)} %bitcast.220), custom_call_target="tpu_custom_call" | custom-call | bytes 134217728 | tf_op jit(solution)/shard_map/gather_rows/pallas_call | solution.py:403
  77.4 72.8 %fetch_blocks.1 = bf16[8,96,512]{2,1,0:T(8,128)(2,1)} custom-call(bf16[2,2,8,96,512]{4,3,2,1,0:T(8,128)(2,1)} %bitcast.225), custom_call_target="tpu_custom_call" | custom-call | bytes 134217728 | tf_op jit(solution)/shard_map/fetch_blocks/pallas_call | solution.py:194
  152.1 7.9 fusion.32.target_ref
  183.0 3.2 fusion.22.qm_ref.km_ref.vm_ref
  186.2 4.8 fusion.40.kv_ref.vv_ref
  191.7 18.5 %attend.1 = (bf16[512,768]{1,0:T(8,128)(2,1)}, bf16[512,768]{1,0:T(8,128)(2,1)}, bf16[512,768]{1,0:T(8,128)(2,1)}, bf16[512,768]{1,0:T(8,128)(2,1)}, f32[6,512,2]{2,1,0:T(8,128)}) custom-call(f32[512,1536]{1,0:T(8,128)} %fusion.40.kv_ref.vv_ref, f32[512,1536]{1,0:T(8,128)} %fusion.40.kv_ref.vv_ref, f32[16,2304]{1,0:T(8,128)} %fusion.22.qm_ref.km_ref.vm_ref, ...), custom_call_target="tpu_custom_call" | custom-call | flops 1207959552 | bytes 4718592 | tf_op jit(solution)/shard_map/attend/pallas_call | solution.py:555
  213.0 5.1 fusion.18
  218.2 9.6 %fusion.117 = (f32[512]{0:T(512)S(1)}, f32[512,768]{1,0:T(8,128)S(1)}, f32[512,768]{1,0:T(8,128)}) fusion(f32[768]{0:T(1024)S(1)} %get-tuple-element.147, f32[512,768]{1,0:T(8,128)S(1)} %get-tuple-element.236, f32[768]{0:T(1024)S(1)} %get-tuple-element.148, f32[768]{0:T(1024)S(1)} %add.567, bf16[768,9984]{1,0:T(8,128)(2,1)} %all-gather.3.cloned.1.call-done, ...), kind=kOutput, calls=%fused_computation.345 | convolution fusion | flops 2432040448 | bytes 15739904 | tf_op jit(solution)/shard_map/dot_general | solution.py:39
  229.9 19.8 %collective-permute-start.8 = (bf16[512,768]{1,0:T(8,128)(2,1)S(1)}, bf16[512,768]{1,0:T(8,128)(2,1)S(1)}, u32[]{:S(2)}, u32[]{:S(2)}) collective-permute-start(bf16[512,768]{1,0:T(8,128)(2,1)S(1)} %copy.207.refs_0_), channel_id=1, source_target_pairs={{0,24},{8,0},{16,8},{24,16},{1,25},{9,1},{17,9},{25,17},{2,26},{10... | collective-permute-start | bytes 2359304 | tf_op jit(solution)/shard_map/ppermute | solution.py:316
  251.1 16.5 %collective-permute-done.8.refs_6_ = bf16[512,768]{1,0:T(8,128)(2,1)S(1)} collective-permute-done((bf16[512,768]{1,0:T(8,128)(2,1)S(1)}, bf16[512,768]{1,0:T(8,128)(2,1)S(1)}, u32[]{:S(2)}, u32[]{:S(2)}) %collective-permute-start.8) | collective-permute-done | bytes 786464 | tf_op jit(solution)/shard_map/ppermute | solution.py:316
  267.7 49.1 %collective-permute-done.6.refs_4_ = bf16[512,768]{1,0:T(8,128)(2,1)S(1)} collective-permute-done((bf16[512,768]{1,0:T(8,128)(2,1)S(1)}, bf16[512,768]{1,0:T(8,128)(2,1)S(1)}, u32[]{:S(2)}, u32[]{:S(2)}) %collective-permute-start.6) | collective-permute-done | bytes 786464 | tf_op jit(solution)/shard_map/ppermute | solution.py:316
  320.5 73.2 %head_logits.1 = (bf16[2,4096,3200]{2,1,0:T(8,128)(2,1)}, f32[4096,4]{1,0:T(8,128)}, bf16[4096,768]{1,0:T(8,128)(2,1)}) custom-call(s32[8]{0:T(128)} %stack.50.places_ref, bf16[2,768,3200]{2,1,0:T(8,128)(2,1)} %bitcast.273, s32[4096,1]{1,0:T(8,128)} %fusion.32.target_ref, bf16[512,768]{1,0:T(8,128)(2,1)} %copy-done.25, ...), custom_call_target="tpu_custom_call" | custom-call | flops 40265318400 | bytes 52428800 | tf_op jit(solution)/shard_map/head_logits/pallas_call | solution.py:709
  397.3 11.5 %share4.1 = f32[4,2,4,32,128]{4,3,2,1,0:T(8,128)} custom-call(f32[4,32,128]{2,1,0:T(8,128)} %copy.225.refs_0_), custom_call_target="tpu_custom_call" | custom-call | tf_op jit(solution)/shard_map/share4/pallas_call | solution.py:104
  412.7 67.7 %head_rows_back.1 = (bf16[2,4096,3200]{2,1,0:T(8,128)(2,1)}, bf16[4096,768]{1,0:T(8,128)(2,1)}) custom-call(s32[8]{0:T(128)} %stack.50.places_ref, bf16[2,4096,3200]{2,1,0:T(8,128)(2,1)} %get-tuple-element.90.e_ref, bf16[2,768,3200]{2,1,0:T(8,128)(2,1)} %bitcast.274, s32[4096,1]{1,0:T(8,128)} %fusion.32.target_ref, ...), custom_call_target="tpu_custom_call", output_to_operand_aliasing={{0}: (1, {})} | custom-call | flops 40265318400 | bytes 104857600 | tf_op jit(solution)/shard_map/head_rows_back/pallas_call | solution.py:771
  483.8 50.6 %convolution_multiply_fusion = f32[2,3200,768]{1,2,0:T(8,128)} fusion(bf16[2,4096,3200]{2,1,0:T(8,128)(2,1)} %get-tuple-element.94, f32[]{:T(128)S(6)} %div.269, bf16[4096,768]{1,0:T(8,128)(2,1)} %get-tuple-element.95), kind=kOutput, calls=%fused_computation | convolution fusion | flops 40270233600 | bytes 78381056 | tf_op jit(solution)/shard_map/rd,yrv->ydv/dot_general | solution.py:986
  534.4 7.8 fusion.118
  542.2 3.7 copy-done.2
  559.8 9.3 fusion.7
  569.2 6.5 multiply_reduce_fusion.4
  581.1 3.0 convolution_convert_fusion.4.datt_ref
  584.1 23.9 %attend_back.1 = (bf16[512,768]{1,0:T(8,128)(2,1)}, bf16[512,768]{1,0:T(8,128)(2,1)}, f32[8,768]{1,0:T(8,128)}) custom-call(bf16[512,768]{1,0:T(8,128)(2,1)} %get-tuple-element.80.q_ref, bf16[512,768]{1,0:T(8,128)(2,1)} %get-tuple-element.81.ku_ref, bf16[512,768]{1,0:T(8,128)(2,1)} %get-tuple-element.82.km_ref, f32[512,1536]{1,0:T(8,128)} %fusion.40.kv_ref.vv_ref, ...), custom_call_target="tpu_custom_call" | custom-call | flops 3221225472 | bytes 5505024 | tf_op jit(solution)/shard_map/attend_back/pallas_call | solution.py:627
  608.0 6.8 convolution_convert_fusion.1
  614.8 8.1 convolution_convert_fusion
  625.0 3.0 convolution_convert_fusion.2
  628.0 2.6 bitcast_add_fusion.3
  631.9 4.5 bitcast_add_fusion.2
  641.0 4.2 pad_maximum_fusion
  645.2 3.3 copy.222
  648.5 17.8 %collective-permute-done.13 = f16[2,96,3200]{2,1,0:T(8,128)(2,1)S(1)} collective-permute-done((f16[2,96,3200]{2,1,0:T(8,128)(2,1)}, f16[2,96,3200]{2,1,0:T(8,128)(2,1)S(1)}, u32[]{:S(2)}, u32[]{:S(2)}) %collective-permute-start.13) | collective-permute-done | bytes 1228832 | tf_op jit(solution)/shard_map/ppermute | solution.py:344
  668.2 3.1 dynamic-slice_bitcast_fusion
  671.3 10.8 %collective-permute-done.17 = bf16[384,8448]{1,0:T(8,128)(2,1)} collective-permute-done((bf16[384,8448]{1,0:T(8,128)(2,1)}, bf16[384,8448]{1,0:T(8,128)(2,1)}, u32[]{:S(2)}, u32[]{:S(2)}) %collective-permute-start.17) | collective-permute-done | bytes 6488096 | tf_op jit(solution)/shard_map/ppermute | solution.py:316
  682.1 8.8 fusion
  692.4 3.1 fusion.53
  698.2 4.1 multiply_reduce_fusion.6
  716.7 11.0 %collective-permute-done.14 = f16[96,3200]{1,0:T(8,128)(2,1)S(1)} collective-permute-done((f16[96,3200]{1,0:T(8,128)(2,1)}, f16[96,3200]{1,0:T(8,128)(2,1)S(1)}, u32[]{:S(2)}, u32[]{:S(2)}) %collective-permute-start.14) | collective-permute-done | bytes 614432 | tf_op jit(solution)/shard_map/ppermute | solution.py:344
  727.7 26.1 %collective-permute-done.15 = f16[96,3200]{1,0:T(8,128)(2,1)} collective-permute-done((f16[96,3200]{1,0:T(8,128)(2,1)}, f16[96,3200]{1,0:T(8,128)(2,1)}, u32[]{:S(2)}, u32[]{:S(2)}) %collective-permute-start.15) | collective-permute-done | bytes 614432 | tf_op jit(solution)/shard_map/ppermute | solution.py:344
  753.8 58.2 %spread_blocks.1 = (bf16[2,2,8,96,512]{4,3,2,1,0:T(8,128)(2,1)}, f32[4,2,2,2,88,128]{5,4,3,2,1,0:T(8,128)}) custom-call(bf16[8,96,512]{2,1,0:T(8,128)(2,1)} %bitcast.237, f32[88,128]{1,0:T(8,128)} %pad.22.small_ref), custom_call_target="tpu_custom_call" | custom-call | bytes 134217728 | tf_op jit(solution)/shard_map/spread_blocks/pallas_call | solution.py:280
  813.6 3.2 collective-permute-start.20
  816.8 4.9 collective-permute-start.19
  822.8 32.0 %scatter_rows.1 = f32[96,12800]{1,0:T(8,128)} custom-call(s32[32]{0:T(128)} %reduce_sum.395.low_ref, s32[32]{0:T(128)} %reduce_sum.397.high_ref, s32[32,512]{1,0:T(8,128)} %bitcast.250, bf16[32,96,512]{2,1,0:T(8,128)(2,1)} %bitcast.236), custom_call_target="tpu_custom_call" | custom-call | bytes 134217728 | tf_op jit(solution)/shard_map/scatter_rows/pallas_call | solution.py:480
  854.9 2.5 collective-permute-done.19
  877.5 13.4 %share2.1 = f32[4,2,2,2,8,128]{5,4,3,2,1,0:T(8,128)} custom-call(f32[8,128]{1,0:T(8,128)} %broadcast_in_dim.144.refs_0_), custom_call_target="tpu_custom_call" | custom-call | tf_op jit(solution)/shard_map/share2/pallas_call | solution.py:104
  894.7 4.4 multiply_add_fusion.5
  899.1 16.5 %multiply_add_fusion = (f32[96,12800]{1,0:T(8,128)}, f32[96,12800]{1,0:T(8,128)}, f32[96,12800]{1,0:T(8,128)}, f32[96,12800]{1,0:T(8,128)}) fusion(f32[96,12800]{1,0:T(8,128)} %param.49, f32[]{:T(128)} %bitcast.90, f32[]{:T(128)S(6)} %sub.303, f32[96,12800]{1,0:T(8,128)} %param.46, f32[]{:T(128)} %bitcast.89, f32[]{:T(128)} %bitcast.88, f32[]{:T(128)S(6)} %min.13, ...), kind=kLoop, calls=%fused_computation.36 | loop fusion | flops 28262400 | bytes 44236824 | tf_op jit(solution)/shard_map/add | solution.py:847
  915.7 13.6 %fusion.11 = (f32[12800,96]{0,1:T(8,128)}, f32[96,12800]{1,0:T(8,128)}, f32[12800,96]{0,1:T(8,128)}, f32[12800,96]{0,1:T(8,128)}) fusion(f32[12800,96]{0,1:T(8,128)} %param.45, f32[]{:T(128)S(6)} %sub.303, f32[]{:T(128)} %bitcast.90, f32[]{:T(128)} %bitcast.89, f32[12800,96]{0,1:T(8,128)} %param.44, f32[]{:T(128)} %bitcast.88, f32[96,12800]{1,0:T(8,128)S(1)} %bitcast.208, ...), kind=kLoop, calls=%fused_computation.32 | loop fusion | flops 23347200 | bytes 44236820 | tf_op jit(solution)/shard_map/transpose | solution.py:1108
  (447 shorter events, 128.7 us)
Async XLA Ops:
  7.2 170.1 %all-gather.3.cloned.1.call-start = ((), (), s32[]{:S(2)}) async-start(), calls=%async_computation.2 | async-start | bytes 15814656 | tf_op jit(solution)/shard_map/all_gather | solution.py:898
  10.3 307.7 %all-gather.5.cloned.1.call-start = ((), (), s32[]{:S(2)}) async-start(), calls=%async_computation.3 | async-start | bytes 12288000 | tf_op jit(solution)/shard_map/all_gather | solution.py:962
  37.5 122.5 %collective-permute-start.2 = (bf16[96,3200]{1,0:T(8,128)(2,1)}, bf16[96,3200]{1,0:T(8,128)(2,1)}, u32[]{:S(2)}, u32[]{:S(2)}) collective-permute-start(bf16[96,3200]{1,0:T(8,128)(2,1)} %get-tuple-element.197), channel_id=1, source_target_pairs={{0,24},{8,0},{16,8},{24,16},{1,25},{9,1},{17,9},{25,17},{2,26},{10... | collective-permute-start | bytes 1843208 | tf_op jit(solution)/shard_map/ppermute | solution.py:316
  41.0 118.9 %collective-permute-start.1 = (bf16[96,3200]{1,0:T(8,128)(2,1)}, bf16[96,3200]{1,0:T(8,128)(2,1)}, u32[]{:S(2)}, u32[]{:S(2)}) collective-permute-start(bf16[96,3200]{1,0:T(8,128)(2,1)} %get-tuple-element.198), channel_id=1, source_target_pairs={{0,16},{8,24},{16,0},{24,8},{1,17},{9,25},{17,1},{25,9},{2,18},{10... | collective-permute-start | bytes 1843208 | tf_op jit(solution)/shard_map/ppermute | solution.py:316
  41.0 118.9 %collective-permute-start = (bf16[96,3200]{1,0:T(8,128)(2,1)}, bf16[96,3200]{1,0:T(8,128)(2,1)}, u32[]{:S(2)}, u32[]{:S(2)}) collective-permute-start(bf16[96,3200]{1,0:T(8,128)(2,1)} %get-tuple-element.199), channel_id=1, source_target_pairs={{0,8},{8,16},{16,24},{24,0},{1,9},{9,17},{17,25},{25,1},{2,10},{10... | collective-permute-start | bytes 1843208 | tf_op jit(solution)/shard_map/ppermute | solution.py:316
  46.9 363.7 %copy-start.35 = (f32[1,4,8,128]{3,1,2,0:T(4,128)}, f32[1,4,8,128]{3,1,2,0:T(4,128)S(1)}, u32[]{:S(2)}) copy-start(f32[1,4,8,128]{3,1,2,0:T(4,128)S(1)} %copy.231) | copy-start | bytes 49156
  152.1 34.2 %copy-start.4 = (f32[768,512]{0,1:T(8,128)}, f32[768,512]{0,1:T(8,128)S(1)}, u32[]{:S(2)}) copy-start(f32[768,512]{0,1:T(8,128)S(1)} %copy.185) | copy-start | bytes 4718596
  168.5 383.0 %reduce-scatter.3.cloned.1.call-start = ((), (), s32[]{:S(2)}) async-start(), calls=%async_computation.4 | async-start | bytes 7077888 | tf_op jit(solution)/shard_map/reduce_scatter | solution.py:981
  171.0 42.0 %copy-start.70 = (f32[768]{0:T(1024)}, f32[768]{0:T(1024)S(1)}, u32[]{:S(2)}) copy-start(f32[768]{0:T(1024)S(1)} %mul.881) | copy-start | bytes 9220
  172.6 45.6 %copy-start.44 = (f32[768]{0:T(1024)}, f32[768]{0:T(1024)S(1)}, u32[]{:S(2)}) copy-start(f32[768]{0:T(1024)S(1)} %add.567) | copy-start | bytes 9220
  172.7 55.4 %copy-start.42 = (f32[768]{0:T(1024)}, f32[768]{0:T(1024)S(1)}, u32[]{:S(2)}) copy-start(f32[768]{0:T(1024)S(1)} %mul.899) | copy-start | bytes 9220
  182.9 30.0 %copy-start.66 = (f32[768]{0:T(1024)}, f32[768]{0:T(1024)S(1)}, u32[]{:S(2)}) copy-start(f32[768]{0:T(1024)S(1)} %get-tuple-element.146) | copy-start | bytes 9220
  182.9 30.1 %copy-start.87 = (f32[768]{0:T(1024)}, f32[768]{0:T(1024)S(1)}, u32[]{:S(2)}) copy-start(f32[768]{0:T(1024)S(1)} %get-tuple-element.151) | copy-start | bytes 9220
  182.9 35.2 %copy-start.46 = (f32[768]{0:T(1024)}, f32[768]{0:T(1024)S(1)}, u32[]{:S(2)}) copy-start(f32[768]{0:T(1024)S(1)} %get-tuple-element.148) | copy-start | bytes 9220
  183.0 35.2 %copy-start.85 = (f32[768]{0:T(1024)}, f32[768]{0:T(1024)S(1)}, u32[]{:S(2)}) copy-start(f32[768]{0:T(1024)S(1)} %get-tuple-element.147) | copy-start | bytes 9220
  229.8 90.7 %copy-start.25 = (bf16[512,768]{1,0:T(8,128)(2,1)}, bf16[512,768]{1,0:T(8,128)(2,1)S(1)}, u32[]{:S(2)}) copy-start(bf16[512,768]{1,0:T(8,128)(2,1)S(1)} %copy.207.refs_0_) | copy-start | bytes 2359300
  229.9 37.8 %collective-permute-start.8 = (bf16[512,768]{1,0:T(8,128)(2,1)S(1)}, bf16[512,768]{1,0:T(8,128)(2,1)S(1)}, u32[]{:S(2)}, u32[]{:S(2)}) collective-permute-start(bf16[512,768]{1,0:T(8,128)(2,1)S(1)} %copy.207.refs_0_), channel_id=1, source_target_pairs={{0,24},{8,0},{16,8},{24,16},{1,25},{9,1},{17,9},{25,17},{2,26},{10... | collective-permute-start | bytes 2359304 | tf_op jit(solution)/shard_map/ppermute | solution.py:316
  249.6 67.1 %collective-permute-start.6 = (bf16[512,768]{1,0:T(8,128)(2,1)S(1)}, bf16[512,768]{1,0:T(8,128)(2,1)S(1)}, u32[]{:S(2)}, u32[]{:S(2)}) collective-permute-start(bf16[512,768]{1,0:T(8,128)(2,1)S(1)} %copy.207.refs_0_), channel_id=1, source_target_pairs={{0,16},{8,24},{16,0},{24,8},{1,17},{9,25},{17,1},{25,9},{2,18},{10... | collective-permute-start | bytes 2359304 | tf_op jit(solution)/shard_map/ppermute | solution.py:316
  251.1 65.7 %collective-permute-start.4 = (bf16[512,768]{1,0:T(8,128)(2,1)S(1)}, bf16[512,768]{1,0:T(8,128)(2,1)}, u32[]{:S(2)}, u32[]{:S(2)}) collective-permute-start(bf16[512,768]{1,0:T(8,128)(2,1)S(1)} %copy.207.refs_0_), channel_id=1, source_target_pairs={{0,8},{8,16},{16,24},{24,0},{1,9},{9,17},{17,25},{25,1},{2,10},{10... | collective-permute-start | bytes 2359304 | tf_op jit(solution)/shard_map/ppermute | solution.py:316
  251.1 66.9 %collective-permute-start.3 = (bf16[512,768]{1,0:T(8,128)(2,1)S(1)}, bf16[512,768]{1,0:T(8,128)(2,1)}, u32[]{:S(2)}, u32[]{:S(2)}) collective-permute-start(bf16[512,768]{1,0:T(8,128)(2,1)S(1)} %copy.207.refs_0_), channel_id=1, source_target_pairs={{0,1},{1,0},{2,3},{3,2},{4,5},{5,4},{6,7},{7,6},{8,9},{9,8},{10,11... | collective-permute-start | bytes 2359304 | tf_op jit(solution)/shard_map/ppermute | solution.py:316
  267.6 52.9 %copy-start.93 = (bf16[512,768]{1,0:T(8,128)(2,1)}, bf16[512,768]{1,0:T(8,128)(2,1)S(1)}, u32[]{:S(2)}) copy-start(bf16[512,768]{1,0:T(8,128)(2,1)S(1)} %collective-permute-done.8.refs_6_) | copy-start | bytes 2359300
  267.6 50.3 %collective-permute-start.9 = (bf16[512,768]{1,0:T(8,128)(2,1)S(1)}, bf16[512,768]{1,0:T(8,128)(2,1)}, u32[]{:S(2)}, u32[]{:S(2)}) collective-permute-start(bf16[512,768]{1,0:T(8,128)(2,1)S(1)} %collective-permute-done.8.refs_6_), channel_id=1, source_target_pairs={{0,1},{1,0},{2,3},{3,2},{4,5},{5,4},{6,7},{7,6},{8,9},{9,8},{10,11... | collective-permute-start | bytes 2359304 | tf_op jit(solution)/shard_map/ppermute | solution.py:316
  316.8 2.8 collective-permute-start.7
  316.8 3.7 collective-permute-start.5
  410.4 70.0 %copy-start.37 = (f32[4096]{0:T(1024)}, f32[4096]{0:T(1024)S(1)}, u32[]{:S(2)}) copy-start(f32[4096]{0:T(1024)S(1)} %get-tuple-element.139) | copy-start | bytes 49156
  410.7 69.8 %copy-start.38 = (f32[4096]{0:T(1024)}, f32[4096]{0:T(1024)S(1)}, u32[]{:S(2)}) copy-start(f32[4096]{0:T(1024)S(1)} %get-tuple-element.182) | copy-start | bytes 49156
  480.5 331.6 %reduce-scatter.5.cloned.1.call-start = ((), (), s32[]{:S(2)}) async-start(), calls=%async_computation.5 | async-start | bytes 8110080 | tf_op jit(solution)/shard_map/reduce_scatter | solution.py:1017
  557.0 66.0 %collective-permute-start.10 = (f16[2,2,96,3200]{3,2,1,0:T(8,128)(2,1)}, f16[2,2,96,3200]{3,2,1,0:T(8,128)(2,1)}, u32[]{:S(2)}, u32[]{:S(2)}) collective-permute-start(f16[2,2,96,3200]{3,2,1,0:T(8,128)(2,1)} %fusion.26), channel_id=1, source_target_pairs={{0,4},{4,0},{1,5},{5,1},{2,6},{6,2},{3,7},{7,3},{8,12},{12,8},{9,1... | collective-permute-start | bytes 7372808 | tf_op jit(solution)/shard_map/ppermute | solution.py:344
  558.5 64.5 %collective-permute-start.11 = (f16[2,2,96,3200]{3,2,1,0:T(8,128)(2,1)}, f16[2,2,96,3200]{3,2,1,0:T(8,128)(2,1)}, u32[]{:S(2)}, u32[]{:S(2)}) collective-permute-start(f16[2,2,96,3200]{3,2,1,0:T(8,128)(2,1)} %fusion.27), channel_id=1, source_target_pairs={{0,2},{2,0},{1,3},{3,1},{4,6},{6,4},{5,7},{7,5},{8,10},{10,8},{9,1... | collective-permute-start | bytes 7372808 | tf_op jit(solution)/shard_map/ppermute | solution.py:344
  584.1 23.9 %copy-start.67 = (f32[768]{0:T(1024)S(1)}, f32[768]{0:T(1024)}, u32[]{:S(2)}) copy-start(f32[768]{0:T(1024)} %copy-done.66) | copy-start | bytes 9220
  584.1 23.9 %copy-start.71 = (f32[768]{0:T(1024)S(1)}, f32[768]{0:T(1024)}, u32[]{:S(2)}) copy-start(f32[768]{0:T(1024)} %copy-done.70) | copy-start | bytes 9220
  584.1 23.9 %copy-start.88 = (f32[768]{0:T(1024)S(1)}, f32[768]{0:T(1024)}, u32[]{:S(2)}) copy-start(f32[768]{0:T(1024)} %copy-done.87) | copy-start | bytes 9220
  608.0 20.0 %slice-start.5 = ((s8[9830400]{0:T(1024)(128)(4,1)}), s8[4194304]{0:T(1024)(128)(4,1)S(1)}, s32[]{:S(2)}) async-start(s8[9830400]{0:T(1024)(128)(4,1)} %bitcast.211), calls=%async_computation.11 | async-start | bytes 8388608
  637.6 28.6 %collective-permute-start.13 = (f16[2,96,3200]{2,1,0:T(8,128)(2,1)}, f16[2,96,3200]{2,1,0:T(8,128)(2,1)S(1)}, u32[]{:S(2)}, u32[]{:S(2)}) collective-permute-start(f16[2,96,3200]{2,1,0:T(8,128)(2,1)} %fusion.44), channel_id=1, source_target_pairs={{0,4},{4,0},{1,5},{5,1},{2,6},{6,2},{3,7},{7,3},{8,12},{12,8},{9,1... | collective-permute-start | bytes 3686408 | tf_op jit(solution)/shard_map/ppermute | solution.py:344
  639.5 28.7 %collective-permute-start.12 = (f16[2,96,3200]{2,1,0:T(8,128)(2,1)}, f16[2,96,3200]{2,1,0:T(8,128)(2,1)}, u32[]{:S(2)}, u32[]{:S(2)}) collective-permute-start(f16[2,96,3200]{2,1,0:T(8,128)(2,1)} %fusion.43), channel_id=1, source_target_pairs={{0,2},{2,0},{1,3},{3,1},{4,6},{6,4},{5,7},{7,5},{8,10},{10,8},{9,1... | collective-permute-start | bytes 3686408 | tf_op jit(solution)/shard_map/ppermute | solution.py:344
  648.4 22.8 %copy-start = (bf16[4,2,2,2,24,8448]{5,4,0,2,1,3:T(8,128)(2,1)}, bf16[4,2,2,2,24,8448]{5,4,0,2,1,3:T(8,128)(2,1)S(1)}, u32[]{:S(2)}) copy-start(bf16[4,2,2,2,24,8448]{5,4,0,2,1,3:T(8,128)(2,1)S(1)} %copy.222) | copy-start | bytes 38928388
  671.3 10.8 %collective-permute-start.17 = (bf16[384,8448]{1,0:T(8,128)(2,1)}, bf16[384,8448]{1,0:T(8,128)(2,1)}, u32[]{:S(2)}, u32[]{:S(2)}) collective-permute-start(bf16[384,8448]{1,0:T(8,128)(2,1)} %dynamic-slice_bitcast_fusion), channel_id=1, source_target_pairs={{0,1},{1,0},{2,3},{3,2},{4,5},{5,4},{6,7},{7,6},{8,9},{9,8},{10,11... | collective-permute-start | bytes 19464200 | tf_op jit(solution)/shard_map/ppermute | solution.py:316
  708.9 18.8 %collective-permute-start.14 = (f16[96,3200]{1,0:T(8,128)(2,1)}, f16[96,3200]{1,0:T(8,128)(2,1)S(1)}, u32[]{:S(2)}, u32[]{:S(2)}) collective-permute-start(f16[96,3200]{1,0:T(8,128)(2,1)} %get-tuple-element.190), channel_id=1, source_target_pairs={{0,8},{8,16},{16,24},{24,0},{1,9},{9,17},{17,25},{25,1},{2,10},{10... | collective-permute-start | bytes 1843208 | tf_op jit(solution)/shard_map/ppermute | solution.py:344
  710.9 42.9 %collective-permute-start.15 = (f16[96,3200]{1,0:T(8,128)(2,1)}, f16[96,3200]{1,0:T(8,128)(2,1)}, u32[]{:S(2)}, u32[]{:S(2)}) collective-permute-start(f16[96,3200]{1,0:T(8,128)(2,1)} %get-tuple-element.191), channel_id=1, source_target_pairs={{0,16},{8,24},{16,0},{24,8},{1,17},{9,25},{17,1},{25,9},{2,18},{10... | collective-permute-start | bytes 1843208 | tf_op jit(solution)/shard_map/ppermute | solution.py:344
  713.3 40.5 %collective-permute-start.16 = (f16[96,3200]{1,0:T(8,128)(2,1)}, f16[96,3200]{1,0:T(8,128)(2,1)}, u32[]{:S(2)}, u32[]{:S(2)}) collective-permute-start(f16[96,3200]{1,0:T(8,128)(2,1)} %get-tuple-element.192), channel_id=1, source_target_pairs={{0,24},{8,0},{16,8},{24,16},{1,25},{9,1},{17,9},{25,17},{2,26},{10... | collective-permute-start | bytes 1843208 | tf_op jit(solution)/shard_map/ppermute | solution.py:344
  716.7 105.9 %copy-start.92 = (f32[32]{0:T(128)S(1)}, f32[32]{0:T(128)}, u32[]{:S(2)}) copy-start(f32[32]{0:T(128)} %get-tuple-element.205) | copy-start | bytes 388
  727.7 84.4 %copy-start.29 = (f16[96,3200]{1,0:T(8,128)(2,1)}, f16[96,3200]{1,0:T(8,128)(2,1)S(1)}, u32[]{:S(2)}) copy-start(f16[96,3200]{1,0:T(8,128)(2,1)S(1)} %collective-permute-done.14) | copy-start | bytes 1843204
  813.6 41.3 %collective-permute-start.20 = (bf16[24,8448]{1,0:T(8,128)(2,1)S(1)}, bf16[24,8448]{1,0:T(8,128)(2,1)S(1)}, u32[]{:S(2)}, u32[]{:S(2)}) collective-permute-start(bf16[24,8448]{1,0:T(8,128)(2,1)S(1)} %get-tuple-element.201), channel_id=1, source_target_pairs={{0,24},{8,0},{16,8},{24,16},{1,25},{9,1},{17,9},{25,17},{2,26},{10... | collective-permute-start | bytes 1216520 | tf_op jit(solution)/shard_map/ppermute | solution.py:316
  816.8 40.6 %collective-permute-start.19 = (bf16[24,8448]{1,0:T(8,128)(2,1)S(1)}, bf16[24,8448]{1,0:T(8,128)(2,1)S(1)}, u32[]{:S(2)}, u32[]{:S(2)}) collective-permute-start(bf16[24,8448]{1,0:T(8,128)(2,1)S(1)} %get-tuple-element.202), channel_id=1, source_target_pairs={{0,16},{8,24},{16,0},{24,8},{1,17},{9,25},{17,1},{25,9},{2,18},{10... | collective-permute-start | bytes 1216520 | tf_op jit(solution)/shard_map/ppermute | solution.py:316
  821.7 35.7 %collective-permute-start.18 = (bf16[24,8448]{1,0:T(8,128)(2,1)S(1)}, bf16[24,8448]{1,0:T(8,128)(2,1)S(1)}, u32[]{:S(2)}, u32[]{:S(2)}) collective-permute-start(bf16[24,8448]{1,0:T(8,128)(2,1)S(1)} %get-tuple-element.203), channel_id=1, source_target_pairs={{0,8},{8,16},{16,24},{24,0},{1,9},{9,17},{17,25},{25,1},{2,10},{10... | collective-permute-start | bytes 1216520 | tf_op jit(solution)/shard_map/ppermute | solution.py:316
  874.4 20.3 %copy-start.22 = (f32[24,1536]{1,0:T(8,128)S(1)}, f32[24,1536]{1,0:T(8,128)}, u32[]{:S(2)}) copy-start(f32[24,1536]{1,0:T(8,128)} %copy-done.21) | copy-start | bytes 442372
  894.7 21.0 %slice-start = ((s8[4915200]{0:T(1024)(128)(4,1)}), s8[4194304]{0:T(1024)(128)(4,1)S(1)}, s32[]{:S(2)}) async-start(s8[4915200]{0:T(1024)(128)(4,1)} %bitcast.207), calls=%async_computation.6 | async-start | bytes 8388608
  894.7 21.0 %slice-start.8 = ((s8[4915200]{0:T(1024)(128)(4,1)}), s8[4194304]{0:T(1024)(128)(4,1)S(1)}, s32[]{:S(2)}) async-start(s8[4915200]{0:T(1024)(128)(4,1)} %bitcast.221), calls=%async_computation.14 | async-start | bytes 8388608
  (86 other events, 594.2 us)
Sparse Core Ops, SparseCore 0:
  11.6 163.6 all-gather.2
  177.7 109.2 all-gather.4
  480.6 69.8 reduce-scatter.2
  691.1 72.1 reduce-scatter.4
